TPU v7x, 32 devices: a whole 2x2x4 slice. The times are simulated.
32 devices in a mesh: leaf: 8 (over z, core), grp: 4 (over y, x).
Axes of the slice: x: 2, y: 2, z: 4, core: 2. Of those that a mesh axis runs over, the one named last changes fastest.
Arguments:
- leaf_rhs: bfloat16 [32768, 512], P(('leaf', 'grp')), may hold values from -6 to 6
- leaf_inv: bfloat16 [32768, 4096], P(('leaf', 'grp')), may hold values from -1 to 1, as said below
- ordering: int32 [8, 4096], P('leaf'), may hold values from 0 to 4095, each once within a row
- leaf_dinv: bfloat16 [32768], P(('leaf', 'grp')), may hold values from -2 to 2, as said below
- leaf_link: bfloat16 [32768, 32], P(('leaf', 'grp')), may hold values from -0.0625 to 0.0625
- sep_rhs: bfloat16 [3, 512, 128], P(None, 'grp', 'leaf'), may hold values from -6 to 6
- sep_factor: bfloat16 [128, 416], P(('leaf', 'grp')), may hold values from -1 to 1, as said below
- sep_dinv: bfloat16 [3, 128], P(None, 'leaf'), may hold values from -2 to 2, as said below
Outputs:
- leaf_solution: float32 [32768, 512], P(('leaf', 'grp'))
- sep_solution: float32 [3, 512, 128], P(None, 'grp', 'leaf')
Inputs may be any that keep to these rules, and one draw needn't show every extreme that they name: Within each leaf's 4096 rows, leaf_inv is unit lower triangular. `sep_factor`: each W block is unit lower triangular within its separator. `leaf_dinv`: every entry has magnitude 0.5 or more. `sep_dinv`: every entry has magnitude 0.5 or more.
All inputs are finite; a program needn't handle non-finite values.
Results may differ from a plain program's by a relative error of at most 0.013.
Values may be sent and summed in bfloat16 or wider, within the bound.
No kernel may reach another device: no remote copies, remote signals or barrier semaphores. Data moves between devices by JAX's collectives and lax.ppermute only.
A program may use at most 128 MiB of HBM per device.

v0:
```python
import jax
import jax.numpy as jnp
from jax import lax
from jax.sharding import PartitionSpec as P


def from_partner(block, axis, distance):
    count = lax.axis_size(axis)
    route = []
    for low in range(count):
        high = low | 1 << distance
        if high != low and high < count:
            route += [(low, high), (high, low)]
    return lax.ppermute(block, axis, route)


def partner(values, level_bit):
    return from_partner(values.astype(jnp.bfloat16), "leaf", level_bit).astype(values.dtype)


def leaf_bit(level_bit):
    return jnp.right_shift(lax.axis_index("leaf"), level_bit) % 2


def spread(values, first_bit, last_bit):
    for level_bit in range(first_bit, last_bit):
        partner_rows = partner(values.astype(jnp.float32), level_bit).astype(jnp.bfloat16)
        low_first = jnp.concatenate([values, partner_rows], axis=-1)
        high_first = jnp.concatenate([partner_rows, values], axis=-1)
        values = jnp.where(leaf_bit(level_bit) == 0, low_first, high_first)
    return values


def halve_sum(values, bit_list):
    for level_bit in bit_list:
        half_width = values.shape[-1] // 2
        low_half = values[..., :half_width]
        high_half = values[..., half_width:]
        is_upper = leaf_bit(level_bit) == 1
        keep_half = jnp.where(is_upper, high_half, low_half)
        send_half = jnp.where(is_upper, low_half, high_half)
        values = keep_half + partner(send_half, level_bit)
    return values


def group_rows(values):
    return lax.all_gather(values, "grp", axis=0, tiled=True)


def level_offset(sep_block, tree_level):
    if tree_level >= 2:
        return sep_block * (2 ** (tree_level + 1) - 6)
    return 0


def level_width(sep_block, tree_level):
    if tree_level >= 2:
        return 2 * sep_block * 2**tree_level
    return sep_block * 2**tree_level


def local(leaf_rhs, leaf_inv, ordering, leaf_dinv, leaf_link, sep_rhs, sep_factor, sep_dinv):
    levels = sep_rhs.shape[0]
    sep_block = sep_rhs.shape[2]
    inverse = jnp.argsort(ordering[0])
    picked = jnp.take(leaf_inv, inverse, axis=1)
    leaf_y = jnp.dot(
        picked,
        lax.all_gather(leaf_rhs, "grp", axis=0, tiled=True),
        preferred_element_type=jnp.float32,
    )
    partial_sum = jnp.einsum("rk,rc->kc", leaf_rhs, leaf_link, preferred_element_type=jnp.float32)
    crossing = lax.psum_scatter(
        partial_sum.astype(jnp.bfloat16), "grp", scatter_dimension=0, tiled=True
    ).astype(jnp.float32)
    leaf_z = (leaf_dinv.astype(jnp.float32)[:, None] * leaf_y).astype(jnp.bfloat16)
    crossing = halve_sum(crossing, [0])
    sep_r = (sep_rhs[0].astype(jnp.float32) - crossing).astype(jnp.bfloat16)
    gathered = group_rows(sep_factor)

    def level_rows(tree_level):
        offset = level_offset(sep_block, tree_level)
        return lax.slice_in_dim(
            gathered, offset, offset + level_width(sep_block, tree_level), axis=1
        )

    z_blocks = []
    full_prev = sep_r
    for tree_level in range(1, levels + 1):
        rows_here = level_rows(tree_level)
        size_here = sep_block * 2**tree_level
        if tree_level >= 2:
            children = spread(full_prev, tree_level - 1, tree_level)
            link_rows = rows_here[:, size_here:]
            coupled = jnp.einsum(
                "kc,qc->kq", children, link_rows, preferred_element_type=jnp.float32
            )
            sep_r = (sep_rhs[tree_level - 1].astype(jnp.float32) - coupled).astype(jnp.bfloat16)
        full_prev = spread(sep_r, 0, tree_level)
        sep_y = jnp.einsum(
            "kc,qc->kq", full_prev, rows_here[:, :size_here], preferred_element_type=jnp.float32
        )
        z_blocks.append(
            (sep_dinv[tree_level - 1].astype(jnp.float32)[None, :] * sep_y).astype(jnp.bfloat16)
        )
    solution = [None] * levels
    upper_rows = level_rows(levels)
    size_top = sep_block * 2**levels
    partial_value = jnp.einsum(
        "kq,qc->kc",
        z_blocks[levels - 1],
        upper_rows[:, :size_top],
        preferred_element_type=jnp.float32,
    )
    current = halve_sum(partial_value, list(range(levels - 1, -1, -1)))
    solution[levels - 1] = current
    for tree_level in range(levels - 1, 0, -1):
        size_here = sep_block * 2**tree_level
        link_rows = upper_rows[:, 2 * size_here :]
        rows_here = level_rows(tree_level)
        pushed = -jnp.einsum(
            "kq,qc->kc", current.astype(jnp.bfloat16), link_rows, preferred_element_type=jnp.float32
        )
        pushed = halve_sum(pushed, [tree_level])
        pushed = pushed + jnp.einsum(
            "kq,qc->kc",
            z_blocks[tree_level - 1],
            rows_here[:, :size_here],
            preferred_element_type=jnp.float32,
        )
        current = halve_sum(pushed, list(range(tree_level - 1, -1, -1)))
        solution[tree_level - 1] = current
        upper_rows = rows_here
    first_full = spread(current.astype(jnp.bfloat16), 0, 1)
    first_all = group_rows(first_full)
    picked = jnp.take(leaf_inv, inverse, axis=1)
    leaf_x = lax.psum_scatter(
        jnp.einsum("rm,rk->mk", picked, leaf_z, preferred_element_type=jnp.float32).astype(
            jnp.bfloat16
        ),
        "grp",
        scatter_dimension=0,
        tiled=True,
    ).astype(jnp.float32)
    leaf_x = leaf_x - jnp.einsum(
        "rc,kc->rk", leaf_link, first_all, preferred_element_type=jnp.float32
    )
    return (leaf_x, jnp.stack(solution, axis=0))


def solution(mesh):
    placed = (
        P(("leaf", "grp"), None),
        P(("leaf", "grp"), None),
        P("leaf", None),
        P(("leaf", "grp")),
        P(("leaf", "grp"), None),
        P(None, "grp", "leaf"),
        P(("leaf", "grp"), None),
        P(None, "leaf"),
    )
    return jax.shard_map(
        local,
        mesh=mesh,
        in_specs=placed,
        out_specs=(P(("leaf", "grp"), None), P(None, "grp", "leaf")),
        check_vma=False,
    )
```

profile of v0, /device:TPU:0, one launch (start us, length us, event | category | flops | bytes accessed | tf_op | source)
XLA Modules:
  0.0 169.4 jit_solution(9795258647874725150)
XLA Ops:
  7.2 0.7 all-gather.3.cloned.1.call-update
  8.0 1.5 convolution_convert_fusion
  9.5 0.8 copy.15
  10.4 6.5 %sort.17 = (s32[4096]{0:T(1024)}, s32[4096]{0:T(1024)S(1)}) sort(s32[4096]{0:T(1024)} %bitcast.59, s32[4096]{0:T(1024)S(1)} %iota.4), dimensions={0}, to_apply=%region_0.0 | sort | flops 49152 | bytes 65536 | tf_op jit(solution)/shard_map/jit(argsort)/sort | solution.py:65
  16.9 11.4 %copy.12 = bf16[1024,4096]{0,1:T(8,128)(2,1)} copy(bf16[1024,4096]{1,0:T(8,128)(2,1)} %param.11) | data formatting | bytes 16777216 | tf_op args[1]
  28.3 25.3 %gather_fusion = bf16[4096,1024]{1,0:T(8,128)(2,1)} fusion(bf16[1024,4096]{0,1:T(8,128)(2,1)} %copy.12, s32[4096]{0:T(1024)S(1)} %fusion.47), kind=kCustom, calls=%fused_computation.clone | custom fusion | bytes 16793600 | tf_op jit(solution)/shard_map/jit(_take)/gather | solution.py:136
  53.6 11.6 %all-gather.3.cloned.1.call-done = bf16[4096,512]{1,0:T(8,128)(2,1)} async-done(((bf16[1024,512]{1,0:T(8,128)(2,1)}), bf16[4096,512]{1,0:T(8,128)(2,1)}) %all-gather.3.cloned.1.call-update) | async-done | bytes 4194320 | tf_op jit(solution)/shard_map/all_gather | solution.py:69
  65.2 9.3 %multiply_convert_fusion.clone.5 = bf16[1024,512]{1,0:T(8,128)(2,1)S(1)} fusion(bf16[4096,512]{1,0:T(8,128)(2,1)} %all-gather.3.cloned.1.call-done, bf16[4096,1024]{1,0:T(8,128)(2,1)} %gather_fusion, pred[4096]{0:T(1024)(128)(4,1)S(1)} %compare_and_fusion, f32[1024]{0:T(1024)S(1)} %convert_element_type.159), kind=kOutput, calls=%fused_computation.8.clone.clone.clone.2 | convolution fusion | flops 4300210176 | bytes 13639680 | tf_op jit(solution)/shard_map/dot_general | solution.py:67
  74.6 7.1 %fusion.4 = bf16[4096,512]{1,0:T(8,128)(2,1)} fusion(bf16[4096,1024]{1,0:T(8,128)(2,1)S(1)} %copy-done.1, pred[4096]{0:T(1024)(128)(4,1)S(1)} %compare_and_fusion, bf16[1024,512]{1,0:T(8,128)(2,1)S(1)} %multiply_convert_fusion.clone.5), kind=kOutput, calls=%fused_computation.6 | convolution fusion | flops 4301258752 | bytes 13635584 | tf_op jit(solution)/shard_map/rm,rk->mk/dot_general | solution.py:138
  81.7 11.0 %reduce-scatter.7.cloned.1.call-done = bf16[128,32]{1,0:T(8,128)(2,1)} async-done(((bf16[512,32]{1,0:T(8,128)(2,1)}), bf16[128,32]{1,0:T(8,128)(2,1)}) %reduce-scatter.7.cloned.1.call-update) | async-done | bytes 8208
  92.7 0.8 copy.16
  93.6 1.2 collective-permute-done
  94.8 0.2 collective-permute-start.1
  95.0 1.0 collective-permute-done.1
  96.0 1.5 collective-permute-start.2
  97.5 8.5 %all-gather = bf16[4,4,416]{2,1,0:T(4,128)(2,1)S(1)} all-gather(bf16[1,4,416]{2,1,0:T(4,128)(2,1)S(1)} %bitcast.60), channel_id=1, replica_groups=mesh['leaf'=8,'grp'=4] {'grp'}, dimensions={0}, use_global_device_ids=true | all-gather | bytes 16640 | tf_op jit(solution)/shard_map/all_gather | solution.py:47
  106.2 1.2 collective-permute-done.3
  107.4 0.4 collective-permute-start.4
  107.8 3.3 %collective-permute-done.4 = bf16[128,32]{0,1:T(8,128)(2,1)S(1)} collective-permute-done((bf16[128,32]{0,1:T(8,128)(2,1)S(1)}, bf16[128,32]{0,1:T(8,128)(2,1)S(1)}, u32[]{:S(2)}, u32[]{:S(2)}) %collective-permute-start.4) | collective-permute-done | bytes 8224 | tf_op jit(solution)/shard_map/ppermute | solution.py:14
  111.1 2.5 %collective-permute-start.5 = (bf16[128,64]{0,1:T(8,128)(2,1)S(1)}, bf16[128,64]{0,1:T(8,128)(2,1)S(1)}, u32[]{:S(2)}, u32[]{:S(2)}) collective-permute-start(bf16[128,64]{0,1:T(8,128)(2,1)S(1)} %maximum_select_fusion.7), channel_id=1, source_target_pairs={{0,16},{16,0},{4,20},{20,4},{8,24},{24,8},{12,28},{28,12},{1,17},{... | collective-permute-start | bytes 49160 | tf_op jit(solution)/shard_map/ppermute | solution.py:14
  113.5 2.2 %collective-permute-done.5 = bf16[128,64]{0,1:T(8,128)(2,1)S(1)} collective-permute-done((bf16[128,64]{0,1:T(8,128)(2,1)S(1)}, bf16[128,64]{0,1:T(8,128)(2,1)S(1)}, u32[]{:S(2)}, u32[]{:S(2)}) %collective-permute-start.5) | collective-permute-done | bytes 16416 | tf_op jit(solution)/shard_map/ppermute | solution.py:14
  116.0 1.2 collective-permute-done.6
  117.1 0.4 collective-permute-start.7
  117.5 3.3 %collective-permute-done.7 = bf16[128,32]{0,1:T(8,128)(2,1)S(1)} collective-permute-done((bf16[128,32]{0,1:T(8,128)(2,1)S(1)}, bf16[128,32]{0,1:T(8,128)(2,1)S(1)}, u32[]{:S(2)}, u32[]{:S(2)}) %collective-permute-start.7) | collective-permute-done | bytes 8224 | tf_op jit(solution)/shard_map/ppermute | solution.py:14
  120.8 2.5 %collective-permute-start.8 = (bf16[128,64]{0,1:T(8,128)(2,1)S(1)}, bf16[128,64]{0,1:T(8,128)(2,1)S(1)}, u32[]{:S(2)}, u32[]{:S(2)}) collective-permute-start(bf16[128,64]{0,1:T(8,128)(2,1)S(1)} %maximum_select_fusion.8), channel_id=1, source_target_pairs={{0,16},{16,0},{4,20},{20,4},{8,24},{24,8},{12,28},{28,12},{1,17},{... | collective-permute-start | bytes 49160 | tf_op jit(solution)/shard_map/ppermute | solution.py:14
  123.3 2.2 %collective-permute-done.8 = bf16[128,64]{0,1:T(8,128)(2,1)S(1)} collective-permute-done((bf16[128,64]{0,1:T(8,128)(2,1)S(1)}, bf16[128,64]{0,1:T(8,128)(2,1)S(1)}, u32[]{:S(2)}, u32[]{:S(2)}) %collective-permute-start.8) | collective-permute-done | bytes 16416 | tf_op jit(solution)/shard_map/ppermute | solution.py:14
  125.5 0.3 fusion.16
  125.8 2.5 %collective-permute-start.9 = (bf16[128,64]{0,1:T(8,128)(2,1)S(1)}, bf16[128,64]{0,1:T(8,128)(2,1)S(1)}, u32[]{:S(2)}, u32[]{:S(2)}) collective-permute-start(bf16[128,64]{0,1:T(8,128)(2,1)S(1)} %select_convert_fusion.1), channel_id=1, source_target_pairs={{0,16},{16,0},{4,20},{20,4},{8,24},{24,8},{12,28},{28,12},{1,17},{... | collective-permute-start | bytes 49160 | tf_op jit(solution)/shard_map/ppermute | solution.py:14
  128.3 2.2 %collective-permute-done.9 = bf16[128,64]{0,1:T(8,128)(2,1)S(1)} collective-permute-done((bf16[128,64]{0,1:T(8,128)(2,1)S(1)}, bf16[128,64]{0,1:T(8,128)(2,1)S(1)}, u32[]{:S(2)}, u32[]{:S(2)}) %collective-permute-start.9) | collective-permute-done | bytes 16416 | tf_op jit(solution)/shard_map/ppermute | solution.py:14
  130.6 0.4 collective-permute-start.10
  131.0 3.3 %collective-permute-done.10 = bf16[128,32]{0,1:T(8,128)(2,1)S(1)} collective-permute-done((bf16[128,32]{0,1:T(8,128)(2,1)S(1)}, bf16[128,32]{0,1:T(8,128)(2,1)S(1)}, u32[]{:S(2)}, u32[]{:S(2)}) %collective-permute-start.10) | collective-permute-done | bytes 8224 | tf_op jit(solution)/shard_map/ppermute | solution.py:14
  134.4 1.2 collective-permute-done.11
  135.5 0.3 convolution_negate_fusion
  135.8 2.5 %collective-permute-start.12 = (bf16[128,64]{0,1:T(8,128)(2,1)S(1)}, bf16[128,64]{0,1:T(8,128)(2,1)S(1)}, u32[]{:S(2)}, u32[]{:S(2)}) collective-permute-start(bf16[128,64]{0,1:T(8,128)(2,1)S(1)} %select_convert_fusion), channel_id=1, source_target_pairs={{0,16},{16,0},{4,20},{20,4},{8,24},{24,8},{12,28},{28,12},{1,17},{... | collective-permute-start | bytes 49160 | tf_op jit(solution)/shard_map/ppermute | solution.py:14
  138.3 2.2 %collective-permute-done.12 = bf16[128,64]{0,1:T(8,128)(2,1)S(1)} collective-permute-done((bf16[128,64]{0,1:T(8,128)(2,1)S(1)}, bf16[128,64]{0,1:T(8,128)(2,1)S(1)}, u32[]{:S(2)}, u32[]{:S(2)}) %collective-permute-start.12) | collective-permute-done | bytes 16416 | tf_op jit(solution)/shard_map/ppermute | solution.py:14
  140.5 0.3 add_add_fusion
  140.9 0.4 collective-permute-start.13
  141.3 3.3 %collective-permute-done.13 = bf16[128,32]{0,1:T(8,128)(2,1)S(1)} collective-permute-done((bf16[128,32]{0,1:T(8,128)(2,1)S(1)}, bf16[128,32]{0,1:T(8,128)(2,1)S(1)}, u32[]{:S(2)}, u32[]{:S(2)}) %collective-permute-start.13) | collective-permute-done | bytes 8224 | tf_op jit(solution)/shard_map/ppermute | solution.py:14
  144.7 1.2 collective-permute-done.14
  145.9 0.3 convolution_negate_fusion.1
  146.1 0.4 collective-permute-start.15
  146.6 3.3 %collective-permute-done.15 = bf16[128,32]{0,1:T(8,128)(2,1)S(1)} collective-permute-done((bf16[128,32]{0,1:T(8,128)(2,1)S(1)}, bf16[128,32]{0,1:T(8,128)(2,1)S(1)}, u32[]{:S(2)}, u32[]{:S(2)}) %collective-permute-start.15) | collective-permute-done | bytes 8224 | tf_op jit(solution)/shard_map/ppermute | solution.py:14
  149.9 0.3 add_add_fusion.1
  150.3 1.1 collective-permute-done.16
  151.6 0.6 pad_maximum_fusion
  152.2 0.4 collective-permute-done.17
  152.6 7.2 %all_gather.11 = bf16[512,32]{0,1:T(8,128)(2,1)S(1)} all-gather(bf16[128,32]{0,1:T(8,128)(2,1)S(1)} %maximum_select_fusion.12), channel_id=1, replica_groups=mesh['leaf'=8,'grp'=4] {'grp'}, dimensions={0}, use_global_device_ids=true | all-gather | bytes 40960 | tf_op jit(solution)/shard_map/all_gather | solution.py:47
  159.8 3.0 %bitcast_subtract_fusion = f32[1024,512]{1,0:T(8,128)} fusion(bf16[1024,512]{1,0:T(8,128)(2,1)} %reduce-scatter.5.cloned.1.call-done, bf16[512,32]{0,1:T(8,128)(2,1)S(1)} %all_gather.11, bf16[1024,32]{0,1:T(8,128)(2,1)S(1)} %copy-done), kind=kOutput, calls=%fused_computation.7 | convolution fusion | flops 34603008 | bytes 3244032 | tf_op jit(solution)/shard_map/rc,kc->rk/dot_general | solution.py:145
  (57 shorter events, 1.3 us)
Async XLA Ops:
  7.2 0.8 copy-start
  7.2 58.0 %all-gather.3.cloned.1.call-start = ((), (), s32[]{:S(2)}) async-start(), calls=%async_computation.2 | async-start | bytes 5242880 | tf_op jit(solution)/shard_map/all_gather | solution.py:69
  7.9 84.8 %reduce-scatter.7.cloned.1.call-start = ((), (), s32[]{:S(2)}) async-start(), calls=%async_computation.4 | async-start | bytes 163840
  10.3 149.5 %reduce-scatter.5.cloned.1.call-start = ((), (), s32[]{:S(2)}) async-start(), calls=%async_computation.3 | async-start | bytes 5242880 | tf_op jit(solution)/shard_map/reduce_scatter | solution.py:137
  16.9 11.4 %copy-start.4 = (bf16[1024]{0:T(1024)(128)(2,1)S(1)}, bf16[1024]{0:T(1024)(128)(2,1)}, u32[]{:S(2)}) copy-start(bf16[1024]{0:T(1024)(128)(2,1)} %param.13) | copy-start | bytes 6148
  65.2 9.4 %copy-start.1 = (bf16[4096,1024]{1,0:T(8,128)(2,1)S(1)}, bf16[4096,1024]{1,0:T(8,128)(2,1)}, u32[]{:S(2)}) copy-start(bf16[4096,1024]{1,0:T(8,128)(2,1)} %gather_fusion) | copy-start | bytes 25165828
  74.6 20.2 %copy-start.5 = (bf16[3,128,16]{1,2,0:T(8,128)(2,1)S(1)}, bf16[3,128,16]{1,2,0:T(8,128)(2,1)}, u32[]{:S(2)}) copy-start(bf16[3,128,16]{1,2,0:T(8,128)(2,1)} %param.15) | copy-start | bytes 36868
  74.6 23.0 %copy-start.2 = (bf16[4,416]{1,0:T(4,128)(2,1)S(1)}, bf16[4,416]{1,0:T(4,128)(2,1)}, u32[]{:S(2)}) copy-start(bf16[4,416]{1,0:T(4,128)(2,1)} %param.16) | copy-start | bytes 9988
  74.6 48.7 %copy-start.3 = (bf16[3,16]{1,0:T(4,128)(2,1)S(1)}, bf16[3,16]{1,0:T(4,128)(2,1)}, u32[]{:S(2)}) copy-start(bf16[3,16]{1,0:T(4,128)(2,1)} %param.17) | copy-start | bytes 292
  93.6 1.2 collective-permute-start
  94.8 1.2 collective-permute-start.1
  96.0 10.0 %collective-permute-start.2 = (bf16[128,32]{0,1:T(8,128)(2,1)S(1)}, bf16[128,32]{0,1:T(8,128)(2,1)S(1)}, u32[]{:S(2)}, u32[]{:S(2)}) collective-permute-start(bf16[128,32]{0,1:T(8,128)(2,1)S(1)} %maximum_select_fusion.9), channel_id=1, source_target_pairs={{0,8},{8,0},{4,12},{12,4},{16,24},{24,16},{20,28},{28,20},{1,9},{9... | collective-permute-start | bytes 24584 | tf_op jit(solution)/shard_map/ppermute | solution.py:14
  106.2 1.2 collective-permute-start.3
  107.4 3.7 %collective-permute-start.4 = (bf16[128,32]{0,1:T(8,128)(2,1)S(1)}, bf16[128,32]{0,1:T(8,128)(2,1)S(1)}, u32[]{:S(2)}, u32[]{:S(2)}) collective-permute-start(bf16[128,32]{0,1:T(8,128)(2,1)S(1)} %maximum_select_fusion.10), channel_id=1, source_target_pairs={{0,8},{8,0},{4,12},{12,4},{16,24},{24,16},{20,28},{28,20},{1,9},{9... | collective-permute-start | bytes 24584 | tf_op jit(solution)/shard_map/ppermute | solution.py:14
  111.1 4.7 %collective-permute-start.5 = (bf16[128,64]{0,1:T(8,128)(2,1)S(1)}, bf16[128,64]{0,1:T(8,128)(2,1)S(1)}, u32[]{:S(2)}, u32[]{:S(2)}) collective-permute-start(bf16[128,64]{0,1:T(8,128)(2,1)S(1)} %maximum_select_fusion.7), channel_id=1, source_target_pairs={{0,16},{16,0},{4,20},{20,4},{8,24},{24,8},{12,28},{28,12},{1,17},{... | collective-permute-start | bytes 49160 | tf_op jit(solution)/shard_map/ppermute | solution.py:14
  116.0 1.2 collective-permute-start.6
  117.1 3.7 %collective-permute-start.7 = (bf16[128,32]{0,1:T(8,128)(2,1)S(1)}, bf16[128,32]{0,1:T(8,128)(2,1)S(1)}, u32[]{:S(2)}, u32[]{:S(2)}) collective-permute-start(bf16[128,32]{0,1:T(8,128)(2,1)S(1)} %maximum_select_fusion.11), channel_id=1, source_target_pairs={{0,8},{8,0},{4,12},{12,4},{16,24},{24,16},{20,28},{28,20},{1,9},{9... | collective-permute-start | bytes 24584 | tf_op jit(solution)/shard_map/ppermute | solution.py:14
  120.8 4.7 %collective-permute-start.8 = (bf16[128,64]{0,1:T(8,128)(2,1)S(1)}, bf16[128,64]{0,1:T(8,128)(2,1)S(1)}, u32[]{:S(2)}, u32[]{:S(2)}) collective-permute-start(bf16[128,64]{0,1:T(8,128)(2,1)S(1)} %maximum_select_fusion.8), channel_id=1, source_target_pairs={{0,16},{16,0},{4,20},{20,4},{8,24},{24,8},{12,28},{28,12},{1,17},{... | collective-permute-start | bytes 49160 | tf_op jit(solution)/shard_map/ppermute | solution.py:14
  125.8 4.7 %collective-permute-start.9 = (bf16[128,64]{0,1:T(8,128)(2,1)S(1)}, bf16[128,64]{0,1:T(8,128)(2,1)S(1)}, u32[]{:S(2)}, u32[]{:S(2)}) collective-permute-start(bf16[128,64]{0,1:T(8,128)(2,1)S(1)} %select_convert_fusion.1), channel_id=1, source_target_pairs={{0,16},{16,0},{4,20},{20,4},{8,24},{24,8},{12,28},{28,12},{1,17},{... | collective-permute-start | bytes 49160 | tf_op jit(solution)/shard_map/ppermute | solution.py:14
  130.6 3.7 %collective-permute-start.10 = (bf16[128,32]{0,1:T(8,128)(2,1)S(1)}, bf16[128,32]{0,1:T(8,128)(2,1)S(1)}, u32[]{:S(2)}, u32[]{:S(2)}) collective-permute-start(bf16[128,32]{0,1:T(8,128)(2,1)S(1)} %select_convert_fusion.4), channel_id=1, source_target_pairs={{0,8},{8,0},{4,12},{12,4},{16,24},{24,16},{20,28},{28,20},{1,9},{9... | collective-permute-start | bytes 24584 | tf_op jit(solution)/shard_map/ppermute | solution.py:14
  134.3 1.2 collective-permute-start.11
  135.8 4.7 %collective-permute-start.12 = (bf16[128,64]{0,1:T(8,128)(2,1)S(1)}, bf16[128,64]{0,1:T(8,128)(2,1)S(1)}, u32[]{:S(2)}, u32[]{:S(2)}) collective-permute-start(bf16[128,64]{0,1:T(8,128)(2,1)S(1)} %select_convert_fusion), channel_id=1, source_target_pairs={{0,16},{16,0},{4,20},{20,4},{8,24},{24,8},{12,28},{28,12},{1,17},{... | collective-permute-start | bytes 49160 | tf_op jit(solution)/shard_map/ppermute | solution.py:14
  140.9 3.7 %collective-permute-start.13 = (bf16[128,32]{0,1:T(8,128)(2,1)S(1)}, bf16[128,32]{0,1:T(8,128)(2,1)S(1)}, u32[]{:S(2)}, u32[]{:S(2)}) collective-permute-start(bf16[128,32]{0,1:T(8,128)(2,1)S(1)} %select_convert_fusion.3), channel_id=1, source_target_pairs={{0,8},{8,0},{4,12},{12,4},{16,24},{24,16},{20,28},{28,20},{1,9},{9... | collective-permute-start | bytes 24584 | tf_op jit(solution)/shard_map/ppermute | solution.py:14
  144.6 1.2 collective-permute-start.14
  146.1 3.7 %collective-permute-start.15 = (bf16[128,32]{0,1:T(8,128)(2,1)S(1)}, bf16[128,32]{0,1:T(8,128)(2,1)S(1)}, u32[]{:S(2)}, u32[]{:S(2)}) collective-permute-start(bf16[128,32]{0,1:T(8,128)(2,1)S(1)} %select_convert_fusion.2), channel_id=1, source_target_pairs={{0,8},{8,0},{4,12},{12,4},{16,24},{24,16},{20,28},{28,20},{1,9},{9... | collective-permute-start | bytes 24584 | tf_op jit(solution)/shard_map/ppermute | solution.py:14
  150.2 1.2 collective-permute-start.16
  151.4 1.2 collective-permute-start.17
Sparse Core Ops, SparseCore 0:
  9.8 55.3 all-gather.2
  68.5 24.1 reduce-scatter.6
  95.7 52.7 reduce-scatter.4
where the time goes:
time: 170 us; the launch traced here: 169 us
  waiting for transfers between devices  57 us (34%)
  local copies, waits for them, and re-layouts  38.4 us (23%)
  matrix products  22.8 us (13%)
  blocking collectives  15.7 us (9%)
  starting transfers between devices  14.2 us (8%)
  between operations  14 us (8%)
  other arithmetic  7.34 us (4%)
    ppermute x18, waiting for transfers between devices, from_partner(): return lax.ppermute(block, axis, route)  33.7 us
    gather x1, local copies, waits for them, and re-layouts, local(): picked = jnp.take(leaf_inv, inverse, axis=1)  25.3 us
    all_gather x2, blocking collectives, group_rows(): return lax.all_gather(values, 'grp', axis=0, tiled=True)  15.7 us
    ppermute x18, starting transfers between devices, from_partner(): return lax.ppermute(block, axis, route)  14 us
    unnamed x16, local copies, waits for them, and re-layouts  13.1 us
    unnamed x4, waiting for transfers between devices  11.7 us
    all_gather x1, waiting for transfers between devices, local(): lax.all_gather(leaf_rhs, 'grp', axis=0, tiled=True)  11.6 us
    dot_general x1, matrix products, local(): jnp.dot(picked, lax.all_gather(leaf_rhs, 'grp', axis=0, tiled=True), pref...  9.34 us
  transfers between devices with their start and end apart: 21, of which 19 were waited for; matrix products, arithmetic and copies ran while one was open for 39% of the time, Pallas kernels for 0%

commit v1 on v0

--- a/solution.py
+++ b/solution.py
@@ -1,7 +1,41 @@
+import functools
+
 import jax
 import jax.numpy as jnp
 from jax import lax
+from jax.experimental import pallas as pl
+from jax.experimental.pallas import tpu as pltpu
 from jax.sharding import PartitionSpec as P
+
+F32 = jnp.float32
+BF16 = jnp.bfloat16
+
+
+def exchange(block, axis, mask):
+    count = lax.axis_size(axis)
+    return lax.ppermute(block, axis, [(low, low ^ mask) for low in range(count)])
+
+
+def level_offset(sep_block, tree_level):
+    if tree_level >= 2:
+        return sep_block * (2 ** (tree_level + 1) - 6)
+    return 0
+
+
+def dot_tn(lhs, rhs):
+    return lax.dot_general(lhs, rhs, (((0,), (0,)), ((), ())), preferred_element_type=F32)
+
+
+def dot_nn(lhs, rhs):
+    return jnp.dot(lhs, rhs, preferred_element_type=F32)
+
+
+def vmem():
+    return pl.BlockSpec(memory_space=pltpu.VMEM)
+
+
+def smem():
+    return pl.BlockSpec(memory_space=pltpu.SMEM)
 
 
 def from_partner(block, axis, distance):
@@ -47,19 +81,13 @@
     return lax.all_gather(values, "grp", axis=0, tiled=True)
 
 
-def level_offset(sep_block, tree_level):
-    if tree_level >= 2:
-        return sep_block * (2 ** (tree_level + 1) - 6)
-    return 0
-
-
 def level_width(sep_block, tree_level):
     if tree_level >= 2:
         return 2 * sep_block * 2**tree_level
     return sep_block * 2**tree_level
 
 
-def local(leaf_rhs, leaf_inv, ordering, leaf_dinv, leaf_link, sep_rhs, sep_factor, sep_dinv):
+def local_general(leaf_rhs, leaf_inv, ordering, leaf_dinv, leaf_link, sep_rhs, sep_factor, sep_dinv):
     levels = sep_rhs.shape[0]
     sep_block = sep_rhs.shape[2]
     inverse = jnp.argsort(ordering[0])
@@ -148,6 +176,236 @@
     return (leaf_x, jnp.stack(solution, axis=0))
 
 
+def pack_body(rhs_ref, link_ref, sep_ref, fac_ref, out_ref):
+    levels, width, sep_block = sep_ref.shape
+    first = link_ref.shape[1]
+    rows, cols = fac_ref.shape
+    out_ref[0:first, :] = dot_tn(link_ref[...], rhs_ref[...]).astype(BF16)
+    out_ref[first:, :] = jnp.zeros((out_ref.shape[0] - first, out_ref.shape[1]), BF16)
+    for level in range(levels):
+        out_ref[first : first + sep_block, level * width : (level + 1) * width] = (
+            sep_ref[level].astype(F32).T.astype(BF16)
+        )
+    out_ref[first + sep_block : first + sep_block + rows, 0:cols] = fac_ref[...]
+
+
+def leaf_body(place_ref, own_ref, x_ref, y_ref, d_ref, dinv_ref, out_ref, *, first, levels, rows, cols):
+    sep_block = dinv_ref.shape[1]
+    width = out_ref.shape[1]
+    me = place_ref[1]
+    parts = (own_ref, x_ref, y_ref, d_ref)
+    total = parts[0][0:first, :].astype(F32)
+    for part in parts[1:]:
+        total = total + part[0:first, :].astype(F32)
+    out_ref[0:first, :] = total.astype(BF16)
+    part_width = width // len(parts)
+    for index, part in enumerate(parts):
+        lanes = pl.ds(pl.multiple_of((me ^ index) * part_width, part_width), part_width)
+        for level in range(levels):
+            out_ref[first + level * sep_block : first + (level + 1) * sep_block, lanes] = part[
+                first : first + sep_block, level * part_width : (level + 1) * part_width
+            ]
+    row_owner = lax.broadcasted_iota(jnp.int32, (sep_block, width), 0) // rows
+    lane = lax.broadcasted_iota(jnp.int32, (sep_block, width), 1)
+    factor = jnp.zeros((sep_block, width), F32)
+    for index, part in enumerate(parts):
+        block = part[first + sep_block : first + 2 * sep_block, :].astype(F32)[0:rows, :]
+        tiled = jnp.concatenate([block] * (sep_block // rows), axis=0)
+        factor = factor + jnp.where(row_owner == (me ^ index), tiled, 0.0)
+    pivots = dinv_ref[...].astype(F32).T
+    for level in range(levels):
+        column = jnp.broadcast_to(pivots[:, level : level + 1], (sep_block, width))
+        factor = jnp.where(lane == cols + level, column, factor)
+    out_ref[first + levels * sep_block :, :] = factor.astype(BF16)
+
+
+def pair_body(place_ref, own_ref, other_ref, out_ref, *, first, levels, sep_block):
+    is_odd = place_ref[0] % 2 == 1
+    own = own_ref[...].astype(F32)
+    other = other_ref[...].astype(F32)
+    even = jnp.where(is_odd, other, own)
+    odd = jnp.where(is_odd, own, other)
+    crossing = even[0:first] + odd[0:first]
+    for level in range(levels + 1):
+        base = first + level * sep_block
+        both = jnp.concatenate([even[base : base + sep_block], odd[base : base + sep_block]], axis=0)
+        if level == 0:
+            both = both - crossing
+        out_ref[level * first : (level + 1) * first, :] = both.astype(BF16)
+
+
+def tree_body(
+    place_ref, *refs, count, first, levels, sep_block, cols, slice_width
+):
+    pairs = refs[:count]
+    first_ref, sol_ref, stage_ref, val_ref = refs[count:]
+    leaf, me = place_ref[0], place_ref[1]
+    pair = leaf // 2
+    nsep = count * first
+    width = pairs[0].shape[1]
+    for index, ref in enumerate(pairs):
+        place = pl.ds(pl.multiple_of((pair ^ index) * first, first), first)
+        for level in range(levels + 1):
+            stage_ref[level, place, :] = ref[level * first : (level + 1) * first, :]
+    factor = stage_ref[levels]
+    column = lax.broadcasted_iota(jnp.int32, (width, nsep), 0)
+    target = lax.broadcasted_iota(jnp.int32, (width, nsep), 1)
+    row = lax.broadcasted_iota(jnp.int32, (nsep, nsep), 0)
+    lane = lax.broadcasted_iota(jnp.int32, (nsep, nsep), 1)
+
+    def block_diagonal(offset, size):
+        choose = jnp.where(column == offset + target % size, 1.0, 0.0).astype(BF16)
+        spread = dot_nn(factor, choose)
+        return jnp.where(row // size == lane // size, spread, 0.0).astype(BF16)
+
+    weights, couplings, z_blocks = [], [], []
+    residual = stage_ref[0]
+    for level in range(1, levels + 1):
+        size = sep_block * 2**level
+        offset = level_offset(sep_block, level)
+        weight = block_diagonal(offset, size)
+        coupling = None
+        if level >= 2:
+            coupling = block_diagonal(offset + size, size)
+            residual = (stage_ref[level - 1].astype(F32) - dot_nn(coupling, residual)).astype(BF16)
+        choose = jnp.where(column == cols + level - 1, 1.0, 0.0).astype(BF16)
+        scale = dot_nn(factor, choose)
+        scale = jnp.concatenate([scale] * (width // nsep), axis=1)
+        z_blocks.append((scale * dot_nn(weight, residual)).astype(BF16))
+        weights.append(weight)
+        couplings.append(coupling)
+    current = None
+    for level in range(levels, 0, -1):
+        value = dot_tn(weights[level - 1], z_blocks[level - 1])
+        if level < levels:
+            value = value - dot_tn(couplings[level], current.astype(BF16))
+        current = value
+        val_ref[...] = value
+        lanes = pl.ds(pl.multiple_of(me * slice_width, slice_width), slice_width)
+        mine = val_ref[pl.ds(pl.multiple_of(leaf * sep_block, sep_block), sep_block), lanes]
+        sol_ref[level - 1] = mine.T
+    first_ref[...] = val_ref[pl.ds(pl.multiple_of(pair * first, first), first), :].astype(BF16)
+
+
+def tree(place, rhs, link, sep_rhs, sep_factor, sep_dinv):
+    levels, slice_width, sep_block = sep_rhs.shape
+    first = link.shape[1]
+    width = rhs.shape[1]
+    rows, cols = sep_factor.shape
+    aux = pl.pallas_call(
+        pack_body,
+        out_shape=jax.ShapeDtypeStruct((first + 2 * sep_block, width), BF16),
+        in_specs=[vmem()] * 4,
+        out_specs=vmem(),
+        name="pack",
+    )(rhs, link, sep_rhs, sep_factor)
+    aux_x, aux_y, aux_d = (exchange(aux, "grp", mask) for mask in (1, 2, 3))
+    leaf_block = pl.pallas_call(
+        functools.partial(leaf_body, first=first, levels=levels, rows=rows, cols=cols),
+        out_shape=jax.ShapeDtypeStruct((first + (levels + 1) * sep_block, width), BF16),
+        in_specs=[smem()] + [vmem()] * 5,
+        out_specs=vmem(),
+        name="leafblock",
+    )(place, aux, aux_x, aux_y, aux_d, sep_dinv)
+    partner = exchange(leaf_block, "leaf", 1)
+    pair_block = pl.pallas_call(
+        functools.partial(pair_body, first=first, levels=levels, sep_block=sep_block),
+        out_shape=jax.ShapeDtypeStruct(((levels + 1) * first, width), BF16),
+        in_specs=[smem(), vmem(), vmem()],
+        out_specs=vmem(),
+        name="pairblock",
+    )(place, leaf_block, partner)
+    count = lax.axis_size("leaf") // 2
+    pairs = [pair_block] + [exchange(pair_block, "leaf", 2 * mask) for mask in range(1, count)]
+    nsep = count * first
+    return pl.pallas_call(
+        functools.partial(
+            tree_body,
+            count=count,
+            first=first,
+            levels=levels,
+            sep_block=sep_block,
+            cols=cols,
+            slice_width=slice_width,
+        ),
+        out_shape=(
+            jax.ShapeDtypeStruct((first, width), BF16),
+            jax.ShapeDtypeStruct((levels, slice_width, sep_block), F32),
+        ),
+        in_specs=[smem()] + [vmem()] * count,
+        out_specs=(vmem(), vmem()),
+        scratch_shapes=[pltpu.VMEM((levels + 1, nsep, width), BF16), pltpu.VMEM((nsep, width), F32)],
+        name="tree",
+    )(place, *pairs)
+
+
+def local_pairs(leaf_rhs, leaf_inv, ordering, leaf_dinv, leaf_link, sep_rhs, sep_factor, sep_dinv):
+    rows = leaf_rhs.shape[0]
+    half = rows // 2
+    leaf = lax.axis_index("leaf").astype(jnp.int32)
+    me = lax.axis_index("grp").astype(jnp.int32)
+    place = jnp.stack([leaf, me])
+
+    rhs_x = exchange(leaf_rhs, "grp", 1)
+    rhs_y = exchange(leaf_rhs, "grp", 2)
+    first_all, solution_here = tree(place, leaf_rhs, leaf_link, sep_rhs, sep_factor, sep_dinv)
+    far_low = exchange(rhs_x[:half], "grp", 2)
+    far_high = exchange(rhs_y[half:], "grp", 1)
+
+    inverse = jnp.argsort(ordering[0])
+    inverse = inverse.reshape(-1, rows)
+    inverse = jnp.concatenate([inverse[me ^ index] for index in range(inverse.shape[0])])
+    picked = jnp.take(leaf_inv, inverse, axis=1).T
+    blocks = [picked[index * rows : (index + 1) * rows] for index in range(lax.axis_size("grp"))]
+
+    leaf_y = dot_tn(blocks[0], leaf_rhs)
+    leaf_y = leaf_y + dot_tn(blocks[1], rhs_x)
+    leaf_y = leaf_y + dot_tn(blocks[2], rhs_y)
+    leaf_y = leaf_y + dot_tn(blocks[3][:half], far_low)
+    leaf_y = leaf_y + dot_tn(blocks[3][half:], far_high)
+    leaf_z = (leaf_dinv.astype(F32)[:, None] * leaf_y).astype(BF16)
+
+    far = dot_nn(blocks[3], leaf_z).astype(BF16)
+    relay_low = exchange(far[:half], "grp", 1)
+    relay_high = exchange(far[half:], "grp", 2)
+    near_x = dot_nn(blocks[1], leaf_z)
+    x_low = exchange(near_x[:half].astype(BF16), "grp", 1)
+    near_y = dot_nn(blocks[2], leaf_z)
+    y_high = exchange(near_y[half:].astype(BF16), "grp", 2)
+    x_high = exchange((near_x[half:] + relay_high.astype(F32)).astype(BF16), "grp", 1)
+    y_low = exchange((near_y[:half] + relay_low.astype(F32)).astype(BF16), "grp", 2)
+    own = dot_nn(blocks[0], leaf_z) - dot_nn(leaf_link, first_all)
+    low = own[:half] + x_low.astype(F32) + y_low.astype(F32)
+    high = own[half:] + x_high.astype(F32) + y_high.astype(F32)
+    return jnp.concatenate([low, high], axis=0), solution_here
+
+
+def fits(leaf_rhs, leaf_inv, sep_rhs, sep_factor, leaf_link):
+    levels, slice_width, sep_block = sep_rhs.shape
+    width = leaf_rhs.shape[1]
+    count = lax.axis_size("grp")
+    leaves = lax.axis_size("leaf")
+    return (
+        count == 2**2
+        and leaf_inv.shape[1] == count * leaf_rhs.shape[0]
+        and leaf_rhs.shape[0] % 256 == 0
+        and leaf_link.shape[1] == 2 * sep_block
+        and sep_block % 16 == 0
+        and slice_width % 128 == 0
+        and levels <= count
+        and sep_block % sep_factor.shape[0] == 0
+        and sep_factor.shape[1] + levels <= width
+        and width % (leaves * sep_block) == 0
+    )
+
+
+def local(*args):
+    leaf_rhs, leaf_inv, _, _, leaf_link, sep_rhs, sep_factor, _ = args
+    if fits(leaf_rhs, leaf_inv, sep_rhs, sep_factor, leaf_link):
+        return local_pairs(*args)
+    return local_general(*args)
+
+
 def solution(mesh):
     placed = (
         P(("leaf", "grp"), None),

time: 170 us -> 152 us (0.89)
  blocking collectives: 15.7 us -> 0 us
  waiting for transfers between devices: 57 us -> 41.6 us
  between operations: 14 us -> 0.86 us
  other arithmetic: 7.34 us -> 17 us
  Pallas kernels: 0 us -> 9.06 us
  local copies, waits for them, and re-layouts: 38.4 us -> 47 us
  matrix products: 22.8 us -> 16.7 us
  starting transfers between devices: 14.2 us -> 19 us
    all_gather x2 -> x0, blocking collectives: 15.7 us -> none  [group_rows(): return lax.all_gather(values, 'grp', axis=0, tiled=True)]
    unnamed x4 -> x0, waiting for transfers between devices: 11.7 us -> none
    all_gather x1 -> x0, waiting for transfers between devices: 11.6 us -> none  [local(): lax.all_gather(leaf_rhs, 'grp', axis=0, tiled=True)]
    pallas_call x0 -> x4, Pallas kernels: none -> 9.06 us  [the longest x1 3.4 us: tree(): pl.pallas_call(functools.partial(tree_body, count=count, first=first, lev...]
    ppermute x18 -> x17, waiting for transfers between devices: 33.7 us -> 41.6 us  [exchange(): lax.ppermute(block, axis, [(low, low ^ mask) for low in range(count)])]
    select_n x6 -> x2, other arithmetic: 0.04 us -> 7.47 us  [local_pairs(): picked = jnp.take(leaf_inv, inverse, axis=1).T]
    dot_general x11 -> x10, matrix products: 22.8 us -> 16.7 us  [the longest x5 11.2 us: dot_tn(): lax.dot_general(lhs, rhs, (((0,), (0,)), ((), ())), preferred_element_typ...]
    unnamed x16 -> x30, local copies, waits for them, and re-layouts: 13.1 us -> 19.1 us
  transfers between devices with their start and end apart: 21 -> 17, of which waited for: 19 -> 9; matrix products, arithmetic and copies ran while one was open for 39% -> 49% of each run, Pallas kernels for 0% -> 6%
where the time goes in v1:
time: 152 us; the launch traced here: 151 us
  local copies, waits for them, and re-layouts  47 us (31%)
  waiting for transfers between devices  41.6 us (27%)
  starting transfers between devices  19 us (12%)
  other arithmetic  17 us (11%)
  matrix products  16.7 us (11%)
  Pallas kernels  9.06 us (6%)
    ppermute x17, waiting for transfers between devices, exchange(): lax.ppermute(block, axis, [(low, low ^ mask) for low in range(count)])  41.6 us
    gather x1, local copies, waits for them, and re-layouts, local_pairs(): picked = jnp.take(leaf_inv, inverse, axis=1).T  25.4 us
    unnamed x30, local copies, waits for them, and re-layouts  19.1 us
    ppermute x17, starting transfers between devices, exchange(): lax.ppermute(block, axis, [(low, low ^ mask) for low in range(count)])  19 us
    dot_general x5, matrix products, dot_tn(): lax.dot_general(lhs, rhs, (((0,), (0,)), ((), ())), preferred_element_typ...  11.2 us
    select_n x2, other arithmetic, local_pairs(): picked = jnp.take(leaf_inv, inverse, axis=1).T  7.47 us
    sort x1, other arithmetic, local_pairs(): inverse = jnp.argsort(ordering[0])  6.5 us
    dot_general x5, matrix products, dot_nn(): return jnp.dot(lhs, rhs, preferred_element_type=F32)  5.45 us
  transfers between devices with their start and end apart: 17, of which 9 were waited for; matrix products, arithmetic and copies ran while one was open for 49% of the time, Pallas kernels for 6%

profile of v1, /device:TPU:0, one launch (start us, length us, event | category | flops | bytes accessed | tf_op | source)
XLA Modules:
  0.0 151.2 jit_solution(9166480688303216505)
XLA Ops:
  0.6 3.0 %collective-permute-start = (bf16[1024,512]{1,0:T(8,128)(2,1)}, bf16[1024,512]{1,0:T(8,128)(2,1)}, u32[]{:S(2)}, u32[]{:S(2)}) collective-permute-start(bf16[1024,512]{1,0:T(8,128)(2,1)} %rhs_ref.1), channel_id=1, source_target_pairs={{0,1},{1,0},{2,3},{3,2},{4,5},{5,4},{6,7},{7,6},{8,9},{9,8},{10,11... | collective-permute-start | bytes 3145736 | tf_op jit(solution)/shard_map/ppermute | solution.py:16
  3.7 1.5 %collective-permute-start.1 = (bf16[1024,512]{1,0:T(8,128)(2,1)}, bf16[1024,512]{1,0:T(8,128)(2,1)}, u32[]{:S(2)}, u32[]{:S(2)}) collective-permute-start(bf16[1024,512]{1,0:T(8,128)(2,1)} %rhs_ref.1), channel_id=1, source_target_pairs={{0,2},{1,3},{2,0},{3,1},{4,6},{5,7},{6,4},{7,5},{8,10},{9,11},{10,... | collective-permute-start | bytes 3145736 | tf_op jit(solution)/shard_map/ppermute | solution.py:16
  5.2 1.7 %copy.16.link_ref = bf16[1024,32]{1,0:T(8,128)(2,1)} copy(bf16[1024,32]{0,1:T(8,128)(2,1)} %param.12) | data formatting | bytes 131072 | tf_op args[4]
  6.9 1.5 copy.17.sep_ref
  8.3 2.3 %pack.1.own_ref = bf16[64,512]{1,0:T(8,128)(2,1)} custom-call(bf16[1024,512]{1,0:T(8,128)(2,1)} %rhs_ref.1, bf16[1024,32]{1,0:T(8,128)(2,1)} %copy.16.link_ref, bf16[3,128,16]{2,1,0:T(8,128)(2,1)} %copy.17.sep_ref, bf16[4,416]{1,0:T(4,128)(2,1)} %fac_ref.1), custom_call_target="tpu_custom_call" | custom-call | tf_op jit(solution)/shard_map/pack/pallas_call | solution.py:295
  11.2 2.9 %collective-permute-start.6 = (bf16[64,512]{1,0:T(8,128)(2,1)}, bf16[64,512]{1,0:T(8,128)(2,1)S(1)}, u32[]{:S(2)}, u32[]{:S(2)}) collective-permute-start(bf16[64,512]{1,0:T(8,128)(2,1)} %pack.1.own_ref), channel_id=1, source_target_pairs={{0,3},{1,2},{2,1},{3,0},{4,7},{5,6},{6,5},{7,4},{8,11},{9,10},{10,... | collective-permute-start | bytes 196616 | tf_op jit(solution)/shard_map/ppermute | solution.py:16
  14.1 6.5 %sort.17 = (s32[4096]{0:T(1024)}, s32[4096]{0:T(1024)S(1)}) sort(s32[4096]{0:T(1024)} %bitcast.36, s32[4096]{0:T(1024)S(1)} %iota.4), dimensions={0}, to_apply=%region_0.0 | sort | flops 49152 | bytes 65536 | tf_op jit(solution)/shard_map/jit(argsort)/sort | solution.py:355
  20.6 11.8 %copy.15 = bf16[1024,4096]{0,1:T(8,128)(2,1)} copy(bf16[1024,4096]{1,0:T(8,128)(2,1)} %param.9) | data formatting | bytes 16777216 | tf_op args[1]
  32.4 25.4 %gather_fusion = bf16[4096,1024]{1,0:T(8,128)(2,1)} fusion(bf16[1024,4096]{0,1:T(8,128)(2,1)} %copy.15, s32[4096]{0:T(1024)S(1)} %broadcast_clamp_fusion), kind=kCustom, calls=%fused_computation | custom fusion | bytes 16793600 | tf_op jit(solution)/shard_map/jit(_take)/gather | solution.py:358
  57.8 0.6 pad_add_fusion.place_ref
  58.5 0.6 copy-done.6
  59.2 0.6 copy-done.8
  59.8 1.7 %leafblock.1.own_ref = bf16[96,512]{1,0:T(8,128)(2,1)} custom-call(s32[2]{0:T(128)} %pad_add_fusion.place_ref, bf16[64,512]{1,0:T(8,128)(2,1)} %pack.1.own_ref, bf16[64,512]{1,0:T(8,128)(2,1)} %copy-done.6, bf16[64,512]{1,0:T(8,128)(2,1)} %copy-done.7, bf16[64,512]{1,0:T(8,128)(2,1)} %copy-done.8, bf16[3,16]{1,0:T(4,128)(2,1)} %dinv_ref.1), custom_call_target="tpu_custom_call" | custom-call | tf_op jit(solution)/shard_map/leafblock/pallas_call | solution.py:303
  61.5 7.4 %broadcast_select_fusion = bf16[4096,1024]{1,0:T(8,128)(2,1)} fusion(bf16[4096,1024]{1,0:T(8,128)(2,1)} %gather_fusion, pred[4096]{0:T(1024)(128)(4,1)S(1)} %compare_and_fusion), kind=kLoop, calls=%fused_computation.1 | loop fusion | flops 4194304 | bytes 16781312 | tf_op jit(solution)/shard_map/jit(_take)/select_n | solution.py:358
  69.0 0.6 copy-done.5
  69.6 1.7 %pairblock.1.refs_0_ = bf16[128,512]{1,0:T(8,128)(2,1)} custom-call(s32[2]{0:T(128)} %pad_add_fusion.place_ref, bf16[96,512]{1,0:T(8,128)(2,1)} %leafblock.1.own_ref, bf16[96,512]{1,0:T(8,128)(2,1)} %copy-done.5), custom_call_target="tpu_custom_call" | custom-call | tf_op jit(solution)/shard_map/pairblock/pallas_call | solution.py:311
  71.3 3.6 %collective-permute-start.10 = (bf16[128,512]{1,0:T(8,128)(2,1)}, bf16[128,512]{1,0:T(8,128)(2,1)S(1)}, u32[]{:S(2)}, u32[]{:S(2)}) collective-permute-start(bf16[128,512]{1,0:T(8,128)(2,1)} %pairblock.1.refs_0_), channel_id=1, source_target_pairs={{0,24},{4,28},{8,16},{12,20},{16,8},{20,12},{24,0},{28,4},{1,25},{... | collective-permute-start | bytes 393224 | tf_op jit(solution)/shard_map/ppermute | solution.py:16
  74.9 0.8 collective-permute-start.9
  75.7 2.9 %fusion.12 = f32[1024,512]{1,0:T(8,128)S(1)} fusion(bf16[1024,512]{1,0:T(8,128)(2,1)S(1)} %copy-done, bf16[4096,1024]{1,0:T(8,128)(2,1)} %broadcast_select_fusion), kind=kOutput, calls=%fused_computation.17 | convolution fusion | flops 1073741824 | bytes 5242880 | tf_op jit(solution)/shard_map/dot_general | solution.py:26
  78.6 1.1 collective-permute-done.10.refs_3_
  79.7 3.4 %collective-permute-done.8.refs_1_ = bf16[128,512]{1,0:T(8,128)(2,1)S(1)} collective-permute-done((bf16[128,512]{1,0:T(8,128)(2,1)}, bf16[128,512]{1,0:T(8,128)(2,1)S(1)}, u32[]{:S(2)}, u32[]{:S(2)}) %collective-permute-start.8) | collective-permute-done | bytes 131104 | tf_op jit(solution)/shard_map/ppermute | solution.py:16
  83.1 3.7 %collective-permute-done.9.refs_2_ = bf16[128,512]{1,0:T(8,128)(2,1)S(1)} collective-permute-done((bf16[128,512]{1,0:T(8,128)(2,1)}, bf16[128,512]{1,0:T(8,128)(2,1)S(1)}, u32[]{:S(2)}, u32[]{:S(2)}) %collective-permute-start.9) | collective-permute-done | bytes 131104 | tf_op jit(solution)/shard_map/ppermute | solution.py:16
  86.8 0.7 copy-done.4
  87.4 3.4 %tree.1 = (bf16[32,512]{1,0:T(8,128)(2,1)}, f32[3,128,16]{2,1,0:T(8,128)}) custom-call(s32[2]{0:T(128)} %pad_add_fusion.place_ref, bf16[128,512]{1,0:T(8,128)(2,1)} %pairblock.1.refs_0_, bf16[128,512]{1,0:T(8,128)(2,1)} %copy-done.3, bf16[128,512]{1,0:T(8,128)(2,1)} %copy-done.4, bf16[128,512]{1,0:T(8,128)(2,1)} %copy-done.2), custom_call_target="tpu_custom_call" | custom-call | tf_op jit(solution)/shard_map/tree/pallas_call | solution.py:321
  90.8 1.6 %copy.19 = f32[3,128,16]{1,2,0:T(8,128)} copy(f32[3,128,16]{2,1,0:T(8,128)} %get-tuple-element.11) | data formatting | bytes 49152
  92.5 1.1 slice.74
  94.1 1.1 slice.76
  95.2 0.6 collective-permute-start.3
  95.8 3.3 %fusion.4 = f32[1024,512]{1,0:T(8,128)S(1)} fusion(bf16[1024,512]{1,0:T(8,128)(2,1)} %collective-permute-done.1, bf16[4096,1024]{1,0:T(8,128)(2,1)} %broadcast_select_fusion), kind=kOutput, calls=%fused_computation.9 | convolution fusion | flops 1073741824 | bytes 5242880 | tf_op jit(solution)/shard_map/dot_general | solution.py:26
  99.1 3.3 %fusion.8 = f32[1024,512]{1,0:T(8,128)S(1)} fusion(bf16[1024,512]{1,0:T(8,128)(2,1)} %collective-permute-done, bf16[4096,1024]{1,0:T(8,128)(2,1)} %broadcast_select_fusion), kind=kOutput, calls=%fused_computation.13 | convolution fusion | flops 1073741824 | bytes 5242880 | tf_op jit(solution)/shard_map/dot_general | solution.py:26
  102.4 4.6 %collective-permute-done.2 = bf16[512,512]{1,0:T(8,128)(2,1)S(1)} collective-permute-done((bf16[512,512]{1,0:T(8,128)(2,1)S(1)}, bf16[512,512]{1,0:T(8,128)(2,1)S(1)}, u32[]{:S(2)}, u32[]{:S(2)}) %collective-permute-start.2) | collective-permute-done | bytes 524320 | tf_op jit(solution)/shard_map/ppermute | solution.py:16
  107.0 0.7 fusion.25
  107.7 0.6 collective-permute-done.3
  108.4 1.0 multiply_convert_fusion
  109.4 1.2 fusion.14
  110.7 1.6 %collective-permute-start.14 = (bf16[512,512]{1,0:T(8,128)(2,1)S(1)}, bf16[512,512]{1,0:T(8,128)(2,1)S(1)}, u32[]{:S(2)}, u32[]{:S(2)}) collective-permute-start(bf16[512,512]{1,0:T(8,128)(2,1)S(1)} %get-tuple-element.15), channel_id=1, source_target_pairs={{0,2},{1,3},{2,0},{3,1},{4,6},{5,7},{6,4},{7,5},{8,10},{9,11},{10,... | collective-permute-start | bytes 1572872 | tf_op jit(solution)/shard_map/ppermute | solution.py:16
  112.3 1.2 fusion.6
  113.6 0.6 collective-permute-start.11
  114.2 1.5 collective-permute-start.12
  115.7 1.2 fusion.2
  117.6 8.0 %collective-permute-done.14 = bf16[512,512]{1,0:T(8,128)(2,1)S(1)} collective-permute-done((bf16[512,512]{1,0:T(8,128)(2,1)S(1)}, bf16[512,512]{1,0:T(8,128)(2,1)S(1)}, u32[]{:S(2)}, u32[]{:S(2)}) %collective-permute-start.14) | collective-permute-done | bytes 524320 | tf_op jit(solution)/shard_map/ppermute | solution.py:16
  125.8 0.6 collective-permute-start.15
  126.4 13.4 %collective-permute-done.12 = bf16[512,512]{1,0:T(8,128)(2,1)S(1)} collective-permute-done((bf16[512,512]{1,0:T(8,128)(2,1)S(1)}, bf16[512,512]{1,0:T(8,128)(2,1)S(1)}, u32[]{:S(2)}, u32[]{:S(2)}) %collective-permute-start.12) | collective-permute-done | bytes 524320 | tf_op jit(solution)/shard_map/ppermute | solution.py:16
  139.9 0.6 collective-permute-start.13
  140.5 1.2 fusion.10
  142.3 5.9 %collective-permute-done.15 = bf16[512,512]{1,0:T(8,128)(2,1)S(1)} collective-permute-done((bf16[512,512]{1,0:T(8,128)(2,1)S(1)}, bf16[512,512]{1,0:T(8,128)(2,1)S(1)}, u32[]{:S(2)}, u32[]{:S(2)}) %collective-permute-start.15) | collective-permute-done | bytes 524320 | tf_op jit(solution)/shard_map/ppermute | solution.py:16
  148.1 1.0 collective-permute-done.13
  149.7 1.5 pad_maximum_fusion
  (51 shorter events, 3.5 us)
Async XLA Ops:
  0.6 91.8 %collective-permute-start = (bf16[1024,512]{1,0:T(8,128)(2,1)}, bf16[1024,512]{1,0:T(8,128)(2,1)}, u32[]{:S(2)}, u32[]{:S(2)}) collective-permute-start(bf16[1024,512]{1,0:T(8,128)(2,1)} %rhs_ref.1), channel_id=1, source_target_pairs={{0,1},{1,0},{2,3},{3,2},{4,5},{5,4},{6,7},{7,6},{8,9},{9,8},{10,11... | collective-permute-start | bytes 3145736 | tf_op jit(solution)/shard_map/ppermute | solution.py:16
  3.7 90.4 %collective-permute-start.1 = (bf16[1024,512]{1,0:T(8,128)(2,1)}, bf16[1024,512]{1,0:T(8,128)(2,1)}, u32[]{:S(2)}, u32[]{:S(2)}) collective-permute-start(bf16[1024,512]{1,0:T(8,128)(2,1)} %rhs_ref.1), channel_id=1, source_target_pairs={{0,2},{1,3},{2,0},{3,1},{4,6},{5,7},{6,4},{7,5},{8,10},{9,11},{10,... | collective-permute-start | bytes 3145736 | tf_op jit(solution)/shard_map/ppermute | solution.py:16
  10.6 47.9 %collective-permute-start.4 = (bf16[64,512]{1,0:T(8,128)(2,1)}, bf16[64,512]{1,0:T(8,128)(2,1)S(1)}, u32[]{:S(2)}, u32[]{:S(2)}) collective-permute-start(bf16[64,512]{1,0:T(8,128)(2,1)} %pack.1.own_ref), channel_id=1, source_target_pairs={{0,1},{1,0},{2,3},{3,2},{4,5},{5,4},{6,7},{7,6},{8,9},{9,8},{10,11... | collective-permute-start | bytes 196616 | tf_op jit(solution)/shard_map/ppermute | solution.py:16
  11.1 47.4 %collective-permute-start.5 = (bf16[64,512]{1,0:T(8,128)(2,1)}, bf16[64,512]{1,0:T(8,128)(2,1)S(1)}, u32[]{:S(2)}, u32[]{:S(2)}) collective-permute-start(bf16[64,512]{1,0:T(8,128)(2,1)} %pack.1.own_ref), channel_id=1, source_target_pairs={{0,2},{1,3},{2,0},{3,1},{4,6},{5,7},{6,4},{7,5},{8,10},{9,11},{10,... | collective-permute-start | bytes 196616 | tf_op jit(solution)/shard_map/ppermute | solution.py:16
  11.2 47.3 %collective-permute-start.6 = (bf16[64,512]{1,0:T(8,128)(2,1)}, bf16[64,512]{1,0:T(8,128)(2,1)S(1)}, u32[]{:S(2)}, u32[]{:S(2)}) collective-permute-start(bf16[64,512]{1,0:T(8,128)(2,1)} %pack.1.own_ref), channel_id=1, source_target_pairs={{0,3},{1,2},{2,1},{3,0},{4,7},{5,6},{6,5},{7,4},{8,11},{9,10},{10,... | collective-permute-start | bytes 196616 | tf_op jit(solution)/shard_map/ppermute | solution.py:16
  58.5 0.6 copy-start.6
  58.5 0.7 copy-start.7
  59.2 0.6 copy-start.8
  61.5 14.2 %copy-start = (bf16[1024,512]{1,0:T(8,128)(2,1)S(1)}, bf16[1024,512]{1,0:T(8,128)(2,1)}, u32[]{:S(2)}) copy-start(bf16[1024,512]{1,0:T(8,128)(2,1)} %rhs_ref.1) | copy-start | bytes 3145732
  61.5 7.5 %collective-permute-start.7 = (bf16[96,512]{1,0:T(8,128)(2,1)}, bf16[96,512]{1,0:T(8,128)(2,1)S(1)}, u32[]{:S(2)}, u32[]{:S(2)}) collective-permute-start(bf16[96,512]{1,0:T(8,128)(2,1)} %leafblock.1.own_ref), channel_id=1, source_target_pairs={{0,4},{4,0},{8,12},{12,8},{16,20},{20,16},{24,28},{28,24},{1,5},{5... | collective-permute-start | bytes 294920 | tf_op jit(solution)/shard_map/ppermute | solution.py:16
  69.0 0.6 copy-start.5
  71.3 7.3 %copy-start.10 = (bf16[1024]{0:T(1024)(128)(2,1)S(1)}, bf16[1024]{0:T(1024)(128)(2,1)}, u32[]{:S(2)}) copy-start(bf16[1024]{0:T(1024)(128)(2,1)} %param.11) | copy-start | bytes 6148
  71.3 8.4 %collective-permute-start.10 = (bf16[128,512]{1,0:T(8,128)(2,1)}, bf16[128,512]{1,0:T(8,128)(2,1)S(1)}, u32[]{:S(2)}, u32[]{:S(2)}) collective-permute-start(bf16[128,512]{1,0:T(8,128)(2,1)} %pairblock.1.refs_0_), channel_id=1, source_target_pairs={{0,24},{4,28},{8,16},{12,20},{16,8},{20,12},{24,0},{28,4},{1,25},{... | collective-permute-start | bytes 393224 | tf_op jit(solution)/shard_map/ppermute | solution.py:16
  74.9 8.2 %collective-permute-start.8 = (bf16[128,512]{1,0:T(8,128)(2,1)}, bf16[128,512]{1,0:T(8,128)(2,1)S(1)}, u32[]{:S(2)}, u32[]{:S(2)}) collective-permute-start(bf16[128,512]{1,0:T(8,128)(2,1)} %pairblock.1.refs_0_), channel_id=1, source_target_pairs={{0,8},{4,12},{8,0},{12,4},{16,24},{20,28},{24,16},{28,20},{1,9},{5... | collective-permute-start | bytes 393224 | tf_op jit(solution)/shard_map/ppermute | solution.py:16
  74.9 11.9 %collective-permute-start.9 = (bf16[128,512]{1,0:T(8,128)(2,1)}, bf16[128,512]{1,0:T(8,128)(2,1)S(1)}, u32[]{:S(2)}, u32[]{:S(2)}) collective-permute-start(bf16[128,512]{1,0:T(8,128)(2,1)} %pairblock.1.refs_0_), channel_id=1, source_target_pairs={{0,16},{4,20},{8,24},{12,28},{16,0},{20,4},{24,8},{28,12},{1,17},{... | collective-permute-start | bytes 393224 | tf_op jit(solution)/shard_map/ppermute | solution.py:16
  79.7 7.0 %copy-start.2 = (bf16[128,512]{1,0:T(8,128)(2,1)}, bf16[128,512]{1,0:T(8,128)(2,1)S(1)}, u32[]{:S(2)}) copy-start(bf16[128,512]{1,0:T(8,128)(2,1)S(1)} %collective-permute-done.10.refs_3_) | copy-start | bytes 393220
  83.1 3.7 %copy-start.3 = (bf16[128,512]{1,0:T(8,128)(2,1)}, bf16[128,512]{1,0:T(8,128)(2,1)S(1)}, u32[]{:S(2)}) copy-start(bf16[128,512]{1,0:T(8,128)(2,1)S(1)} %collective-permute-done.8.refs_1_) | copy-start | bytes 393220
  86.8 0.7 copy-start.4
  93.5 13.5 %collective-permute-start.2 = (bf16[512,512]{1,0:T(8,128)(2,1)S(1)}, bf16[512,512]{1,0:T(8,128)(2,1)S(1)}, u32[]{:S(2)}, u32[]{:S(2)}) collective-permute-start(bf16[512,512]{1,0:T(8,128)(2,1)S(1)} %slice.74), channel_id=1, source_target_pairs={{0,2},{1,3},{2,0},{3,1},{4,6},{5,7},{6,4},{7,5},{8,10},{9,11},{10,... | collective-permute-start | bytes 1572872 | tf_op jit(solution)/shard_map/ppermute | solution.py:16
  95.2 13.2 %collective-permute-start.3 = (bf16[512,512]{1,0:T(8,128)(2,1)S(1)}, bf16[512,512]{1,0:T(8,128)(2,1)S(1)}, u32[]{:S(2)}, u32[]{:S(2)}) collective-permute-start(bf16[512,512]{1,0:T(8,128)(2,1)S(1)} %slice.76), channel_id=1, source_target_pairs={{0,1},{1,0},{2,3},{3,2},{4,5},{5,4},{6,7},{7,6},{8,9},{9,8},{10,11... | collective-permute-start | bytes 1572872 | tf_op jit(solution)/shard_map/ppermute | solution.py:16
  95.8 11.2 %slice-start = ((s8[8388608]{0:T(1024)(128)(4,1)}), s8[4194304]{0:T(1024)(128)(4,1)S(1)}, s32[]{:S(2)}) async-start(s8[8388608]{0:T(1024)(128)(4,1)} %bitcast.25), calls=%async_computation | async-start | bytes 8388608
  99.1 7.9 %slice-start.1 = ((s8[8388608]{0:T(1024)(128)(4,1)}), s8[4194304]{0:T(1024)(128)(4,1)S(1)}, s32[]{:S(2)}) async-start(s8[8388608]{0:T(1024)(128)(4,1)} %bitcast.25), calls=%async_computation.1 | async-start | bytes 8388608
  110.7 14.9 %collective-permute-start.14 = (bf16[512,512]{1,0:T(8,128)(2,1)S(1)}, bf16[512,512]{1,0:T(8,128)(2,1)S(1)}, u32[]{:S(2)}, u32[]{:S(2)}) collective-permute-start(bf16[512,512]{1,0:T(8,128)(2,1)S(1)} %get-tuple-element.15), channel_id=1, source_target_pairs={{0,2},{1,3},{2,0},{3,1},{4,6},{5,7},{6,4},{7,5},{8,10},{9,11},{10,... | collective-permute-start | bytes 1572872 | tf_op jit(solution)/shard_map/ppermute | solution.py:16
  113.6 28.6 %collective-permute-start.11 = (bf16[512,512]{1,0:T(8,128)(2,1)S(1)}, bf16[512,512]{1,0:T(8,128)(2,1)S(1)}, u32[]{:S(2)}, u32[]{:S(2)}) collective-permute-start(bf16[512,512]{1,0:T(8,128)(2,1)S(1)} %slice.123), channel_id=1, source_target_pairs={{0,1},{1,0},{2,3},{3,2},{4,5},{5,4},{6,7},{7,6},{8,9},{9,8},{10,11... | collective-permute-start | bytes 1572872 | tf_op jit(solution)/shard_map/ppermute | solution.py:16
  114.2 25.5 %collective-permute-start.12 = (bf16[512,512]{1,0:T(8,128)(2,1)S(1)}, bf16[512,512]{1,0:T(8,128)(2,1)S(1)}, u32[]{:S(2)}, u32[]{:S(2)}) collective-permute-start(bf16[512,512]{1,0:T(8,128)(2,1)S(1)} %get-tuple-element.14), channel_id=1, source_target_pairs={{0,1},{1,0},{2,3},{3,2},{4,5},{5,4},{6,7},{7,6},{8,9},{9,8},{10,11... | collective-permute-start | bytes 1572872 | tf_op jit(solution)/shard_map/ppermute | solution.py:16
  117.0 25.2 %collective-permute-start.16 = (bf16[512,512]{1,0:T(8,128)(2,1)S(1)}, bf16[512,512]{1,0:T(8,128)(2,1)S(1)}, u32[]{:S(2)}, u32[]{:S(2)}) collective-permute-start(bf16[512,512]{1,0:T(8,128)(2,1)S(1)} %slice.122), channel_id=1, source_target_pairs={{0,2},{1,3},{2,0},{3,1},{4,6},{5,7},{6,4},{7,5},{8,10},{9,11},{10,... | collective-permute-start | bytes 1572872 | tf_op jit(solution)/shard_map/ppermute | solution.py:16
  125.8 22.4 %collective-permute-start.15 = (bf16[512,512]{1,0:T(8,128)(2,1)S(1)}, bf16[512,512]{1,0:T(8,128)(2,1)S(1)}, u32[]{:S(2)}, u32[]{:S(2)}) collective-permute-start(bf16[512,512]{1,0:T(8,128)(2,1)S(1)} %fusion.17), channel_id=1, source_target_pairs={{0,1},{1,0},{2,3},{3,2},{4,5},{5,4},{6,7},{7,6},{8,9},{9,8},{10,11... | collective-permute-start | bytes 1572872 | tf_op jit(solution)/shard_map/ppermute | solution.py:16
  139.9 1.9 %copy-start.1 = (bf16[1024,32]{0,1:T(8,128)(2,1)S(1)}, bf16[1024,32]{0,1:T(8,128)(2,1)}, u32[]{:S(2)}) copy-start(bf16[1024,32]{0,1:T(8,128)(2,1)} %param.12) | copy-start | bytes 196612
  139.9 1.9 %copy-start.9 = (bf16[32,512]{1,0:T(8,128)(2,1)S(1)}, bf16[32,512]{1,0:T(8,128)(2,1)}, u32[]{:S(2)}) copy-start(bf16[32,512]{1,0:T(8,128)(2,1)} %get-tuple-element.6) | copy-start | bytes 98308
  139.9 9.2 %collective-permute-start.13 = (bf16[512,512]{1,0:T(8,128)(2,1)S(1)}, bf16[512,512]{1,0:T(8,128)(2,1)S(1)}, u32[]{:S(2)}, u32[]{:S(2)}) collective-permute-start(bf16[512,512]{1,0:T(8,128)(2,1)S(1)} %fusion.19), channel_id=1, source_target_pairs={{0,2},{1,3},{2,0},{3,1},{4,6},{5,7},{6,4},{7,5},{8,10},{9,11},{10,... | collective-permute-start | bytes 1572872 | tf_op jit(solution)/shard_map/ppermute | solution.py:16

commit v2 on v1

--- a/solution.py
+++ b/solution.py
@@ -1,4 +1,5 @@
 import functools
+import math
 
 import jax
 import jax.numpy as jnp
@@ -7,8 +8,11 @@
 from jax.experimental.pallas import tpu as pltpu
 from jax.sharding import PartitionSpec as P
 
+
 F32 = jnp.float32
 BF16 = jnp.bfloat16
+LANES = 128
+UNROLL = 32
 
 
 def exchange(block, axis, mask):
@@ -36,6 +40,22 @@
 
 def smem():
     return pl.BlockSpec(memory_space=pltpu.SMEM)
+
+
+def call(body, ops, specs, out_shape, after=(), **rest):
+    skip = len(after)
+
+    def skipping(*refs):
+        body(*refs[skip:])
+
+    out_specs = jax.tree.map(lambda _: vmem(), out_shape)
+    return pl.pallas_call(
+        skipping,
+        out_shape=out_shape,
+        in_specs=[pl.BlockSpec(memory_space=pl.ANY)] * skip + specs,
+        out_specs=out_specs,
+        **rest,
+    )(*after, *ops)
 
 
 def from_partner(block, axis, distance):
@@ -177,15 +197,15 @@
 
 
 def pack_body(rhs_ref, link_ref, sep_ref, fac_ref, out_ref):
-    levels, width, sep_block = sep_ref.shape
-    first = link_ref.shape[1]
+    levels, sep_block, width = sep_ref.shape
+    first = link_ref.shape[0]
     rows, cols = fac_ref.shape
-    out_ref[0:first, :] = dot_tn(link_ref[...], rhs_ref[...]).astype(BF16)
+    out_ref[0:first, :] = dot_nn(link_ref[...], rhs_ref[...]).astype(BF16)
     out_ref[first:, :] = jnp.zeros((out_ref.shape[0] - first, out_ref.shape[1]), BF16)
     for level in range(levels):
-        out_ref[first : first + sep_block, level * width : (level + 1) * width] = (
-            sep_ref[level].astype(F32).T.astype(BF16)
-        )
+        out_ref[first : first + sep_block, level * width : (level + 1) * width] = sep_ref[
+            level
+        ]
     out_ref[first + sep_block : first + sep_block + rows, 0:cols] = fac_ref[...]
 
 
@@ -283,42 +303,133 @@
         val_ref[...] = value
         lanes = pl.ds(pl.multiple_of(me * slice_width, slice_width), slice_width)
         mine = val_ref[pl.ds(pl.multiple_of(leaf * sep_block, sep_block), sep_block), lanes]
-        sol_ref[level - 1] = mine.T
+        sol_ref[level - 1] = mine
     first_ref[...] = val_ref[pl.ds(pl.multiple_of(pair * first, first), first), :].astype(BF16)
 
 
-def tree(place, rhs, link, sep_rhs, sep_factor, sep_dinv):
+def arrange_body(dest_ref, factor_ref, *refs):
+    outs, (turned_ref, sorted_ref) = refs[:-2], refs[-2:]
+    step = pl.program_id(0)
+    rows, width = factor_ref.shape
+    tiles = rows // LANES
+    turned = factor_ref[...].astype(F32).T
+    for tile in range(tiles):
+        turned_ref[pl.ds(tile, width, stride=tiles), :] = turned[:, tile * LANES : (tile + 1) * LANES]
+
+    def move(group, carry):
+        for lane in range(UNROLL):
+            source = group * UNROLL + lane
+            target = dest_ref[step * width + source]
+            sorted_ref[pl.ds(pl.multiple_of(target * tiles, tiles), tiles), :] = turned_ref[
+                pl.ds(pl.multiple_of(source * tiles, tiles), tiles), :
+            ]
+        return carry
+
+    lax.fori_loop(0, width // UNROLL, move, 0)
+
+    @pl.when(step == pl.num_programs(0) - 1)
+    def _():
+        for index, out_ref in enumerate(outs):
+            count = out_ref.shape[0]
+            chunk = min(count, 256)
+
+            def write(part, carry, index=index, out_ref=out_ref, count=count, chunk=chunk):
+                base = index * count * tiles + part * chunk * tiles
+                for tile in range(tiles):
+                    out_ref[
+                        pl.ds(pl.multiple_of(part * chunk, chunk), chunk),
+                        tile * LANES : (tile + 1) * LANES,
+                    ] = sorted_ref[pl.ds(base + tile, chunk, stride=tiles), :].astype(BF16)
+                return carry
+
+            lax.fori_loop(0, count // chunk, write, 0)
+
+
+def arrange(factor, dest, count):
+    rows, cols = factor.shape
+    width = math.gcd(cols, 4 * LANES)
+    part = cols // count
+    return pl.pallas_call(
+        arrange_body,
+        grid=(cols // width,),
+        out_shape=[jax.ShapeDtypeStruct((part, rows), BF16)] * count,
+        in_specs=[smem(), pl.BlockSpec((rows, width), lambda step: (0, step))],
+        out_specs=[vmem()] * count,
+        scratch_shapes=[
+            pltpu.VMEM((width * rows // LANES, LANES), F32),
+            pltpu.VMEM((cols * rows // LANES, LANES), F32),
+        ],
+        compiler_params=pltpu.CompilerParams(vmem_limit_bytes=48 * 2**20),
+        name="arrange",
+    )(dest, factor)
+
+
+def local_pairs(leaf_rhs, leaf_inv, ordering, leaf_dinv, leaf_link, sep_rhs, sep_factor, sep_dinv):
+    rows, width = leaf_rhs.shape
+    half = rows // 2
+    group = lax.axis_size("grp")
     levels, slice_width, sep_block = sep_rhs.shape
-    first = link.shape[1]
-    width = rhs.shape[1]
-    rows, cols = sep_factor.shape
-    aux = pl.pallas_call(
+    first = leaf_link.shape[1]
+    fac_rows, cols = sep_factor.shape
+    leaf = lax.axis_index("leaf").astype(jnp.int32)
+    me = lax.axis_index("grp").astype(jnp.int32)
+    place = jnp.stack([leaf, me])
+    link_turned = leaf_link.T
+
+    low, high = leaf_rhs[:half], leaf_rhs[half:]
+    x_low = exchange(low, "grp", 1)
+    y_high = exchange(high, "grp", 2)
+    x_high = exchange(high, "grp", 1)
+    y_low = exchange(low, "grp", 2)
+    dest = (ordering[0] // rows ^ me) * rows + ordering[0] % rows
+    blocks = arrange(leaf_inv, dest, group)
+    d_low = exchange(x_low, "grp", 2)
+    d_high = exchange(y_high, "grp", 1)
+
+    aux = call(
         pack_body,
-        out_shape=jax.ShapeDtypeStruct((first + 2 * sep_block, width), BF16),
-        in_specs=[vmem()] * 4,
-        out_specs=vmem(),
-        name="pack",
-    )(rhs, link, sep_rhs, sep_factor)
-    aux_x, aux_y, aux_d = (exchange(aux, "grp", mask) for mask in (1, 2, 3))
-    leaf_block = pl.pallas_call(
-        functools.partial(leaf_body, first=first, levels=levels, rows=rows, cols=cols),
-        out_shape=jax.ShapeDtypeStruct((first + (levels + 1) * sep_block, width), BF16),
-        in_specs=[smem()] + [vmem()] * 5,
-        out_specs=vmem(),
-        name="leafblock",
-    )(place, aux, aux_x, aux_y, aux_d, sep_dinv)
+        (leaf_rhs, link_turned, jnp.swapaxes(sep_rhs, 1, 2), sep_factor),
+        [vmem()] * 4,
+        jax.ShapeDtypeStruct((first + 2 * sep_block, width), BF16),
+        after=(x_low, y_high),
+    )
+    aux_parts = [aux] + [exchange(aux, "grp", mask) for mask in range(1, group)]
+
+    leaf_y = dot_tn(blocks[0], leaf_rhs)
+    leaf_y = leaf_y + dot_tn(blocks[1][:half], x_low)
+    leaf_y = leaf_y + dot_tn(blocks[2][half:], y_high)
+    leaf_y = leaf_y + dot_tn(blocks[1][half:], x_high)
+    leaf_y = leaf_y + dot_tn(blocks[2][:half], y_low)
+    leaf_y = leaf_y + dot_tn(blocks[3][:half], d_low)
+    leaf_y = leaf_y + dot_tn(blocks[3][half:], d_high)
+    leaf_z = (leaf_dinv.astype(F32)[:, None] * leaf_y).astype(BF16)
+
+    relay_low = exchange(dot_nn(blocks[3][:half], leaf_z).astype(BF16), "grp", 1)
+    relay_high = exchange(dot_nn(blocks[3][half:], leaf_z).astype(BF16), "grp", 2)
+    sum_x_low = exchange(dot_nn(blocks[1][:half], leaf_z).astype(BF16), "grp", 1)
+    sum_y_high = exchange(dot_nn(blocks[2][half:], leaf_z).astype(BF16), "grp", 2)
+    near_x_high = dot_nn(blocks[1][half:], leaf_z)
+    near_y_low = dot_nn(blocks[2][:half], leaf_z)
+
+    own = dot_nn(blocks[0], leaf_z)
+    leaf_block = call(
+        functools.partial(leaf_body, first=first, levels=levels, rows=fac_rows, cols=cols),
+        (place, *aux_parts, sep_dinv),
+        [smem()] + [vmem()] * 5,
+        jax.ShapeDtypeStruct((first + (levels + 1) * sep_block, width), BF16),
+        after=(near_x_high, near_y_low, own),
+    )
     partner = exchange(leaf_block, "leaf", 1)
-    pair_block = pl.pallas_call(
+    pair_block = call(
         functools.partial(pair_body, first=first, levels=levels, sep_block=sep_block),
-        out_shape=jax.ShapeDtypeStruct(((levels + 1) * first, width), BF16),
-        in_specs=[smem(), vmem(), vmem()],
-        out_specs=vmem(),
-        name="pairblock",
-    )(place, leaf_block, partner)
+        (place, leaf_block, partner),
+        [smem(), vmem(), vmem()],
+        jax.ShapeDtypeStruct(((levels + 1) * first, width), BF16),
+    )
     count = lax.axis_size("leaf") // 2
     pairs = [pair_block] + [exchange(pair_block, "leaf", 2 * mask) for mask in range(1, count)]
     nsep = count * first
-    return pl.pallas_call(
+    first_all, sep_turned = pl.pallas_call(
         functools.partial(
             tree_body,
             count=count,
@@ -330,7 +441,7 @@
         ),
         out_shape=(
             jax.ShapeDtypeStruct((first, width), BF16),
-            jax.ShapeDtypeStruct((levels, slice_width, sep_block), F32),
+            jax.ShapeDtypeStruct((levels, sep_block, slice_width), F32),
         ),
         in_specs=[smem()] + [vmem()] * count,
         out_specs=(vmem(), vmem()),
@@ -338,46 +449,12 @@
         name="tree",
     )(place, *pairs)
 
-
-def local_pairs(leaf_rhs, leaf_inv, ordering, leaf_dinv, leaf_link, sep_rhs, sep_factor, sep_dinv):
-    rows = leaf_rhs.shape[0]
-    half = rows // 2
-    leaf = lax.axis_index("leaf").astype(jnp.int32)
-    me = lax.axis_index("grp").astype(jnp.int32)
-    place = jnp.stack([leaf, me])
-
-    rhs_x = exchange(leaf_rhs, "grp", 1)
-    rhs_y = exchange(leaf_rhs, "grp", 2)
-    first_all, solution_here = tree(place, leaf_rhs, leaf_link, sep_rhs, sep_factor, sep_dinv)
-    far_low = exchange(rhs_x[:half], "grp", 2)
-    far_high = exchange(rhs_y[half:], "grp", 1)
-
-    inverse = jnp.argsort(ordering[0])
-    inverse = inverse.reshape(-1, rows)
-    inverse = jnp.concatenate([inverse[me ^ index] for index in range(inverse.shape[0])])
-    picked = jnp.take(leaf_inv, inverse, axis=1).T
-    blocks = [picked[index * rows : (index + 1) * rows] for index in range(lax.axis_size("grp"))]
-
-    leaf_y = dot_tn(blocks[0], leaf_rhs)
-    leaf_y = leaf_y + dot_tn(blocks[1], rhs_x)
-    leaf_y = leaf_y + dot_tn(blocks[2], rhs_y)
-    leaf_y = leaf_y + dot_tn(blocks[3][:half], far_low)
-    leaf_y = leaf_y + dot_tn(blocks[3][half:], far_high)
-    leaf_z = (leaf_dinv.astype(F32)[:, None] * leaf_y).astype(BF16)
-
-    far = dot_nn(blocks[3], leaf_z).astype(BF16)
-    relay_low = exchange(far[:half], "grp", 1)
-    relay_high = exchange(far[half:], "grp", 2)
-    near_x = dot_nn(blocks[1], leaf_z)
-    x_low = exchange(near_x[:half].astype(BF16), "grp", 1)
-    near_y = dot_nn(blocks[2], leaf_z)
-    y_high = exchange(near_y[half:].astype(BF16), "grp", 2)
-    x_high = exchange((near_x[half:] + relay_high.astype(F32)).astype(BF16), "grp", 1)
-    y_low = exchange((near_y[:half] + relay_low.astype(F32)).astype(BF16), "grp", 2)
-    own = dot_nn(blocks[0], leaf_z) - dot_nn(leaf_link, first_all)
-    low = own[:half] + x_low.astype(F32) + y_low.astype(F32)
-    high = own[half:] + x_high.astype(F32) + y_high.astype(F32)
-    return jnp.concatenate([low, high], axis=0), solution_here
+    sum_x_high = exchange((near_x_high + relay_high.astype(F32)).astype(BF16), "grp", 1)
+    sum_y_low = exchange((near_y_low + relay_low.astype(F32)).astype(BF16), "grp", 2)
+    own = own - dot_tn(link_turned, first_all)
+    own_low = own[:half] + sum_x_low.astype(F32) + sum_y_low.astype(F32)
+    own_high = own[half:] + sum_x_high.astype(F32) + sum_y_high.astype(F32)
+    return jnp.concatenate([own_low, own_high], axis=0), jnp.swapaxes(sep_turned, 1, 2)
 
 
 def fits(leaf_rhs, leaf_inv, sep_rhs, sep_factor, leaf_link):
@@ -389,6 +466,7 @@
         count == 2**2
         and leaf_inv.shape[1] == count * leaf_rhs.shape[0]
         and leaf_rhs.shape[0] % 256 == 0
+        and leaf_rhs.shape[0] // LANES == 8
         and leaf_link.shape[1] == 2 * sep_block
         and sep_block % 16 == 0
         and slice_width % 128 == 0

time: 152 us -> 114 us (0.75)
  local copies, waits for them, and re-layouts: 47 us -> 4.61 us
  Pallas kernels: 9.06 us -> 26.9 us
  other arithmetic: 17 us -> 3.67 us
  waiting for transfers between devices: 41.6 us -> 28.7 us
  matrix products: 16.7 us -> 25.6 us
  starting transfers between devices: 19 us -> 22.9 us
    gather x1 -> x0, local copies, waits for them, and re-layouts: 25.4 us -> none  [local_pairs(): picked = jnp.take(leaf_inv, inverse, axis=1).T]
    pallas_call x4 -> x5, Pallas kernels: 9.06 us -> 26.9 us  [the longest x1 18.1 us: arrange(): pl.pallas_call(arrange_body, grid=(cols // width,), out_shape=[jax.ShapeD...]
    unnamed x30 -> x34, local copies, waits for them, and re-layouts: 19.1 us -> 3.33 us
    ppermute x17 -> x19, waiting for transfers between devices: 41.6 us -> 28.7 us  [exchange(): lax.ppermute(block, axis, [(low, low ^ mask) for low in range(count)])]
    select_n x2 -> x0, other arithmetic: 7.47 us -> none  [local_pairs(): picked = jnp.take(leaf_inv, inverse, axis=1).T]
    dot_general x5 -> x7, matrix products: 5.45 us -> 12 us  [dot_nn(): return jnp.dot(lhs, rhs, preferred_element_type=F32)]
    sort x1 -> x0, other arithmetic: 6.5 us -> none  [local_pairs(): inverse = jnp.argsort(ordering[0])]
    ppermute x17 -> x19, starting transfers between devices: 19 us -> 22.9 us  [exchange(): lax.ppermute(block, axis, [(low, low ^ mask) for low in range(count)])]
  transfers between devices with their start and end apart: 17 -> 19, of which waited for: 9 -> 7; matrix products, arithmetic and copies ran while one was open for 49% -> 23% of each run, Pallas kernels for 6% -> 21%
where the time goes in v2:
time: 114 us; the launch traced here: 113 us
  waiting for transfers between devices  28.7 us (25%)
  Pallas kernels  26.9 us (24%)
  matrix products  25.6 us (22%)
  starting transfers between devices  22.9 us (20%)
  local copies, waits for them, and re-layouts  4.61 us (4%)
  other arithmetic  3.67 us (3%)
    ppermute x19, waiting for transfers between devices, exchange(): lax.ppermute(block, axis, [(low, low ^ mask) for low in range(count)])  28.7 us
    ppermute x19, starting transfers between devices, exchange(): lax.ppermute(block, axis, [(low, low ^ mask) for low in range(count)])  22.9 us
    pallas_call x1, Pallas kernels, arrange(): pl.pallas_call(arrange_body, grid=(cols // width,), out_shape=[jax.ShapeD...  18.1 us
    dot_general x8, matrix products, dot_tn(): lax.dot_general(lhs, rhs, (((0,), (0,)), ((), ())), preferred_element_typ...  13.7 us
    dot_general x7, matrix products, dot_nn(): return jnp.dot(lhs, rhs, preferred_element_type=F32)  12 us
    pallas_call x3, Pallas kernels, call(): pl.pallas_call(skipping, out_shape=out_shape, in_specs=[pl.BlockSpec(memo...  5.54 us
    unnamed x34, local copies, waits for them, and re-layouts  3.33 us
    pallas_call x1, Pallas kernels, local_pairs(): pl.pallas_call(functools.partial(tree_body, count=count, first=first, lev...  3.24 us
  transfers between devices with their start and end apart: 19, of which 7 were waited for; matrix products, arithmetic and copies ran while one was open for 23% of the time, Pallas kernels for 21%

profile of v2, /device:TPU:0, one launch (start us, length us, event | category | flops | bytes accessed | tf_op | source)
XLA Modules:
  0.0 113.2 jit_solution(9227712865168989576)
XLA Ops:
  0.6 1.3 %fusion.31 = (bf16[512,512]{1,0:T(8,128)(2,1)S(1)}, bf16[512,512]{1,0:T(8,128)(2,1)S(1)}) fusion(bf16[1024,512]{1,0:T(8,128)(2,1)} %refs_2_.1), kind=kLoop, calls=%fused_computation.47 | loop fusion | bytes 2097152 | tf_op jit(solution)/shard_map/slice | solution.py:379
  1.9 3.0 %collective-permute-start.2 = (bf16[512,512]{1,0:T(8,128)(2,1)S(1)}, bf16[512,512]{1,0:T(8,128)(2,1)}, u32[]{:S(2)}, u32[]{:S(2)}) collective-permute-start(bf16[512,512]{1,0:T(8,128)(2,1)S(1)} %get-tuple-element.16), channel_id=1, source_target_pairs={{0,1},{1,0},{2,3},{3,2},{4,5},{5,4},{6,7},{7,6},{8,9},{9,8},{10,11... | collective-permute-start | bytes 1572872 | tf_op jit(solution)/shard_map/ppermute | solution.py:20
  4.9 1.5 %collective-permute-start.1 = (bf16[512,512]{1,0:T(8,128)(2,1)S(1)}, bf16[512,512]{1,0:T(8,128)(2,1)}, u32[]{:S(2)}, u32[]{:S(2)}) collective-permute-start(bf16[512,512]{1,0:T(8,128)(2,1)S(1)} %get-tuple-element.16), channel_id=1, source_target_pairs={{0,2},{1,3},{2,0},{3,1},{4,6},{5,7},{6,4},{7,5},{8,10},{9,11},{10,... | collective-permute-start | bytes 1572872 | tf_op jit(solution)/shard_map/ppermute | solution.py:20
  6.5 0.5 collective-permute-start.3
  7.1 18.1 %arrange.1 = (bf16[1024,1024]{1,0:T(8,128)(2,1)S(1)}, bf16[1024,1024]{1,0:T(8,128)(2,1)S(1)}, bf16[1024,1024]{1,0:T(8,128)(2,1)}, bf16[1024,1024]{1,0:T(8,128)(2,1)}) custom-call(s32[4096]{0:T(1024)S(1)} %fusion.26.dest_ref, bf16[1024,4096]{1,0:T(8,128)(2,1)} %factor_ref.1), custom_call_target="tpu_custom_call" | custom-call | tf_op jit(solution)/shard_map/arrange/pallas_call | solution.py:352
  25.2 1.4 %copy-done = bf16[1024,1024]{1,0:T(8,128)(2,1)} copy-done((bf16[1024,1024]{1,0:T(8,128)(2,1)}, bf16[1024,1024]{1,0:T(8,128)(2,1)S(1)}, u32[]{:S(2)}) %copy-start) | copy-done | bytes 2097176
  26.6 2.7 %fusion.32 = f32[1024,512]{1,0:T(8,128)} fusion(bf16[1024,1024]{1,0:T(8,128)(2,1)S(1)} %get-tuple-element.8, bf16[1024,512]{1,0:T(8,128)(2,1)S(1)} %copy-done.3), kind=kOutput, calls=%fused_computation.48 | convolution fusion | flops 1073741824 | bytes 5242880 | tf_op jit(solution)/shard_map/dot_general | solution.py:30
  29.2 0.6 pad_add_fusion.refs_3_.refs_0_.place_ref
  29.8 2.2 %shard_map.95.refs_4_ = bf16[64,512]{1,0:T(8,128)(2,1)} custom-call(bf16[512,512]{1,0:T(8,128)(2,1)} %collective-permute-done.refs_0_, bf16[512,512]{1,0:T(8,128)(2,1)} %collective-permute-done.1.refs_1_, bf16[1024,512]{1,0:T(8,128)(2,1)} %refs_2_.1, bf16[32,1024]{1,0:T(8,128)(2,1)} %bitcast.26, bf16[3,16,128]{2,1,0:T(8,128)(2,1)} %bitcast.28, ...), custom_call_target="tpu_custom_call" | custom-call | tf_op jit(solution)/shard_map/pallas_call | solution.py:52
  32.0 2.9 %collective-permute-start.8 = (bf16[64,512]{1,0:T(8,128)(2,1)}, bf16[64,512]{1,0:T(8,128)(2,1)S(1)}, u32[]{:S(2)}, u32[]{:S(2)}) collective-permute-start(bf16[64,512]{1,0:T(8,128)(2,1)} %shard_map.95.refs_4_), channel_id=1, source_target_pairs={{0,3},{1,2},{2,1},{3,0},{4,7},{5,6},{6,5},{7,4},{8,11},{9,10},{10,... | collective-permute-start | bytes 196616 | tf_op jit(solution)/shard_map/ppermute | solution.py:20
  34.9 0.5 collective-permute-start.7
  35.5 1.8 %fusion.22 = f32[1024,512]{1,0:T(8,128)S(1)} fusion(bf16[512,512]{1,0:T(8,128)(2,1)} %collective-permute-done.refs_0_, bf16[1024,1024]{1,0:T(8,128)(2,1)S(1)} %get-tuple-element.9), kind=kOutput, calls=%fused_computation.31 | convolution fusion | flops 536870912 | bytes 3670016 | tf_op jit(solution)/shard_map/dot_general | solution.py:30
  37.3 2.0 %collective-permute-start.4 = (bf16[512,512]{1,0:T(8,128)(2,1)}, bf16[512,512]{1,0:T(8,128)(2,1)S(1)}, u32[]{:S(2)}, u32[]{:S(2)}) collective-permute-start(bf16[512,512]{1,0:T(8,128)(2,1)} %collective-permute-done.refs_0_), channel_id=1, source_target_pairs={{0,2},{1,3},{2,0},{3,1},{4,6},{5,7},{6,4},{7,5},{8,10},{9,11},{10,... | collective-permute-start | bytes 1572872 | tf_op jit(solution)/shard_map/ppermute | solution.py:20
  39.3 1.8 %fusion.16 = f32[1024,512]{1,0:T(8,128)S(1)} fusion(bf16[512,512]{1,0:T(8,128)(2,1)} %collective-permute-done.2, bf16[1024,1024]{1,0:T(8,128)(2,1)S(1)} %get-tuple-element.9), kind=kOutput, calls=%fused_computation.25 | convolution fusion | flops 536870912 | bytes 3670016 | tf_op jit(solution)/shard_map/dot_general | solution.py:30
  41.1 1.8 %fusion.19 = f32[1024,512]{1,0:T(8,128)S(1)} fusion(bf16[512,512]{1,0:T(8,128)(2,1)} %collective-permute-done.1.refs_1_, bf16[1024,1024]{1,0:T(8,128)(2,1)S(1)} %copy-done.2), kind=kOutput, calls=%fused_computation.28 | convolution fusion | flops 536870912 | bytes 3670016 | tf_op jit(solution)/shard_map/dot_general | solution.py:30
  42.9 1.6 %collective-permute-start.5 = (bf16[512,512]{1,0:T(8,128)(2,1)}, bf16[512,512]{1,0:T(8,128)(2,1)S(1)}, u32[]{:S(2)}, u32[]{:S(2)}) collective-permute-start(bf16[512,512]{1,0:T(8,128)(2,1)} %collective-permute-done.1.refs_1_), channel_id=1, source_target_pairs={{0,1},{1,0},{2,3},{3,2},{4,5},{5,4},{6,7},{7,6},{8,9},{9,8},{10,11... | collective-permute-start | bytes 1572872 | tf_op jit(solution)/shard_map/ppermute | solution.py:20
  44.5 1.8 %fusion.12 = f32[1024,512]{1,0:T(8,128)S(1)} fusion(bf16[512,512]{1,0:T(8,128)(2,1)} %collective-permute-done.3, bf16[1024,1024]{1,0:T(8,128)(2,1)S(1)} %copy-done.2), kind=kOutput, calls=%fused_computation.21 | convolution fusion | flops 536870912 | bytes 3670016 | tf_op jit(solution)/shard_map/dot_general | solution.py:30
  46.3 4.0 %collective-permute-done.4 = bf16[512,512]{1,0:T(8,128)(2,1)S(1)} collective-permute-done((bf16[512,512]{1,0:T(8,128)(2,1)}, bf16[512,512]{1,0:T(8,128)(2,1)S(1)}, u32[]{:S(2)}, u32[]{:S(2)}) %collective-permute-start.4) | collective-permute-done | bytes 524320 | tf_op jit(solution)/shard_map/ppermute | solution.py:20
  50.2 0.7 fusion.8
  51.0 3.6 %collective-permute-done.5 = bf16[512,512]{1,0:T(8,128)(2,1)S(1)} collective-permute-done((bf16[512,512]{1,0:T(8,128)(2,1)}, bf16[512,512]{1,0:T(8,128)(2,1)S(1)}, u32[]{:S(2)}, u32[]{:S(2)}) %collective-permute-start.5) | collective-permute-done | bytes 524320 | tf_op jit(solution)/shard_map/ppermute | solution.py:20
  54.6 1.1 multiply_convert_fusion
  55.7 0.7 convolution_convert_fusion.2
  56.4 1.6 %collective-permute-start.14 = (bf16[512,512]{1,0:T(8,128)(2,1)S(1)}, bf16[512,512]{1,0:T(8,128)(2,1)S(1)}, u32[]{:S(2)}, u32[]{:S(2)}) collective-permute-start(bf16[512,512]{1,0:T(8,128)(2,1)S(1)} %convolution_convert_fusion.2), channel_id=1, source_target_pairs={{0,1},{1,0},{2,3},{3,2},{4,5},{5,4},{6,7},{7,6},{8,9},{9,8},{10,11... | collective-permute-start | bytes 1572872 | tf_op jit(solution)/shard_map/ppermute | solution.py:20
  58.0 0.7 convolution_convert_fusion.1
  58.7 0.7 collective-permute-start.16
  59.4 2.6 %fusion.33.refs_2_ = f32[1024,512]{1,0:T(8,128)} fusion(bf16[1024,1024]{1,0:T(8,128)(2,1)S(1)} %copy-done.1, bf16[1024,512]{1,0:T(8,128)(2,1)S(1)} %multiply_convert_fusion), kind=kOutput, calls=%fused_computation.49 | convolution fusion | flops 1073741824 | bytes 5242880 | tf_op jit(solution)/shard_map/dot_general | solution.py:34
  62.0 5.0 %collective-permute-done.14 = bf16[512,512]{1,0:T(8,128)(2,1)S(1)} collective-permute-done((bf16[512,512]{1,0:T(8,128)(2,1)S(1)}, bf16[512,512]{1,0:T(8,128)(2,1)S(1)}, u32[]{:S(2)}, u32[]{:S(2)}) %collective-permute-start.14) | collective-permute-done | bytes 524320 | tf_op jit(solution)/shard_map/ppermute | solution.py:20
  67.0 1.9 %add_convert_fusion.1 = (bf16[512,512]{1,0:T(8,128)(2,1)}, f32[512,512]{1,0:T(8,128)}) fusion(bf16[512,512]{1,0:T(8,128)(2,1)S(1)} %collective-permute-done.14, bf16[1024,512]{1,0:T(8,128)(2,1)S(1)} %multiply_convert_fusion, bf16[1024,1024]{1,0:T(8,128)(2,1)S(1)} %copy-done.2), kind=kOutput, calls=%fused_computation.12 | convolution fusion | flops 537657344 | bytes 4194304 | tf_op jit(solution)/shard_map/dot_general | solution.py:34
  69.0 1.9 %add_convert_fusion = (bf16[512,512]{1,0:T(8,128)(2,1)}, f32[512,512]{1,0:T(8,128)}) fusion(bf16[512,512]{1,0:T(8,128)(2,1)S(1)} %collective-permute-done.16, bf16[1024,512]{1,0:T(8,128)(2,1)S(1)} %multiply_convert_fusion, bf16[1024,1024]{1,0:T(8,128)(2,1)S(1)} %get-tuple-element.9), kind=kOutput, calls=%fused_computation.11 | convolution fusion | flops 537657344 | bytes 4194304 | tf_op jit(solution)/shard_map/dot_general | solution.py:34
  70.9 0.6 copy-done.12
  71.5 1.7 %shard_map.96.refs_1_ = bf16[96,512]{1,0:T(8,128)(2,1)} custom-call(f32[512,512]{1,0:T(8,128)} %get-tuple-element.21.refs_0_, f32[512,512]{1,0:T(8,128)} %get-tuple-element.19.refs_1_, f32[1024,512]{1,0:T(8,128)} %fusion.33.refs_2_, s32[2]{0:T(128)} %pad_add_fusion.refs_3_.refs_0_.place_ref, bf16[64,512]{1,0:T(8,128)(2,1)} %shard_map.95.refs_4_, ...), custom_call_target="tpu_custom_call" | custom-call | tf_op jit(solution)/shard_map/pallas_call | solution.py:52
  73.3 2.7 %convolution_convert_fusion = bf16[512,512]{1,0:T(8,128)(2,1)} fusion(bf16[1024,512]{1,0:T(8,128)(2,1)S(1)} %multiply_convert_fusion, bf16[1024,1024]{1,0:T(8,128)(2,1)} %get-tuple-element.10), kind=kOutput, calls=%fused_computation.3 | convolution fusion | flops 537133056 | bytes 2621440 | tf_op jit(solution)/shard_map/dot_general | solution.py:34
  76.0 0.6 copy-done.11
  76.6 1.6 %shard_map.97.refs_0_ = bf16[128,512]{1,0:T(8,128)(2,1)} custom-call(s32[2]{0:T(128)} %pad_add_fusion.refs_3_.refs_0_.place_ref, bf16[96,512]{1,0:T(8,128)(2,1)} %shard_map.96.refs_1_, bf16[96,512]{1,0:T(8,128)(2,1)} %copy-done.11), custom_call_target="tpu_custom_call" | custom-call | tf_op jit(solution)/shard_map/pallas_call | solution.py:52
  78.3 3.6 %collective-permute-start.12 = (bf16[128,512]{1,0:T(8,128)(2,1)}, bf16[128,512]{1,0:T(8,128)(2,1)S(1)}, u32[]{:S(2)}, u32[]{:S(2)}) collective-permute-start(bf16[128,512]{1,0:T(8,128)(2,1)} %shard_map.97.refs_0_), channel_id=1, source_target_pairs={{0,24},{4,28},{8,16},{12,20},{16,8},{20,12},{24,0},{28,4},{1,25},{... | collective-permute-start | bytes 393224 | tf_op jit(solution)/shard_map/ppermute | solution.py:20
  81.9 1.5 %convolution_convert_fusion.3 = bf16[512,512]{1,0:T(8,128)(2,1)} fusion(bf16[1024,512]{1,0:T(8,128)(2,1)S(1)} %multiply_convert_fusion, bf16[1024,1024]{1,0:T(8,128)(2,1)S(1)} %get-tuple-element.9), kind=kOutput, calls=%fused_computation.6 | convolution fusion | flops 537133056 | bytes 2621440 | tf_op jit(solution)/shard_map/dot_general | solution.py:34
  83.4 1.4 %collective-permute-start.13 = (bf16[512,512]{1,0:T(8,128)(2,1)}, bf16[512,512]{1,0:T(8,128)(2,1)S(1)}, u32[]{:S(2)}, u32[]{:S(2)}) collective-permute-start(bf16[512,512]{1,0:T(8,128)(2,1)} %convolution_convert_fusion.3), channel_id=1, source_target_pairs={{0,1},{1,0},{2,3},{3,2},{4,5},{5,4},{6,7},{7,6},{8,9},{9,8},{10,11... | collective-permute-start | bytes 1572872 | tf_op jit(solution)/shard_map/ppermute | solution.py:20
  84.8 0.8 collective-permute-start.18
  85.6 1.3 %collective-permute-start.15 = (bf16[512,512]{1,0:T(8,128)(2,1)}, bf16[512,512]{1,0:T(8,128)(2,1)}, u32[]{:S(2)}, u32[]{:S(2)}) collective-permute-start(bf16[512,512]{1,0:T(8,128)(2,1)} %get-tuple-element.18), channel_id=1, source_target_pairs={{0,2},{1,3},{2,0},{3,1},{4,6},{5,7},{6,4},{7,5},{8,10},{9,11},{10,... | collective-permute-start | bytes 1572872 | tf_op jit(solution)/shard_map/ppermute | solution.py:20
  86.9 1.3 %collective-permute-start.17 = (bf16[512,512]{1,0:T(8,128)(2,1)}, bf16[512,512]{1,0:T(8,128)(2,1)}, u32[]{:S(2)}, u32[]{:S(2)}) collective-permute-start(bf16[512,512]{1,0:T(8,128)(2,1)} %get-tuple-element.20), channel_id=1, source_target_pairs={{0,1},{1,0},{2,3},{3,2},{4,5},{5,4},{6,7},{7,6},{8,9},{9,8},{10,11... | collective-permute-start | bytes 1572872 | tf_op jit(solution)/shard_map/ppermute | solution.py:20
  88.2 5.7 %collective-permute-done.11.refs_2_ = bf16[128,512]{1,0:T(8,128)(2,1)S(1)} collective-permute-done((bf16[128,512]{1,0:T(8,128)(2,1)}, bf16[128,512]{1,0:T(8,128)(2,1)S(1)}, u32[]{:S(2)}, u32[]{:S(2)}) %collective-permute-start.11) | collective-permute-done | bytes 131104 | tf_op jit(solution)/shard_map/ppermute | solution.py:20
  93.9 5.0 %collective-permute-done.10.refs_1_ = bf16[128,512]{1,0:T(8,128)(2,1)S(1)} collective-permute-done((bf16[128,512]{1,0:T(8,128)(2,1)S(1)}, bf16[128,512]{1,0:T(8,128)(2,1)S(1)}, u32[]{:S(2)}, u32[]{:S(2)}) %collective-permute-start.10) | collective-permute-done | bytes 131104 | tf_op jit(solution)/shard_map/ppermute | solution.py:20
  98.9 0.7 copy-done.10
  99.6 3.2 %tree.1 = (bf16[32,512]{1,0:T(8,128)(2,1)}, f32[3,16,128]{2,1,0:T(8,128)}) custom-call(s32[2]{0:T(128)} %pad_add_fusion.refs_3_.refs_0_.place_ref, bf16[128,512]{1,0:T(8,128)(2,1)} %shard_map.97.refs_0_, bf16[128,512]{1,0:T(8,128)(2,1)} %copy-done.10, bf16[128,512]{1,0:T(8,128)(2,1)} %copy-done.9, bf16[128,512]{1,0:T(8,128)(2,1)} %copy-done.8), custom_call_target="tpu_custom_call" | custom-call | tf_op jit(solution)/shard_map/tree/pallas_call | solution.py:432
  102.8 2.1 %bitcast_subtract_fusion = f32[1024,512]{1,0:T(8,128)S(1)} fusion(f32[1024,512]{1,0:T(8,128)} %fusion.33.refs_2_, bf16[32,512]{1,0:T(8,128)(2,1)} %get-tuple-element.12, bf16[1024,32]{0,1:T(8,128)(2,1)S(1)} %copy-done.7), kind=kOutput, calls=%fused_computation.1 | convolution fusion | flops 34078720 | bytes 4292608 | tf_op jit(solution)/shard_map/dot_general | solution.py:30
  104.9 5.2 %collective-permute-done.15 = bf16[512,512]{1,0:T(8,128)(2,1)} collective-permute-done((bf16[512,512]{1,0:T(8,128)(2,1)}, bf16[512,512]{1,0:T(8,128)(2,1)}, u32[]{:S(2)}, u32[]{:S(2)}) %collective-permute-start.15) | collective-permute-done | bytes 524320 | tf_op jit(solution)/shard_map/ppermute | solution.py:20
  110.1 1.6 %fusion.1 = (f32[512,512]{1,0:T(8,128)S(1)}, f32[512,512]{1,0:T(8,128)S(1)}) fusion(f32[1024,512]{1,0:T(8,128)S(1)} %bitcast_subtract_fusion, bf16[512,512]{1,0:T(8,128)(2,1)} %collective-permute-done.15, bf16[512,512]{1,0:T(8,128)(2,1)S(1)} %collective-permute-done.13, bf16[512,512]{1,0:T(8,128)(2,1)S(1)} %collective-permute-done.18, ...), kind=kLoop, calls=%fused_computation.10 | loop fusion | flops 2097152 | bytes 6291456 | tf_op jit(solution)/shard_map/add | solution.py:455
  111.8 1.5 %pad_maximum_fusion = f32[1024,512]{1,0:T(8,128)} fusion(f32[512,512]{1,0:T(8,128)S(1)} %get-tuple-element.15, f32[512,512]{1,0:T(8,128)S(1)} %get-tuple-element.14), kind=kLoop, calls=%fused_computation | loop fusion | flops 524288 | bytes 4194304 | tf_op jit(solution)/shard_map/concatenate | solution.py:457
  (50 shorter events, 0.4 us)
Async XLA Ops:
  0.6 6.4 %copy-start.15 = (s32[1,4096]{1,0:T(1,128)S(1)}, s32[1,4096]{1,0:T(1,128)}, u32[]{:S(2)}) copy-start(s32[1,4096]{1,0:T(1,128)} %param.10) | copy-start | bytes 49156
  1.9 35.3 %collective-permute-start.2 = (bf16[512,512]{1,0:T(8,128)(2,1)S(1)}, bf16[512,512]{1,0:T(8,128)(2,1)}, u32[]{:S(2)}, u32[]{:S(2)}) collective-permute-start(bf16[512,512]{1,0:T(8,128)(2,1)S(1)} %get-tuple-element.16), channel_id=1, source_target_pairs={{0,1},{1,0},{2,3},{3,2},{4,5},{5,4},{6,7},{7,6},{8,9},{9,8},{10,11... | collective-permute-start | bytes 1572872 | tf_op jit(solution)/shard_map/ppermute | solution.py:20
  4.9 24.8 %collective-permute-start.1 = (bf16[512,512]{1,0:T(8,128)(2,1)S(1)}, bf16[512,512]{1,0:T(8,128)(2,1)}, u32[]{:S(2)}, u32[]{:S(2)}) collective-permute-start(bf16[512,512]{1,0:T(8,128)(2,1)S(1)} %get-tuple-element.16), channel_id=1, source_target_pairs={{0,2},{1,3},{2,0},{3,1},{4,6},{5,7},{6,4},{7,5},{8,10},{9,11},{10,... | collective-permute-start | bytes 1572872 | tf_op jit(solution)/shard_map/ppermute | solution.py:20
  6.5 36.4 %collective-permute-start.3 = (bf16[512,512]{1,0:T(8,128)(2,1)S(1)}, bf16[512,512]{1,0:T(8,128)(2,1)}, u32[]{:S(2)}, u32[]{:S(2)}) collective-permute-start(bf16[512,512]{1,0:T(8,128)(2,1)S(1)} %get-tuple-element.17), channel_id=1, source_target_pairs={{0,2},{1,3},{2,0},{3,1},{4,6},{5,7},{6,4},{7,5},{8,10},{9,11},{10,... | collective-permute-start | bytes 1572872 | tf_op jit(solution)/shard_map/ppermute | solution.py:20
  7.0 22.8 %collective-permute-start = (bf16[512,512]{1,0:T(8,128)(2,1)S(1)}, bf16[512,512]{1,0:T(8,128)(2,1)}, u32[]{:S(2)}, u32[]{:S(2)}) collective-permute-start(bf16[512,512]{1,0:T(8,128)(2,1)S(1)} %get-tuple-element.17), channel_id=1, source_target_pairs={{0,1},{1,0},{2,3},{3,2},{4,5},{5,4},{6,7},{7,6},{8,9},{9,8},{10,11... | collective-permute-start | bytes 1572872 | tf_op jit(solution)/shard_map/ppermute | solution.py:20
  7.1 19.5 %copy-start.3 = (bf16[1024,512]{1,0:T(8,128)(2,1)S(1)}, bf16[1024,512]{1,0:T(8,128)(2,1)}, u32[]{:S(2)}) copy-start(bf16[1024,512]{1,0:T(8,128)(2,1)} %refs_2_.1) | copy-start | bytes 3145732
  25.2 1.4 %copy-start = (bf16[1024,1024]{1,0:T(8,128)(2,1)}, bf16[1024,1024]{1,0:T(8,128)(2,1)S(1)}, u32[]{:S(2)}) copy-start(bf16[1024,1024]{1,0:T(8,128)(2,1)S(1)} %get-tuple-element.8) | copy-start | bytes 6291460
  26.6 2.7 %copy-start.16 = (bf16[1024]{0:T(1024)(128)(2,1)S(1)}, bf16[1024]{0:T(1024)(128)(2,1)}, u32[]{:S(2)}) copy-start(bf16[1024]{0:T(1024)(128)(2,1)} %param.11) | copy-start | bytes 6148
  32.0 38.9 %collective-permute-start.8 = (bf16[64,512]{1,0:T(8,128)(2,1)}, bf16[64,512]{1,0:T(8,128)(2,1)S(1)}, u32[]{:S(2)}, u32[]{:S(2)}) collective-permute-start(bf16[64,512]{1,0:T(8,128)(2,1)} %shard_map.95.refs_4_), channel_id=1, source_target_pairs={{0,3},{1,2},{2,1},{3,0},{4,7},{5,6},{6,5},{7,4},{8,11},{9,10},{10,... | collective-permute-start | bytes 196616 | tf_op jit(solution)/shard_map/ppermute | solution.py:20
  34.9 36.0 %collective-permute-start.7 = (bf16[64,512]{1,0:T(8,128)(2,1)}, bf16[64,512]{1,0:T(8,128)(2,1)S(1)}, u32[]{:S(2)}, u32[]{:S(2)}) collective-permute-start(bf16[64,512]{1,0:T(8,128)(2,1)} %shard_map.95.refs_4_), channel_id=1, source_target_pairs={{0,2},{1,3},{2,0},{3,1},{4,6},{5,7},{6,4},{7,5},{8,10},{9,11},{10,... | collective-permute-start | bytes 196616 | tf_op jit(solution)/shard_map/ppermute | solution.py:20
  35.4 35.5 %collective-permute-start.6 = (bf16[64,512]{1,0:T(8,128)(2,1)}, bf16[64,512]{1,0:T(8,128)(2,1)S(1)}, u32[]{:S(2)}, u32[]{:S(2)}) collective-permute-start(bf16[64,512]{1,0:T(8,128)(2,1)} %shard_map.95.refs_4_), channel_id=1, source_target_pairs={{0,1},{1,0},{2,3},{3,2},{4,5},{5,4},{6,7},{7,6},{8,9},{9,8},{10,11... | collective-permute-start | bytes 196616 | tf_op jit(solution)/shard_map/ppermute | solution.py:20
  37.2 3.9 %copy-start.2 = (bf16[1024,1024]{1,0:T(8,128)(2,1)S(1)}, bf16[1024,1024]{1,0:T(8,128)(2,1)}, u32[]{:S(2)}) copy-start(bf16[1024,1024]{1,0:T(8,128)(2,1)} %get-tuple-element.10) | copy-start | bytes 6291460
  37.3 13.0 %collective-permute-start.4 = (bf16[512,512]{1,0:T(8,128)(2,1)}, bf16[512,512]{1,0:T(8,128)(2,1)S(1)}, u32[]{:S(2)}, u32[]{:S(2)}) collective-permute-start(bf16[512,512]{1,0:T(8,128)(2,1)} %collective-permute-done.refs_0_), channel_id=1, source_target_pairs={{0,2},{1,3},{2,0},{3,1},{4,6},{5,7},{6,4},{7,5},{8,10},{9,11},{10,... | collective-permute-start | bytes 1572872 | tf_op jit(solution)/shard_map/ppermute | solution.py:20
  42.9 7.3 %copy-start.4 = (bf16[1024,1024]{1,0:T(8,128)(2,1)S(1)}, bf16[1024,1024]{1,0:T(8,128)(2,1)}, u32[]{:S(2)}) copy-start(bf16[1024,1024]{1,0:T(8,128)(2,1)} %get-tuple-element.11) | copy-start | bytes 6291460
  42.9 11.7 %collective-permute-start.5 = (bf16[512,512]{1,0:T(8,128)(2,1)}, bf16[512,512]{1,0:T(8,128)(2,1)S(1)}, u32[]{:S(2)}, u32[]{:S(2)}) collective-permute-start(bf16[512,512]{1,0:T(8,128)(2,1)} %collective-permute-done.1.refs_1_), channel_id=1, source_target_pairs={{0,1},{1,0},{2,3},{3,2},{4,5},{5,4},{6,7},{7,6},{8,9},{9,8},{10,11... | collective-permute-start | bytes 1572872 | tf_op jit(solution)/shard_map/ppermute | solution.py:20
  46.3 8.4 %copy-start.5 = (f32[1024,512]{1,0:T(8,128)S(1)}, f32[1024,512]{1,0:T(8,128)}, u32[]{:S(2)}) copy-start(f32[1024,512]{1,0:T(8,128)} %fusion.32) | copy-start | bytes 6291460
  56.4 3.0 %copy-start.1 = (bf16[1024,1024]{1,0:T(8,128)(2,1)S(1)}, bf16[1024,1024]{1,0:T(8,128)(2,1)}, u32[]{:S(2)}) copy-start(bf16[1024,1024]{1,0:T(8,128)(2,1)} %copy-done) | copy-start | bytes 6291460
  56.4 10.6 %collective-permute-start.14 = (bf16[512,512]{1,0:T(8,128)(2,1)S(1)}, bf16[512,512]{1,0:T(8,128)(2,1)S(1)}, u32[]{:S(2)}, u32[]{:S(2)}) collective-permute-start(bf16[512,512]{1,0:T(8,128)(2,1)S(1)} %convolution_convert_fusion.2), channel_id=1, source_target_pairs={{0,1},{1,0},{2,3},{3,2},{4,5},{5,4},{6,7},{7,6},{8,9},{9,8},{10,11... | collective-permute-start | bytes 1572872 | tf_op jit(solution)/shard_map/ppermute | solution.py:20
  58.7 10.3 %collective-permute-start.16 = (bf16[512,512]{1,0:T(8,128)(2,1)S(1)}, bf16[512,512]{1,0:T(8,128)(2,1)S(1)}, u32[]{:S(2)}, u32[]{:S(2)}) collective-permute-start(bf16[512,512]{1,0:T(8,128)(2,1)S(1)} %convolution_convert_fusion.1), channel_id=1, source_target_pairs={{0,2},{1,3},{2,0},{3,1},{4,6},{5,7},{6,4},{7,5},{8,10},{9,11},{10,... | collective-permute-start | bytes 1572872 | tf_op jit(solution)/shard_map/ppermute | solution.py:20
  70.9 0.6 copy-start.12
  70.9 0.6 copy-start.13
  70.9 0.6 copy-start.14
  73.3 2.7 %collective-permute-start.9 = (bf16[96,512]{1,0:T(8,128)(2,1)}, bf16[96,512]{1,0:T(8,128)(2,1)S(1)}, u32[]{:S(2)}, u32[]{:S(2)}) collective-permute-start(bf16[96,512]{1,0:T(8,128)(2,1)} %shard_map.96.refs_1_), channel_id=1, source_target_pairs={{0,4},{4,0},{8,12},{12,8},{16,20},{20,16},{24,28},{28,24},{1,5},{5... | collective-permute-start | bytes 294920 | tf_op jit(solution)/shard_map/ppermute | solution.py:20
  76.0 0.6 copy-start.11
  78.3 15.6 %copy-start.6 = (bf16[128,512]{1,0:T(8,128)(2,1)S(1)}, bf16[128,512]{1,0:T(8,128)(2,1)}, u32[]{:S(2)}) copy-start(bf16[128,512]{1,0:T(8,128)(2,1)} %shard_map.97.refs_0_) | copy-start | bytes 393220
  78.3 24.5 %copy-start.7 = (bf16[1024,32]{0,1:T(8,128)(2,1)S(1)}, bf16[1024,32]{0,1:T(8,128)(2,1)}, u32[]{:S(2)}) copy-start(bf16[1024,32]{0,1:T(8,128)(2,1)} %param.12) | copy-start | bytes 196612
  78.3 8.6 %collective-permute-start.12 = (bf16[128,512]{1,0:T(8,128)(2,1)}, bf16[128,512]{1,0:T(8,128)(2,1)S(1)}, u32[]{:S(2)}, u32[]{:S(2)}) collective-permute-start(bf16[128,512]{1,0:T(8,128)(2,1)} %shard_map.97.refs_0_), channel_id=1, source_target_pairs={{0,24},{4,28},{8,16},{12,20},{16,8},{20,12},{24,0},{28,4},{1,25},{... | collective-permute-start | bytes 393224 | tf_op jit(solution)/shard_map/ppermute | solution.py:20
  81.9 11.9 %collective-permute-start.11 = (bf16[128,512]{1,0:T(8,128)(2,1)}, bf16[128,512]{1,0:T(8,128)(2,1)S(1)}, u32[]{:S(2)}, u32[]{:S(2)}) collective-permute-start(bf16[128,512]{1,0:T(8,128)(2,1)} %shard_map.97.refs_0_), channel_id=1, source_target_pairs={{0,16},{4,20},{8,24},{12,28},{16,0},{20,4},{24,8},{28,12},{1,17},{... | collective-permute-start | bytes 393224 | tf_op jit(solution)/shard_map/ppermute | solution.py:20
  83.4 21.5 %collective-permute-start.13 = (bf16[512,512]{1,0:T(8,128)(2,1)}, bf16[512,512]{1,0:T(8,128)(2,1)S(1)}, u32[]{:S(2)}, u32[]{:S(2)}) collective-permute-start(bf16[512,512]{1,0:T(8,128)(2,1)} %convolution_convert_fusion.3), channel_id=1, source_target_pairs={{0,1},{1,0},{2,3},{3,2},{4,5},{5,4},{6,7},{7,6},{8,9},{9,8},{10,11... | collective-permute-start | bytes 1572872 | tf_op jit(solution)/shard_map/ppermute | solution.py:20
  84.8 20.1 %collective-permute-start.18 = (bf16[512,512]{1,0:T(8,128)(2,1)}, bf16[512,512]{1,0:T(8,128)(2,1)S(1)}, u32[]{:S(2)}, u32[]{:S(2)}) collective-permute-start(bf16[512,512]{1,0:T(8,128)(2,1)} %convolution_convert_fusion), channel_id=1, source_target_pairs={{0,2},{1,3},{2,0},{3,1},{4,6},{5,7},{6,4},{7,5},{8,10},{9,11},{10,... | collective-permute-start | bytes 1572872 | tf_op jit(solution)/shard_map/ppermute | solution.py:20
  85.6 24.6 %collective-permute-start.15 = (bf16[512,512]{1,0:T(8,128)(2,1)}, bf16[512,512]{1,0:T(8,128)(2,1)}, u32[]{:S(2)}, u32[]{:S(2)}) collective-permute-start(bf16[512,512]{1,0:T(8,128)(2,1)} %get-tuple-element.18), channel_id=1, source_target_pairs={{0,2},{1,3},{2,0},{3,1},{4,6},{5,7},{6,4},{7,5},{8,10},{9,11},{10,... | collective-permute-start | bytes 1572872 | tf_op jit(solution)/shard_map/ppermute | solution.py:20
  86.8 12.1 %copy-start.8 = (bf16[128,512]{1,0:T(8,128)(2,1)}, bf16[128,512]{1,0:T(8,128)(2,1)S(1)}, u32[]{:S(2)}) copy-start(bf16[128,512]{1,0:T(8,128)(2,1)S(1)} %collective-permute-done.12.refs_3_) | copy-start | bytes 393220
  86.9 23.3 %collective-permute-start.17 = (bf16[512,512]{1,0:T(8,128)(2,1)}, bf16[512,512]{1,0:T(8,128)(2,1)}, u32[]{:S(2)}, u32[]{:S(2)}) collective-permute-start(bf16[512,512]{1,0:T(8,128)(2,1)} %get-tuple-element.20), channel_id=1, source_target_pairs={{0,1},{1,0},{2,3},{3,2},{4,5},{5,4},{6,7},{7,6},{8,9},{9,8},{10,11... | collective-permute-start | bytes 1572872 | tf_op jit(solution)/shard_map/ppermute | solution.py:20
  93.9 5.1 %copy-start.9 = (bf16[128,512]{1,0:T(8,128)(2,1)}, bf16[128,512]{1,0:T(8,128)(2,1)S(1)}, u32[]{:S(2)}) copy-start(bf16[128,512]{1,0:T(8,128)(2,1)S(1)} %collective-permute-done.11.refs_2_) | copy-start | bytes 393220
  93.9 5.0 %collective-permute-start.10 = (bf16[128,512]{1,0:T(8,128)(2,1)S(1)}, bf16[128,512]{1,0:T(8,128)(2,1)S(1)}, u32[]{:S(2)}, u32[]{:S(2)}) collective-permute-start(bf16[128,512]{1,0:T(8,128)(2,1)S(1)} %copy-done.6), channel_id=1, source_target_pairs={{0,8},{4,12},{8,0},{12,4},{16,24},{20,28},{24,16},{28,20},{1,9},{5... | collective-permute-start | bytes 393224 | tf_op jit(solution)/shard_map/ppermute | solution.py:20
  98.9 0.7 copy-start.10

commit v3 on v2

--- a/solution.py
+++ b/solution.py
@@ -42,18 +42,18 @@
     return pl.BlockSpec(memory_space=pltpu.SMEM)
 
 
-def call(body, ops, specs, out_shape, after=(), **rest):
+def call(body, ops, specs, out_shape, after=(), grant=16, **rest):
     skip = len(after)
+    rest.setdefault("out_specs", jax.tree.map(lambda _: vmem(), out_shape))
 
     def skipping(*refs):
         body(*refs[skip:])
 
-    out_specs = jax.tree.map(lambda _: vmem(), out_shape)
     return pl.pallas_call(
         skipping,
         out_shape=out_shape,
         in_specs=[pl.BlockSpec(memory_space=pl.ANY)] * skip + specs,
-        out_specs=out_specs,
+        compiler_params=pltpu.CompilerParams(vmem_limit_bytes=grant * 2**20),
         **rest,
     )(*after, *ops)
 
@@ -196,11 +196,13 @@
     return (leaf_x, jnp.stack(solution, axis=0))
 
 
-def pack_body(rhs_ref, link_ref, sep_ref, fac_ref, out_ref):
+def pack_body(low_ref, high_ref, link_ref, sep_ref, fac_ref, out_ref):
     levels, sep_block, width = sep_ref.shape
     first = link_ref.shape[0]
     rows, cols = fac_ref.shape
-    out_ref[0:first, :] = dot_nn(link_ref[...], rhs_ref[...]).astype(BF16)
+    half = low_ref.shape[0]
+    crossing = dot_nn(link_ref[:, :half], low_ref[...]) + dot_nn(link_ref[:, half:], high_ref[...])
+    out_ref[0:first, :] = crossing.astype(BF16)
     out_ref[first:, :] = jnp.zeros((out_ref.shape[0] - first, out_ref.shape[1]), BF16)
     for level in range(levels):
         out_ref[first : first + sep_block, level * width : (level + 1) * width] = sep_ref[
@@ -209,10 +211,10 @@
     out_ref[first + sep_block : first + sep_block + rows, 0:cols] = fac_ref[...]
 
 
-def leaf_body(place_ref, own_ref, x_ref, y_ref, d_ref, dinv_ref, out_ref, *, first, levels, rows, cols):
+def leaf_body(own_ref, x_ref, y_ref, d_ref, dinv_ref, out_ref, *, first, levels, rows, cols):
     sep_block = dinv_ref.shape[1]
     width = out_ref.shape[1]
-    me = place_ref[1]
+    me = lax.axis_index("grp")
     parts = (own_ref, x_ref, y_ref, d_ref)
     total = parts[0][0:first, :].astype(F32)
     for part in parts[1:]:
@@ -239,8 +241,8 @@
     out_ref[first + levels * sep_block :, :] = factor.astype(BF16)
 
 
-def pair_body(place_ref, own_ref, other_ref, out_ref, *, first, levels, sep_block):
-    is_odd = place_ref[0] % 2 == 1
+def pair_body(own_ref, other_ref, out_ref, *, first, levels, sep_block):
+    is_odd = lax.axis_index("leaf") % 2 == 1
     own = own_ref[...].astype(F32)
     other = other_ref[...].astype(F32)
     even = jnp.where(is_odd, other, own)
@@ -255,11 +257,11 @@
 
 
 def tree_body(
-    place_ref, *refs, count, first, levels, sep_block, cols, slice_width
+    *refs, count, first, levels, sep_block, cols, slice_width
 ):
     pairs = refs[:count]
     first_ref, sol_ref, stage_ref, val_ref = refs[count:]
-    leaf, me = place_ref[0], place_ref[1]
+    leaf, me = lax.axis_index("leaf"), lax.axis_index("grp")
     pair = leaf // 2
     nsep = count * first
     width = pairs[0].shape[1]
@@ -349,19 +351,85 @@
     rows, cols = factor.shape
     width = math.gcd(cols, 4 * LANES)
     part = cols // count
-    return pl.pallas_call(
+    return call(
         arrange_body,
+        (dest, pltpu.with_memory_space_constraint(factor, pltpu.HBM)),
+        [smem(), pl.BlockSpec((rows, width), lambda step: (0, step))],
+        [jax.ShapeDtypeStruct((part, rows), BF16)] * count,
+        grant=26,
         grid=(cols // width,),
-        out_shape=[jax.ShapeDtypeStruct((part, rows), BF16)] * count,
-        in_specs=[smem(), pl.BlockSpec((rows, width), lambda step: (0, step))],
-        out_specs=[vmem()] * count,
         scratch_shapes=[
             pltpu.VMEM((width * rows // LANES, LANES), F32),
             pltpu.VMEM((cols * rows // LANES, LANES), F32),
         ],
-        compiler_params=pltpu.CompilerParams(vmem_limit_bytes=48 * 2**20),
-        name="arrange",
-    )(dest, factor)
+    )
+
+
+def split_body(rhs_ref, low_ref, high_ref, sems):
+    half = low_ref.shape[0]
+    copies = [
+        pltpu.make_async_copy(rhs_ref.at[pl.ds(index * half, half), :], ref, sems.at[index])
+        for index, ref in enumerate((low_ref, high_ref))
+    ]
+    for copy in copies:
+        copy.start()
+    for copy in copies:
+        copy.wait()
+
+
+def forward_body(own_ref, x_ref, y_ref, *refs):
+    pieces, (out_ref, factor_ref, loads_ref) = refs[:-3], refs[-3:]
+    rows = own_ref.shape[0]
+    half = rows // 2
+    for index, ref in enumerate((own_ref, x_ref, y_ref)):
+        factor_ref[index * rows : (index + 1) * rows, :] = ref[...]
+    for index, ref in enumerate(pieces):
+        loads_ref[index * half : (index + 1) * half, :] = ref[...]
+    out_ref[...] = dot_tn(factor_ref[...], loads_ref[...])
+
+
+def far_body(
+    far_ref, low_ref, high_ref, near_ref, dinv_ref, z_ref, relay_low_ref, relay_high_ref, loads_ref, part_ref
+):
+    half = low_ref.shape[0]
+    loads_ref[:half, :] = low_ref[...]
+    loads_ref[half:, :] = high_ref[...]
+    part_ref[...] = near_ref[...] + dot_tn(far_ref[...], loads_ref[...])
+    pivots = dinv_ref[...].astype(F32)
+    width = part_ref.shape[1]
+    for tile in range(pivots.shape[0]):
+        rows = slice(tile * LANES, (tile + 1) * LANES)
+        scale = jnp.broadcast_to(pivots[tile : tile + 1, :], (LANES, LANES)).T
+        scale = jnp.concatenate([scale] * (width // LANES), axis=1)
+        z_ref[rows, :] = (scale * part_ref[rows, :]).astype(BF16)
+    relay_low_ref[...] = dot_nn(far_ref[:half, :], z_ref[...]).astype(BF16)
+    relay_high_ref[...] = dot_nn(far_ref[half:, :], z_ref[...]).astype(BF16)
+
+
+def near_body(own_ref, x_ref, y_ref, z_ref, x_low_ref, y_high_ref, x_high_ref, y_low_ref, out_ref):
+    half = x_low_ref.shape[0]
+    x_low_ref[...] = dot_nn(x_ref[:half, :], z_ref[...]).astype(BF16)
+    y_high_ref[...] = dot_nn(y_ref[half:, :], z_ref[...]).astype(BF16)
+    x_high_ref[...] = dot_nn(x_ref[half:, :], z_ref[...])
+    y_low_ref[...] = dot_nn(y_ref[:half, :], z_ref[...])
+    out_ref[...] = dot_nn(own_ref[...], z_ref[...])
+
+
+def last_body(own_ref, link_ref, first_ref, x_low_ref, x_high_ref, y_low_ref, y_high_ref, out_ref):
+    block = out_ref.shape[0]
+    step = pl.program_id(0)
+    per_half = x_low_ref.shape[0] // block
+    rows = pl.ds(pl.multiple_of(step * block, block), block)
+    base = own_ref[rows, :] - dot_tn(link_ref[:, rows], first_ref[...])
+    part = pl.ds(pl.multiple_of(step % per_half * block, block), block)
+
+    @pl.when(step < per_half)
+    def _():
+        out_ref[...] = base + x_low_ref[part, :].astype(F32) + y_low_ref[part, :].astype(F32)
+
+    @pl.when(step >= per_half)
+    def _():
+        out_ref[...] = base + x_high_ref[part, :].astype(F32) + y_high_ref[part, :].astype(F32)
 
 
 def local_pairs(leaf_rhs, leaf_inv, ordering, leaf_dinv, leaf_link, sep_rhs, sep_factor, sep_dinv):
@@ -371,12 +439,19 @@
     levels, slice_width, sep_block = sep_rhs.shape
     first = leaf_link.shape[1]
     fac_rows, cols = sep_factor.shape
-    leaf = lax.axis_index("leaf").astype(jnp.int32)
     me = lax.axis_index("grp").astype(jnp.int32)
-    place = jnp.stack([leaf, me])
     link_turned = leaf_link.T
-
-    low, high = leaf_rhs[:half], leaf_rhs[half:]
+    half_bf16 = jax.ShapeDtypeStruct((half, width), BF16)
+    half_f32 = jax.ShapeDtypeStruct((half, width), F32)
+    full_f32 = jax.ShapeDtypeStruct((rows, width), F32)
+
+    low, high = call(
+        split_body,
+        (pltpu.with_memory_space_constraint(leaf_rhs, pltpu.HBM),),
+        [pl.BlockSpec(memory_space=pltpu.HBM)],
+        (half_bf16, half_bf16),
+        scratch_shapes=[pltpu.SemaphoreType.DMA((2,))],
+    )
     x_low = exchange(low, "grp", 1)
     y_high = exchange(high, "grp", 2)
     x_high = exchange(high, "grp", 1)
@@ -388,48 +463,59 @@
 
     aux = call(
         pack_body,
-        (leaf_rhs, link_turned, jnp.swapaxes(sep_rhs, 1, 2), sep_factor),
-        [vmem()] * 4,
+        (low, high, link_turned, jnp.swapaxes(sep_rhs, 1, 2), sep_factor),
+        [vmem()] * 5,
         jax.ShapeDtypeStruct((first + 2 * sep_block, width), BF16),
         after=(x_low, y_high),
     )
     aux_parts = [aux] + [exchange(aux, "grp", mask) for mask in range(1, group)]
 
-    leaf_y = dot_tn(blocks[0], leaf_rhs)
-    leaf_y = leaf_y + dot_tn(blocks[1][:half], x_low)
-    leaf_y = leaf_y + dot_tn(blocks[2][half:], y_high)
-    leaf_y = leaf_y + dot_tn(blocks[1][half:], x_high)
-    leaf_y = leaf_y + dot_tn(blocks[2][:half], y_low)
-    leaf_y = leaf_y + dot_tn(blocks[3][:half], d_low)
-    leaf_y = leaf_y + dot_tn(blocks[3][half:], d_high)
-    leaf_z = (leaf_dinv.astype(F32)[:, None] * leaf_y).astype(BF16)
-
-    relay_low = exchange(dot_nn(blocks[3][:half], leaf_z).astype(BF16), "grp", 1)
-    relay_high = exchange(dot_nn(blocks[3][half:], leaf_z).astype(BF16), "grp", 2)
-    sum_x_low = exchange(dot_nn(blocks[1][:half], leaf_z).astype(BF16), "grp", 1)
-    sum_y_high = exchange(dot_nn(blocks[2][half:], leaf_z).astype(BF16), "grp", 2)
-    near_x_high = dot_nn(blocks[1][half:], leaf_z)
-    near_y_low = dot_nn(blocks[2][:half], leaf_z)
-
-    own = dot_nn(blocks[0], leaf_z)
+    part_y = call(
+        forward_body,
+        (*blocks[:3], low, high, x_low, x_high, y_low, y_high),
+        [vmem()] * 9,
+        full_f32,
+        after=(aux,),
+        scratch_shapes=[pltpu.VMEM((3 * rows, rows), BF16), pltpu.VMEM((3 * rows, width), BF16)],
+    )
+    leaf_z, far_low, far_high = call(
+        far_body,
+        (blocks[3], d_low, d_high, part_y, leaf_dinv.reshape(-1, LANES)),
+        [vmem()] * 5,
+        (jax.ShapeDtypeStruct((rows, width), BF16), half_bf16, half_bf16),
+        scratch_shapes=[pltpu.VMEM((rows, width), BF16), pltpu.VMEM((rows, width), F32)],
+    )
+    relay_low = exchange(far_low, "grp", 1)
+    relay_high = exchange(far_high, "grp", 2)
+
     leaf_block = call(
         functools.partial(leaf_body, first=first, levels=levels, rows=fac_rows, cols=cols),
-        (place, *aux_parts, sep_dinv),
-        [smem()] + [vmem()] * 5,
+        (*aux_parts, sep_dinv),
+        [vmem()] * 5,
         jax.ShapeDtypeStruct((first + (levels + 1) * sep_block, width), BF16),
-        after=(near_x_high, near_y_low, own),
+        after=(far_low,),
     )
     partner = exchange(leaf_block, "leaf", 1)
+    near_x_low, near_y_high, near_x_high, near_y_low, own = call(
+        near_body,
+        (*blocks[:3], leaf_z),
+        [vmem()] * 4,
+        (half_bf16, half_bf16, half_f32, half_f32, full_f32),
+        after=(leaf_block,),
+    )
+    sum_x_low = exchange(near_x_low, "grp", 1)
+    sum_y_high = exchange(near_y_high, "grp", 2)
     pair_block = call(
         functools.partial(pair_body, first=first, levels=levels, sep_block=sep_block),
-        (place, leaf_block, partner),
-        [smem(), vmem(), vmem()],
+        (leaf_block, partner),
+        [vmem(), vmem()],
         jax.ShapeDtypeStruct(((levels + 1) * first, width), BF16),
+        after=(own,),
     )
     count = lax.axis_size("leaf") // 2
     pairs = [pair_block] + [exchange(pair_block, "leaf", 2 * mask) for mask in range(1, count)]
     nsep = count * first
-    first_all, sep_turned = pl.pallas_call(
+    first_all, sep_turned = call(
         functools.partial(
             tree_body,
             count=count,
@@ -439,22 +525,26 @@
             cols=cols,
             slice_width=slice_width,
         ),
-        out_shape=(
+        pairs,
+        [vmem()] * count,
+        (
             jax.ShapeDtypeStruct((first, width), BF16),
             jax.ShapeDtypeStruct((levels, sep_block, slice_width), F32),
         ),
-        in_specs=[smem()] + [vmem()] * count,
-        out_specs=(vmem(), vmem()),
         scratch_shapes=[pltpu.VMEM((levels + 1, nsep, width), BF16), pltpu.VMEM((nsep, width), F32)],
-        name="tree",
-    )(place, *pairs)
-
+    )
     sum_x_high = exchange((near_x_high + relay_high.astype(F32)).astype(BF16), "grp", 1)
     sum_y_low = exchange((near_y_low + relay_low.astype(F32)).astype(BF16), "grp", 2)
-    own = own - dot_tn(link_turned, first_all)
-    own_low = own[:half] + sum_x_low.astype(F32) + sum_y_low.astype(F32)
-    own_high = own[half:] + sum_x_high.astype(F32) + sum_y_high.astype(F32)
-    return jnp.concatenate([own_low, own_high], axis=0), jnp.swapaxes(sep_turned, 1, 2)
+    block = rows // 4
+    leaf_x = call(
+        last_body,
+        (own, link_turned, first_all, sum_x_low, sum_x_high, sum_y_low, sum_y_high),
+        [vmem()] * 7,
+        full_f32,
+        grid=(rows // block,),
+        out_specs=pl.BlockSpec((block, width), lambda step: (step, 0)),
+    )
+    return leaf_x, jnp.swapaxes(sep_turned, 1, 2)
 
 
 def fits(leaf_rhs, leaf_inv, sep_rhs, sep_factor, leaf_link):

time: 114 us -> 96.4 us (0.85)
  matrix products: 25.6 us -> 0 us
  Pallas kernels: 26.9 us -> 33.8 us
  waiting for transfers between devices: 28.7 us -> 34.2 us
  local copies, waits for them, and re-layouts: 4.61 us -> 0.03 us
  starting transfers between devices: 22.9 us -> 26.2 us
  other arithmetic: 3.67 us -> 1.06 us
    pallas_call x3 -> x10, Pallas kernels: 5.54 us -> 33.8 us  [call(): pl.pallas_call(skipping, out_shape=out_shape, in_specs=[pl.BlockSpec(memo...]
    dot_general x15 -> x0, matrix products: 25.6 us -> none  [the longest x8 13.7 us: dot_tn(): lax.dot_general(lhs, rhs, (((0,), (0,)), ((), ())), preferred_element_typ...]
    pallas_call x2 -> x0, Pallas kernels: 21.4 us -> none  [the longest x1 18.1 us: arrange(): pl.pallas_call(arrange_body, grid=(cols // width,), out_shape=[jax.ShapeD...]
    ppermute x19, waiting for transfers between devices: 28.7 us -> 34.2 us  [exchange(): lax.ppermute(block, axis, [(low, low ^ mask) for low in range(count)])]
    ppermute x19, starting transfers between devices: 22.9 us -> 26.2 us  [exchange(): lax.ppermute(block, axis, [(low, low ^ mask) for low in range(count)])]
    unnamed x34 -> x10, local copies, waits for them, and re-layouts: 3.33 us -> 0.03 us
    add x1 -> x0, other arithmetic: 1.6 us -> none  [local_pairs(): own_low = own[:half] + sum_x_low.astype(F32) + sum_y_low.astype(F32)]
    concatenate x1 -> x0, other arithmetic: 1.49 us -> none  [local_pairs(): jnp.concatenate([own_low, own_high], axis=0)]
  transfers between devices with their start and end apart: 19 -> 19, of which waited for: 7 -> 8; matrix products, arithmetic and copies ran while one was open for 23% -> 1% of each run, Pallas kernels for 21% -> 28%
where the time goes in v3:
time: 96.4 us; the launch traced here: 96.1 us
  waiting for transfers between devices  34.2 us (35%)
  Pallas kernels  33.8 us (35%)
  starting transfers between devices  26.2 us (27%)
  other arithmetic  1.06 us (1%)
    ppermute x19, waiting for transfers between devices, exchange(): lax.ppermute(block, axis, [(low, low ^ mask) for low in range(count)])  34.2 us
    pallas_call x10, Pallas kernels, call(): pl.pallas_call(skipping, out_shape=out_shape, in_specs=[pl.BlockSpec(memo...  33.8 us
    ppermute x19, starting transfers between devices, exchange(): lax.ppermute(block, axis, [(low, low ^ mask) for low in range(count)])  26.2 us
  transfers between devices with their start and end apart: 19, of which 8 were waited for; matrix products, arithmetic and copies ran while one was open for 1% of the time, Pallas kernels for 28%

profile of v3, /device:TPU:0, one launch (start us, length us, event | category | flops | bytes accessed | tf_op | source)
XLA Modules:
  0.0 96.1 jit_solution(12188447291804762770)
XLA Ops:
  0.6 1.2 %shard_map.96 = (bf16[512,512]{1,0:T(8,128)(2,1)S(1)}, bf16[512,512]{1,0:T(8,128)(2,1)S(1)}) custom-call(bf16[1024,512]{1,0:T(8,128)(2,1)} %refs_0_.1), custom_call_target="tpu_custom_call" | custom-call | tf_op jit(solution)/shard_map/pallas_call | solution.py:52
  1.9 3.0 %collective-permute-start = (bf16[512,512]{1,0:T(8,128)(2,1)S(1)}, bf16[512,512]{1,0:T(8,128)(2,1)S(1)}, u32[]{:S(2)}, u32[]{:S(2)}) collective-permute-start(bf16[512,512]{1,0:T(8,128)(2,1)S(1)} %get-tuple-element.19.refs_2_.refs_4_), channel_id=1, source_target_pairs={{0,1},{1,0},{2,3},{3,2},{4,5},{5,4},{6,7},{7,6},{8,9},{9,8},{10,11... | collective-permute-start | bytes 1572872 | tf_op jit(solution)/shard_map/ppermute | solution.py:20
  4.9 1.5 %collective-permute-start.2 = (bf16[512,512]{1,0:T(8,128)(2,1)S(1)}, bf16[512,512]{1,0:T(8,128)(2,1)S(1)}, u32[]{:S(2)}, u32[]{:S(2)}) collective-permute-start(bf16[512,512]{1,0:T(8,128)(2,1)S(1)} %get-tuple-element.20.refs_3_.refs_5_), channel_id=1, source_target_pairs={{0,2},{1,3},{2,0},{3,1},{4,6},{5,7},{6,4},{7,5},{8,10},{9,11},{10,... | collective-permute-start | bytes 1572872 | tf_op jit(solution)/shard_map/ppermute | solution.py:20
  6.4 0.5 collective-permute-start.4
  6.9 0.1 collective-permute-start.5
  7.0 10.7 %collective-permute-done.refs_0_.refs_6_ = bf16[512,512]{1,0:T(8,128)(2,1)S(1)} collective-permute-done((bf16[512,512]{1,0:T(8,128)(2,1)S(1)}, bf16[512,512]{1,0:T(8,128)(2,1)S(1)}, u32[]{:S(2)}, u32[]{:S(2)}) %collective-permute-start) | collective-permute-done | bytes 524320 | tf_op jit(solution)/shard_map/ppermute | solution.py:20
  17.7 2.0 %collective-permute-start.1 = (bf16[512,512]{1,0:T(8,128)(2,1)S(1)}, bf16[512,512]{1,0:T(8,128)(2,1)S(1)}, u32[]{:S(2)}, u32[]{:S(2)}) collective-permute-start(bf16[512,512]{1,0:T(8,128)(2,1)S(1)} %collective-permute-done.refs_0_.refs_6_), channel_id=1, source_target_pairs={{0,2},{1,3},{2,0},{3,1},{4,6},{5,7},{6,4},{7,5},{8,10},{9,11},{10,... | collective-permute-start | bytes 1572872 | tf_op jit(solution)/shard_map/ppermute | solution.py:20
  19.7 1.5 %collective-permute-start.3 = (bf16[512,512]{1,0:T(8,128)(2,1)S(1)}, bf16[512,512]{1,0:T(8,128)(2,1)}, u32[]{:S(2)}, u32[]{:S(2)}) collective-permute-start(bf16[512,512]{1,0:T(8,128)(2,1)S(1)} %collective-permute-done.2.refs_1_.refs_9_), channel_id=1, source_target_pairs={{0,1},{1,0},{2,3},{3,2},{4,5},{5,4},{6,7},{7,6},{8,9},{9,8},{10,11... | collective-permute-start | bytes 1572872 | tf_op jit(solution)/shard_map/ppermute | solution.py:20
  21.2 0.7 fusion.2.refs_0_
  21.9 0.0 copy-start
  22.0 0.0 copy-start.1
  22.0 0.0 copy-start.2
  22.0 16.0 %shard_map.95 = (bf16[1024,1024]{1,0:T(8,128)(2,1)S(1)}, bf16[1024,1024]{1,0:T(8,128)(2,1)S(1)}, bf16[1024,1024]{1,0:T(8,128)(2,1)S(1)}, bf16[1024,1024]{1,0:T(8,128)(2,1)S(1)}) custom-call(s32[4096]{0:T(1024)S(1)} %fusion.2.refs_0_, bf16[1024,4096]{1,0:T(8,128)(2,1)} %refs_1_.1), custom_call_target="tpu_custom_call" | custom-call | tf_op jit(solution)/shard_map/pallas_call | solution.py:52
  38.0 0.3 shard_map.97.refs_0_.refs_1_
  38.3 0.0 collective-permute-done.4.refs_7_
  38.3 0.0 collective-permute-done.5.refs_8_
  38.3 0.0 copy-start.3
  38.3 4.5 %shard_map.98.refs_3_ = f32[1024,512]{1,0:T(8,128)S(1)} custom-call(bf16[64,512]{1,0:T(8,128)(2,1)S(1)} %shard_map.97.refs_0_.refs_1_, bf16[1024,1024]{1,0:T(8,128)(2,1)S(1)} %get-tuple-element.21.refs_1_, bf16[1024,1024]{1,0:T(8,128)(2,1)S(1)} %get-tuple-element.22.refs_2_, bf16[1024,1024]{1,0:T(8,128)(2,1)S(1)} %get-tuple-element.23.refs_3_, ...), custom_call_target="tpu_custom_call" | custom-call | tf_op jit(solution)/shard_map/pallas_call | solution.py:52
  42.8 0.0 collective-permute-done.1.refs_1_
  42.8 0.0 copy-start.4
  42.9 3.4 %shard_map.99 = (bf16[1024,512]{1,0:T(8,128)(2,1)S(1)}, bf16[512,512]{1,0:T(8,128)(2,1)S(1)}, bf16[512,512]{1,0:T(8,128)(2,1)S(1)}) custom-call(bf16[1024,1024]{1,0:T(8,128)(2,1)S(1)} %get-tuple-element.18.refs_0_, bf16[512,512]{1,0:T(8,128)(2,1)S(1)} %collective-permute-done.1.refs_1_, bf16[512,512]{1,0:T(8,128)(2,1)} %collective-permute-done.3.refs_2_, ...), custom_call_target="tpu_custom_call" | custom-call | tf_op jit(solution)/shard_map/pallas_call | solution.py:52
  46.3 0.6 collective-permute-start.16
  46.9 1.5 %collective-permute-start.14 = (bf16[512,512]{1,0:T(8,128)(2,1)S(1)}, bf16[512,512]{1,0:T(8,128)(2,1)S(1)}, u32[]{:S(2)}, u32[]{:S(2)}) collective-permute-start(bf16[512,512]{1,0:T(8,128)(2,1)S(1)} %get-tuple-element.30), channel_id=1, source_target_pairs={{0,2},{1,3},{2,0},{3,1},{4,6},{5,7},{6,4},{7,5},{8,10},{9,11},{10,... | collective-permute-start | bytes 1572872 | tf_op jit(solution)/shard_map/ppermute | solution.py:20
  48.4 0.5 collective-permute-start.6
  48.9 1.5 %collective-permute-start.7 = (bf16[64,512]{1,0:T(8,128)(2,1)S(1)}, bf16[64,512]{1,0:T(8,128)(2,1)S(1)}, u32[]{:S(2)}, u32[]{:S(2)}) collective-permute-start(bf16[64,512]{1,0:T(8,128)(2,1)S(1)} %shard_map.97.refs_0_.refs_1_), channel_id=1, source_target_pairs={{0,2},{1,3},{2,0},{3,1},{4,6},{5,7},{6,4},{7,5},{8,10},{9,11},{10,... | collective-permute-start | bytes 196616 | tf_op jit(solution)/shard_map/ppermute | solution.py:20
  50.4 1.5 %collective-permute-start.8 = (bf16[64,512]{1,0:T(8,128)(2,1)S(1)}, bf16[64,512]{1,0:T(8,128)(2,1)S(1)}, u32[]{:S(2)}, u32[]{:S(2)}) collective-permute-start(bf16[64,512]{1,0:T(8,128)(2,1)S(1)} %shard_map.97.refs_0_.refs_1_), channel_id=1, source_target_pairs={{0,3},{1,2},{2,1},{3,0},{4,7},{5,6},{6,5},{7,4},{8,11},{9,10},{10,... | collective-permute-start | bytes 196616 | tf_op jit(solution)/shard_map/ppermute | solution.py:20
  51.9 7.7 %collective-permute-done.6.refs_2_ = bf16[64,512]{1,0:T(8,128)(2,1)S(1)} collective-permute-done((bf16[64,512]{1,0:T(8,128)(2,1)S(1)}, bf16[64,512]{1,0:T(8,128)(2,1)S(1)}, u32[]{:S(2)}, u32[]{:S(2)}) %collective-permute-start.6) | collective-permute-done | bytes 65568 | tf_op jit(solution)/shard_map/ppermute | solution.py:20
  59.6 0.3 collective-permute-done.7.refs_3_
  59.9 0.8 collective-permute-done.8.refs_4_
  60.7 0.1 shard_map.100.refs_0_.refs_1_
  60.8 3.5 %shard_map.101 = (bf16[512,512]{1,0:T(8,128)(2,1)S(1)}, bf16[512,512]{1,0:T(8,128)(2,1)S(1)}, f32[512,512]{1,0:T(8,128)S(1)}, f32[512,512]{1,0:T(8,128)S(1)}, f32[1024,512]{1,0:T(8,128)S(1)}) custom-call(bf16[96,512]{1,0:T(8,128)(2,1)S(1)} %shard_map.100.refs_0_.refs_1_, bf16[1024,1024]{1,0:T(8,128)(2,1)S(1)} %get-tuple-element.21.refs_1_, ...), custom_call_target="tpu_custom_call" | custom-call | tf_op jit(solution)/shard_map/pallas_call | solution.py:52
  64.3 1.5 %collective-permute-start.13 = (bf16[512,512]{1,0:T(8,128)(2,1)S(1)}, bf16[512,512]{1,0:T(8,128)(2,1)S(1)}, u32[]{:S(2)}, u32[]{:S(2)}) collective-permute-start(bf16[512,512]{1,0:T(8,128)(2,1)S(1)} %get-tuple-element.28), channel_id=1, source_target_pairs={{0,1},{1,0},{2,3},{3,2},{4,5},{5,4},{6,7},{7,6},{8,9},{9,8},{10,11... | collective-permute-start | bytes 1572872 | tf_op jit(solution)/shard_map/ppermute | solution.py:20
  65.7 0.9 collective-permute-start.18
  66.7 0.2 add_convert_fusion
  66.8 1.2 %collective-permute-start.17 = (bf16[512,512]{1,0:T(8,128)(2,1)S(1)}, bf16[512,512]{1,0:T(8,128)(2,1)S(1)}, u32[]{:S(2)}, u32[]{:S(2)}) collective-permute-start(bf16[512,512]{1,0:T(8,128)(2,1)S(1)} %add_convert_fusion), channel_id=1, source_target_pairs={{0,2},{1,3},{2,0},{3,1},{4,6},{5,7},{6,4},{7,5},{8,10},{9,11},{10,... | collective-permute-start | bytes 1572872 | tf_op jit(solution)/shard_map/ppermute | solution.py:20
  68.0 0.2 add_convert_fusion.1
  68.2 0.7 collective-permute-start.15
  68.9 0.0 collective-permute-start.9
  68.9 1.3 %collective-permute-done.9.refs_2_ = bf16[96,512]{1,0:T(8,128)(2,1)S(1)} collective-permute-done((bf16[96,512]{1,0:T(8,128)(2,1)S(1)}, bf16[96,512]{1,0:T(8,128)(2,1)S(1)}, u32[]{:S(2)}, u32[]{:S(2)}) %collective-permute-start.9) | collective-permute-done | bytes 98336 | tf_op jit(solution)/shard_map/ppermute | solution.py:20
  70.2 0.1 shard_map.102.refs_0_
  70.2 1.6 %collective-permute-start.10 = (bf16[128,512]{1,0:T(8,128)(2,1)S(1)}, bf16[128,512]{1,0:T(8,128)(2,1)S(1)}, u32[]{:S(2)}, u32[]{:S(2)}) collective-permute-start(bf16[128,512]{1,0:T(8,128)(2,1)S(1)} %shard_map.102.refs_0_), channel_id=1, source_target_pairs={{0,8},{4,12},{8,0},{12,4},{16,24},{20,28},{24,16},{28,20},{1,9},{5... | collective-permute-start | bytes 393224 | tf_op jit(solution)/shard_map/ppermute | solution.py:20
  71.9 4.0 %collective-permute-done.10.refs_1_ = bf16[128,512]{1,0:T(8,128)(2,1)S(1)} collective-permute-done((bf16[128,512]{1,0:T(8,128)(2,1)S(1)}, bf16[128,512]{1,0:T(8,128)(2,1)S(1)}, u32[]{:S(2)}, u32[]{:S(2)}) %collective-permute-start.10) | collective-permute-done | bytes 131104 | tf_op jit(solution)/shard_map/ppermute | solution.py:20
  75.9 2.6 %collective-permute-start.11 = (bf16[128,512]{1,0:T(8,128)(2,1)S(1)}, bf16[128,512]{1,0:T(8,128)(2,1)S(1)}, u32[]{:S(2)}, u32[]{:S(2)}) collective-permute-start(bf16[128,512]{1,0:T(8,128)(2,1)S(1)} %shard_map.102.refs_0_), channel_id=1, source_target_pairs={{0,16},{4,20},{8,24},{12,28},{16,0},{20,4},{24,8},{28,12},{1,17},{... | collective-permute-start | bytes 393224 | tf_op jit(solution)/shard_map/ppermute | solution.py:20
  78.4 5.8 %collective-permute-done.11.refs_2_ = bf16[128,512]{1,0:T(8,128)(2,1)S(1)} collective-permute-done((bf16[128,512]{1,0:T(8,128)(2,1)S(1)}, bf16[128,512]{1,0:T(8,128)(2,1)S(1)}, u32[]{:S(2)}, u32[]{:S(2)}) %collective-permute-start.11) | collective-permute-done | bytes 131104 | tf_op jit(solution)/shard_map/ppermute | solution.py:20
  84.3 3.5 %collective-permute-start.12 = (bf16[128,512]{1,0:T(8,128)(2,1)S(1)}, bf16[128,512]{1,0:T(8,128)(2,1)S(1)}, u32[]{:S(2)}, u32[]{:S(2)}) collective-permute-start(bf16[128,512]{1,0:T(8,128)(2,1)S(1)} %shard_map.102.refs_0_), channel_id=1, source_target_pairs={{0,24},{4,28},{8,16},{12,20},{16,8},{20,12},{24,0},{28,4},{1,25},{... | collective-permute-start | bytes 393224 | tf_op jit(solution)/shard_map/ppermute | solution.py:20
  87.8 3.6 %collective-permute-done.12.refs_3_ = bf16[128,512]{1,0:T(8,128)(2,1)S(1)} collective-permute-done((bf16[128,512]{1,0:T(8,128)(2,1)S(1)}, bf16[128,512]{1,0:T(8,128)(2,1)S(1)}, u32[]{:S(2)}, u32[]{:S(2)}) %collective-permute-start.12) | collective-permute-done | bytes 131104 | tf_op jit(solution)/shard_map/ppermute | solution.py:20
  91.4 2.1 %shard_map.103 = (bf16[32,512]{1,0:T(8,128)(2,1)S(1)}, f32[3,16,128]{2,1,0:T(8,128)}) custom-call(bf16[128,512]{1,0:T(8,128)(2,1)S(1)} %shard_map.102.refs_0_, bf16[128,512]{1,0:T(8,128)(2,1)S(1)} %collective-permute-done.10.refs_1_, bf16[128,512]{1,0:T(8,128)(2,1)S(1)} %collective-permute-done.11.refs_2_, bf16[128,512]{1,0:T(8,128)(2,1)S(1)} %collective-permute-done.12.refs_3_), custom_call_target="tpu_custom_call" | custom-call | tf_op jit(solution)/shard_map/pallas_call | solution.py:52
  93.5 2.6 %shard_map.104 = f32[1024,512]{1,0:T(8,128)} custom-call(f32[1024,512]{1,0:T(8,128)S(1)} %get-tuple-element.26.refs_0_, bf16[32,1024]{1,0:T(8,128)(2,1)S(1)} %bitcast.6, bf16[32,512]{1,0:T(8,128)(2,1)S(1)} %get-tuple-element.27.refs_2_, bf16[512,512]{1,0:T(8,128)(2,1)S(1)} %collective-permute-done.13.refs_3_, ...), custom_call_target="tpu_custom_call" | custom-call | tf_op jit(solution)/shard_map/pallas_call | solution.py:52
  (13 shorter events, 0.0 us)
Async XLA Ops:
  1.9 15.8 %collective-permute-start = (bf16[512,512]{1,0:T(8,128)(2,1)S(1)}, bf16[512,512]{1,0:T(8,128)(2,1)S(1)}, u32[]{:S(2)}, u32[]{:S(2)}) collective-permute-start(bf16[512,512]{1,0:T(8,128)(2,1)S(1)} %get-tuple-element.19.refs_2_.refs_4_), channel_id=1, source_target_pairs={{0,1},{1,0},{2,3},{3,2},{4,5},{5,4},{6,7},{7,6},{8,9},{9,8},{10,11... | collective-permute-start | bytes 1572872 | tf_op jit(solution)/shard_map/ppermute | solution.py:20
  4.9 14.8 %collective-permute-start.2 = (bf16[512,512]{1,0:T(8,128)(2,1)S(1)}, bf16[512,512]{1,0:T(8,128)(2,1)S(1)}, u32[]{:S(2)}, u32[]{:S(2)}) collective-permute-start(bf16[512,512]{1,0:T(8,128)(2,1)S(1)} %get-tuple-element.20.refs_3_.refs_5_), channel_id=1, source_target_pairs={{0,2},{1,3},{2,0},{3,1},{4,6},{5,7},{6,4},{7,5},{8,10},{9,11},{10,... | collective-permute-start | bytes 1572872 | tf_op jit(solution)/shard_map/ppermute | solution.py:20
  6.4 31.9 %collective-permute-start.4 = (bf16[512,512]{1,0:T(8,128)(2,1)S(1)}, bf16[512,512]{1,0:T(8,128)(2,1)S(1)}, u32[]{:S(2)}, u32[]{:S(2)}) collective-permute-start(bf16[512,512]{1,0:T(8,128)(2,1)S(1)} %get-tuple-element.20.refs_3_.refs_5_), channel_id=1, source_target_pairs={{0,1},{1,0},{2,3},{3,2},{4,5},{5,4},{6,7},{7,6},{8,9},{9,8},{10,11... | collective-permute-start | bytes 1572872 | tf_op jit(solution)/shard_map/ppermute | solution.py:20
  6.9 31.4 %collective-permute-start.5 = (bf16[512,512]{1,0:T(8,128)(2,1)S(1)}, bf16[512,512]{1,0:T(8,128)(2,1)}, u32[]{:S(2)}, u32[]{:S(2)}) collective-permute-start(bf16[512,512]{1,0:T(8,128)(2,1)S(1)} %get-tuple-element.19.refs_2_.refs_4_), channel_id=1, source_target_pairs={{0,2},{1,3},{2,0},{3,1},{4,6},{5,7},{6,4},{7,5},{8,10},{9,11},{10,... | collective-permute-start | bytes 1572872 | tf_op jit(solution)/shard_map/ppermute | solution.py:20
  17.7 25.2 %collective-permute-start.1 = (bf16[512,512]{1,0:T(8,128)(2,1)S(1)}, bf16[512,512]{1,0:T(8,128)(2,1)S(1)}, u32[]{:S(2)}, u32[]{:S(2)}) collective-permute-start(bf16[512,512]{1,0:T(8,128)(2,1)S(1)} %collective-permute-done.refs_0_.refs_6_), channel_id=1, source_target_pairs={{0,2},{1,3},{2,0},{3,1},{4,6},{5,7},{6,4},{7,5},{8,10},{9,11},{10,... | collective-permute-start | bytes 1572872 | tf_op jit(solution)/shard_map/ppermute | solution.py:20
  19.7 23.1 %collective-permute-start.3 = (bf16[512,512]{1,0:T(8,128)(2,1)S(1)}, bf16[512,512]{1,0:T(8,128)(2,1)}, u32[]{:S(2)}, u32[]{:S(2)}) collective-permute-start(bf16[512,512]{1,0:T(8,128)(2,1)S(1)} %collective-permute-done.2.refs_1_.refs_9_), channel_id=1, source_target_pairs={{0,1},{1,0},{2,3},{3,2},{4,5},{5,4},{6,7},{7,6},{8,9},{9,8},{10,11... | collective-permute-start | bytes 1572872 | tf_op jit(solution)/shard_map/ppermute | solution.py:20
  21.9 16.0 %copy-start = (bf16[1024,32]{0,1:T(8,128)(2,1)S(1)}, bf16[1024,32]{0,1:T(8,128)(2,1)}, u32[]{:S(2)}) copy-start(bf16[1024,32]{0,1:T(8,128)(2,1)} %param.12) | copy-start | bytes 196612
  22.0 16.0 %copy-start.1 = (bf16[3,128,16]{1,2,0:T(8,128)(2,1)S(1)}, bf16[3,128,16]{1,2,0:T(8,128)(2,1)}, u32[]{:S(2)}) copy-start(bf16[3,128,16]{1,2,0:T(8,128)(2,1)} %param.13) | copy-start | bytes 36868
  22.0 16.0 %copy-start.2 = (bf16[4,416]{1,0:T(4,128)(2,1)S(1)}, bf16[4,416]{1,0:T(4,128)(2,1)}, u32[]{:S(2)}) copy-start(bf16[4,416]{1,0:T(4,128)(2,1)} %refs_6_.1) | copy-start | bytes 9988
  38.3 4.5 %copy-start.3 = (bf16[1024]{0:T(1024)(128)(2,1)S(1)}, bf16[1024]{0:T(1024)(128)(2,1)}, u32[]{:S(2)}) copy-start(bf16[1024]{0:T(1024)(128)(2,1)} %param.11) | copy-start | bytes 6148
  42.8 17.8 %copy-start.4 = (bf16[3,16]{1,0:T(4,128)(2,1)S(1)}, bf16[3,16]{1,0:T(4,128)(2,1)}, u32[]{:S(2)}) copy-start(bf16[3,16]{1,0:T(4,128)(2,1)} %refs_5_.1) | copy-start | bytes 292
  46.3 20.3 %collective-permute-start.16 = (bf16[512,512]{1,0:T(8,128)(2,1)S(1)}, bf16[512,512]{1,0:T(8,128)(2,1)S(1)}, u32[]{:S(2)}, u32[]{:S(2)}) collective-permute-start(bf16[512,512]{1,0:T(8,128)(2,1)S(1)} %get-tuple-element.24.refs_0_), channel_id=1, source_target_pairs={{0,1},{1,0},{2,3},{3,2},{4,5},{5,4},{6,7},{7,6},{8,9},{9,8},{10,11... | collective-permute-start | bytes 1572872 | tf_op jit(solution)/shard_map/ppermute | solution.py:20
  46.9 21.1 %collective-permute-start.14 = (bf16[512,512]{1,0:T(8,128)(2,1)S(1)}, bf16[512,512]{1,0:T(8,128)(2,1)S(1)}, u32[]{:S(2)}, u32[]{:S(2)}) collective-permute-start(bf16[512,512]{1,0:T(8,128)(2,1)S(1)} %get-tuple-element.30), channel_id=1, source_target_pairs={{0,2},{1,3},{2,0},{3,1},{4,6},{5,7},{6,4},{7,5},{8,10},{9,11},{10,... | collective-permute-start | bytes 1572872 | tf_op jit(solution)/shard_map/ppermute | solution.py:20
  48.4 11.2 %collective-permute-start.6 = (bf16[64,512]{1,0:T(8,128)(2,1)S(1)}, bf16[64,512]{1,0:T(8,128)(2,1)S(1)}, u32[]{:S(2)}, u32[]{:S(2)}) collective-permute-start(bf16[64,512]{1,0:T(8,128)(2,1)S(1)} %shard_map.97.refs_0_.refs_1_), channel_id=1, source_target_pairs={{0,1},{1,0},{2,3},{3,2},{4,5},{5,4},{6,7},{7,6},{8,9},{9,8},{10,11... | collective-permute-start | bytes 196616 | tf_op jit(solution)/shard_map/ppermute | solution.py:20
  48.9 10.9 %collective-permute-start.7 = (bf16[64,512]{1,0:T(8,128)(2,1)S(1)}, bf16[64,512]{1,0:T(8,128)(2,1)S(1)}, u32[]{:S(2)}, u32[]{:S(2)}) collective-permute-start(bf16[64,512]{1,0:T(8,128)(2,1)S(1)} %shard_map.97.refs_0_.refs_1_), channel_id=1, source_target_pairs={{0,2},{1,3},{2,0},{3,1},{4,6},{5,7},{6,4},{7,5},{8,10},{9,11},{10,... | collective-permute-start | bytes 196616 | tf_op jit(solution)/shard_map/ppermute | solution.py:20
  50.4 10.2 %collective-permute-start.8 = (bf16[64,512]{1,0:T(8,128)(2,1)S(1)}, bf16[64,512]{1,0:T(8,128)(2,1)S(1)}, u32[]{:S(2)}, u32[]{:S(2)}) collective-permute-start(bf16[64,512]{1,0:T(8,128)(2,1)S(1)} %shard_map.97.refs_0_.refs_1_), channel_id=1, source_target_pairs={{0,3},{1,2},{2,1},{3,0},{4,7},{5,6},{6,5},{7,4},{8,11},{9,10},{10,... | collective-permute-start | bytes 196616 | tf_op jit(solution)/shard_map/ppermute | solution.py:20
  64.3 29.2 %collective-permute-start.13 = (bf16[512,512]{1,0:T(8,128)(2,1)S(1)}, bf16[512,512]{1,0:T(8,128)(2,1)S(1)}, u32[]{:S(2)}, u32[]{:S(2)}) collective-permute-start(bf16[512,512]{1,0:T(8,128)(2,1)S(1)} %get-tuple-element.28), channel_id=1, source_target_pairs={{0,1},{1,0},{2,3},{3,2},{4,5},{5,4},{6,7},{7,6},{8,9},{9,8},{10,11... | collective-permute-start | bytes 1572872 | tf_op jit(solution)/shard_map/ppermute | solution.py:20
  65.7 27.8 %collective-permute-start.18 = (bf16[512,512]{1,0:T(8,128)(2,1)S(1)}, bf16[512,512]{1,0:T(8,128)(2,1)S(1)}, u32[]{:S(2)}, u32[]{:S(2)}) collective-permute-start(bf16[512,512]{1,0:T(8,128)(2,1)S(1)} %get-tuple-element.32), channel_id=1, source_target_pairs={{0,2},{1,3},{2,0},{3,1},{4,6},{5,7},{6,4},{7,5},{8,10},{9,11},{10,... | collective-permute-start | bytes 1572872 | tf_op jit(solution)/shard_map/ppermute | solution.py:20
  66.8 26.7 %collective-permute-start.17 = (bf16[512,512]{1,0:T(8,128)(2,1)S(1)}, bf16[512,512]{1,0:T(8,128)(2,1)S(1)}, u32[]{:S(2)}, u32[]{:S(2)}) collective-permute-start(bf16[512,512]{1,0:T(8,128)(2,1)S(1)} %add_convert_fusion), channel_id=1, source_target_pairs={{0,2},{1,3},{2,0},{3,1},{4,6},{5,7},{6,4},{7,5},{8,10},{9,11},{10,... | collective-permute-start | bytes 1572872 | tf_op jit(solution)/shard_map/ppermute | solution.py:20
  68.2 25.3 %collective-permute-start.15 = (bf16[512,512]{1,0:T(8,128)(2,1)S(1)}, bf16[512,512]{1,0:T(8,128)(2,1)S(1)}, u32[]{:S(2)}, u32[]{:S(2)}) collective-permute-start(bf16[512,512]{1,0:T(8,128)(2,1)S(1)} %add_convert_fusion.1), channel_id=1, source_target_pairs={{0,1},{1,0},{2,3},{3,2},{4,5},{5,4},{6,7},{7,6},{8,9},{9,8},{10,11... | collective-permute-start | bytes 1572872 | tf_op jit(solution)/shard_map/ppermute | solution.py:20
  68.9 1.3 %collective-permute-start.9 = (bf16[96,512]{1,0:T(8,128)(2,1)S(1)}, bf16[96,512]{1,0:T(8,128)(2,1)S(1)}, u32[]{:S(2)}, u32[]{:S(2)}) collective-permute-start(bf16[96,512]{1,0:T(8,128)(2,1)S(1)} %shard_map.100.refs_0_.refs_1_), channel_id=1, source_target_pairs={{0,4},{4,0},{8,12},{12,8},{16,20},{20,16},{24,28},{28,24},{1,5},{5... | collective-permute-start | bytes 294920 | tf_op jit(solution)/shard_map/ppermute | solution.py:20
  70.2 5.6 %collective-permute-start.10 = (bf16[128,512]{1,0:T(8,128)(2,1)S(1)}, bf16[128,512]{1,0:T(8,128)(2,1)S(1)}, u32[]{:S(2)}, u32[]{:S(2)}) collective-permute-start(bf16[128,512]{1,0:T(8,128)(2,1)S(1)} %shard_map.102.refs_0_), channel_id=1, source_target_pairs={{0,8},{4,12},{8,0},{12,4},{16,24},{20,28},{24,16},{28,20},{1,9},{5... | collective-permute-start | bytes 393224 | tf_op jit(solution)/shard_map/ppermute | solution.py:20
  75.9 8.4 %collective-permute-start.11 = (bf16[128,512]{1,0:T(8,128)(2,1)S(1)}, bf16[128,512]{1,0:T(8,128)(2,1)S(1)}, u32[]{:S(2)}, u32[]{:S(2)}) collective-permute-start(bf16[128,512]{1,0:T(8,128)(2,1)S(1)} %shard_map.102.refs_0_), channel_id=1, source_target_pairs={{0,16},{4,20},{8,24},{12,28},{16,0},{20,4},{24,8},{28,12},{1,17},{... | collective-permute-start | bytes 393224 | tf_op jit(solution)/shard_map/ppermute | solution.py:20
  84.3 7.1 %collective-permute-start.12 = (bf16[128,512]{1,0:T(8,128)(2,1)S(1)}, bf16[128,512]{1,0:T(8,128)(2,1)S(1)}, u32[]{:S(2)}, u32[]{:S(2)}) collective-permute-start(bf16[128,512]{1,0:T(8,128)(2,1)S(1)} %shard_map.102.refs_0_), channel_id=1, source_target_pairs={{0,24},{4,28},{8,16},{12,20},{16,8},{20,12},{24,0},{28,4},{1,25},{... | collective-permute-start | bytes 393224 | tf_op jit(solution)/shard_map/ppermute | solution.py:20

commit v4 on v3

--- a/solution.py
+++ b/solution.py
@@ -203,12 +203,15 @@
     half = low_ref.shape[0]
     crossing = dot_nn(link_ref[:, :half], low_ref[...]) + dot_nn(link_ref[:, half:], high_ref[...])
     out_ref[0:first, :] = crossing.astype(BF16)
-    out_ref[first:, :] = jnp.zeros((out_ref.shape[0] - first, out_ref.shape[1]), BF16)
     for level in range(levels):
         out_ref[first : first + sep_block, level * width : (level + 1) * width] = sep_ref[
             level
         ]
-    out_ref[first + sep_block : first + sep_block + rows, 0:cols] = fac_ref[...]
+    tiles = sep_block // rows
+    factor = fac_ref[...].astype(F32)
+    factor = jnp.concatenate([factor, jnp.zeros((rows, tiles * LANES - cols), F32)], axis=1)
+    folded = [factor[:, tile * LANES : (tile + 1) * LANES] for tile in range(tiles)]
+    out_ref[first:, levels * width :] = jnp.concatenate(folded, axis=0).astype(BF16)
 
 
 def leaf_body(own_ref, x_ref, y_ref, d_ref, dinv_ref, out_ref, *, first, levels, rows, cols):
@@ -231,7 +234,9 @@
     lane = lax.broadcasted_iota(jnp.int32, (sep_block, width), 1)
     factor = jnp.zeros((sep_block, width), F32)
     for index, part in enumerate(parts):
-        block = part[first + sep_block : first + 2 * sep_block, :].astype(F32)[0:rows, :]
+        folded = part[first:, levels * part_width :].astype(F32)
+        block = [folded[tile * rows : (tile + 1) * rows, :] for tile in range(sep_block // rows)]
+        block = jnp.concatenate(block, axis=1)
         tiled = jnp.concatenate([block] * (sep_block // rows), axis=0)
         factor = factor + jnp.where(row_owner == (me ^ index), tiled, 0.0)
     pivots = dinv_ref[...].astype(F32).T
@@ -377,15 +382,25 @@
         copy.wait()
 
 
+def cut_body(*refs):
+    half = len(refs) // 3
+    for index, ref in enumerate(refs[:half]):
+        width = ref.shape[1] // 2
+        for part in range(2):
+            refs[half + 2 * index + part][...] = ref[:, part * width : (part + 1) * width]
+
+
 def forward_body(own_ref, x_ref, y_ref, *refs):
-    pieces, (out_ref, factor_ref, loads_ref) = refs[:-3], refs[-3:]
+    pieces, (out_0_ref, out_1_ref, factor_ref, loads_ref) = refs[:-4], refs[-4:]
     rows = own_ref.shape[0]
     half = rows // 2
+    width = out_0_ref.shape[1]
     for index, ref in enumerate((own_ref, x_ref, y_ref)):
         factor_ref[index * rows : (index + 1) * rows, :] = ref[...]
     for index, ref in enumerate(pieces):
         loads_ref[index * half : (index + 1) * half, :] = ref[...]
-    out_ref[...] = dot_tn(factor_ref[...], loads_ref[...])
+    out_0_ref[...] = dot_tn(factor_ref[...], loads_ref[:, :width])
+    out_1_ref[...] = dot_tn(factor_ref[...], loads_ref[:, width:])
 
 
 def far_body(
@@ -406,30 +421,47 @@
     relay_high_ref[...] = dot_nn(far_ref[half:, :], z_ref[...]).astype(BF16)
 
 
-def near_body(own_ref, x_ref, y_ref, z_ref, x_low_ref, y_high_ref, x_high_ref, y_low_ref, out_ref):
+def near_body(own_ref, x_ref, y_ref, z_0_ref, z_1_ref, x_low_ref, y_high_ref, *refs):
+    highs, lows, out_ref = refs[:2], refs[2:4], refs[4]
     half = x_low_ref.shape[0]
-    x_low_ref[...] = dot_nn(x_ref[:half, :], z_ref[...]).astype(BF16)
-    y_high_ref[...] = dot_nn(y_ref[half:, :], z_ref[...]).astype(BF16)
-    x_high_ref[...] = dot_nn(x_ref[half:, :], z_ref[...])
-    y_low_ref[...] = dot_nn(y_ref[:half, :], z_ref[...])
-    out_ref[...] = dot_nn(own_ref[...], z_ref[...])
-
-
-def last_body(own_ref, link_ref, first_ref, x_low_ref, x_high_ref, y_low_ref, y_high_ref, out_ref):
+    for part, z_ref in enumerate((z_0_ref, z_1_ref)):
+        width = z_ref.shape[1]
+        cols = slice(part * width, (part + 1) * width)
+        x_low_ref[:, cols] = dot_nn(x_ref[:half, :], z_ref[...]).astype(BF16)
+        y_high_ref[:, cols] = dot_nn(y_ref[half:, :], z_ref[...]).astype(BF16)
+        highs[part][...] = dot_nn(x_ref[half:, :], z_ref[...])
+        lows[part][...] = dot_nn(y_ref[:half, :], z_ref[...])
+        out_ref[:, cols] = dot_nn(own_ref[...], z_ref[...])
+
+
+def add_body(near_ref, relay_ref, out_ref):
+    out_ref[...] = (near_ref[...] + relay_ref[...].astype(F32)).astype(BF16)
+
+
+def base_body(own_ref, link_ref, first_ref, x_low_ref, y_high_ref, out_0_ref, out_1_ref):
+    half = x_low_ref.shape[0]
+    width = out_0_ref.shape[1]
+    for part, ref in enumerate((out_0_ref, out_1_ref)):
+        cols = slice(part * width, (part + 1) * width)
+        ref[...] = own_ref[:, cols] - dot_tn(link_ref[...], first_ref[:, cols])
+        ref[:half, :] += x_low_ref[:, cols].astype(F32)
+        ref[half:, :] += y_high_ref[:, cols].astype(F32)
+
+
+def last_body(base_ref, low_ref, high_ref, out_ref):
     block = out_ref.shape[0]
     step = pl.program_id(0)
-    per_half = x_low_ref.shape[0] // block
+    per_half = low_ref.shape[0] // block
     rows = pl.ds(pl.multiple_of(step * block, block), block)
-    base = own_ref[rows, :] - dot_tn(link_ref[:, rows], first_ref[...])
     part = pl.ds(pl.multiple_of(step % per_half * block, block), block)
 
     @pl.when(step < per_half)
     def _():
-        out_ref[...] = base + x_low_ref[part, :].astype(F32) + y_low_ref[part, :].astype(F32)
+        out_ref[...] = base_ref[rows, :] + low_ref[part, :].astype(F32)
 
     @pl.when(step >= per_half)
     def _():
-        out_ref[...] = base + x_high_ref[part, :].astype(F32) + y_high_ref[part, :].astype(F32)
+        out_ref[...] = base_ref[rows, :] + high_ref[part, :].astype(F32)
 
 
 def local_pairs(leaf_rhs, leaf_inv, ordering, leaf_dinv, leaf_link, sep_rhs, sep_factor, sep_dinv):
@@ -442,7 +474,6 @@
     me = lax.axis_index("grp").astype(jnp.int32)
     link_turned = leaf_link.T
     half_bf16 = jax.ShapeDtypeStruct((half, width), BF16)
-    half_f32 = jax.ShapeDtypeStruct((half, width), F32)
     full_f32 = jax.ShapeDtypeStruct((rows, width), F32)
 
     low, high = call(
@@ -458,14 +489,22 @@
     y_low = exchange(low, "grp", 2)
     dest = (ordering[0] // rows ^ me) * rows + ordering[0] % rows
     blocks = arrange(leaf_inv, dest, group)
-    d_low = exchange(x_low, "grp", 2)
-    d_high = exchange(y_high, "grp", 1)
+    parts = range(2)
+    part_bf16 = jax.ShapeDtypeStruct((half, width // 2), BF16)
+    part_f32 = jax.ShapeDtypeStruct((half, width // 2), F32)
+    tall_bf16 = jax.ShapeDtypeStruct((rows, width // 2), BF16)
+    tall_f32 = jax.ShapeDtypeStruct((rows, width // 2), F32)
+    *x_cut, y_cut_0, y_cut_1 = call(
+        cut_body, (x_low, y_high), [vmem()] * 2, [part_bf16] * 4, after=(blocks[0],)
+    )
+    d_low = [exchange(x_cut[part], "grp", 2) for part in parts]
+    d_high = [exchange((y_cut_0, y_cut_1)[part], "grp", 1) for part in parts]
 
     aux = call(
         pack_body,
         (low, high, link_turned, jnp.swapaxes(sep_rhs, 1, 2), sep_factor),
         [vmem()] * 5,
-        jax.ShapeDtypeStruct((first + 2 * sep_block, width), BF16),
+        jax.ShapeDtypeStruct((first + sep_block, width), BF16),
         after=(x_low, y_high),
     )
     aux_parts = [aux] + [exchange(aux, "grp", mask) for mask in range(1, group)]
@@ -474,33 +513,36 @@
         forward_body,
         (*blocks[:3], low, high, x_low, x_high, y_low, y_high),
         [vmem()] * 9,
-        full_f32,
+        [tall_f32] * 2,
         after=(aux,),
         scratch_shapes=[pltpu.VMEM((3 * rows, rows), BF16), pltpu.VMEM((3 * rows, width), BF16)],
     )
-    leaf_z, far_low, far_high = call(
-        far_body,
-        (blocks[3], d_low, d_high, part_y, leaf_dinv.reshape(-1, LANES)),
-        [vmem()] * 5,
-        (jax.ShapeDtypeStruct((rows, width), BF16), half_bf16, half_bf16),
-        scratch_shapes=[pltpu.VMEM((rows, width), BF16), pltpu.VMEM((rows, width), F32)],
-    )
-    relay_low = exchange(far_low, "grp", 1)
-    relay_high = exchange(far_high, "grp", 2)
+    leaf_z, relay_low, relay_high = [], [], []
+    for part in parts:
+        z_part, far_low, far_high = call(
+            far_body,
+            (blocks[3], d_low[part], d_high[part], part_y[part], leaf_dinv.reshape(-1, LANES)),
+            [vmem()] * 5,
+            (tall_bf16, part_bf16, part_bf16),
+            scratch_shapes=[pltpu.VMEM((rows, width // 2), BF16), pltpu.VMEM((rows, width // 2), F32)],
+        )
+        leaf_z.append(z_part)
+        relay_low.append(exchange(far_low, "grp", 1))
+        relay_high.append(exchange(far_high, "grp", 2))
 
     leaf_block = call(
         functools.partial(leaf_body, first=first, levels=levels, rows=fac_rows, cols=cols),
         (*aux_parts, sep_dinv),
         [vmem()] * 5,
         jax.ShapeDtypeStruct((first + (levels + 1) * sep_block, width), BF16),
-        after=(far_low,),
+        after=(leaf_z[1],),
     )
     partner = exchange(leaf_block, "leaf", 1)
-    near_x_low, near_y_high, near_x_high, near_y_low, own = call(
+    near_x_low, near_y_high, *near, own = call(
         near_body,
-        (*blocks[:3], leaf_z),
-        [vmem()] * 4,
-        (half_bf16, half_bf16, half_f32, half_f32, full_f32),
+        (*blocks[:3], *leaf_z),
+        [vmem()] * 5,
+        [half_bf16] * 2 + [part_f32] * 4 + [full_f32],
         after=(leaf_block,),
     )
     sum_x_low = exchange(near_x_low, "grp", 1)
@@ -533,17 +575,36 @@
         ),
         scratch_shapes=[pltpu.VMEM((levels + 1, nsep, width), BF16), pltpu.VMEM((nsep, width), F32)],
     )
-    sum_x_high = exchange((near_x_high + relay_high.astype(F32)).astype(BF16), "grp", 1)
-    sum_y_low = exchange((near_y_low + relay_low.astype(F32)).astype(BF16), "grp", 2)
+    sum_x_high, sum_y_low = [], []
+    for part in parts:
+        for mask, kept, relay, into in (
+            (1, near[part], relay_high[part], sum_x_high),
+            (2, near[2 + part], relay_low[part], sum_y_low),
+        ):
+            total = call(add_body, (kept, relay), [vmem()] * 2, part_bf16)
+            into.append(exchange(total, "grp", mask))
+    base = call(
+        base_body,
+        (own, link_turned, first_all, sum_x_low, sum_y_high),
+        [vmem()] * 5,
+        [tall_f32] * 2,
+    )
     block = rows // 4
-    leaf_x = call(
-        last_body,
-        (own, link_turned, first_all, sum_x_low, sum_x_high, sum_y_low, sum_y_high),
-        [vmem()] * 7,
-        full_f32,
-        grid=(rows // block,),
-        out_specs=pl.BlockSpec((block, width), lambda step: (step, 0)),
-    )
+    leaf_x = ()
+    for part in parts:
+        leaf_x = (
+            call(
+                last_body,
+                (base[part], sum_y_low[part], sum_x_high[part]),
+                [vmem()] * 3,
+                full_f32,
+                after=leaf_x,
+                grid=(rows // block,),
+                out_specs=pl.BlockSpec((block, width // 2), lambda step, part=part: (step, part)),
+                input_output_aliases={0: 0} if leaf_x else {},
+            ),
+        )
+    leaf_x = leaf_x[0]
     return leaf_x, jnp.swapaxes(sep_turned, 1, 2)
 
 
@@ -563,6 +624,8 @@
         and levels <= count
         and sep_block % sep_factor.shape[0] == 0
         and sep_factor.shape[1] + levels <= width
+        and width == (levels + 1) * slice_width == sep_block // sep_factor.shape[0] * LANES
+        and slice_width == LANES
         and width % (leaves * sep_block) == 0
     )
 

time: 96.4 us -> 91.2 us (0.946)
  waiting for transfers between devices: 34.2 us -> 21 us
  starting transfers between devices: 26.2 us -> 33.4 us
  Pallas kernels: 33.8 us -> 35 us
    ppermute x19 -> x25, waiting for transfers between devices: 34.2 us -> 21 us  [exchange(): lax.ppermute(block, axis, [(low, low ^ mask) for low in range(count)])]
    ppermute x19 -> x25, starting transfers between devices: 26.2 us -> 33.4 us  [exchange(): lax.ppermute(block, axis, [(low, low ^ mask) for low in range(count)])]
    pallas_call x10 -> x18, Pallas kernels: 33.8 us -> 35 us  [call(): pl.pallas_call(skipping, out_shape=out_shape, in_specs=[pl.BlockSpec(memo...]
  transfers between devices with their start and end apart: 19 -> 25, of which waited for: 8 -> 7; matrix products, arithmetic and copies ran while one was open for 1% -> 1% of each run, Pallas kernels for 28% -> 35%
where the time goes in v4:
time: 91.2 us; the launch traced here: 91 us
  Pallas kernels  35 us (38%)
  starting transfers between devices  33.4 us (37%)
  waiting for transfers between devices  21 us (23%)
    pallas_call x18, Pallas kernels, call(): pl.pallas_call(skipping, out_shape=out_shape, in_specs=[pl.BlockSpec(memo...  35 us
    ppermute x25, starting transfers between devices, exchange(): lax.ppermute(block, axis, [(low, low ^ mask) for low in range(count)])  33.4 us
    ppermute x25, waiting for transfers between devices, exchange(): lax.ppermute(block, axis, [(low, low ^ mask) for low in range(count)])  21 us
  transfers between devices with their start and end apart: 25, of which 7 were waited for; matrix products, arithmetic and copies ran while one was open for 1% of the time, Pallas kernels for 35%

profile of v4, /device:TPU:0, one launch (start us, length us, event | category | flops | bytes accessed | tf_op | source)
XLA Modules:
  0.0 91.0 jit_solution(3057192300530278940)
XLA Ops:
  0.6 1.2 %shard_map.96 = (bf16[512,512]{1,0:T(8,128)(2,1)S(1)}, bf16[512,512]{1,0:T(8,128)(2,1)S(1)}) custom-call(bf16[1024,512]{1,0:T(8,128)(2,1)} %refs_0_.1), custom_call_target="tpu_custom_call" | custom-call | tf_op jit(solution)/shard_map/pallas_call | solution.py:52
  1.9 3.0 %collective-permute-start = (bf16[512,512]{1,0:T(8,128)(2,1)S(1)}, bf16[512,512]{1,0:T(8,128)(2,1)S(1)}, u32[]{:S(2)}, u32[]{:S(2)}) collective-permute-start(bf16[512,512]{1,0:T(8,128)(2,1)S(1)} %get-tuple-element.33.refs_2_.refs_4_), channel_id=1, source_target_pairs={{0,1},{1,0},{2,3},{3,2},{4,5},{5,4},{6,7},{7,6},{8,9},{9,8},{10,11... | collective-permute-start | bytes 1572872 | tf_op jit(solution)/shard_map/ppermute | solution.py:20
  4.9 1.5 %collective-permute-start.1 = (bf16[512,512]{1,0:T(8,128)(2,1)S(1)}, bf16[512,512]{1,0:T(8,128)(2,1)S(1)}, u32[]{:S(2)}, u32[]{:S(2)}) collective-permute-start(bf16[512,512]{1,0:T(8,128)(2,1)S(1)} %get-tuple-element.34.refs_3_.refs_5_), channel_id=1, source_target_pairs={{0,2},{1,3},{2,0},{3,1},{4,6},{5,7},{6,4},{7,5},{8,10},{9,11},{10,... | collective-permute-start | bytes 1572872 | tf_op jit(solution)/shard_map/ppermute | solution.py:20
  6.4 0.5 collective-permute-start.4
  6.9 0.1 collective-permute-start.5
  7.0 0.7 fusion.2.refs_0_
  7.7 16.0 %shard_map.95 = (bf16[1024,1024]{1,0:T(8,128)(2,1)S(1)}, bf16[1024,1024]{1,0:T(8,128)(2,1)S(1)}, bf16[1024,1024]{1,0:T(8,128)(2,1)S(1)}, bf16[1024,1024]{1,0:T(8,128)(2,1)S(1)}) custom-call(s32[4096]{0:T(1024)S(1)} %fusion.2.refs_0_, bf16[1024,4096]{1,0:T(8,128)(2,1)} %refs_1_.1), custom_call_target="tpu_custom_call" | custom-call | tf_op jit(solution)/shard_map/pallas_call | solution.py:52
  23.8 0.0 copy-start.3
  23.8 0.1 shard_map.97
  23.9 2.0 %collective-permute-start.2 = (bf16[512,256]{1,0:T(8,128)(2,1)S(1)}, bf16[512,256]{1,0:T(8,128)(2,1)S(1)}, u32[]{:S(2)}, u32[]{:S(2)}) collective-permute-start(bf16[512,256]{1,0:T(8,128)(2,1)S(1)} %get-tuple-element.35), channel_id=1, source_target_pairs={{0,2},{1,3},{2,0},{3,1},{4,6},{5,7},{6,4},{7,5},{8,10},{9,11},{10,... | collective-permute-start | bytes 786440 | tf_op jit(solution)/shard_map/ppermute | solution.py:20
  25.9 1.5 %collective-permute-start.3 = (bf16[512,256]{1,0:T(8,128)(2,1)S(1)}, bf16[512,256]{1,0:T(8,128)(2,1)S(1)}, u32[]{:S(2)}, u32[]{:S(2)}) collective-permute-start(bf16[512,256]{1,0:T(8,128)(2,1)S(1)} %get-tuple-element.36), channel_id=1, source_target_pairs={{0,1},{1,0},{2,3},{3,2},{4,5},{5,4},{6,7},{7,6},{8,9},{9,8},{10,11... | collective-permute-start | bytes 786440 | tf_op jit(solution)/shard_map/ppermute | solution.py:20
  27.4 0.5 collective-permute-start.10
  27.9 1.0 %collective-permute-done.4.refs_7_ = bf16[512,512]{1,0:T(8,128)(2,1)S(1)} collective-permute-done((bf16[512,512]{1,0:T(8,128)(2,1)S(1)}, bf16[512,512]{1,0:T(8,128)(2,1)S(1)}, u32[]{:S(2)}, u32[]{:S(2)}) %collective-permute-start.4) | collective-permute-done | bytes 524320 | tf_op jit(solution)/shard_map/ppermute | solution.py:20
  28.9 2.0 %collective-permute-start.9 = (bf16[512,256]{1,0:T(8,128)(2,1)S(1)}, bf16[512,256]{1,0:T(8,128)(2,1)S(1)}, u32[]{:S(2)}, u32[]{:S(2)}) collective-permute-start(bf16[512,256]{1,0:T(8,128)(2,1)S(1)} %get-tuple-element.41), channel_id=1, source_target_pairs={{0,2},{1,3},{2,0},{3,1},{4,6},{5,7},{6,4},{7,5},{8,10},{9,11},{10,... | collective-permute-start | bytes 786440 | tf_op jit(solution)/shard_map/ppermute | solution.py:20
  31.0 0.3 shard_map.98.refs_0_.refs_1_
  31.2 1.6 %collective-permute-start.6 = (bf16[48,512]{1,0:T(8,128)(2,1)S(1)}, bf16[48,512]{1,0:T(8,128)(2,1)S(1)}, u32[]{:S(2)}, u32[]{:S(2)}) collective-permute-start(bf16[48,512]{1,0:T(8,128)(2,1)S(1)} %shard_map.98.refs_0_.refs_1_), channel_id=1, source_target_pairs={{0,1},{1,0},{2,3},{3,2},{4,5},{5,4},{6,7},{7,6},{8,9},{9,8},{10,11... | collective-permute-start | bytes 147464 | tf_op jit(solution)/shard_map/ppermute | solution.py:20
  32.8 3.7 %collective-permute-done.2.refs_1_ = bf16[512,256]{1,0:T(8,128)(2,1)S(1)} collective-permute-done((bf16[512,256]{1,0:T(8,128)(2,1)S(1)}, bf16[512,256]{1,0:T(8,128)(2,1)S(1)}, u32[]{:S(2)}, u32[]{:S(2)}) %collective-permute-start.2) | collective-permute-done | bytes 262176 | tf_op jit(solution)/shard_map/ppermute | solution.py:20
  36.5 1.5 %collective-permute-start.7 = (bf16[48,512]{1,0:T(8,128)(2,1)S(1)}, bf16[48,512]{1,0:T(8,128)(2,1)S(1)}, u32[]{:S(2)}, u32[]{:S(2)}) collective-permute-start(bf16[48,512]{1,0:T(8,128)(2,1)S(1)} %shard_map.98.refs_0_.refs_1_), channel_id=1, source_target_pairs={{0,2},{1,3},{2,0},{3,1},{4,6},{5,7},{6,4},{7,5},{8,10},{9,11},{10,... | collective-permute-start | bytes 147464 | tf_op jit(solution)/shard_map/ppermute | solution.py:20
  38.1 0.0 collective-permute-start.8
  38.1 3.5 %shard_map.99 = (f32[1024,256]{1,0:T(8,128)S(1)}, f32[1024,256]{1,0:T(8,128)S(1)}) custom-call(bf16[48,512]{1,0:T(8,128)(2,1)S(1)} %shard_map.98.refs_0_.refs_1_, bf16[1024,1024]{1,0:T(8,128)(2,1)S(1)} %get-tuple-element.32.refs_0_.refs_1_, bf16[1024,1024]{1,0:T(8,128)(2,1)S(1)} %get-tuple-element.37.refs_2_, ...), custom_call_target="tpu_custom_call" | custom-call | tf_op jit(solution)/shard_map/pallas_call | solution.py:52
  41.6 2.3 %shard_map.100 = (bf16[1024,256]{1,0:T(8,128)(2,1)S(1)}, bf16[512,256]{1,0:T(8,128)(2,1)S(1)}, bf16[512,256]{1,0:T(8,128)(2,1)S(1)}) custom-call(bf16[1024,1024]{1,0:T(8,128)(2,1)S(1)} %get-tuple-element.31.refs_0_, bf16[512,256]{1,0:T(8,128)(2,1)S(1)} %collective-permute-done.2.refs_1_, bf16[512,256]{1,0:T(8,128)(2,1)S(1)} %collective-permute-done.3.refs_2_, ...), custom_call_target="tpu_custom_call" | custom-call | tf_op jit(solution)/shard_map/pallas_call | solution.py:52
  43.8 0.0 copy-start.4
  43.8 2.0 %collective-permute-start.23 = (bf16[512,256]{1,0:T(8,128)(2,1)S(1)}, bf16[512,256]{1,0:T(8,128)(2,1)S(1)}, u32[]{:S(2)}, u32[]{:S(2)}) collective-permute-start(bf16[512,256]{1,0:T(8,128)(2,1)S(1)} %get-tuple-element.58), channel_id=1, source_target_pairs={{0,2},{1,3},{2,0},{3,1},{4,6},{5,7},{6,4},{7,5},{8,10},{9,11},{10,... | collective-permute-start | bytes 786440 | tf_op jit(solution)/shard_map/ppermute | solution.py:20
  45.9 2.3 %shard_map.102 = (bf16[1024,256]{1,0:T(8,128)(2,1)S(1)}, bf16[512,256]{1,0:T(8,128)(2,1)S(1)}, bf16[512,256]{1,0:T(8,128)(2,1)S(1)}) custom-call(bf16[1024,1024]{1,0:T(8,128)(2,1)S(1)} %get-tuple-element.31.refs_0_, bf16[512,256]{1,0:T(8,128)(2,1)S(1)} %collective-permute-done.9.refs_1_, bf16[512,256]{1,0:T(8,128)(2,1)S(1)} %collective-permute-done.10.refs_2_, ...), custom_call_target="tpu_custom_call" | custom-call | tf_op jit(solution)/shard_map/pallas_call | solution.py:52
  48.2 0.1 shard_map.101.refs_0_.refs_1_
  48.3 3.4 %shard_map.103 = (bf16[512,512]{1,0:T(8,128)(2,1)S(1)}, bf16[512,512]{1,0:T(8,128)(2,1)S(1)}, f32[512,256]{1,0:T(8,128)S(1)}, f32[512,256]{1,0:T(8,128)S(1)}, f3...) custom-call(bf16[96,512]{1,0:T(8,128)(2,1)S(1)} %shard_map.101.refs_0_.refs_1_, ...), custom_call_target="tpu_custom_call" | custom-call | tf_op jit(solution)/shard_map/pallas_call | solution.py:52
  51.8 1.6 %collective-permute-start.15 = (bf16[512,512]{1,0:T(8,128)(2,1)S(1)}, bf16[512,512]{1,0:T(8,128)(2,1)S(1)}, u32[]{:S(2)}, u32[]{:S(2)}) collective-permute-start(bf16[512,512]{1,0:T(8,128)(2,1)S(1)} %get-tuple-element.47), channel_id=1, source_target_pairs={{0,1},{1,0},{2,3},{3,2},{4,5},{5,4},{6,7},{7,6},{8,9},{9,8},{10,11... | collective-permute-start | bytes 1572872 | tf_op jit(solution)/shard_map/ppermute | solution.py:20
  53.3 0.5 collective-permute-start.21
  53.9 0.1 collective-permute-start.19
  54.0 0.6 collective-permute-done.11.refs_2_
  54.6 1.2 %collective-permute-start.17 = (bf16[512,256]{1,0:T(8,128)(2,1)S(1)}, bf16[512,256]{1,0:T(8,128)(2,1)S(1)}, u32[]{:S(2)}, u32[]{:S(2)}) collective-permute-start(bf16[512,256]{1,0:T(8,128)(2,1)S(1)} %get-tuple-element.51), channel_id=1, source_target_pairs={{0,1},{1,0},{2,3},{3,2},{4,5},{5,4},{6,7},{7,6},{8,9},{9,8},{10,11... | collective-permute-start | bytes 786440 | tf_op jit(solution)/shard_map/ppermute | solution.py:20
  55.9 1.5 %collective-permute-start.16 = (bf16[512,512]{1,0:T(8,128)(2,1)S(1)}, bf16[512,512]{1,0:T(8,128)(2,1)S(1)}, u32[]{:S(2)}, u32[]{:S(2)}) collective-permute-start(bf16[512,512]{1,0:T(8,128)(2,1)S(1)} %get-tuple-element.48), channel_id=1, source_target_pairs={{0,2},{1,3},{2,0},{3,1},{4,6},{5,7},{6,4},{7,5},{8,10},{9,11},{10,... | collective-permute-start | bytes 1572872 | tf_op jit(solution)/shard_map/ppermute | solution.py:20
  57.4 0.1 shard_map.104.refs_0_
  57.5 13.1 %collective-permute-done.21.refs_1_ = bf16[512,256]{1,0:T(8,128)(2,1)S(1)} collective-permute-done((bf16[512,256]{1,0:T(8,128)(2,1)S(1)}, bf16[512,256]{1,0:T(8,128)(2,1)S(1)}, u32[]{:S(2)}, u32[]{:S(2)}) %collective-permute-start.21) | collective-permute-done | bytes 262176 | tf_op jit(solution)/shard_map/ppermute | solution.py:20
  70.5 1.6 %collective-permute-start.12 = (bf16[128,512]{1,0:T(8,128)(2,1)S(1)}, bf16[128,512]{1,0:T(8,128)(2,1)S(1)}, u32[]{:S(2)}, u32[]{:S(2)}) collective-permute-start(bf16[128,512]{1,0:T(8,128)(2,1)S(1)} %shard_map.104.refs_0_), channel_id=1, source_target_pairs={{0,8},{4,12},{8,0},{12,4},{16,24},{20,28},{24,16},{28,20},{1,9},{5... | collective-permute-start | bytes 393224 | tf_op jit(solution)/shard_map/ppermute | solution.py:20
  72.1 2.6 %collective-permute-start.13 = (bf16[128,512]{1,0:T(8,128)(2,1)S(1)}, bf16[128,512]{1,0:T(8,128)(2,1)S(1)}, u32[]{:S(2)}, u32[]{:S(2)}) collective-permute-start(bf16[128,512]{1,0:T(8,128)(2,1)S(1)} %shard_map.104.refs_0_), channel_id=1, source_target_pairs={{0,16},{4,20},{8,24},{12,28},{16,0},{20,4},{24,8},{28,12},{1,17},{... | collective-permute-start | bytes 393224 | tf_op jit(solution)/shard_map/ppermute | solution.py:20
  74.7 3.8 %collective-permute-start.14 = (bf16[128,512]{1,0:T(8,128)(2,1)S(1)}, bf16[128,512]{1,0:T(8,128)(2,1)S(1)}, u32[]{:S(2)}, u32[]{:S(2)}) collective-permute-start(bf16[128,512]{1,0:T(8,128)(2,1)S(1)} %shard_map.104.refs_0_), channel_id=1, source_target_pairs={{0,24},{4,28},{8,16},{12,20},{16,8},{20,12},{24,0},{28,4},{1,25},{... | collective-permute-start | bytes 393224 | tf_op jit(solution)/shard_map/ppermute | solution.py:20
  78.7 1.6 %collective-permute-start.20 = (bf16[512,256]{1,0:T(8,128)(2,1)S(1)}, bf16[512,256]{1,0:T(8,128)(2,1)S(1)}, u32[]{:S(2)}, u32[]{:S(2)}) collective-permute-start(bf16[512,256]{1,0:T(8,128)(2,1)S(1)} %shard_map.108), channel_id=1, source_target_pairs={{0,1},{1,0},{2,3},{3,2},{4,5},{5,4},{6,7},{7,6},{8,9},{9,8},{10,11... | collective-permute-start | bytes 786440 | tf_op jit(solution)/shard_map/ppermute | solution.py:20
  80.3 0.5 collective-permute-start.18
  80.8 0.8 collective-permute-done.14.refs_3_
  81.6 1.5 %collective-permute-start.24 = (bf16[512,256]{1,0:T(8,128)(2,1)S(1)}, bf16[512,256]{1,0:T(8,128)(2,1)S(1)}, u32[]{:S(2)}, u32[]{:S(2)}) collective-permute-start(bf16[512,256]{1,0:T(8,128)(2,1)S(1)} %shard_map.111), channel_id=1, source_target_pairs={{0,1},{1,0},{2,3},{3,2},{4,5},{5,4},{6,7},{7,6},{8,9},{9,8},{10,11... | collective-permute-start | bytes 786440 | tf_op jit(solution)/shard_map/ppermute | solution.py:20
  83.1 0.5 collective-permute-start.22
  83.6 2.1 %shard_map.105 = (bf16[32,512]{1,0:T(8,128)(2,1)S(1)}, f32[3,16,128]{2,1,0:T(8,128)}) custom-call(bf16[128,512]{1,0:T(8,128)(2,1)S(1)} %shard_map.104.refs_0_, bf16[128,512]{1,0:T(8,128)(2,1)S(1)} %collective-permute-done.12.refs_1_, bf16[128,512]{1,0:T(8,128)(2,1)S(1)} %collective-permute-done.13.refs_2_, bf16[128,512]{1,0:T(8,128)(2,1)S(1)} %collective-permute-done.14.refs_3_), custom_call_target="tpu_custom_call" | custom-call | tf_op jit(solution)/shard_map/pallas_call | solution.py:52
  85.7 0.5 shard_map.106
  86.2 0.4 collective-permute-done.18.refs_1_
  86.6 1.5 %shard_map.109.refs_0_ = f32[1024,512]{1,0:T(8,128)} custom-call(f32[1024,256]{1,0:T(8,128)S(1)} %get-tuple-element.49.refs_0_, bf16[512,256]{1,0:T(8,128)(2,1)S(1)} %collective-permute-done.18.refs_1_, bf16[512,256]{1,0:T(8,128)(2,1)S(1)} %collective-permute-done.20.refs_2_), custom_call_target="tpu_custom_call" | custom-call | tf_op jit(solution)/shard_map/pallas_call | solution.py:52
  88.2 1.3 %collective-permute-done.22.refs_2_ = bf16[512,256]{1,0:T(8,128)(2,1)S(1)} collective-permute-done((bf16[512,256]{1,0:T(8,128)(2,1)S(1)}, bf16[512,256]{1,0:T(8,128)(2,1)S(1)}, u32[]{:S(2)}, u32[]{:S(2)}) %collective-permute-start.22) | collective-permute-done | bytes 262176 | tf_op jit(solution)/shard_map/ppermute | solution.py:20
  89.4 1.5 %shard_map.112 = f32[1024,512]{1,0:T(8,128)} custom-call(f32[1024,512]{1,0:T(8,128)} %shard_map.109.refs_0_, f32[1024,256]{1,0:T(8,128)S(1)} %get-tuple-element.54.refs_1_, bf16[512,256]{1,0:T(8,128)(2,1)S(1)} %collective-permute-done.22.refs_2_, bf16[512,256]{1,0:T(8,128)(2,1)S(1)} %collective-permute-done.24.refs_3_), custom_call_target="tpu_custom_call", output_to_operand_aliasing={{}: (0, {})} | custom-call | tf_op jit(solution)/shard_map/pallas_call | solution.py:52
  (31 shorter events, 0.3 us)
Async XLA Ops:
  1.9 21.9 %collective-permute-start = (bf16[512,512]{1,0:T(8,128)(2,1)S(1)}, bf16[512,512]{1,0:T(8,128)(2,1)S(1)}, u32[]{:S(2)}, u32[]{:S(2)}) collective-permute-start(bf16[512,512]{1,0:T(8,128)(2,1)S(1)} %get-tuple-element.33.refs_2_.refs_4_), channel_id=1, source_target_pairs={{0,1},{1,0},{2,3},{3,2},{4,5},{5,4},{6,7},{7,6},{8,9},{9,8},{10,11... | collective-permute-start | bytes 1572872 | tf_op jit(solution)/shard_map/ppermute | solution.py:20
  4.9 18.9 %collective-permute-start.1 = (bf16[512,512]{1,0:T(8,128)(2,1)S(1)}, bf16[512,512]{1,0:T(8,128)(2,1)S(1)}, u32[]{:S(2)}, u32[]{:S(2)}) collective-permute-start(bf16[512,512]{1,0:T(8,128)(2,1)S(1)} %get-tuple-element.34.refs_3_.refs_5_), channel_id=1, source_target_pairs={{0,2},{1,3},{2,0},{3,1},{4,6},{5,7},{6,4},{7,5},{8,10},{9,11},{10,... | collective-permute-start | bytes 1572872 | tf_op jit(solution)/shard_map/ppermute | solution.py:20
  6.4 22.5 %collective-permute-start.4 = (bf16[512,512]{1,0:T(8,128)(2,1)S(1)}, bf16[512,512]{1,0:T(8,128)(2,1)S(1)}, u32[]{:S(2)}, u32[]{:S(2)}) collective-permute-start(bf16[512,512]{1,0:T(8,128)(2,1)S(1)} %get-tuple-element.34.refs_3_.refs_5_), channel_id=1, source_target_pairs={{0,1},{1,0},{2,3},{3,2},{4,5},{5,4},{6,7},{7,6},{8,9},{9,8},{10,11... | collective-permute-start | bytes 1572872 | tf_op jit(solution)/shard_map/ppermute | solution.py:20
  6.9 24.3 %collective-permute-start.5 = (bf16[512,512]{1,0:T(8,128)(2,1)S(1)}, bf16[512,512]{1,0:T(8,128)(2,1)S(1)}, u32[]{:S(2)}, u32[]{:S(2)}) collective-permute-start(bf16[512,512]{1,0:T(8,128)(2,1)S(1)} %get-tuple-element.33.refs_2_.refs_4_), channel_id=1, source_target_pairs={{0,2},{1,3},{2,0},{3,1},{4,6},{5,7},{6,4},{7,5},{8,10},{9,11},{10,... | collective-permute-start | bytes 1572872 | tf_op jit(solution)/shard_map/ppermute | solution.py:20
  23.7 7.2 %copy-start = (bf16[1024,32]{0,1:T(8,128)(2,1)S(1)}, bf16[1024,32]{0,1:T(8,128)(2,1)}, u32[]{:S(2)}) copy-start(bf16[1024,32]{0,1:T(8,128)(2,1)} %param.12) | copy-start | bytes 196612
  23.7 7.2 %copy-start.1 = (bf16[3,128,16]{1,2,0:T(8,128)(2,1)S(1)}, bf16[3,128,16]{1,2,0:T(8,128)(2,1)}, u32[]{:S(2)}) copy-start(bf16[3,128,16]{1,2,0:T(8,128)(2,1)} %param.13) | copy-start | bytes 36868
  23.8 7.2 %copy-start.3 = (bf16[4,416]{1,0:T(4,128)(2,1)S(1)}, bf16[4,416]{1,0:T(4,128)(2,1)}, u32[]{:S(2)}) copy-start(bf16[4,416]{1,0:T(4,128)(2,1)} %refs_6_.1) | copy-start | bytes 9988
  23.9 12.7 %collective-permute-start.2 = (bf16[512,256]{1,0:T(8,128)(2,1)S(1)}, bf16[512,256]{1,0:T(8,128)(2,1)S(1)}, u32[]{:S(2)}, u32[]{:S(2)}) collective-permute-start(bf16[512,256]{1,0:T(8,128)(2,1)S(1)} %get-tuple-element.35), channel_id=1, source_target_pairs={{0,2},{1,3},{2,0},{3,1},{4,6},{5,7},{6,4},{7,5},{8,10},{9,11},{10,... | collective-permute-start | bytes 786440 | tf_op jit(solution)/shard_map/ppermute | solution.py:20
  25.9 12.2 %collective-permute-start.3 = (bf16[512,256]{1,0:T(8,128)(2,1)S(1)}, bf16[512,256]{1,0:T(8,128)(2,1)S(1)}, u32[]{:S(2)}, u32[]{:S(2)}) collective-permute-start(bf16[512,256]{1,0:T(8,128)(2,1)S(1)} %get-tuple-element.36), channel_id=1, source_target_pairs={{0,1},{1,0},{2,3},{3,2},{4,5},{5,4},{6,7},{7,6},{8,9},{9,8},{10,11... | collective-permute-start | bytes 786440 | tf_op jit(solution)/shard_map/ppermute | solution.py:20
  27.4 16.4 %collective-permute-start.10 = (bf16[512,256]{1,0:T(8,128)(2,1)S(1)}, bf16[512,256]{1,0:T(8,128)(2,1)S(1)}, u32[]{:S(2)}, u32[]{:S(2)}) collective-permute-start(bf16[512,256]{1,0:T(8,128)(2,1)S(1)} %get-tuple-element.42), channel_id=1, source_target_pairs={{0,1},{1,0},{2,3},{3,2},{4,5},{5,4},{6,7},{7,6},{8,9},{9,8},{10,11... | collective-permute-start | bytes 786440 | tf_op jit(solution)/shard_map/ppermute | solution.py:20
  28.9 17.0 %collective-permute-start.9 = (bf16[512,256]{1,0:T(8,128)(2,1)S(1)}, bf16[512,256]{1,0:T(8,128)(2,1)S(1)}, u32[]{:S(2)}, u32[]{:S(2)}) collective-permute-start(bf16[512,256]{1,0:T(8,128)(2,1)S(1)} %get-tuple-element.41), channel_id=1, source_target_pairs={{0,2},{1,3},{2,0},{3,1},{4,6},{5,7},{6,4},{7,5},{8,10},{9,11},{10,... | collective-permute-start | bytes 786440 | tf_op jit(solution)/shard_map/ppermute | solution.py:20
  31.2 16.9 %collective-permute-start.6 = (bf16[48,512]{1,0:T(8,128)(2,1)S(1)}, bf16[48,512]{1,0:T(8,128)(2,1)S(1)}, u32[]{:S(2)}, u32[]{:S(2)}) collective-permute-start(bf16[48,512]{1,0:T(8,128)(2,1)S(1)} %shard_map.98.refs_0_.refs_1_), channel_id=1, source_target_pairs={{0,1},{1,0},{2,3},{3,2},{4,5},{5,4},{6,7},{7,6},{8,9},{9,8},{10,11... | collective-permute-start | bytes 147464 | tf_op jit(solution)/shard_map/ppermute | solution.py:20
  36.5 11.6 %collective-permute-start.7 = (bf16[48,512]{1,0:T(8,128)(2,1)S(1)}, bf16[48,512]{1,0:T(8,128)(2,1)S(1)}, u32[]{:S(2)}, u32[]{:S(2)}) collective-permute-start(bf16[48,512]{1,0:T(8,128)(2,1)S(1)} %shard_map.98.refs_0_.refs_1_), channel_id=1, source_target_pairs={{0,2},{1,3},{2,0},{3,1},{4,6},{5,7},{6,4},{7,5},{8,10},{9,11},{10,... | collective-permute-start | bytes 147464 | tf_op jit(solution)/shard_map/ppermute | solution.py:20
  38.1 10.1 %collective-permute-start.8 = (bf16[48,512]{1,0:T(8,128)(2,1)S(1)}, bf16[48,512]{1,0:T(8,128)(2,1)S(1)}, u32[]{:S(2)}, u32[]{:S(2)}) collective-permute-start(bf16[48,512]{1,0:T(8,128)(2,1)S(1)} %shard_map.98.refs_0_.refs_1_), channel_id=1, source_target_pairs={{0,3},{1,2},{2,1},{3,0},{4,7},{5,6},{6,5},{7,4},{8,11},{9,10},{10,... | collective-permute-start | bytes 147464 | tf_op jit(solution)/shard_map/ppermute | solution.py:20
  38.1 3.5 %copy-start.2 = (bf16[1024]{0:T(1024)(128)(2,1)S(1)}, bf16[1024]{0:T(1024)(128)(2,1)}, u32[]{:S(2)}) copy-start(bf16[1024]{0:T(1024)(128)(2,1)} %param.11) | copy-start | bytes 6148
  43.8 4.4 %copy-start.4 = (bf16[3,16]{1,0:T(4,128)(2,1)S(1)}, bf16[3,16]{1,0:T(4,128)(2,1)}, u32[]{:S(2)}) copy-start(bf16[3,16]{1,0:T(4,128)(2,1)} %refs_5_.1) | copy-start | bytes 292
  43.8 12.0 %collective-permute-start.23 = (bf16[512,256]{1,0:T(8,128)(2,1)S(1)}, bf16[512,256]{1,0:T(8,128)(2,1)S(1)}, u32[]{:S(2)}, u32[]{:S(2)}) collective-permute-start(bf16[512,256]{1,0:T(8,128)(2,1)S(1)} %get-tuple-element.58), channel_id=1, source_target_pairs={{0,2},{1,3},{2,0},{3,1},{4,6},{5,7},{6,4},{7,5},{8,10},{9,11},{10,... | collective-permute-start | bytes 786440 | tf_op jit(solution)/shard_map/ppermute | solution.py:20
  51.8 31.3 %collective-permute-start.15 = (bf16[512,512]{1,0:T(8,128)(2,1)S(1)}, bf16[512,512]{1,0:T(8,128)(2,1)S(1)}, u32[]{:S(2)}, u32[]{:S(2)}) collective-permute-start(bf16[512,512]{1,0:T(8,128)(2,1)S(1)} %get-tuple-element.47), channel_id=1, source_target_pairs={{0,1},{1,0},{2,3},{3,2},{4,5},{5,4},{6,7},{7,6},{8,9},{9,8},{10,11... | collective-permute-start | bytes 1572872 | tf_op jit(solution)/shard_map/ppermute | solution.py:20
  53.3 1.3 %collective-permute-start.11 = (bf16[96,512]{1,0:T(8,128)(2,1)S(1)}, bf16[96,512]{1,0:T(8,128)(2,1)S(1)}, u32[]{:S(2)}, u32[]{:S(2)}) collective-permute-start(bf16[96,512]{1,0:T(8,128)(2,1)S(1)} %shard_map.101.refs_0_.refs_1_), channel_id=1, source_target_pairs={{0,4},{4,0},{8,12},{12,8},{16,20},{20,16},{24,28},{28,24},{1,5},{5... | collective-permute-start | bytes 294920 | tf_op jit(solution)/shard_map/ppermute | solution.py:20
  53.3 17.2 %collective-permute-start.21 = (bf16[512,256]{1,0:T(8,128)(2,1)S(1)}, bf16[512,256]{1,0:T(8,128)(2,1)S(1)}, u32[]{:S(2)}, u32[]{:S(2)}) collective-permute-start(bf16[512,256]{1,0:T(8,128)(2,1)S(1)} %get-tuple-element.56), channel_id=1, source_target_pairs={{0,1},{1,0},{2,3},{3,2},{4,5},{5,4},{6,7},{7,6},{8,9},{9,8},{10,11... | collective-permute-start | bytes 786440 | tf_op jit(solution)/shard_map/ppermute | solution.py:20
  53.9 18.2 %collective-permute-start.19 = (bf16[512,256]{1,0:T(8,128)(2,1)S(1)}, bf16[512,256]{1,0:T(8,128)(2,1)S(1)}, u32[]{:S(2)}, u32[]{:S(2)}) collective-permute-start(bf16[512,256]{1,0:T(8,128)(2,1)S(1)} %get-tuple-element.53), channel_id=1, source_target_pairs={{0,2},{1,3},{2,0},{3,1},{4,6},{5,7},{6,4},{7,5},{8,10},{9,11},{10,... | collective-permute-start | bytes 786440 | tf_op jit(solution)/shard_map/ppermute | solution.py:20
  54.6 20.1 %collective-permute-start.17 = (bf16[512,256]{1,0:T(8,128)(2,1)S(1)}, bf16[512,256]{1,0:T(8,128)(2,1)S(1)}, u32[]{:S(2)}, u32[]{:S(2)}) collective-permute-start(bf16[512,256]{1,0:T(8,128)(2,1)S(1)} %get-tuple-element.51), channel_id=1, source_target_pairs={{0,1},{1,0},{2,3},{3,2},{4,5},{5,4},{6,7},{7,6},{8,9},{9,8},{10,11... | collective-permute-start | bytes 786440 | tf_op jit(solution)/shard_map/ppermute | solution.py:20
  55.9 29.8 %collective-permute-start.16 = (bf16[512,512]{1,0:T(8,128)(2,1)S(1)}, bf16[512,512]{1,0:T(8,128)(2,1)S(1)}, u32[]{:S(2)}, u32[]{:S(2)}) collective-permute-start(bf16[512,512]{1,0:T(8,128)(2,1)S(1)} %get-tuple-element.48), channel_id=1, source_target_pairs={{0,2},{1,3},{2,0},{3,1},{4,6},{5,7},{6,4},{7,5},{8,10},{9,11},{10,... | collective-permute-start | bytes 1572872 | tf_op jit(solution)/shard_map/ppermute | solution.py:20
  70.5 8.2 %collective-permute-start.12 = (bf16[128,512]{1,0:T(8,128)(2,1)S(1)}, bf16[128,512]{1,0:T(8,128)(2,1)S(1)}, u32[]{:S(2)}, u32[]{:S(2)}) collective-permute-start(bf16[128,512]{1,0:T(8,128)(2,1)S(1)} %shard_map.104.refs_0_), channel_id=1, source_target_pairs={{0,8},{4,12},{8,0},{12,4},{16,24},{20,28},{24,16},{28,20},{1,9},{5... | collective-permute-start | bytes 393224 | tf_op jit(solution)/shard_map/ppermute | solution.py:20
  72.1 8.1 %collective-permute-start.13 = (bf16[128,512]{1,0:T(8,128)(2,1)S(1)}, bf16[128,512]{1,0:T(8,128)(2,1)S(1)}, u32[]{:S(2)}, u32[]{:S(2)}) collective-permute-start(bf16[128,512]{1,0:T(8,128)(2,1)S(1)} %shard_map.104.refs_0_), channel_id=1, source_target_pairs={{0,16},{4,20},{8,24},{12,28},{16,0},{20,4},{24,8},{28,12},{1,17},{... | collective-permute-start | bytes 393224 | tf_op jit(solution)/shard_map/ppermute | solution.py:20
  74.7 6.9 %collective-permute-start.14 = (bf16[128,512]{1,0:T(8,128)(2,1)S(1)}, bf16[128,512]{1,0:T(8,128)(2,1)S(1)}, u32[]{:S(2)}, u32[]{:S(2)}) collective-permute-start(bf16[128,512]{1,0:T(8,128)(2,1)S(1)} %shard_map.104.refs_0_), channel_id=1, source_target_pairs={{0,24},{4,28},{8,16},{12,20},{16,8},{20,12},{24,0},{28,4},{1,25},{... | collective-permute-start | bytes 393224 | tf_op jit(solution)/shard_map/ppermute | solution.py:20
  78.7 7.5 %collective-permute-start.20 = (bf16[512,256]{1,0:T(8,128)(2,1)S(1)}, bf16[512,256]{1,0:T(8,128)(2,1)S(1)}, u32[]{:S(2)}, u32[]{:S(2)}) collective-permute-start(bf16[512,256]{1,0:T(8,128)(2,1)S(1)} %shard_map.108), channel_id=1, source_target_pairs={{0,1},{1,0},{2,3},{3,2},{4,5},{5,4},{6,7},{7,6},{8,9},{9,8},{10,11... | collective-permute-start | bytes 786440 | tf_op jit(solution)/shard_map/ppermute | solution.py:20
  80.3 6.4 %collective-permute-start.18 = (bf16[512,256]{1,0:T(8,128)(2,1)S(1)}, bf16[512,256]{1,0:T(8,128)(2,1)S(1)}, u32[]{:S(2)}, u32[]{:S(2)}) collective-permute-start(bf16[512,256]{1,0:T(8,128)(2,1)S(1)} %shard_map.107), channel_id=1, source_target_pairs={{0,2},{1,3},{2,0},{3,1},{4,6},{5,7},{6,4},{7,5},{8,10},{9,11},{10,... | collective-permute-start | bytes 786440 | tf_op jit(solution)/shard_map/ppermute | solution.py:20
  81.6 6.6 %collective-permute-start.24 = (bf16[512,256]{1,0:T(8,128)(2,1)S(1)}, bf16[512,256]{1,0:T(8,128)(2,1)S(1)}, u32[]{:S(2)}, u32[]{:S(2)}) collective-permute-start(bf16[512,256]{1,0:T(8,128)(2,1)S(1)} %shard_map.111), channel_id=1, source_target_pairs={{0,1},{1,0},{2,3},{3,2},{4,5},{5,4},{6,7},{7,6},{8,9},{9,8},{10,11... | collective-permute-start | bytes 786440 | tf_op jit(solution)/shard_map/ppermute | solution.py:20
  83.1 6.4 %collective-permute-start.22 = (bf16[512,256]{1,0:T(8,128)(2,1)S(1)}, bf16[512,256]{1,0:T(8,128)(2,1)S(1)}, u32[]{:S(2)}, u32[]{:S(2)}) collective-permute-start(bf16[512,256]{1,0:T(8,128)(2,1)S(1)} %shard_map.110), channel_id=1, source_target_pairs={{0,2},{1,3},{2,0},{3,1},{4,6},{5,7},{6,4},{7,5},{8,10},{9,11},{10,... | collective-permute-start | bytes 786440 | tf_op jit(solution)/shard_map/ppermute | solution.py:20

commit v5 on v4

--- a/solution.py
+++ b/solution.py
@@ -196,85 +196,86 @@
     return (leaf_x, jnp.stack(solution, axis=0))
 
 
-def pack_body(low_ref, high_ref, link_ref, sep_ref, fac_ref, out_ref):
-    levels, sep_block, width = sep_ref.shape
+def pack_body(low_ref, high_ref, link_ref, fac_ref, *refs):
+    outs, crossing_ref = refs[:-1], refs[-1]
     first = link_ref.shape[0]
     rows, cols = fac_ref.shape
-    half = low_ref.shape[0]
-    crossing = dot_nn(link_ref[:, :half], low_ref[...]) + dot_nn(link_ref[:, half:], high_ref[...])
-    out_ref[0:first, :] = crossing.astype(BF16)
-    for level in range(levels):
-        out_ref[first : first + sep_block, level * width : (level + 1) * width] = sep_ref[
-            level
-        ]
-    tiles = sep_block // rows
+    split = low_ref.shape[0]
+    crossing = dot_nn(link_ref[:, :split], low_ref[...]) + dot_nn(link_ref[:, split:], high_ref[...])
+    crossing_ref[...] = crossing
+    tiles = (outs[0].shape[0] - first) // rows
     factor = fac_ref[...].astype(F32)
     factor = jnp.concatenate([factor, jnp.zeros((rows, tiles * LANES - cols), F32)], axis=1)
     folded = [factor[:, tile * LANES : (tile + 1) * LANES] for tile in range(tiles)]
-    out_ref[first:, levels * width :] = jnp.concatenate(folded, axis=0).astype(BF16)
-
-
-def leaf_body(own_ref, x_ref, y_ref, d_ref, dinv_ref, out_ref, *, first, levels, rows, cols):
-    sep_block = dinv_ref.shape[1]
-    width = out_ref.shape[1]
+    folded = jnp.concatenate(folded, axis=0).astype(BF16)
     me = lax.axis_index("grp")
+    for mask, ref in enumerate(outs):
+        lanes = pl.ds(pl.multiple_of((me ^ mask) * LANES, LANES), LANES)
+        ref[:first, :] = crossing_ref[:, lanes].astype(BF16)
+        ref[first:, :] = folded
+
+
+def leaf_body(own_ref, x_ref, y_ref, d_ref, sep_ref, dinv_ref, out_ref, *, rows, cols):
+    levels, sep_block, _ = sep_ref.shape
     parts = (own_ref, x_ref, y_ref, d_ref)
-    total = parts[0][0:first, :].astype(F32)
+    first = own_ref.shape[0] - sep_block
+    tiles = sep_block // rows
+    me = lax.axis_index("grp")
+    total = own_ref[:first, :].astype(F32)
     for part in parts[1:]:
-        total = total + part[0:first, :].astype(F32)
-    out_ref[0:first, :] = total.astype(BF16)
-    part_width = width // len(parts)
+        total = total + part[:first, :].astype(F32)
+    out_ref[:first, :] = total.astype(BF16)
+    for level in range(levels):
+        out_ref[first + level * sep_block : first + (level + 1) * sep_block, :] = sep_ref[level]
+    row_owner = lax.broadcasted_iota(jnp.int32, (sep_block, tiles * LANES), 0) // rows
+    lane = lax.broadcasted_iota(jnp.int32, (sep_block, tiles * LANES), 1)
+    factor = jnp.zeros((sep_block, tiles * LANES), F32)
     for index, part in enumerate(parts):
-        lanes = pl.ds(pl.multiple_of((me ^ index) * part_width, part_width), part_width)
-        for level in range(levels):
-            out_ref[first + level * sep_block : first + (level + 1) * sep_block, lanes] = part[
-                first : first + sep_block, level * part_width : (level + 1) * part_width
-            ]
-    row_owner = lax.broadcasted_iota(jnp.int32, (sep_block, width), 0) // rows
-    lane = lax.broadcasted_iota(jnp.int32, (sep_block, width), 1)
-    factor = jnp.zeros((sep_block, width), F32)
-    for index, part in enumerate(parts):
-        folded = part[first:, levels * part_width :].astype(F32)
-        block = [folded[tile * rows : (tile + 1) * rows, :] for tile in range(sep_block // rows)]
+        folded = part[first:, :].astype(F32)
+        block = [folded[tile * rows : (tile + 1) * rows, :] for tile in range(tiles)]
         block = jnp.concatenate(block, axis=1)
         tiled = jnp.concatenate([block] * (sep_block // rows), axis=0)
         factor = factor + jnp.where(row_owner == (me ^ index), tiled, 0.0)
     pivots = dinv_ref[...].astype(F32).T
     for level in range(levels):
-        column = jnp.broadcast_to(pivots[:, level : level + 1], (sep_block, width))
+        column = jnp.broadcast_to(pivots[:, level : level + 1], factor.shape)
         factor = jnp.where(lane == cols + level, column, factor)
-    out_ref[first + levels * sep_block :, :] = factor.astype(BF16)
-
-
-def pair_body(own_ref, other_ref, out_ref, *, first, levels, sep_block):
+    base = first + levels * sep_block
+    for tile in range(tiles):
+        out_ref[base + tile * sep_block : base + (tile + 1) * sep_block, :] = factor[
+            :, tile * LANES : (tile + 1) * LANES
+        ].astype(BF16)
+
+
+def pair_body(own_ref, other_ref, out_ref, *, first, sep_block):
     is_odd = lax.axis_index("leaf") % 2 == 1
     own = own_ref[...].astype(F32)
     other = other_ref[...].astype(F32)
     even = jnp.where(is_odd, other, own)
     odd = jnp.where(is_odd, own, other)
     crossing = even[0:first] + odd[0:first]
-    for level in range(levels + 1):
-        base = first + level * sep_block
+    for index in range((own.shape[0] - first) // sep_block):
+        base = first + index * sep_block
         both = jnp.concatenate([even[base : base + sep_block], odd[base : base + sep_block]], axis=0)
-        if level == 0:
+        if index == 0:
             both = both - crossing
-        out_ref[level * first : (level + 1) * first, :] = both.astype(BF16)
-
-
-def tree_body(
-    *refs, count, first, levels, sep_block, cols, slice_width
-):
+        out_ref[index * first : (index + 1) * first, :] = both.astype(BF16)
+
+
+def tree_body(*refs, count, first, levels, sep_block, cols):
     pairs = refs[:count]
-    first_ref, sol_ref, stage_ref, val_ref = refs[count:]
-    leaf, me = lax.axis_index("leaf"), lax.axis_index("grp")
+    first_ref, sol_ref, stage_ref, factor_ref, val_ref = refs[count:]
+    leaf = lax.axis_index("leaf")
     pair = leaf // 2
-    nsep = count * first
-    width = pairs[0].shape[1]
+    nsep, width = factor_ref.shape
     for index, ref in enumerate(pairs):
         place = pl.ds(pl.multiple_of((pair ^ index) * first, first), first)
-        for level in range(levels + 1):
+        for level in range(levels):
             stage_ref[level, place, :] = ref[level * first : (level + 1) * first, :]
-    factor = stage_ref[levels]
+        for tile in range(width // LANES):
+            base = (levels + tile) * first
+            factor_ref[place, tile * LANES : (tile + 1) * LANES] = ref[base : base + first, :]
+    factor = factor_ref[...]
     column = lax.broadcasted_iota(jnp.int32, (width, nsep), 0)
     target = lax.broadcasted_iota(jnp.int32, (width, nsep), 1)
     row = lax.broadcasted_iota(jnp.int32, (nsep, nsep), 0)
@@ -295,9 +296,8 @@
         if level >= 2:
             coupling = block_diagonal(offset + size, size)
             residual = (stage_ref[level - 1].astype(F32) - dot_nn(coupling, residual)).astype(BF16)
-        choose = jnp.where(column == cols + level - 1, 1.0, 0.0).astype(BF16)
-        scale = dot_nn(factor, choose)
-        scale = jnp.concatenate([scale] * (width // nsep), axis=1)
+        pick = lax.broadcasted_iota(jnp.int32, (width, LANES), 0) == cols + level - 1
+        scale = dot_nn(factor, jnp.where(pick, 1.0, 0.0).astype(BF16))
         z_blocks.append((scale * dot_nn(weight, residual)).astype(BF16))
         weights.append(weight)
         couplings.append(coupling)
@@ -308,9 +308,7 @@
             value = value - dot_tn(couplings[level], current.astype(BF16))
         current = value
         val_ref[...] = value
-        lanes = pl.ds(pl.multiple_of(me * slice_width, slice_width), slice_width)
-        mine = val_ref[pl.ds(pl.multiple_of(leaf * sep_block, sep_block), sep_block), lanes]
-        sol_ref[level - 1] = mine
+        sol_ref[level - 1] = val_ref[pl.ds(pl.multiple_of(leaf * sep_block, sep_block), sep_block), :]
     first_ref[...] = val_ref[pl.ds(pl.multiple_of(pair * first, first), first), :].astype(BF16)
 
 
@@ -371,9 +369,9 @@
 
 
 def split_body(rhs_ref, low_ref, high_ref, sems):
-    half = low_ref.shape[0]
+    split = low_ref.shape[0]
     copies = [
-        pltpu.make_async_copy(rhs_ref.at[pl.ds(index * half, half), :], ref, sems.at[index])
+        pltpu.make_async_copy(rhs_ref.at[pl.ds(index * split, ref.shape[0]), :], ref, sems.at[index])
         for index, ref in enumerate((low_ref, high_ref))
     ]
     for copy in copies:
@@ -382,23 +380,22 @@
         copy.wait()
 
 
-def cut_body(*refs):
-    half = len(refs) // 3
-    for index, ref in enumerate(refs[:half]):
-        width = ref.shape[1] // 2
-        for part in range(2):
-            refs[half + 2 * index + part][...] = ref[:, part * width : (part + 1) * width]
+def cut_body(whole_ref, *outs):
+    for part, ref in enumerate(outs):
+        height, width = ref.shape
+        ref[...] = whole_ref[:height, part * width : (part + 1) * width]
 
 
 def forward_body(own_ref, x_ref, y_ref, *refs):
     pieces, (out_0_ref, out_1_ref, factor_ref, loads_ref) = refs[:-4], refs[-4:]
     rows = own_ref.shape[0]
-    half = rows // 2
     width = out_0_ref.shape[1]
     for index, ref in enumerate((own_ref, x_ref, y_ref)):
         factor_ref[index * rows : (index + 1) * rows, :] = ref[...]
-    for index, ref in enumerate(pieces):
-        loads_ref[index * half : (index + 1) * half, :] = ref[...]
+    start = 0
+    for ref in pieces:
+        loads_ref[start : start + ref.shape[0], :] = ref[...]
+        start += ref.shape[0]
     out_0_ref[...] = dot_tn(factor_ref[...], loads_ref[:, :width])
     out_1_ref[...] = dot_tn(factor_ref[...], loads_ref[:, width:])
 
@@ -406,9 +403,9 @@
 def far_body(
     far_ref, low_ref, high_ref, near_ref, dinv_ref, z_ref, relay_low_ref, relay_high_ref, loads_ref, part_ref
 ):
-    half = low_ref.shape[0]
-    loads_ref[:half, :] = low_ref[...]
-    loads_ref[half:, :] = high_ref[...]
+    split, half = low_ref.shape[0], relay_low_ref.shape[0]
+    loads_ref[:split, :] = low_ref[...]
+    loads_ref[split:, :] = high_ref[...]
     part_ref[...] = near_ref[...] + dot_tn(far_ref[...], loads_ref[...])
     pivots = dinv_ref[...].astype(F32)
     width = part_ref.shape[1]
@@ -421,28 +418,35 @@
     relay_high_ref[...] = dot_nn(far_ref[half:, :], z_ref[...]).astype(BF16)
 
 
-def near_body(own_ref, x_ref, y_ref, z_0_ref, z_1_ref, x_low_ref, y_high_ref, *refs):
-    highs, lows, out_ref = refs[:2], refs[2:4], refs[4]
+def near_body(own_ref, x_ref, y_ref, z_0_ref, z_1_ref, x_low_ref, y_high_ref, x_high_ref, y_low_ref, out_ref, z_ref):
+    half, split = x_low_ref.shape[0], z_0_ref.shape[1]
+    z_ref[:, :split] = z_0_ref[...]
+    z_ref[:, split:] = z_1_ref[...]
+    x_low_ref[...] = dot_nn(x_ref[:half, :], z_ref[...]).astype(BF16)
+    y_high_ref[...] = dot_nn(y_ref[half:, :], z_ref[...]).astype(BF16)
+    x_high_ref[...] = dot_nn(x_ref[half:, :], z_ref[...])
+    y_low_ref[...] = dot_nn(y_ref[:half, :], z_ref[...])
+    out_ref[...] = dot_nn(own_ref[...], z_ref[...])
+
+
+def add_body(near_ref, relay_0_ref, relay_1_ref, out_0_ref, out_1_ref):
+    relay = jnp.concatenate([relay_0_ref[...], relay_1_ref[...]], axis=1).astype(F32)
+    total = (near_ref[...] + relay).astype(BF16)
+    split = out_0_ref.shape[1]
+    out_0_ref[...] = total[:, :split]
+    out_1_ref[...] = total[:, split:]
+
+
+def base_body(own_ref, link_ref, mine_ref, x_ref, y_ref, d_ref, x_low_ref, y_high_ref, out_0_ref, out_1_ref, first_ref):
     half = x_low_ref.shape[0]
-    for part, z_ref in enumerate((z_0_ref, z_1_ref)):
-        width = z_ref.shape[1]
-        cols = slice(part * width, (part + 1) * width)
-        x_low_ref[:, cols] = dot_nn(x_ref[:half, :], z_ref[...]).astype(BF16)
-        y_high_ref[:, cols] = dot_nn(y_ref[half:, :], z_ref[...]).astype(BF16)
-        highs[part][...] = dot_nn(x_ref[half:, :], z_ref[...])
-        lows[part][...] = dot_nn(y_ref[:half, :], z_ref[...])
-        out_ref[:, cols] = dot_nn(own_ref[...], z_ref[...])
-
-
-def add_body(near_ref, relay_ref, out_ref):
-    out_ref[...] = (near_ref[...] + relay_ref[...].astype(F32)).astype(BF16)
-
-
-def base_body(own_ref, link_ref, first_ref, x_low_ref, y_high_ref, out_0_ref, out_1_ref):
-    half = x_low_ref.shape[0]
-    width = out_0_ref.shape[1]
-    for part, ref in enumerate((out_0_ref, out_1_ref)):
-        cols = slice(part * width, (part + 1) * width)
+    me = lax.axis_index("grp")
+    for mask, ref in enumerate((mine_ref, x_ref, y_ref, d_ref)):
+        lanes = pl.ds(pl.multiple_of((me ^ mask) * LANES, LANES), LANES)
+        first_ref[:, lanes] = ref[...]
+    start = 0
+    for ref in (out_0_ref, out_1_ref):
+        cols = slice(start, start + ref.shape[1])
+        start += ref.shape[1]
         ref[...] = own_ref[:, cols] - dot_tn(link_ref[...], first_ref[:, cols])
         ref[:half, :] += x_low_ref[:, cols].astype(F32)
         ref[half:, :] += y_high_ref[:, cols].astype(F32)
@@ -466,55 +470,54 @@
 
 def local_pairs(leaf_rhs, leaf_inv, ordering, leaf_dinv, leaf_link, sep_rhs, sep_factor, sep_dinv):
     rows, width = leaf_rhs.shape
-    half = rows // 2
+    half, split, quarter = rows // 2, rows // 16 * 7, width // 4
     group = lax.axis_size("grp")
     levels, slice_width, sep_block = sep_rhs.shape
     first = leaf_link.shape[1]
     fac_rows, cols = sep_factor.shape
+    tiles = sep_block // fac_rows
+    parts = range(2)
     me = lax.axis_index("grp").astype(jnp.int32)
     link_turned = leaf_link.T
-    half_bf16 = jax.ShapeDtypeStruct((half, width), BF16)
-    full_f32 = jax.ShapeDtypeStruct((rows, width), F32)
-
+
+    def bf16(height, breadth):
+        return jax.ShapeDtypeStruct((height, breadth), BF16)
+
+    def f32(height, breadth):
+        return jax.ShapeDtypeStruct((height, breadth), F32)
+
+    x_all = exchange(leaf_rhs, "grp", 1)
     low, high = call(
         split_body,
         (pltpu.with_memory_space_constraint(leaf_rhs, pltpu.HBM),),
         [pl.BlockSpec(memory_space=pltpu.HBM)],
-        (half_bf16, half_bf16),
+        (bf16(split, width), bf16(rows - split, width)),
         scratch_shapes=[pltpu.SemaphoreType.DMA((2,))],
     )
-    x_low = exchange(low, "grp", 1)
     y_high = exchange(high, "grp", 2)
-    x_high = exchange(high, "grp", 1)
     y_low = exchange(low, "grp", 2)
     dest = (ordering[0] // rows ^ me) * rows + ordering[0] % rows
     blocks = arrange(leaf_inv, dest, group)
-    parts = range(2)
-    part_bf16 = jax.ShapeDtypeStruct((half, width // 2), BF16)
-    part_f32 = jax.ShapeDtypeStruct((half, width // 2), F32)
-    tall_bf16 = jax.ShapeDtypeStruct((rows, width // 2), BF16)
-    tall_f32 = jax.ShapeDtypeStruct((rows, width // 2), F32)
-    *x_cut, y_cut_0, y_cut_1 = call(
-        cut_body, (x_low, y_high), [vmem()] * 2, [part_bf16] * 4, after=(blocks[0],)
-    )
-    d_low = [exchange(x_cut[part], "grp", 2) for part in parts]
-    d_high = [exchange((y_cut_0, y_cut_1)[part], "grp", 1) for part in parts]
 
     aux = call(
         pack_body,
-        (low, high, link_turned, jnp.swapaxes(sep_rhs, 1, 2), sep_factor),
-        [vmem()] * 5,
-        jax.ShapeDtypeStruct((first + sep_block, width), BF16),
-        after=(x_low, y_high),
-    )
-    aux_parts = [aux] + [exchange(aux, "grp", mask) for mask in range(1, group)]
+        (low, high, link_turned, sep_factor),
+        [vmem()] * 4,
+        [bf16(first + sep_block, LANES)] * group,
+        after=(blocks[0],),
+        scratch_shapes=[pltpu.VMEM((first, width), F32)],
+    )
+    high_cut = call(cut_body, (y_high,), [vmem()], [bf16(rows - split, width // 2)] * 2, after=(blocks[0],))
+    d_high = [exchange(high_cut[part], "grp", 1) for part in parts]
+    low_cut = call(cut_body, (x_all,), [vmem()], [bf16(split, width // 2)] * 2, after=(blocks[0],))
+    d_low = [exchange(low_cut[part], "grp", 2) for part in parts]
+    aux_parts = [aux[0]] + [exchange(aux[mask], "grp", mask) for mask in range(1, group)]
 
     part_y = call(
         forward_body,
-        (*blocks[:3], low, high, x_low, x_high, y_low, y_high),
-        [vmem()] * 9,
-        [tall_f32] * 2,
-        after=(aux,),
+        (*blocks[:3], low, high, x_all, y_low, y_high),
+        [vmem()] * 8,
+        [f32(rows, width // 2)] * 2,
         scratch_shapes=[pltpu.VMEM((3 * rows, rows), BF16), pltpu.VMEM((3 * rows, width), BF16)],
     )
     leaf_z, relay_low, relay_high = [], [], []
@@ -523,7 +526,7 @@
             far_body,
             (blocks[3], d_low[part], d_high[part], part_y[part], leaf_dinv.reshape(-1, LANES)),
             [vmem()] * 5,
-            (tall_bf16, part_bf16, part_bf16),
+            (bf16(rows, width // 2), bf16(half, width // 2), bf16(half, width // 2)),
             scratch_shapes=[pltpu.VMEM((rows, width // 2), BF16), pltpu.VMEM((rows, width // 2), F32)],
         )
         leaf_z.append(z_part)
@@ -531,81 +534,76 @@
         relay_high.append(exchange(far_high, "grp", 2))
 
     leaf_block = call(
-        functools.partial(leaf_body, first=first, levels=levels, rows=fac_rows, cols=cols),
-        (*aux_parts, sep_dinv),
-        [vmem()] * 5,
-        jax.ShapeDtypeStruct((first + (levels + 1) * sep_block, width), BF16),
+        functools.partial(leaf_body, rows=fac_rows, cols=cols),
+        (*aux_parts, jnp.swapaxes(sep_rhs, 1, 2), sep_dinv),
+        [vmem()] * 6,
+        bf16(first + (levels + tiles) * sep_block, LANES),
         after=(leaf_z[1],),
     )
     partner = exchange(leaf_block, "leaf", 1)
-    near_x_low, near_y_high, *near, own = call(
+    near_x_low, near_y_high, near_x_high, near_y_low, own = call(
         near_body,
         (*blocks[:3], *leaf_z),
         [vmem()] * 5,
-        [half_bf16] * 2 + [part_f32] * 4 + [full_f32],
+        [bf16(half, width)] * 2 + [f32(half, width)] * 2 + [f32(rows, width)],
         after=(leaf_block,),
+        scratch_shapes=[pltpu.VMEM((rows, width), BF16)],
     )
     sum_x_low = exchange(near_x_low, "grp", 1)
     sum_y_high = exchange(near_y_high, "grp", 2)
     pair_block = call(
-        functools.partial(pair_body, first=first, levels=levels, sep_block=sep_block),
+        functools.partial(pair_body, first=first, sep_block=sep_block),
         (leaf_block, partner),
         [vmem(), vmem()],
-        jax.ShapeDtypeStruct(((levels + 1) * first, width), BF16),
+        bf16((levels + tiles) * first, LANES),
         after=(own,),
     )
     count = lax.axis_size("leaf") // 2
     pairs = [pair_block] + [exchange(pair_block, "leaf", 2 * mask) for mask in range(1, count)]
     nsep = count * first
-    first_all, sep_turned = call(
+    first_here, sep_turned = call(
         functools.partial(
-            tree_body,
-            count=count,
-            first=first,
-            levels=levels,
-            sep_block=sep_block,
-            cols=cols,
-            slice_width=slice_width,
+            tree_body, count=count, first=first, levels=levels, sep_block=sep_block, cols=cols
         ),
         pairs,
         [vmem()] * count,
-        (
-            jax.ShapeDtypeStruct((first, width), BF16),
-            jax.ShapeDtypeStruct((levels, sep_block, slice_width), F32),
-        ),
-        scratch_shapes=[pltpu.VMEM((levels + 1, nsep, width), BF16), pltpu.VMEM((nsep, width), F32)],
-    )
-    sum_x_high, sum_y_low = [], []
-    for part in parts:
-        for mask, kept, relay, into in (
-            (1, near[part], relay_high[part], sum_x_high),
-            (2, near[2 + part], relay_low[part], sum_y_low),
-        ):
-            total = call(add_body, (kept, relay), [vmem()] * 2, part_bf16)
-            into.append(exchange(total, "grp", mask))
+        (bf16(first, LANES), jax.ShapeDtypeStruct((levels, sep_block, slice_width), F32)),
+        scratch_shapes=[
+            pltpu.VMEM((levels, nsep, LANES), BF16),
+            pltpu.VMEM((nsep, tiles * LANES), BF16),
+            pltpu.VMEM((nsep, LANES), F32),
+        ],
+    )
+    first_all = [first_here] + [exchange(first_here, "grp", mask) for mask in range(1, group)]
+    breadths = (width - quarter, quarter)
+    into = [bf16(half, breadth) for breadth in breadths]
+    x_sums = call(add_body, (near_x_high, *relay_high), [vmem()] * 3, into)
+    y_sums = call(add_body, (near_y_low, *relay_low), [vmem()] * 3, into)
+    sum_x_high = [exchange(x_sums[part], "grp", 1) for part in parts]
+    sum_y_low = [exchange(y_sums[part], "grp", 2) for part in parts]
     base = call(
         base_body,
-        (own, link_turned, first_all, sum_x_low, sum_y_high),
-        [vmem()] * 5,
-        [tall_f32] * 2,
+        (own, link_turned, *first_all, sum_x_low, sum_y_high),
+        [vmem()] * (4 + group),
+        [f32(rows, breadth) for breadth in breadths],
+        scratch_shapes=[pltpu.VMEM((first, width), BF16)],
     )
     block = rows // 4
     leaf_x = ()
-    for part in parts:
+    for part, start in zip(parts, (0, breadths[0] // breadths[1])):
         leaf_x = (
             call(
                 last_body,
                 (base[part], sum_y_low[part], sum_x_high[part]),
                 [vmem()] * 3,
-                full_f32,
+                f32(rows, width),
                 after=leaf_x,
                 grid=(rows // block,),
-                out_specs=pl.BlockSpec((block, width // 2), lambda step, part=part: (step, part)),
+                out_specs=pl.BlockSpec((block, breadths[part]), lambda step, start=start: (step, start)),
                 input_output_aliases={0: 0} if leaf_x else {},
             ),
         )
-    leaf_x = leaf_x[0]
-    return leaf_x, jnp.swapaxes(sep_turned, 1, 2)
+    return leaf_x[0], jnp.swapaxes(sep_turned, 1, 2)
 
 
 def fits(leaf_rhs, leaf_inv, sep_rhs, sep_factor, leaf_link):
@@ -621,10 +619,9 @@
         and leaf_link.shape[1] == 2 * sep_block
         and sep_block % 16 == 0
         and slice_width % 128 == 0
-        and levels <= count
         and sep_block % sep_factor.shape[0] == 0
-        and sep_factor.shape[1] + levels <= width
-        and width == (levels + 1) * slice_width == sep_block // sep_factor.shape[0] * LANES
+        and sep_factor.shape[1] + levels <= sep_block // sep_factor.shape[0] * LANES
+        and width == count * slice_width
         and slice_width == LANES
         and width % (leaves * sep_block) == 0
     )

time: 91.2 us -> 102 us (1.12)
  waiting for transfers between devices: 21 us -> 30.1 us
  starting transfers between devices: 33.4 us -> 35.2 us
    ppermute x25 -> x27, waiting for transfers between devices: 21 us -> 30.1 us  [exchange(): lax.ppermute(block, axis, [(low, low ^ mask) for low in range(count)])]
    ppermute x25 -> x27, starting transfers between devices: 33.4 us -> 35.2 us  [exchange(): lax.ppermute(block, axis, [(low, low ^ mask) for low in range(count)])]
    pallas_call x18 -> x17, Pallas kernels: 35 us -> 35 us  [call(): pl.pallas_call(skipping, out_shape=out_shape, in_specs=[pl.BlockSpec(memo...]
  transfers between devices with their start and end apart: 25 -> 27, of which waited for: 7 -> 12; matrix products, arithmetic and copies ran while one was open for 1% -> 1% of each run, Pallas kernels for 35% -> 33%
where the time goes in v5:
time: 102 us
  starting transfers between devices  35.2 us (35%)
  Pallas kernels  35 us (34%)
  waiting for transfers between devices  30.1 us (30%)
    ppermute x27, starting transfers between devices, exchange(): lax.ppermute(block, axis, [(low, low ^ mask) for low in range(count)])  35.2 us
    pallas_call x17, Pallas kernels, call(): pl.pallas_call(skipping, out_shape=out_shape, in_specs=[pl.BlockSpec(memo...  35 us
    ppermute x27, waiting for transfers between devices, exchange(): lax.ppermute(block, axis, [(low, low ^ mask) for low in range(count)])  30.1 us
  transfers between devices with their start and end apart: 27, of which 12 were waited for; matrix products, arithmetic and copies ran while one was open for 1% of the time, Pallas kernels for 33%

profile of v5, /device:TPU:0, one launch (start us, length us, event | category | flops | bytes accessed | tf_op | source)
XLA Modules:
  0.0 101.9 jit_solution(9550061314327776208)
XLA Ops:
  0.6 3.0 %collective-permute-start = (bf16[1024,512]{1,0:T(8,128)(2,1)}, bf16[1024,512]{1,0:T(8,128)(2,1)S(1)}, u32[]{:S(2)}, u32[]{:S(2)}) collective-permute-start(bf16[1024,512]{1,0:T(8,128)(2,1)} %refs_0_.1), channel_id=1, source_target_pairs={{0,1},{1,0},{2,3},{3,2},{4,5},{5,4},{6,7},{7,6},{8,9},{9,8},{10,11... | collective-permute-start | bytes 3145736 | tf_op jit(solution)/shard_map/ppermute | solution.py:20
  3.7 1.2 %shard_map.97 = (bf16[448,512]{1,0:T(8,128)(2,1)S(1)}, bf16[576,512]{1,0:T(8,128)(2,1)S(1)}) custom-call(bf16[1024,512]{1,0:T(8,128)(2,1)} %refs_0_.1), custom_call_target="tpu_custom_call" | custom-call | tf_op jit(solution)/shard_map/pallas_call | solution.py:52
  4.9 1.6 %collective-permute-start.2 = (bf16[576,512]{1,0:T(8,128)(2,1)S(1)}, bf16[576,512]{1,0:T(8,128)(2,1)S(1)}, u32[]{:S(2)}, u32[]{:S(2)}) collective-permute-start(bf16[576,512]{1,0:T(8,128)(2,1)S(1)} %get-tuple-element.40.refs_4_.refs_2_), channel_id=1, source_target_pairs={{0,2},{1,3},{2,0},{3,1},{4,6},{5,7},{6,4},{7,5},{8,10},{9,11},{10,... | collective-permute-start | bytes 1769480 | tf_op jit(solution)/shard_map/ppermute | solution.py:20
  6.5 0.5 collective-permute-start.4
  7.0 0.7 fusion.2.refs_0_
  7.7 16.0 %shard_map.95 = (bf16[1024,1024]{1,0:T(8,128)(2,1)S(1)}, bf16[1024,1024]{1,0:T(8,128)(2,1)S(1)}, bf16[1024,1024]{1,0:T(8,128)(2,1)S(1)}, bf16[1024,1024]{1,0:T(8,128)(2,1)S(1)}) custom-call(s32[4096]{0:T(1024)S(1)} %fusion.2.refs_0_, bf16[1024,4096]{1,0:T(8,128)(2,1)} %refs_1_.1), custom_call_target="tpu_custom_call" | custom-call | tf_op jit(solution)/shard_map/pallas_call | solution.py:52
  23.9 3.9 %collective-permute-done.refs_1_.refs_5_ = bf16[1024,512]{1,0:T(8,128)(2,1)S(1)} collective-permute-done((bf16[1024,512]{1,0:T(8,128)(2,1)}, bf16[1024,512]{1,0:T(8,128)(2,1)S(1)}, u32[]{:S(2)}, u32[]{:S(2)}) %collective-permute-start) | collective-permute-done | bytes 1048608 | tf_op jit(solution)/shard_map/ppermute | solution.py:20
  27.9 2.1 %collective-permute-start.8 = (bf16[448,256]{1,0:T(8,128)(2,1)S(1)}, bf16[448,256]{1,0:T(8,128)(2,1)S(1)}, u32[]{:S(2)}, u32[]{:S(2)}) collective-permute-start(bf16[448,256]{1,0:T(8,128)(2,1)S(1)} %get-tuple-element.51), channel_id=1, source_target_pairs={{0,2},{1,3},{2,0},{3,1},{4,6},{5,7},{6,4},{7,5},{8,10},{9,11},{10,... | collective-permute-start | bytes 688136 | tf_op jit(solution)/shard_map/ppermute | solution.py:20
  30.0 1.5 %collective-permute-start.3 = (bf16[576,256]{1,0:T(8,128)(2,1)S(1)}, bf16[576,256]{1,0:T(8,128)(2,1)S(1)}, u32[]{:S(2)}, u32[]{:S(2)}) collective-permute-start(bf16[576,256]{1,0:T(8,128)(2,1)S(1)} %get-tuple-element.41), channel_id=1, source_target_pairs={{0,1},{1,0},{2,3},{3,2},{4,5},{5,4},{6,7},{7,6},{8,9},{9,8},{10,11... | collective-permute-start | bytes 884744 | tf_op jit(solution)/shard_map/ppermute | solution.py:20
  31.5 0.5 collective-permute-start.1
  32.0 3.5 %shard_map.99 = (f32[1024,256]{1,0:T(8,128)S(1)}, f32[1024,256]{1,0:T(8,128)S(1)}) custom-call(bf16[1024,1024]{1,0:T(8,128)(2,1)S(1)} %get-tuple-element.38.refs_0_.refs_1_, bf16[1024,1024]{1,0:T(8,128)(2,1)S(1)} %get-tuple-element.42.refs_1_.refs_2_, bf16[1024,1024]{1,0:T(8,128)(2,1)S(1)} %get-tuple-element.43.refs_2_.refs_3_, ...), custom_call_target="tpu_custom_call" | custom-call | tf_op jit(solution)/shard_map/pallas_call | solution.py:52
  35.5 0.9 collective-permute-done.8.refs_1_
  36.5 2.3 %shard_map.103 = (bf16[1024,256]{1,0:T(8,128)(2,1)S(1)}, bf16[512,256]{1,0:T(8,128)(2,1)S(1)}, bf16[512,256]{1,0:T(8,128)(2,1)S(1)}) custom-call(bf16[1024,1024]{1,0:T(8,128)(2,1)S(1)} %get-tuple-element.37.refs_0_, bf16[448,256]{1,0:T(8,128)(2,1)S(1)} %collective-permute-done.8.refs_1_, bf16[576,256]{1,0:T(8,128)(2,1)S(1)} %collective-permute-done.9.refs_2_, ...), custom_call_target="tpu_custom_call" | custom-call | tf_op jit(solution)/shard_map/pallas_call | solution.py:52
  38.8 2.0 %collective-permute-start.22 = (bf16[512,256]{1,0:T(8,128)(2,1)S(1)}, bf16[512,256]{1,0:T(8,128)(2,1)S(1)}, u32[]{:S(2)}, u32[]{:S(2)}) collective-permute-start(bf16[512,256]{1,0:T(8,128)(2,1)S(1)} %get-tuple-element.65), channel_id=1, source_target_pairs={{0,2},{1,3},{2,0},{3,1},{4,6},{5,7},{6,4},{7,5},{8,10},{9,11},{10,... | collective-permute-start | bytes 786440 | tf_op jit(solution)/shard_map/ppermute | solution.py:20
  40.8 0.3 shard_map.101
  41.2 0.9 collective-permute-start.5
  42.1 0.5 collective-permute-start.6
  42.6 2.1 %collective-permute-start.7 = (bf16[48,128]{1,0:T(8,128)(2,1)S(1)}, bf16[48,128]{1,0:T(8,128)(2,1)S(1)}, u32[]{:S(2)}, u32[]{:S(2)}) collective-permute-start(bf16[48,128]{1,0:T(8,128)(2,1)S(1)} %get-tuple-element.50), channel_id=1, source_target_pairs={{0,3},{1,2},{2,1},{3,0},{4,7},{5,6},{6,5},{7,4},{8,11},{9,10},{10,... | collective-permute-start | bytes 36872 | tf_op jit(solution)/shard_map/ppermute | solution.py:20
  44.7 2.3 %shard_map.100 = (bf16[1024,256]{1,0:T(8,128)(2,1)S(1)}, bf16[512,256]{1,0:T(8,128)(2,1)S(1)}, bf16[512,256]{1,0:T(8,128)(2,1)S(1)}) custom-call(bf16[1024,1024]{1,0:T(8,128)(2,1)S(1)} %get-tuple-element.37.refs_0_, bf16[448,256]{1,0:T(8,128)(2,1)S(1)} %collective-permute-done.1.refs_1_, bf16[576,256]{1,0:T(8,128)(2,1)S(1)} %collective-permute-done.3.refs_2_, ...), custom_call_target="tpu_custom_call" | custom-call | tf_op jit(solution)/shard_map/pallas_call | solution.py:52
  47.1 1.3 %collective-permute-start.19 = (bf16[512,256]{1,0:T(8,128)(2,1)S(1)}, bf16[512,256]{1,0:T(8,128)(2,1)S(1)}, u32[]{:S(2)}, u32[]{:S(2)}) collective-permute-start(bf16[512,256]{1,0:T(8,128)(2,1)S(1)} %get-tuple-element.61), channel_id=1, source_target_pairs={{0,1},{1,0},{2,3},{3,2},{4,5},{5,4},{6,7},{7,6},{8,9},{9,8},{10,11... | collective-permute-start | bytes 786440 | tf_op jit(solution)/shard_map/ppermute | solution.py:20
  48.5 0.7 collective-permute-start.20
  49.3 3.4 %shard_map.104 = (bf16[512,512]{1,0:T(8,128)(2,1)S(1)}, bf16[512,512]{1,0:T(8,128)(2,1)S(1)}, f32[512,512]{1,0:T(8,128)S(1)}, f32[512,512]{1,0:T(8,128)S(1)}, f32[1024,512]{1,0:T(8,128)S(1)}) custom-call(bf16[144,128]{1,0:T(8,128)(2,1)S(1)} %shard_map.102.refs_0_.refs_1_, bf16[1024,1024]{1,0:T(8,128)(2,1)S(1)} %get-tuple-element.38.refs_0_.refs_1_, ...), custom_call_target="tpu_custom_call" | custom-call | tf_op jit(solution)/shard_map/pallas_call | solution.py:52
  52.8 1.4 %collective-permute-start.17 = (bf16[512,512]{1,0:T(8,128)(2,1)S(1)}, bf16[512,512]{1,0:T(8,128)(2,1)S(1)}, u32[]{:S(2)}, u32[]{:S(2)}) collective-permute-start(bf16[512,512]{1,0:T(8,128)(2,1)S(1)} %get-tuple-element.57), channel_id=1, source_target_pairs={{0,1},{1,0},{2,3},{3,2},{4,5},{5,4},{6,7},{7,6},{8,9},{9,8},{10,11... | collective-permute-start | bytes 1572872 | tf_op jit(solution)/shard_map/ppermute | solution.py:20
  54.2 1.5 %collective-permute-start.18 = (bf16[512,512]{1,0:T(8,128)(2,1)S(1)}, bf16[512,512]{1,0:T(8,128)(2,1)S(1)}, u32[]{:S(2)}, u32[]{:S(2)}) collective-permute-start(bf16[512,512]{1,0:T(8,128)(2,1)S(1)} %get-tuple-element.58), channel_id=1, source_target_pairs={{0,2},{1,3},{2,0},{3,1},{4,6},{5,7},{6,4},{7,5},{8,10},{9,11},{10,... | collective-permute-start | bytes 1572872 | tf_op jit(solution)/shard_map/ppermute | solution.py:20
  55.8 1.2 %collective-permute-start.24 = (bf16[512,384]{1,0:T(8,128)(2,1)S(1)}, bf16[512,384]{1,0:T(8,128)(2,1)S(1)}, u32[]{:S(2)}, u32[]{:S(2)}) collective-permute-start(bf16[512,384]{1,0:T(8,128)(2,1)S(1)} %get-tuple-element.67), channel_id=1, source_target_pairs={{0,1},{1,0},{2,3},{3,2},{4,5},{5,4},{6,7},{7,6},{8,9},{9,8},{10,11... | collective-permute-start | bytes 1179656 | tf_op jit(solution)/shard_map/ppermute | solution.py:20
  57.0 4.9 %collective-permute-done.20.refs_2_ = bf16[512,256]{1,0:T(8,128)(2,1)S(1)} collective-permute-done((bf16[512,256]{1,0:T(8,128)(2,1)S(1)}, bf16[512,256]{1,0:T(8,128)(2,1)S(1)}, u32[]{:S(2)}, u32[]{:S(2)}) %collective-permute-start.20) | collective-permute-done | bytes 262176 | tf_op jit(solution)/shard_map/ppermute | solution.py:20
  62.1 2.0 %collective-permute-start.21 = (bf16[512,384]{1,0:T(8,128)(2,1)S(1)}, bf16[512,384]{1,0:T(8,128)(2,1)S(1)}, u32[]{:S(2)}, u32[]{:S(2)}) collective-permute-start(bf16[512,384]{1,0:T(8,128)(2,1)S(1)} %get-tuple-element.63), channel_id=1, source_target_pairs={{0,2},{1,3},{2,0},{3,1},{4,6},{5,7},{6,4},{7,5},{8,10},{9,11},{10,... | collective-permute-start | bytes 1179656 | tf_op jit(solution)/shard_map/ppermute | solution.py:20
  64.1 1.2 %collective-permute-done.10.refs_2_ = bf16[144,128]{1,0:T(8,128)(2,1)S(1)} collective-permute-done((bf16[144,128]{1,0:T(8,128)(2,1)S(1)}, bf16[144,128]{1,0:T(8,128)(2,1)S(1)}, u32[]{:S(2)}, u32[]{:S(2)}) %collective-permute-start.10) | collective-permute-done | bytes 36896 | tf_op jit(solution)/shard_map/ppermute | solution.py:20
  65.3 1.6 %collective-permute-start.11 = (bf16[224,128]{1,0:T(8,128)(2,1)S(1)}, bf16[224,128]{1,0:T(8,128)(2,1)S(1)}, u32[]{:S(2)}, u32[]{:S(2)}) collective-permute-start(bf16[224,128]{1,0:T(8,128)(2,1)S(1)} %shard_map.105.refs_0_), channel_id=1, source_target_pairs={{0,8},{4,12},{8,0},{12,4},{16,24},{20,28},{24,16},{28,20},{1,9},{5... | collective-permute-start | bytes 172040 | tf_op jit(solution)/shard_map/ppermute | solution.py:20
  67.0 2.6 %collective-permute-done.11.refs_1_ = bf16[224,128]{1,0:T(8,128)(2,1)S(1)} collective-permute-done((bf16[224,128]{1,0:T(8,128)(2,1)S(1)}, bf16[224,128]{1,0:T(8,128)(2,1)S(1)}, u32[]{:S(2)}, u32[]{:S(2)}) %collective-permute-start.11) | collective-permute-done | bytes 57376 | tf_op jit(solution)/shard_map/ppermute | solution.py:20
  69.6 2.6 %collective-permute-start.12 = (bf16[224,128]{1,0:T(8,128)(2,1)S(1)}, bf16[224,128]{1,0:T(8,128)(2,1)S(1)}, u32[]{:S(2)}, u32[]{:S(2)}) collective-permute-start(bf16[224,128]{1,0:T(8,128)(2,1)S(1)} %shard_map.105.refs_0_), channel_id=1, source_target_pairs={{0,16},{4,20},{8,24},{12,28},{16,0},{20,4},{24,8},{28,12},{1,17},{... | collective-permute-start | bytes 172040 | tf_op jit(solution)/shard_map/ppermute | solution.py:20
  72.2 2.5 %collective-permute-done.12.refs_2_ = bf16[224,128]{1,0:T(8,128)(2,1)S(1)} collective-permute-done((bf16[224,128]{1,0:T(8,128)(2,1)S(1)}, bf16[224,128]{1,0:T(8,128)(2,1)S(1)}, u32[]{:S(2)}, u32[]{:S(2)}) %collective-permute-start.12) | collective-permute-done | bytes 57376 | tf_op jit(solution)/shard_map/ppermute | solution.py:20
  74.7 4.1 %collective-permute-start.13 = (bf16[224,128]{1,0:T(8,128)(2,1)S(1)}, bf16[224,128]{1,0:T(8,128)(2,1)S(1)}, u32[]{:S(2)}, u32[]{:S(2)}) collective-permute-start(bf16[224,128]{1,0:T(8,128)(2,1)S(1)} %shard_map.105.refs_0_), channel_id=1, source_target_pairs={{0,24},{4,28},{8,16},{12,20},{16,8},{20,12},{24,0},{28,4},{1,25},{... | collective-permute-start | bytes 172040 | tf_op jit(solution)/shard_map/ppermute | solution.py:20
  78.8 2.2 %collective-permute-done.13.refs_3_ = bf16[224,128]{1,0:T(8,128)(2,1)S(1)} collective-permute-done((bf16[224,128]{1,0:T(8,128)(2,1)S(1)}, bf16[224,128]{1,0:T(8,128)(2,1)S(1)}, u32[]{:S(2)}, u32[]{:S(2)}) %collective-permute-start.13) | collective-permute-done | bytes 57376 | tf_op jit(solution)/shard_map/ppermute | solution.py:20
  80.9 1.9 %shard_map.106 = (bf16[32,128]{1,0:T(8,128)(2,1)S(1)}, f32[3,16,128]{2,1,0:T(8,128)}) custom-call(bf16[224,128]{1,0:T(8,128)(2,1)S(1)} %shard_map.105.refs_0_, bf16[224,128]{1,0:T(8,128)(2,1)S(1)} %collective-permute-done.11.refs_1_, bf16[224,128]{1,0:T(8,128)(2,1)S(1)} %collective-permute-done.12.refs_2_, bf16[224,128]{1,0:T(8,128)(2,1)S(1)} %collective-permute-done.13.refs_3_), custom_call_target="tpu_custom_call" | custom-call | tf_op jit(solution)/shard_map/pallas_call | solution.py:52
  82.9 0.9 collective-permute-start.14
  83.7 2.8 %collective-permute-done.14.refs_3_ = bf16[32,128]{1,0:T(8,128)(2,1)S(1)} collective-permute-done((bf16[32,128]{1,0:T(8,128)(2,1)S(1)}, bf16[32,128]{1,0:T(8,128)(2,1)S(1)}, u32[]{:S(2)}, u32[]{:S(2)}) %collective-permute-start.14) | collective-permute-done | bytes 8224 | tf_op jit(solution)/shard_map/ppermute | solution.py:20
  86.5 0.5 collective-permute-start.15
  87.0 3.1 %collective-permute-done.15.refs_4_ = bf16[32,128]{1,0:T(8,128)(2,1)S(1)} collective-permute-done((bf16[32,128]{1,0:T(8,128)(2,1)S(1)}, bf16[32,128]{1,0:T(8,128)(2,1)S(1)}, u32[]{:S(2)}, u32[]{:S(2)}) %collective-permute-start.15) | collective-permute-done | bytes 8224 | tf_op jit(solution)/shard_map/ppermute | solution.py:20
  90.2 0.8 collective-permute-start.16
  91.0 3.7 %collective-permute-done.16.refs_5_ = bf16[32,128]{1,0:T(8,128)(2,1)S(1)} collective-permute-done((bf16[32,128]{1,0:T(8,128)(2,1)S(1)}, bf16[32,128]{1,0:T(8,128)(2,1)S(1)}, u32[]{:S(2)}, u32[]{:S(2)}) %collective-permute-start.16) | collective-permute-done | bytes 8224 | tf_op jit(solution)/shard_map/ppermute | solution.py:20
  94.7 0.9 collective-permute-start.26
  95.6 0.5 collective-permute-start.25
  96.1 0.5 shard_map.107
  96.7 1.7 %shard_map.110.refs_0_ = f32[1024,512]{1,0:T(8,128)} custom-call(f32[1024,384]{1,0:T(8,128)S(1)} %get-tuple-element.59.refs_0_, bf16[512,384]{1,0:T(8,128)(2,1)S(1)} %collective-permute-done.21.refs_1_, bf16[512,384]{1,0:T(8,128)(2,1)S(1)} %collective-permute-done.24.refs_2_), custom_call_target="tpu_custom_call" | custom-call | tf_op jit(solution)/shard_map/pallas_call | solution.py:52
  98.4 1.3 %collective-permute-done.26.refs_3_ = bf16[512,128]{1,0:T(8,128)(2,1)S(1)} collective-permute-done((bf16[512,128]{1,0:T(8,128)(2,1)S(1)}, bf16[512,128]{1,0:T(8,128)(2,1)S(1)}, u32[]{:S(2)}, u32[]{:S(2)}) %collective-permute-start.26) | collective-permute-done | bytes 131104 | tf_op jit(solution)/shard_map/ppermute | solution.py:20
  99.7 0.9 collective-permute-done.25.refs_2_
  100.6 1.4 %shard_map.111 = f32[1024,512]{1,0:T(8,128)} custom-call(f32[1024,512]{1,0:T(8,128)} %shard_map.110.refs_0_, f32[1024,128]{1,0:T(8,128)S(1)} %get-tuple-element.68.refs_1_, bf16[512,128]{1,0:T(8,128)(2,1)S(1)} %collective-permute-done.25.refs_2_, bf16[512,128]{1,0:T(8,128)(2,1)S(1)} %collective-permute-done.26.refs_3_), custom_call_target="tpu_custom_call", output_to_operand_aliasing={{}: (0, {})} | custom-call | tf_op jit(solution)/shard_map/pallas_call | solution.py:52
  (34 shorter events, 0.8 us)
Async XLA Ops:
  0.6 27.3 %collective-permute-start = (bf16[1024,512]{1,0:T(8,128)(2,1)}, bf16[1024,512]{1,0:T(8,128)(2,1)S(1)}, u32[]{:S(2)}, u32[]{:S(2)}) collective-permute-start(bf16[1024,512]{1,0:T(8,128)(2,1)} %refs_0_.1), channel_id=1, source_target_pairs={{0,1},{1,0},{2,3},{3,2},{4,5},{5,4},{6,7},{7,6},{8,9},{9,8},{10,11... | collective-permute-start | bytes 3145736 | tf_op jit(solution)/shard_map/ppermute | solution.py:20
  4.9 18.8 %collective-permute-start.2 = (bf16[576,512]{1,0:T(8,128)(2,1)S(1)}, bf16[576,512]{1,0:T(8,128)(2,1)S(1)}, u32[]{:S(2)}, u32[]{:S(2)}) collective-permute-start(bf16[576,512]{1,0:T(8,128)(2,1)S(1)} %get-tuple-element.40.refs_4_.refs_2_), channel_id=1, source_target_pairs={{0,2},{1,3},{2,0},{3,1},{4,6},{5,7},{6,4},{7,5},{8,10},{9,11},{10,... | collective-permute-start | bytes 1769480 | tf_op jit(solution)/shard_map/ppermute | solution.py:20
  6.5 25.6 %collective-permute-start.4 = (bf16[448,512]{1,0:T(8,128)(2,1)S(1)}, bf16[448,512]{1,0:T(8,128)(2,1)S(1)}, u32[]{:S(2)}, u32[]{:S(2)}) collective-permute-start(bf16[448,512]{1,0:T(8,128)(2,1)S(1)} %get-tuple-element.44.refs_3_.refs_1_), channel_id=1, source_target_pairs={{0,2},{1,3},{2,0},{3,1},{4,6},{5,7},{6,4},{7,5},{8,10},{9,11},{10,... | collective-permute-start | bytes 1376264 | tf_op jit(solution)/shard_map/ppermute | solution.py:20
  23.8 11.8 %collective-permute-start.9 = (bf16[576,256]{1,0:T(8,128)(2,1)S(1)}, bf16[576,256]{1,0:T(8,128)(2,1)S(1)}, u32[]{:S(2)}, u32[]{:S(2)}) collective-permute-start(bf16[576,256]{1,0:T(8,128)(2,1)S(1)} %get-tuple-element.52), channel_id=1, source_target_pairs={{0,1},{1,0},{2,3},{3,2},{4,5},{5,4},{6,7},{7,6},{8,9},{9,8},{10,11... | collective-permute-start | bytes 884744 | tf_op jit(solution)/shard_map/ppermute | solution.py:20
  27.9 8.6 %collective-permute-start.8 = (bf16[448,256]{1,0:T(8,128)(2,1)S(1)}, bf16[448,256]{1,0:T(8,128)(2,1)S(1)}, u32[]{:S(2)}, u32[]{:S(2)}) collective-permute-start(bf16[448,256]{1,0:T(8,128)(2,1)S(1)} %get-tuple-element.51), channel_id=1, source_target_pairs={{0,2},{1,3},{2,0},{3,1},{4,6},{5,7},{6,4},{7,5},{8,10},{9,11},{10,... | collective-permute-start | bytes 688136 | tf_op jit(solution)/shard_map/ppermute | solution.py:20
  30.0 12.6 %collective-permute-start.3 = (bf16[576,256]{1,0:T(8,128)(2,1)S(1)}, bf16[576,256]{1,0:T(8,128)(2,1)S(1)}, u32[]{:S(2)}, u32[]{:S(2)}) collective-permute-start(bf16[576,256]{1,0:T(8,128)(2,1)S(1)} %get-tuple-element.41), channel_id=1, source_target_pairs={{0,1},{1,0},{2,3},{3,2},{4,5},{5,4},{6,7},{7,6},{8,9},{9,8},{10,11... | collective-permute-start | bytes 884744 | tf_op jit(solution)/shard_map/ppermute | solution.py:20
  31.5 13.2 %collective-permute-start.1 = (bf16[448,256]{1,0:T(8,128)(2,1)S(1)}, bf16[448,256]{1,0:T(8,128)(2,1)S(1)}, u32[]{:S(2)}, u32[]{:S(2)}) collective-permute-start(bf16[448,256]{1,0:T(8,128)(2,1)S(1)} %get-tuple-element.39), channel_id=1, source_target_pairs={{0,2},{1,3},{2,0},{3,1},{4,6},{5,7},{6,4},{7,5},{8,10},{9,11},{10,... | collective-permute-start | bytes 688136 | tf_op jit(solution)/shard_map/ppermute | solution.py:20
  32.0 4.5 %copy-start.2 = (bf16[1024]{0:T(1024)(128)(2,1)S(1)}, bf16[1024]{0:T(1024)(128)(2,1)}, u32[]{:S(2)}) copy-start(bf16[1024]{0:T(1024)(128)(2,1)} %param.11) | copy-start | bytes 6148
  35.5 5.3 %copy-start = (bf16[1024,32]{0,1:T(8,128)(2,1)S(1)}, bf16[1024,32]{0,1:T(8,128)(2,1)}, u32[]{:S(2)}) copy-start(bf16[1024,32]{0,1:T(8,128)(2,1)} %param.12) | copy-start | bytes 196612
  35.5 5.3 %copy-start.3 = (bf16[4,416]{1,0:T(4,128)(2,1)S(1)}, bf16[4,416]{1,0:T(4,128)(2,1)}, u32[]{:S(2)}) copy-start(bf16[4,416]{1,0:T(4,128)(2,1)} %refs_4_.1) | copy-start | bytes 9988
  38.8 15.4 %collective-permute-start.22 = (bf16[512,256]{1,0:T(8,128)(2,1)S(1)}, bf16[512,256]{1,0:T(8,128)(2,1)S(1)}, u32[]{:S(2)}, u32[]{:S(2)}) collective-permute-start(bf16[512,256]{1,0:T(8,128)(2,1)S(1)} %get-tuple-element.65), channel_id=1, source_target_pairs={{0,2},{1,3},{2,0},{3,1},{4,6},{5,7},{6,4},{7,5},{8,10},{9,11},{10,... | collective-permute-start | bytes 786440 | tf_op jit(solution)/shard_map/ppermute | solution.py:20
  41.2 8.0 %copy-start.1 = (bf16[3,128,16]{1,2,0:T(8,128)(2,1)S(1)}, bf16[3,128,16]{1,2,0:T(8,128)(2,1)}, u32[]{:S(2)}) copy-start(bf16[3,128,16]{1,2,0:T(8,128)(2,1)} %param.13) | copy-start | bytes 36868
  41.2 8.0 %copy-start.4 = (bf16[3,16]{1,0:T(4,128)(2,1)S(1)}, bf16[3,16]{1,0:T(4,128)(2,1)}, u32[]{:S(2)}) copy-start(bf16[3,16]{1,0:T(4,128)(2,1)} %refs_6_.1) | copy-start | bytes 292
  41.2 5.9 %collective-permute-start.5 = (bf16[48,128]{1,0:T(8,128)(2,1)S(1)}, bf16[48,128]{1,0:T(8,128)(2,1)S(1)}, u32[]{:S(2)}, u32[]{:S(2)}) collective-permute-start(bf16[48,128]{1,0:T(8,128)(2,1)S(1)} %get-tuple-element.48), channel_id=1, source_target_pairs={{0,1},{1,0},{2,3},{3,2},{4,5},{5,4},{6,7},{7,6},{8,9},{9,8},{10,11... | collective-permute-start | bytes 36872 | tf_op jit(solution)/shard_map/ppermute | solution.py:20
  42.1 6.3 %collective-permute-start.6 = (bf16[48,128]{1,0:T(8,128)(2,1)S(1)}, bf16[48,128]{1,0:T(8,128)(2,1)S(1)}, u32[]{:S(2)}, u32[]{:S(2)}) collective-permute-start(bf16[48,128]{1,0:T(8,128)(2,1)S(1)} %get-tuple-element.49), channel_id=1, source_target_pairs={{0,2},{1,3},{2,0},{3,1},{4,6},{5,7},{6,4},{7,5},{8,10},{9,11},{10,... | collective-permute-start | bytes 36872 | tf_op jit(solution)/shard_map/ppermute | solution.py:20
  42.6 6.6 %collective-permute-start.7 = (bf16[48,128]{1,0:T(8,128)(2,1)S(1)}, bf16[48,128]{1,0:T(8,128)(2,1)S(1)}, u32[]{:S(2)}, u32[]{:S(2)}) collective-permute-start(bf16[48,128]{1,0:T(8,128)(2,1)S(1)} %get-tuple-element.50), channel_id=1, source_target_pairs={{0,3},{1,2},{2,1},{3,0},{4,7},{5,6},{6,5},{7,4},{8,11},{9,10},{10,... | collective-permute-start | bytes 36872 | tf_op jit(solution)/shard_map/ppermute | solution.py:20
  47.0 8.7 %collective-permute-start.23 = (bf16[512,256]{1,0:T(8,128)(2,1)S(1)}, bf16[512,256]{1,0:T(8,128)(2,1)S(1)}, u32[]{:S(2)}, u32[]{:S(2)}) collective-permute-start(bf16[512,256]{1,0:T(8,128)(2,1)S(1)} %get-tuple-element.66), channel_id=1, source_target_pairs={{0,2},{1,3},{2,0},{3,1},{4,6},{5,7},{6,4},{7,5},{8,10},{9,11},{10,... | collective-permute-start | bytes 786440 | tf_op jit(solution)/shard_map/ppermute | solution.py:20
  47.1 9.9 %collective-permute-start.19 = (bf16[512,256]{1,0:T(8,128)(2,1)S(1)}, bf16[512,256]{1,0:T(8,128)(2,1)S(1)}, u32[]{:S(2)}, u32[]{:S(2)}) collective-permute-start(bf16[512,256]{1,0:T(8,128)(2,1)S(1)} %get-tuple-element.61), channel_id=1, source_target_pairs={{0,1},{1,0},{2,3},{3,2},{4,5},{5,4},{6,7},{7,6},{8,9},{9,8},{10,11... | collective-permute-start | bytes 786440 | tf_op jit(solution)/shard_map/ppermute | solution.py:20
  48.5 13.5 %collective-permute-start.20 = (bf16[512,256]{1,0:T(8,128)(2,1)S(1)}, bf16[512,256]{1,0:T(8,128)(2,1)S(1)}, u32[]{:S(2)}, u32[]{:S(2)}) collective-permute-start(bf16[512,256]{1,0:T(8,128)(2,1)S(1)} %get-tuple-element.62), channel_id=1, source_target_pairs={{0,1},{1,0},{2,3},{3,2},{4,5},{5,4},{6,7},{7,6},{8,9},{9,8},{10,11... | collective-permute-start | bytes 786440 | tf_op jit(solution)/shard_map/ppermute | solution.py:20
  52.8 42.8 %collective-permute-start.17 = (bf16[512,512]{1,0:T(8,128)(2,1)S(1)}, bf16[512,512]{1,0:T(8,128)(2,1)S(1)}, u32[]{:S(2)}, u32[]{:S(2)}) collective-permute-start(bf16[512,512]{1,0:T(8,128)(2,1)S(1)} %get-tuple-element.57), channel_id=1, source_target_pairs={{0,1},{1,0},{2,3},{3,2},{4,5},{5,4},{6,7},{7,6},{8,9},{9,8},{10,11... | collective-permute-start | bytes 1572872 | tf_op jit(solution)/shard_map/ppermute | solution.py:20
  54.2 41.9 %collective-permute-start.18 = (bf16[512,512]{1,0:T(8,128)(2,1)S(1)}, bf16[512,512]{1,0:T(8,128)(2,1)S(1)}, u32[]{:S(2)}, u32[]{:S(2)}) collective-permute-start(bf16[512,512]{1,0:T(8,128)(2,1)S(1)} %get-tuple-element.58), channel_id=1, source_target_pairs={{0,2},{1,3},{2,0},{3,1},{4,6},{5,7},{6,4},{7,5},{8,10},{9,11},{10,... | collective-permute-start | bytes 1572872 | tf_op jit(solution)/shard_map/ppermute | solution.py:20
  55.8 40.8 %collective-permute-start.24 = (bf16[512,384]{1,0:T(8,128)(2,1)S(1)}, bf16[512,384]{1,0:T(8,128)(2,1)S(1)}, u32[]{:S(2)}, u32[]{:S(2)}) collective-permute-start(bf16[512,384]{1,0:T(8,128)(2,1)S(1)} %get-tuple-element.67), channel_id=1, source_target_pairs={{0,1},{1,0},{2,3},{3,2},{4,5},{5,4},{6,7},{7,6},{8,9},{9,8},{10,11... | collective-permute-start | bytes 1179656 | tf_op jit(solution)/shard_map/ppermute | solution.py:20
  62.1 34.5 %collective-permute-start.21 = (bf16[512,384]{1,0:T(8,128)(2,1)S(1)}, bf16[512,384]{1,0:T(8,128)(2,1)S(1)}, u32[]{:S(2)}, u32[]{:S(2)}) collective-permute-start(bf16[512,384]{1,0:T(8,128)(2,1)S(1)} %get-tuple-element.63), channel_id=1, source_target_pairs={{0,2},{1,3},{2,0},{3,1},{4,6},{5,7},{6,4},{7,5},{8,10},{9,11},{10,... | collective-permute-start | bytes 1179656 | tf_op jit(solution)/shard_map/ppermute | solution.py:20
  64.1 1.2 %collective-permute-start.10 = (bf16[144,128]{1,0:T(8,128)(2,1)S(1)}, bf16[144,128]{1,0:T(8,128)(2,1)S(1)}, u32[]{:S(2)}, u32[]{:S(2)}) collective-permute-start(bf16[144,128]{1,0:T(8,128)(2,1)S(1)} %shard_map.102.refs_0_.refs_1_), channel_id=1, source_target_pairs={{0,4},{4,0},{8,12},{12,8},{16,20},{20,16},{24,28},{28,24},{1,5},{5... | collective-permute-start | bytes 110600 | tf_op jit(solution)/shard_map/ppermute | solution.py:20
  65.3 4.2 %collective-permute-start.11 = (bf16[224,128]{1,0:T(8,128)(2,1)S(1)}, bf16[224,128]{1,0:T(8,128)(2,1)S(1)}, u32[]{:S(2)}, u32[]{:S(2)}) collective-permute-start(bf16[224,128]{1,0:T(8,128)(2,1)S(1)} %shard_map.105.refs_0_), channel_id=1, source_target_pairs={{0,8},{4,12},{8,0},{12,4},{16,24},{20,28},{24,16},{28,20},{1,9},{5... | collective-permute-start | bytes 172040 | tf_op jit(solution)/shard_map/ppermute | solution.py:20
  69.6 5.1 %collective-permute-start.12 = (bf16[224,128]{1,0:T(8,128)(2,1)S(1)}, bf16[224,128]{1,0:T(8,128)(2,1)S(1)}, u32[]{:S(2)}, u32[]{:S(2)}) collective-permute-start(bf16[224,128]{1,0:T(8,128)(2,1)S(1)} %shard_map.105.refs_0_), channel_id=1, source_target_pairs={{0,16},{4,20},{8,24},{12,28},{16,0},{20,4},{24,8},{28,12},{1,17},{... | collective-permute-start | bytes 172040 | tf_op jit(solution)/shard_map/ppermute | solution.py:20
  74.7 6.3 %collective-permute-start.13 = (bf16[224,128]{1,0:T(8,128)(2,1)S(1)}, bf16[224,128]{1,0:T(8,128)(2,1)S(1)}, u32[]{:S(2)}, u32[]{:S(2)}) collective-permute-start(bf16[224,128]{1,0:T(8,128)(2,1)S(1)} %shard_map.105.refs_0_), channel_id=1, source_target_pairs={{0,24},{4,28},{8,16},{12,20},{16,8},{20,12},{24,0},{28,4},{1,25},{... | collective-permute-start | bytes 172040 | tf_op jit(solution)/shard_map/ppermute | solution.py:20
  82.9 3.7 %collective-permute-start.14 = (bf16[32,128]{1,0:T(8,128)(2,1)S(1)}, bf16[32,128]{1,0:T(8,128)(2,1)S(1)}, u32[]{:S(2)}, u32[]{:S(2)}) collective-permute-start(bf16[32,128]{1,0:T(8,128)(2,1)S(1)} %get-tuple-element.56.refs_2_), channel_id=1, source_target_pairs={{0,1},{1,0},{2,3},{3,2},{4,5},{5,4},{6,7},{7,6},{8,9},{9,8},{10,11... | collective-permute-start | bytes 24584 | tf_op jit(solution)/shard_map/ppermute | solution.py:20
  86.5 3.7 %collective-permute-start.15 = (bf16[32,128]{1,0:T(8,128)(2,1)S(1)}, bf16[32,128]{1,0:T(8,128)(2,1)S(1)}, u32[]{:S(2)}, u32[]{:S(2)}) collective-permute-start(bf16[32,128]{1,0:T(8,128)(2,1)S(1)} %get-tuple-element.56.refs_2_), channel_id=1, source_target_pairs={{0,2},{1,3},{2,0},{3,1},{4,6},{5,7},{6,4},{7,5},{8,10},{9,11},{10,... | collective-permute-start | bytes 24584 | tf_op jit(solution)/shard_map/ppermute | solution.py:20
  90.2 4.5 %collective-permute-start.16 = (bf16[32,128]{1,0:T(8,128)(2,1)S(1)}, bf16[32,128]{1,0:T(8,128)(2,1)S(1)}, u32[]{:S(2)}, u32[]{:S(2)}) collective-permute-start(bf16[32,128]{1,0:T(8,128)(2,1)S(1)} %get-tuple-element.56.refs_2_), channel_id=1, source_target_pairs={{0,3},{1,2},{2,1},{3,0},{4,7},{5,6},{6,5},{7,4},{8,11},{9,10},{10,... | collective-permute-start | bytes 24584 | tf_op jit(solution)/shard_map/ppermute | solution.py:20
  94.7 5.0 %collective-permute-start.26 = (bf16[512,128]{1,0:T(8,128)(2,1)S(1)}, bf16[512,128]{1,0:T(8,128)(2,1)S(1)}, u32[]{:S(2)}, u32[]{:S(2)}) collective-permute-start(bf16[512,128]{1,0:T(8,128)(2,1)S(1)} %get-tuple-element.70), channel_id=1, source_target_pairs={{0,1},{1,0},{2,3},{3,2},{4,5},{5,4},{6,7},{7,6},{8,9},{9,8},{10,11... | collective-permute-start | bytes 393224 | tf_op jit(solution)/shard_map/ppermute | solution.py:20
  95.6 5.0 %collective-permute-start.25 = (bf16[512,128]{1,0:T(8,128)(2,1)S(1)}, bf16[512,128]{1,0:T(8,128)(2,1)S(1)}, u32[]{:S(2)}, u32[]{:S(2)}) collective-permute-start(bf16[512,128]{1,0:T(8,128)(2,1)S(1)} %get-tuple-element.69), channel_id=1, source_target_pairs={{0,2},{1,3},{2,0},{3,1},{4,6},{5,7},{6,4},{7,5},{8,10},{9,11},{10,... | collective-permute-start | bytes 393224 | tf_op jit(solution)/shard_map/ppermute | solution.py:20

commit v6 on v5

--- a/solution.py
+++ b/solution.py
@@ -196,42 +196,52 @@
     return (leaf_x, jnp.stack(solution, axis=0))
 
 
-def pack_body(low_ref, high_ref, link_ref, fac_ref, *refs):
-    outs, crossing_ref = refs[:-1], refs[-1]
+def send_body(whole_ref, low_ref, high_ref, link_ref, fac_ref, out_0_ref, out_1_ref, kept_ref, crossing_ref):
+    height, width = out_1_ref.shape
+    out_0_ref[:height, :] = whole_ref[:, :width]
+    out_1_ref[...] = whole_ref[:, width:]
     first = link_ref.shape[0]
     rows, cols = fac_ref.shape
     split = low_ref.shape[0]
     crossing = dot_nn(link_ref[:, :split], low_ref[...]) + dot_nn(link_ref[:, split:], high_ref[...])
     crossing_ref[...] = crossing
-    tiles = (outs[0].shape[0] - first) // rows
+    tiles = (kept_ref.shape[0] - first) // rows
     factor = fac_ref[...].astype(F32)
     factor = jnp.concatenate([factor, jnp.zeros((rows, tiles * LANES - cols), F32)], axis=1)
     folded = [factor[:, tile * LANES : (tile + 1) * LANES] for tile in range(tiles)]
-    folded = jnp.concatenate(folded, axis=0).astype(BF16)
+    folded = jnp.concatenate(folded, axis=0)
     me = lax.axis_index("grp")
-    for mask, ref in enumerate(outs):
-        lanes = pl.ds(pl.multiple_of((me ^ mask) * LANES, LANES), LANES)
-        ref[:first, :] = crossing_ref[:, lanes].astype(BF16)
-        ref[first:, :] = folded
-
-
-def leaf_body(own_ref, x_ref, y_ref, d_ref, sep_ref, dinv_ref, out_ref, *, rows, cols):
+    kept_ref[first:, :] = jnp.concatenate([folded, folded], axis=1)
+    out_0_ref[height + first :, :] = jnp.concatenate([folded, folded], axis=1).astype(BF16)
+    for index, (mine, sent) in enumerate(((0, 1), (2, 3))):
+        place = slice(index * LANES, (index + 1) * LANES)
+        lanes = pl.ds(pl.multiple_of((me ^ mine) * LANES, LANES), LANES)
+        kept_ref[:first, place] = crossing_ref[:, lanes]
+        lanes = pl.ds(pl.multiple_of((me ^ sent) * LANES, LANES), LANES)
+        out_0_ref[height : height + first, place] = crossing_ref[:, lanes].astype(BF16)
+
+
+def leaf_body(kept_ref, x_ref, y_ref, sep_ref, dinv_ref, out_ref, *, rows, cols):
     levels, sep_block, _ = sep_ref.shape
-    parts = (own_ref, x_ref, y_ref, d_ref)
-    first = own_ref.shape[0] - sep_block
+    first = kept_ref.shape[0] - sep_block
     tiles = sep_block // rows
     me = lax.axis_index("grp")
-    total = own_ref[:first, :].astype(F32)
-    for part in parts[1:]:
-        total = total + part[:first, :].astype(F32)
+    x_part = x_ref[x_ref.shape[0] - first - sep_block :, :].astype(F32)
+    y_part = y_ref[y_ref.shape[0] - first :, :].astype(F32)
+    total = kept_ref[:first, :LANES] + x_part[:first, :LANES] + y_part[:, :LANES]
     out_ref[:first, :] = total.astype(BF16)
     for level in range(levels):
         out_ref[first + level * sep_block : first + (level + 1) * sep_block, :] = sep_ref[level]
     row_owner = lax.broadcasted_iota(jnp.int32, (sep_block, tiles * LANES), 0) // rows
     lane = lax.broadcasted_iota(jnp.int32, (sep_block, tiles * LANES), 1)
     factor = jnp.zeros((sep_block, tiles * LANES), F32)
-    for index, part in enumerate(parts):
-        folded = part[first:, :].astype(F32)
+    folds = (
+        kept_ref[first:, :LANES],
+        x_part[first:, :LANES],
+        y_part[:sep_block, LANES:],
+        y_part[sep_block : 2 * sep_block, LANES:],
+    )
+    for index, folded in enumerate(folds):
         block = [folded[tile * rows : (tile + 1) * rows, :] for tile in range(tiles)]
         block = jnp.concatenate(block, axis=1)
         tiled = jnp.concatenate([block] * (sep_block // rows), axis=0)
@@ -400,12 +410,13 @@
     out_1_ref[...] = dot_tn(factor_ref[...], loads_ref[:, width:])
 
 
-def far_body(
-    far_ref, low_ref, high_ref, near_ref, dinv_ref, z_ref, relay_low_ref, relay_high_ref, loads_ref, part_ref
-):
+def far_body(far_ref, low_ref, high_ref, near_ref, dinv_ref, *refs, first):
+    kept = refs[:-5]
+    z_ref, relay_low_ref, relay_high_ref, loads_ref, part_ref = refs[-5:]
     split, half = low_ref.shape[0], relay_low_ref.shape[0]
+    rest = loads_ref.shape[0] - split
     loads_ref[:split, :] = low_ref[...]
-    loads_ref[split:, :] = high_ref[...]
+    loads_ref[split:, :] = high_ref[:rest, :]
     part_ref[...] = near_ref[...] + dot_tn(far_ref[...], loads_ref[...])
     pivots = dinv_ref[...].astype(F32)
     width = part_ref.shape[1]
@@ -415,7 +426,12 @@
         scale = jnp.concatenate([scale] * (width // LANES), axis=1)
         z_ref[rows, :] = (scale * part_ref[rows, :]).astype(BF16)
     relay_low_ref[...] = dot_nn(far_ref[:half, :], z_ref[...]).astype(BF16)
-    relay_high_ref[...] = dot_nn(far_ref[half:, :], z_ref[...]).astype(BF16)
+    relay_high_ref[:half, :] = dot_nn(far_ref[half:, :], z_ref[...]).astype(BF16)
+    for kept_ref in kept:
+        crossing = kept_ref[:first, LANES:] + high_ref[rest : rest + first, LANES:].astype(F32)
+        relay_high_ref[half:, :LANES] = crossing.astype(BF16)
+        folds = [kept_ref[first:, LANES:], high_ref[rest + first :, :LANES].astype(F32)]
+        relay_high_ref[half:, LANES:] = jnp.concatenate(folds, axis=0).astype(BF16)
 
 
 def near_body(own_ref, x_ref, y_ref, z_0_ref, z_1_ref, x_low_ref, y_high_ref, x_high_ref, y_low_ref, out_ref, z_ref):
@@ -430,7 +446,8 @@
 
 
 def add_body(near_ref, relay_0_ref, relay_1_ref, out_0_ref, out_1_ref):
-    relay = jnp.concatenate([relay_0_ref[...], relay_1_ref[...]], axis=1).astype(F32)
+    half = near_ref.shape[0]
+    relay = jnp.concatenate([relay_0_ref[:half, :], relay_1_ref[:half, :]], axis=1).astype(F32)
     total = (near_ref[...] + relay).astype(BF16)
     split = out_0_ref.shape[1]
     out_0_ref[...] = total[:, :split]
@@ -470,7 +487,7 @@
 
 def local_pairs(leaf_rhs, leaf_inv, ordering, leaf_dinv, leaf_link, sep_rhs, sep_factor, sep_dinv):
     rows, width = leaf_rhs.shape
-    half, split, quarter = rows // 2, rows // 16 * 7, width // 4
+    half, split = rows // 2, rows // 16 * 7
     group = lax.axis_size("grp")
     levels, slice_width, sep_block = sep_rhs.shape
     first = leaf_link.shape[1]
@@ -499,19 +516,21 @@
     dest = (ordering[0] // rows ^ me) * rows + ordering[0] % rows
     blocks = arrange(leaf_inv, dest, group)
 
-    aux = call(
-        pack_body,
-        (low, high, link_turned, sep_factor),
-        [vmem()] * 4,
-        [bf16(first + sep_block, LANES)] * group,
+    *high_cut, kept = call(
+        send_body,
+        (y_high, low, high, link_turned, sep_factor),
+        [vmem()] * 5,
+        [
+            bf16(rows - split + first + sep_block, width // 2),
+            bf16(rows - split, width // 2),
+            f32(first + sep_block, 2 * LANES),
+        ],
         after=(blocks[0],),
         scratch_shapes=[pltpu.VMEM((first, width), F32)],
     )
-    high_cut = call(cut_body, (y_high,), [vmem()], [bf16(rows - split, width // 2)] * 2, after=(blocks[0],))
     d_high = [exchange(high_cut[part], "grp", 1) for part in parts]
     low_cut = call(cut_body, (x_all,), [vmem()], [bf16(split, width // 2)] * 2, after=(blocks[0],))
     d_low = [exchange(low_cut[part], "grp", 2) for part in parts]
-    aux_parts = [aux[0]] + [exchange(aux[mask], "grp", mask) for mask in range(1, group)]
 
     part_y = call(
         forward_body,
@@ -522,33 +541,37 @@
     )
     leaf_z, relay_low, relay_high = [], [], []
     for part in parts:
+        shared = (kept,) if part == 0 else ()
         z_part, far_low, far_high = call(
-            far_body,
-            (blocks[3], d_low[part], d_high[part], part_y[part], leaf_dinv.reshape(-1, LANES)),
-            [vmem()] * 5,
-            (bf16(rows, width // 2), bf16(half, width // 2), bf16(half, width // 2)),
+            functools.partial(far_body, first=first),
+            (blocks[3], d_low[part], d_high[part], part_y[part], leaf_dinv.reshape(-1, LANES), *shared),
+            [vmem()] * (5 + len(shared)),
+            (
+                bf16(rows, width // 2),
+                bf16(half, width // 2),
+                bf16(half + first * len(shared), width // 2),
+            ),
             scratch_shapes=[pltpu.VMEM((rows, width // 2), BF16), pltpu.VMEM((rows, width // 2), F32)],
         )
         leaf_z.append(z_part)
         relay_low.append(exchange(far_low, "grp", 1))
         relay_high.append(exchange(far_high, "grp", 2))
 
-    leaf_block = call(
-        functools.partial(leaf_body, rows=fac_rows, cols=cols),
-        (*aux_parts, jnp.swapaxes(sep_rhs, 1, 2), sep_dinv),
-        [vmem()] * 6,
-        bf16(first + (levels + tiles) * sep_block, LANES),
-        after=(leaf_z[1],),
-    )
-    partner = exchange(leaf_block, "leaf", 1)
     near_x_low, near_y_high, near_x_high, near_y_low, own = call(
         near_body,
         (*blocks[:3], *leaf_z),
         [vmem()] * 5,
         [bf16(half, width)] * 2 + [f32(half, width)] * 2 + [f32(rows, width)],
-        after=(leaf_block,),
         scratch_shapes=[pltpu.VMEM((rows, width), BF16)],
     )
+    leaf_block = call(
+        functools.partial(leaf_body, rows=fac_rows, cols=cols),
+        (kept, d_high[0], relay_high[0], jnp.swapaxes(sep_rhs, 1, 2), sep_dinv),
+        [vmem()] * 5,
+        bf16(first + (levels + tiles) * sep_block, LANES),
+        after=(own,),
+    )
+    partner = exchange(leaf_block, "leaf", 1)
     sum_x_low = exchange(near_x_low, "grp", 1)
     sum_y_high = exchange(near_y_high, "grp", 2)
     pair_block = call(
@@ -556,7 +579,6 @@
         (leaf_block, partner),
         [vmem(), vmem()],
         bf16((levels + tiles) * first, LANES),
-        after=(own,),
     )
     count = lax.axis_size("leaf") // 2
     pairs = [pair_block] + [exchange(pair_block, "leaf", 2 * mask) for mask in range(1, count)]
@@ -575,7 +597,7 @@
         ],
     )
     first_all = [first_here] + [exchange(first_here, "grp", mask) for mask in range(1, group)]
-    breadths = (width - quarter, quarter)
+    breadths = (width // 2, width // 2)
     into = [bf16(half, breadth) for breadth in breadths]
     x_sums = call(add_body, (near_x_high, *relay_high), [vmem()] * 3, into)
     y_sums = call(add_body, (near_y_low, *relay_low), [vmem()] * 3, into)

time: 102 us -> 87 us (0.85)
  waiting for transfers between devices: 30.1 us -> 19.7 us
  starting transfers between devices: 35.2 us -> 30.6 us
    ppermute x27 -> x24, waiting for transfers between devices: 30.1 us -> 19.7 us  [exchange(): lax.ppermute(block, axis, [(low, low ^ mask) for low in range(count)])]
    ppermute x27 -> x24, starting transfers between devices: 35.2 us -> 30.6 us  [exchange(): lax.ppermute(block, axis, [(low, low ^ mask) for low in range(count)])]
    pallas_call x17 -> x16, Pallas kernels: 35 us -> 34.9 us  [call(): pl.pallas_call(skipping, out_shape=out_shape, in_specs=[pl.BlockSpec(memo...]
  transfers between devices with their start and end apart: 27 -> 24, of which waited for: 12 -> 13; matrix products, arithmetic and copies ran while one was open for 1% -> 1% of each run, Pallas kernels for 33% -> 38%
where the time goes in v6:
time: 87 us; the launch traced here: 86.8 us
  Pallas kernels  34.9 us (40%)
  starting transfers between devices  30.6 us (35%)
  waiting for transfers between devices  19.7 us (23%)
    pallas_call x16, Pallas kernels, call(): pl.pallas_call(skipping, out_shape=out_shape, in_specs=[pl.BlockSpec(memo...  34.9 us
    ppermute x24, starting transfers between devices, exchange(): lax.ppermute(block, axis, [(low, low ^ mask) for low in range(count)])  30.6 us
    ppermute x24, waiting for transfers between devices, exchange(): lax.ppermute(block, axis, [(low, low ^ mask) for low in range(count)])  19.7 us
  transfers between devices with their start and end apart: 24, of which 13 were waited for; matrix products, arithmetic and copies ran while one was open for 1% of the time, Pallas kernels for 38%

profile of v6, /device:TPU:0, one launch (start us, length us, event | category | flops | bytes accessed | tf_op | source)
XLA Modules:
  0.0 86.8 jit_solution(11124355327434519162)
XLA Ops:
  0.6 3.0 %collective-permute-start = (bf16[1024,512]{1,0:T(8,128)(2,1)}, bf16[1024,512]{1,0:T(8,128)(2,1)S(1)}, u32[]{:S(2)}, u32[]{:S(2)}) collective-permute-start(bf16[1024,512]{1,0:T(8,128)(2,1)} %refs_0_.1), channel_id=1, source_target_pairs={{0,1},{1,0},{2,3},{3,2},{4,5},{5,4},{6,7},{7,6},{8,9},{9,8},{10,11... | collective-permute-start | bytes 3145736 | tf_op jit(solution)/shard_map/ppermute | solution.py:20
  3.7 1.2 %shard_map.97 = (bf16[448,512]{1,0:T(8,128)(2,1)S(1)}, bf16[576,512]{1,0:T(8,128)(2,1)S(1)}) custom-call(bf16[1024,512]{1,0:T(8,128)(2,1)} %refs_0_.1), custom_call_target="tpu_custom_call" | custom-call | tf_op jit(solution)/shard_map/pallas_call | solution.py:52
  4.9 1.6 %collective-permute-start.2 = (bf16[576,512]{1,0:T(8,128)(2,1)S(1)}, bf16[576,512]{1,0:T(8,128)(2,1)S(1)}, u32[]{:S(2)}, u32[]{:S(2)}) collective-permute-start(bf16[576,512]{1,0:T(8,128)(2,1)S(1)} %get-tuple-element.39.refs_3_.refs_4_), channel_id=1, source_target_pairs={{0,2},{1,3},{2,0},{3,1},{4,6},{5,7},{6,4},{7,5},{8,10},{9,11},{10,... | collective-permute-start | bytes 1769480 | tf_op jit(solution)/shard_map/ppermute | solution.py:20
  6.5 0.5 collective-permute-start.4
  7.0 0.7 fusion.2.refs_0_
  7.7 16.0 %shard_map.95 = (bf16[1024,1024]{1,0:T(8,128)(2,1)S(1)}, bf16[1024,1024]{1,0:T(8,128)(2,1)S(1)}, bf16[1024,1024]{1,0:T(8,128)(2,1)S(1)}, bf16[1024,1024]{1,0:T(8,128)(2,1)S(1)}) custom-call(s32[4096]{0:T(1024)S(1)} %fusion.2.refs_0_, bf16[1024,4096]{1,0:T(8,128)(2,1)} %refs_1_.1), custom_call_target="tpu_custom_call" | custom-call | tf_op jit(solution)/shard_map/pallas_call | solution.py:52
  23.8 0.3 shard_map.98
  24.1 0.2 collective-permute-start.3
  24.3 3.6 %collective-permute-done.refs_1_.refs_5_ = bf16[1024,512]{1,0:T(8,128)(2,1)S(1)} collective-permute-done((bf16[1024,512]{1,0:T(8,128)(2,1)}, bf16[1024,512]{1,0:T(8,128)(2,1)S(1)}, u32[]{:S(2)}, u32[]{:S(2)}) %collective-permute-start) | collective-permute-done | bytes 1048608 | tf_op jit(solution)/shard_map/ppermute | solution.py:20
  27.9 2.1 %collective-permute-start.1 = (bf16[448,256]{1,0:T(8,128)(2,1)S(1)}, bf16[448,256]{1,0:T(8,128)(2,1)S(1)}, u32[]{:S(2)}, u32[]{:S(2)}) collective-permute-start(bf16[448,256]{1,0:T(8,128)(2,1)S(1)} %get-tuple-element.38), channel_id=1, source_target_pairs={{0,2},{1,3},{2,0},{3,1},{4,6},{5,7},{6,4},{7,5},{8,10},{9,11},{10,... | collective-permute-start | bytes 688136 | tf_op jit(solution)/shard_map/ppermute | solution.py:20
  30.0 1.5 %collective-permute-start.6 = (bf16[576,256]{1,0:T(8,128)(2,1)S(1)}, bf16[576,256]{1,0:T(8,128)(2,1)S(1)}, u32[]{:S(2)}, u32[]{:S(2)}) collective-permute-start(bf16[576,256]{1,0:T(8,128)(2,1)S(1)} %get-tuple-element.46), channel_id=1, source_target_pairs={{0,1},{1,0},{2,3},{3,2},{4,5},{5,4},{6,7},{7,6},{8,9},{9,8},{10,11... | collective-permute-start | bytes 884744 | tf_op jit(solution)/shard_map/ppermute | solution.py:20
  31.5 0.5 collective-permute-start.5
  32.0 3.5 %shard_map.99 = (f32[1024,256]{1,0:T(8,128)S(1)}, f32[1024,256]{1,0:T(8,128)S(1)}) custom-call(bf16[1024,1024]{1,0:T(8,128)(2,1)S(1)} %get-tuple-element.34.refs_0_, bf16[1024,1024]{1,0:T(8,128)(2,1)S(1)} %get-tuple-element.35.refs_1_, bf16[1024,1024]{1,0:T(8,128)(2,1)S(1)} %get-tuple-element.36.refs_2_, ...), custom_call_target="tpu_custom_call" | custom-call | tf_op jit(solution)/shard_map/pallas_call | solution.py:52
  35.5 1.0 %collective-permute-done.1.refs_1_ = bf16[448,256]{1,0:T(8,128)(2,1)S(1)} collective-permute-done((bf16[448,256]{1,0:T(8,128)(2,1)S(1)}, bf16[448,256]{1,0:T(8,128)(2,1)S(1)}, u32[]{:S(2)}, u32[]{:S(2)}) %collective-permute-start.1) | collective-permute-done | bytes 229408 | tf_op jit(solution)/shard_map/ppermute | solution.py:20
  36.5 2.3 %shard_map.100 = (bf16[1024,256]{1,0:T(8,128)(2,1)S(1)}, bf16[512,256]{1,0:T(8,128)(2,1)S(1)}, bf16[544,256]{1,0:T(8,128)(2,1)S(1)}) custom-call(bf16[1024,1024]{1,0:T(8,128)(2,1)S(1)} %get-tuple-element.37.refs_0_, bf16[448,256]{1,0:T(8,128)(2,1)S(1)} %collective-permute-done.1.refs_1_, bf16[624,256]{1,0:T(8,128)(2,1)S(1)} %collective-permute-done.3.refs_2_, ...), custom_call_target="tpu_custom_call" | custom-call | tf_op jit(solution)/shard_map/pallas_call | solution.py:52
  38.7 2.0 %collective-permute-start.7 = (bf16[544,256]{1,0:T(8,128)(2,1)S(1)}, bf16[544,256]{1,0:T(8,128)(2,1)S(1)}, u32[]{:S(2)}, u32[]{:S(2)}) collective-permute-start(bf16[544,256]{1,0:T(8,128)(2,1)S(1)} %get-tuple-element.50), channel_id=1, source_target_pairs={{0,2},{1,3},{2,0},{3,1},{4,6},{5,7},{6,4},{7,5},{8,10},{9,11},{10,... | collective-permute-start | bytes 835592 | tf_op jit(solution)/shard_map/ppermute | solution.py:20
  40.8 2.3 %shard_map.101 = (bf16[1024,256]{1,0:T(8,128)(2,1)S(1)}, bf16[512,256]{1,0:T(8,128)(2,1)S(1)}, bf16[512,256]{1,0:T(8,128)(2,1)S(1)}) custom-call(bf16[1024,1024]{1,0:T(8,128)(2,1)S(1)} %get-tuple-element.37.refs_0_, bf16[448,256]{1,0:T(8,128)(2,1)S(1)} %collective-permute-done.5.refs_1_, bf16[576,256]{1,0:T(8,128)(2,1)S(1)} %collective-permute-done.6.refs_2_, ...), custom_call_target="tpu_custom_call" | custom-call | tf_op jit(solution)/shard_map/pallas_call | solution.py:52
  43.1 3.4 %shard_map.102 = (bf16[512,512]{1,0:T(8,128)(2,1)S(1)}, bf16[512,512]{1,0:T(8,128)(2,1)S(1)}, f32[512,512]{1,0:T(8,128)S(1)}, f32[512,512]{1,0:T(8,128)S(1)}, f32[1024,512]{1,0:T(8,128)S(1)}) custom-call(bf16[1024,1024]{1,0:T(8,128)(2,1)S(1)} %get-tuple-element.34.refs_0_, bf16[1024,1024]{1,0:T(8,128)(2,1)S(1)} %get-tuple-element.35.refs_1_, ...), custom_call_target="tpu_custom_call" | custom-call | tf_op jit(solution)/shard_map/pallas_call | solution.py:52
  46.5 1.2 %collective-permute-start.15 = (bf16[512,512]{1,0:T(8,128)(2,1)S(1)}, bf16[512,512]{1,0:T(8,128)(2,1)S(1)}, u32[]{:S(2)}, u32[]{:S(2)}) collective-permute-start(bf16[512,512]{1,0:T(8,128)(2,1)S(1)} %get-tuple-element.52), channel_id=1, source_target_pairs={{0,1},{1,0},{2,3},{3,2},{4,5},{5,4},{6,7},{7,6},{8,9},{9,8},{10,11... | collective-permute-start | bytes 1572872 | tf_op jit(solution)/shard_map/ppermute | solution.py:20
  47.9 1.2 %collective-permute-done.8.refs_1_ = bf16[144,128]{1,0:T(8,128)(2,1)S(1)} collective-permute-done((bf16[144,128]{1,0:T(8,128)(2,1)S(1)}, bf16[144,128]{1,0:T(8,128)(2,1)S(1)}, u32[]{:S(2)}, u32[]{:S(2)}) %collective-permute-start.8) | collective-permute-done | bytes 36896 | tf_op jit(solution)/shard_map/ppermute | solution.py:20
  49.1 2.7 %collective-permute-start.10 = (bf16[224,128]{1,0:T(8,128)(2,1)S(1)}, bf16[224,128]{1,0:T(8,128)(2,1)S(1)}, u32[]{:S(2)}, u32[]{:S(2)}) collective-permute-start(bf16[224,128]{1,0:T(8,128)(2,1)S(1)} %shard_map.104.refs_0_), channel_id=1, source_target_pairs={{0,16},{4,20},{8,24},{12,28},{16,0},{20,4},{24,8},{28,12},{1,17},{... | collective-permute-start | bytes 172040 | tf_op jit(solution)/shard_map/ppermute | solution.py:20
  51.8 1.3 %collective-permute-start.11 = (bf16[224,128]{1,0:T(8,128)(2,1)S(1)}, bf16[224,128]{1,0:T(8,128)(2,1)S(1)}, u32[]{:S(2)}, u32[]{:S(2)}) collective-permute-start(bf16[224,128]{1,0:T(8,128)(2,1)S(1)} %shard_map.104.refs_0_), channel_id=1, source_target_pairs={{0,24},{4,28},{8,16},{12,20},{16,8},{20,12},{24,0},{28,4},{1,25},{... | collective-permute-start | bytes 172040 | tf_op jit(solution)/shard_map/ppermute | solution.py:20
  53.1 0.2 collective-permute-start.9
  53.4 1.5 %collective-permute-start.20 = (bf16[512,256]{1,0:T(8,128)(2,1)S(1)}, bf16[512,256]{1,0:T(8,128)(2,1)S(1)}, u32[]{:S(2)}, u32[]{:S(2)}) collective-permute-start(bf16[512,256]{1,0:T(8,128)(2,1)S(1)} %get-tuple-element.60), channel_id=1, source_target_pairs={{0,2},{1,3},{2,0},{3,1},{4,6},{5,7},{6,4},{7,5},{8,10},{9,11},{10,... | collective-permute-start | bytes 786440 | tf_op jit(solution)/shard_map/ppermute | solution.py:20
  54.9 0.8 collective-permute-done.10.refs_2_
  55.7 0.9 %collective-permute-start.17 = (bf16[512,256]{1,0:T(8,128)(2,1)S(1)}, bf16[512,256]{1,0:T(8,128)(2,1)S(1)}, u32[]{:S(2)}, u32[]{:S(2)}) collective-permute-start(bf16[512,256]{1,0:T(8,128)(2,1)S(1)} %get-tuple-element.56), channel_id=1, source_target_pairs={{0,1},{1,0},{2,3},{3,2},{4,5},{5,4},{6,7},{7,6},{8,9},{9,8},{10,11... | collective-permute-start | bytes 786440 | tf_op jit(solution)/shard_map/ppermute | solution.py:20
  56.6 1.3 %collective-permute-done.11.refs_3_ = bf16[224,128]{1,0:T(8,128)(2,1)S(1)} collective-permute-done((bf16[224,128]{1,0:T(8,128)(2,1)S(1)}, bf16[224,128]{1,0:T(8,128)(2,1)S(1)}, u32[]{:S(2)}, u32[]{:S(2)}) %collective-permute-start.11) | collective-permute-done | bytes 57376 | tf_op jit(solution)/shard_map/ppermute | solution.py:20
  57.9 0.9 %collective-permute-start.18 = (bf16[512,256]{1,0:T(8,128)(2,1)S(1)}, bf16[512,256]{1,0:T(8,128)(2,1)S(1)}, u32[]{:S(2)}, u32[]{:S(2)}) collective-permute-start(bf16[512,256]{1,0:T(8,128)(2,1)S(1)} %get-tuple-element.57), channel_id=1, source_target_pairs={{0,1},{1,0},{2,3},{3,2},{4,5},{5,4},{6,7},{7,6},{8,9},{9,8},{10,11... | collective-permute-start | bytes 786440 | tf_op jit(solution)/shard_map/ppermute | solution.py:20
  58.8 1.5 %collective-permute-start.16 = (bf16[512,512]{1,0:T(8,128)(2,1)S(1)}, bf16[512,512]{1,0:T(8,128)(2,1)S(1)}, u32[]{:S(2)}, u32[]{:S(2)}) collective-permute-start(bf16[512,512]{1,0:T(8,128)(2,1)S(1)} %get-tuple-element.53), channel_id=1, source_target_pairs={{0,2},{1,3},{2,0},{3,1},{4,6},{5,7},{6,4},{7,5},{8,10},{9,11},{10,... | collective-permute-start | bytes 1572872 | tf_op jit(solution)/shard_map/ppermute | solution.py:20
  60.3 1.9 %shard_map.105 = (bf16[32,128]{1,0:T(8,128)(2,1)S(1)}, f32[3,16,128]{2,1,0:T(8,128)}) custom-call(bf16[224,128]{1,0:T(8,128)(2,1)S(1)} %shard_map.104.refs_0_, bf16[224,128]{1,0:T(8,128)(2,1)S(1)} %collective-permute-done.9.refs_1_, bf16[224,128]{1,0:T(8,128)(2,1)S(1)} %collective-permute-done.10.refs_2_, bf16[224,128]{1,0:T(8,128)(2,1)S(1)} %collective-permute-done.11.refs_3_), custom_call_target="tpu_custom_call" | custom-call | tf_op jit(solution)/shard_map/pallas_call | solution.py:52
  62.2 0.3 collective-permute-done.20.refs_2_
  62.6 0.9 collective-permute-start.12
  63.4 3.6 %collective-permute-done.17.refs_1_ = bf16[512,256]{1,0:T(8,128)(2,1)S(1)} collective-permute-done((bf16[512,256]{1,0:T(8,128)(2,1)S(1)}, bf16[512,256]{1,0:T(8,128)(2,1)S(1)}, u32[]{:S(2)}, u32[]{:S(2)}) %collective-permute-start.17) | collective-permute-done | bytes 262176 | tf_op jit(solution)/shard_map/ppermute | solution.py:20
  67.0 1.5 %collective-permute-start.13 = (bf16[32,128]{1,0:T(8,128)(2,1)S(1)}, bf16[32,128]{1,0:T(8,128)(2,1)S(1)}, u32[]{:S(2)}, u32[]{:S(2)}) collective-permute-start(bf16[32,128]{1,0:T(8,128)(2,1)S(1)} %get-tuple-element.51.refs_2_), channel_id=1, source_target_pairs={{0,2},{1,3},{2,0},{3,1},{4,6},{5,7},{6,4},{7,5},{8,10},{9,11},{10,... | collective-permute-start | bytes 24584 | tf_op jit(solution)/shard_map/ppermute | solution.py:20
  68.5 1.9 %collective-permute-done.18.refs_2_ = bf16[512,256]{1,0:T(8,128)(2,1)S(1)} collective-permute-done((bf16[512,256]{1,0:T(8,128)(2,1)S(1)}, bf16[512,256]{1,0:T(8,128)(2,1)S(1)}, u32[]{:S(2)}, u32[]{:S(2)}) %collective-permute-start.18) | collective-permute-done | bytes 262176 | tf_op jit(solution)/shard_map/ppermute | solution.py:20
  70.4 2.4 %collective-permute-start.14 = (bf16[32,128]{1,0:T(8,128)(2,1)S(1)}, bf16[32,128]{1,0:T(8,128)(2,1)S(1)}, u32[]{:S(2)}, u32[]{:S(2)}) collective-permute-start(bf16[32,128]{1,0:T(8,128)(2,1)S(1)} %get-tuple-element.51.refs_2_), channel_id=1, source_target_pairs={{0,3},{1,2},{2,1},{3,0},{4,7},{5,6},{6,5},{7,4},{8,11},{9,10},{10,... | collective-permute-start | bytes 24584 | tf_op jit(solution)/shard_map/ppermute | solution.py:20
  73.1 0.6 collective-permute-start.19
  73.6 0.6 collective-permute-start.21
  74.2 0.9 collective-permute-done.14.refs_5_
  75.1 1.5 %collective-permute-start.22 = (bf16[512,256]{1,0:T(8,128)(2,1)S(1)}, bf16[512,256]{1,0:T(8,128)(2,1)S(1)}, u32[]{:S(2)}, u32[]{:S(2)}) collective-permute-start(bf16[512,256]{1,0:T(8,128)(2,1)S(1)} %get-tuple-element.63), channel_id=1, source_target_pairs={{0,2},{1,3},{2,0},{3,1},{4,6},{5,7},{6,4},{7,5},{8,10},{9,11},{10,... | collective-permute-start | bytes 786440 | tf_op jit(solution)/shard_map/ppermute | solution.py:20
  76.5 1.5 %collective-permute-start.23 = (bf16[512,256]{1,0:T(8,128)(2,1)S(1)}, bf16[512,256]{1,0:T(8,128)(2,1)S(1)}, u32[]{:S(2)}, u32[]{:S(2)}) collective-permute-start(bf16[512,256]{1,0:T(8,128)(2,1)S(1)} %get-tuple-element.64), channel_id=1, source_target_pairs={{0,1},{1,0},{2,3},{3,2},{4,5},{5,4},{6,7},{7,6},{8,9},{9,8},{10,11... | collective-permute-start | bytes 786440 | tf_op jit(solution)/shard_map/ppermute | solution.py:20
  78.0 0.5 shard_map.106
  78.5 3.5 %collective-permute-done.19.refs_1_ = bf16[512,256]{1,0:T(8,128)(2,1)S(1)} collective-permute-done((bf16[512,256]{1,0:T(8,128)(2,1)S(1)}, bf16[512,256]{1,0:T(8,128)(2,1)S(1)}, u32[]{:S(2)}, u32[]{:S(2)}) %collective-permute-start.19) | collective-permute-done | bytes 262176 | tf_op jit(solution)/shard_map/ppermute | solution.py:20
  82.0 0.5 collective-permute-done.21.refs_2_
  82.4 1.6 %shard_map.109.refs_0_ = f32[1024,512]{1,0:T(8,128)} custom-call(f32[1024,256]{1,0:T(8,128)S(1)} %get-tuple-element.54.refs_0_, bf16[512,256]{1,0:T(8,128)(2,1)S(1)} %collective-permute-done.19.refs_1_, bf16[512,256]{1,0:T(8,128)(2,1)S(1)} %collective-permute-done.21.refs_2_), custom_call_target="tpu_custom_call" | custom-call | tf_op jit(solution)/shard_map/pallas_call | solution.py:52
  84.0 0.8 collective-permute-done.22.refs_2_
  84.8 0.5 collective-permute-done.23.refs_3_
  85.3 1.5 %shard_map.110 = f32[1024,512]{1,0:T(8,128)} custom-call(f32[1024,512]{1,0:T(8,128)} %shard_map.109.refs_0_, f32[1024,256]{1,0:T(8,128)S(1)} %get-tuple-element.62.refs_1_, bf16[512,256]{1,0:T(8,128)(2,1)S(1)} %collective-permute-done.22.refs_2_, bf16[512,256]{1,0:T(8,128)(2,1)S(1)} %collective-permute-done.23.refs_3_), custom_call_target="tpu_custom_call", output_to_operand_aliasing={{}: (0, {})} | custom-call | tf_op jit(solution)/shard_map/pallas_call | solution.py:52
  (27 shorter events, 0.5 us)
Async XLA Ops:
  0.6 27.3 %collective-permute-start = (bf16[1024,512]{1,0:T(8,128)(2,1)}, bf16[1024,512]{1,0:T(8,128)(2,1)S(1)}, u32[]{:S(2)}, u32[]{:S(2)}) collective-permute-start(bf16[1024,512]{1,0:T(8,128)(2,1)} %refs_0_.1), channel_id=1, source_target_pairs={{0,1},{1,0},{2,3},{3,2},{4,5},{5,4},{6,7},{7,6},{8,9},{9,8},{10,11... | collective-permute-start | bytes 3145736 | tf_op jit(solution)/shard_map/ppermute | solution.py:20
  4.9 18.9 %collective-permute-start.2 = (bf16[576,512]{1,0:T(8,128)(2,1)S(1)}, bf16[576,512]{1,0:T(8,128)(2,1)S(1)}, u32[]{:S(2)}, u32[]{:S(2)}) collective-permute-start(bf16[576,512]{1,0:T(8,128)(2,1)S(1)} %get-tuple-element.39.refs_3_.refs_4_), channel_id=1, source_target_pairs={{0,2},{1,3},{2,0},{3,1},{4,6},{5,7},{6,4},{7,5},{8,10},{9,11},{10,... | collective-permute-start | bytes 1769480 | tf_op jit(solution)/shard_map/ppermute | solution.py:20
  6.5 25.6 %collective-permute-start.4 = (bf16[448,512]{1,0:T(8,128)(2,1)S(1)}, bf16[448,512]{1,0:T(8,128)(2,1)S(1)}, u32[]{:S(2)}, u32[]{:S(2)}) collective-permute-start(bf16[448,512]{1,0:T(8,128)(2,1)S(1)} %get-tuple-element.40.refs_2_.refs_3_), channel_id=1, source_target_pairs={{0,2},{1,3},{2,0},{3,1},{4,6},{5,7},{6,4},{7,5},{8,10},{9,11},{10,... | collective-permute-start | bytes 1376264 | tf_op jit(solution)/shard_map/ppermute | solution.py:20
  7.7 16.0 %copy-start = (bf16[1024,32]{0,1:T(8,128)(2,1)S(1)}, bf16[1024,32]{0,1:T(8,128)(2,1)}, u32[]{:S(2)}) copy-start(bf16[1024,32]{0,1:T(8,128)(2,1)} %param.12) | copy-start | bytes 196612
  7.7 16.0 %copy-start.3 = (bf16[4,416]{1,0:T(4,128)(2,1)S(1)}, bf16[4,416]{1,0:T(4,128)(2,1)}, u32[]{:S(2)}) copy-start(bf16[4,416]{1,0:T(4,128)(2,1)} %refs_5_.2) | copy-start | bytes 9988
  24.1 11.4 %collective-permute-start.3 = (bf16[624,256]{1,0:T(8,128)(2,1)S(1)}, bf16[624,256]{1,0:T(8,128)(2,1)S(1)}, u32[]{:S(2)}, u32[]{:S(2)}) collective-permute-start(bf16[624,256]{1,0:T(8,128)(2,1)S(1)} %get-tuple-element.41), channel_id=1, source_target_pairs={{0,1},{1,0},{2,3},{3,2},{4,5},{5,4},{6,7},{7,6},{8,9},{9,8},{10,11... | collective-permute-start | bytes 958472 | tf_op jit(solution)/shard_map/ppermute | solution.py:20
  27.9 8.6 %collective-permute-start.1 = (bf16[448,256]{1,0:T(8,128)(2,1)S(1)}, bf16[448,256]{1,0:T(8,128)(2,1)S(1)}, u32[]{:S(2)}, u32[]{:S(2)}) collective-permute-start(bf16[448,256]{1,0:T(8,128)(2,1)S(1)} %get-tuple-element.38), channel_id=1, source_target_pairs={{0,2},{1,3},{2,0},{3,1},{4,6},{5,7},{6,4},{7,5},{8,10},{9,11},{10,... | collective-permute-start | bytes 688136 | tf_op jit(solution)/shard_map/ppermute | solution.py:20
  30.0 10.8 %collective-permute-start.6 = (bf16[576,256]{1,0:T(8,128)(2,1)S(1)}, bf16[576,256]{1,0:T(8,128)(2,1)S(1)}, u32[]{:S(2)}, u32[]{:S(2)}) collective-permute-start(bf16[576,256]{1,0:T(8,128)(2,1)S(1)} %get-tuple-element.46), channel_id=1, source_target_pairs={{0,1},{1,0},{2,3},{3,2},{4,5},{5,4},{6,7},{7,6},{8,9},{9,8},{10,11... | collective-permute-start | bytes 884744 | tf_op jit(solution)/shard_map/ppermute | solution.py:20
  31.5 9.3 %collective-permute-start.5 = (bf16[448,256]{1,0:T(8,128)(2,1)S(1)}, bf16[448,256]{1,0:T(8,128)(2,1)S(1)}, u32[]{:S(2)}, u32[]{:S(2)}) collective-permute-start(bf16[448,256]{1,0:T(8,128)(2,1)S(1)} %get-tuple-element.45), channel_id=1, source_target_pairs={{0,2},{1,3},{2,0},{3,1},{4,6},{5,7},{6,4},{7,5},{8,10},{9,11},{10,... | collective-permute-start | bytes 688136 | tf_op jit(solution)/shard_map/ppermute | solution.py:20
  32.0 4.5 %copy-start.2 = (bf16[1024]{0:T(1024)(128)(2,1)S(1)}, bf16[1024]{0:T(1024)(128)(2,1)}, u32[]{:S(2)}) copy-start(bf16[1024]{0:T(1024)(128)(2,1)} %param.11) | copy-start | bytes 6148
  38.7 9.0 %collective-permute-start.7 = (bf16[544,256]{1,0:T(8,128)(2,1)S(1)}, bf16[544,256]{1,0:T(8,128)(2,1)S(1)}, u32[]{:S(2)}, u32[]{:S(2)}) collective-permute-start(bf16[544,256]{1,0:T(8,128)(2,1)S(1)} %get-tuple-element.50), channel_id=1, source_target_pairs={{0,2},{1,3},{2,0},{3,1},{4,6},{5,7},{6,4},{7,5},{8,10},{9,11},{10,... | collective-permute-start | bytes 835592 | tf_op jit(solution)/shard_map/ppermute | solution.py:20
  43.1 4.7 %copy-start.1 = (bf16[3,128,16]{1,2,0:T(8,128)(2,1)S(1)}, bf16[3,128,16]{1,2,0:T(8,128)(2,1)}, u32[]{:S(2)}) copy-start(bf16[3,128,16]{1,2,0:T(8,128)(2,1)} %param.13) | copy-start | bytes 36868
  43.1 4.7 %copy-start.4 = (bf16[3,16]{1,0:T(4,128)(2,1)S(1)}, bf16[3,16]{1,0:T(4,128)(2,1)}, u32[]{:S(2)}) copy-start(bf16[3,16]{1,0:T(4,128)(2,1)} %refs_5_.3) | copy-start | bytes 292
  46.5 30.0 %collective-permute-start.15 = (bf16[512,512]{1,0:T(8,128)(2,1)S(1)}, bf16[512,512]{1,0:T(8,128)(2,1)S(1)}, u32[]{:S(2)}, u32[]{:S(2)}) collective-permute-start(bf16[512,512]{1,0:T(8,128)(2,1)S(1)} %get-tuple-element.52), channel_id=1, source_target_pairs={{0,1},{1,0},{2,3},{3,2},{4,5},{5,4},{6,7},{7,6},{8,9},{9,8},{10,11... | collective-permute-start | bytes 1572872 | tf_op jit(solution)/shard_map/ppermute | solution.py:20
  47.9 1.2 %collective-permute-start.8 = (bf16[144,128]{1,0:T(8,128)(2,1)S(1)}, bf16[144,128]{1,0:T(8,128)(2,1)S(1)}, u32[]{:S(2)}, u32[]{:S(2)}) collective-permute-start(bf16[144,128]{1,0:T(8,128)(2,1)S(1)} %shard_map.103.refs_0_), channel_id=1, source_target_pairs={{0,4},{4,0},{8,12},{12,8},{16,20},{20,16},{24,28},{28,24},{1,5},{5... | collective-permute-start | bytes 110600 | tf_op jit(solution)/shard_map/ppermute | solution.py:20
  49.1 6.6 %collective-permute-start.10 = (bf16[224,128]{1,0:T(8,128)(2,1)S(1)}, bf16[224,128]{1,0:T(8,128)(2,1)S(1)}, u32[]{:S(2)}, u32[]{:S(2)}) collective-permute-start(bf16[224,128]{1,0:T(8,128)(2,1)S(1)} %shard_map.104.refs_0_), channel_id=1, source_target_pairs={{0,16},{4,20},{8,24},{12,28},{16,0},{20,4},{24,8},{28,12},{1,17},{... | collective-permute-start | bytes 172040 | tf_op jit(solution)/shard_map/ppermute | solution.py:20
  51.8 6.1 %collective-permute-start.11 = (bf16[224,128]{1,0:T(8,128)(2,1)S(1)}, bf16[224,128]{1,0:T(8,128)(2,1)S(1)}, u32[]{:S(2)}, u32[]{:S(2)}) collective-permute-start(bf16[224,128]{1,0:T(8,128)(2,1)S(1)} %shard_map.104.refs_0_), channel_id=1, source_target_pairs={{0,24},{4,28},{8,16},{12,20},{16,8},{20,12},{24,0},{28,4},{1,25},{... | collective-permute-start | bytes 172040 | tf_op jit(solution)/shard_map/ppermute | solution.py:20
  53.1 5.7 %collective-permute-start.9 = (bf16[224,128]{1,0:T(8,128)(2,1)S(1)}, bf16[224,128]{1,0:T(8,128)(2,1)S(1)}, u32[]{:S(2)}, u32[]{:S(2)}) collective-permute-start(bf16[224,128]{1,0:T(8,128)(2,1)S(1)} %shard_map.104.refs_0_), channel_id=1, source_target_pairs={{0,8},{4,12},{8,0},{12,4},{16,24},{20,28},{24,16},{28,20},{1,9},{5... | collective-permute-start | bytes 172040 | tf_op jit(solution)/shard_map/ppermute | solution.py:20
  53.4 9.2 %collective-permute-start.20 = (bf16[512,256]{1,0:T(8,128)(2,1)S(1)}, bf16[512,256]{1,0:T(8,128)(2,1)S(1)}, u32[]{:S(2)}, u32[]{:S(2)}) collective-permute-start(bf16[512,256]{1,0:T(8,128)(2,1)S(1)} %get-tuple-element.60), channel_id=1, source_target_pairs={{0,2},{1,3},{2,0},{3,1},{4,6},{5,7},{6,4},{7,5},{8,10},{9,11},{10,... | collective-permute-start | bytes 786440 | tf_op jit(solution)/shard_map/ppermute | solution.py:20
  55.7 11.2 %collective-permute-start.17 = (bf16[512,256]{1,0:T(8,128)(2,1)S(1)}, bf16[512,256]{1,0:T(8,128)(2,1)S(1)}, u32[]{:S(2)}, u32[]{:S(2)}) collective-permute-start(bf16[512,256]{1,0:T(8,128)(2,1)S(1)} %get-tuple-element.56), channel_id=1, source_target_pairs={{0,1},{1,0},{2,3},{3,2},{4,5},{5,4},{6,7},{7,6},{8,9},{9,8},{10,11... | collective-permute-start | bytes 786440 | tf_op jit(solution)/shard_map/ppermute | solution.py:20
  57.9 12.5 %collective-permute-start.18 = (bf16[512,256]{1,0:T(8,128)(2,1)S(1)}, bf16[512,256]{1,0:T(8,128)(2,1)S(1)}, u32[]{:S(2)}, u32[]{:S(2)}) collective-permute-start(bf16[512,256]{1,0:T(8,128)(2,1)S(1)} %get-tuple-element.57), channel_id=1, source_target_pairs={{0,1},{1,0},{2,3},{3,2},{4,5},{5,4},{6,7},{7,6},{8,9},{9,8},{10,11... | collective-permute-start | bytes 786440 | tf_op jit(solution)/shard_map/ppermute | solution.py:20
  58.8 19.2 %collective-permute-start.16 = (bf16[512,512]{1,0:T(8,128)(2,1)S(1)}, bf16[512,512]{1,0:T(8,128)(2,1)S(1)}, u32[]{:S(2)}, u32[]{:S(2)}) collective-permute-start(bf16[512,512]{1,0:T(8,128)(2,1)S(1)} %get-tuple-element.53), channel_id=1, source_target_pairs={{0,2},{1,3},{2,0},{3,1},{4,6},{5,7},{6,4},{7,5},{8,10},{9,11},{10,... | collective-permute-start | bytes 1572872 | tf_op jit(solution)/shard_map/ppermute | solution.py:20
  62.6 10.5 %collective-permute-start.12 = (bf16[32,128]{1,0:T(8,128)(2,1)S(1)}, bf16[32,128]{1,0:T(8,128)(2,1)S(1)}, u32[]{:S(2)}, u32[]{:S(2)}) collective-permute-start(bf16[32,128]{1,0:T(8,128)(2,1)S(1)} %get-tuple-element.51.refs_2_), channel_id=1, source_target_pairs={{0,1},{1,0},{2,3},{3,2},{4,5},{5,4},{6,7},{7,6},{8,9},{9,8},{10,11... | collective-permute-start | bytes 24584 | tf_op jit(solution)/shard_map/ppermute | solution.py:20
  67.0 6.7 %collective-permute-start.13 = (bf16[32,128]{1,0:T(8,128)(2,1)S(1)}, bf16[32,128]{1,0:T(8,128)(2,1)S(1)}, u32[]{:S(2)}, u32[]{:S(2)}) collective-permute-start(bf16[32,128]{1,0:T(8,128)(2,1)S(1)} %get-tuple-element.51.refs_2_), channel_id=1, source_target_pairs={{0,2},{1,3},{2,0},{3,1},{4,6},{5,7},{6,4},{7,5},{8,10},{9,11},{10,... | collective-permute-start | bytes 24584 | tf_op jit(solution)/shard_map/ppermute | solution.py:20
  70.4 4.7 %collective-permute-start.14 = (bf16[32,128]{1,0:T(8,128)(2,1)S(1)}, bf16[32,128]{1,0:T(8,128)(2,1)S(1)}, u32[]{:S(2)}, u32[]{:S(2)}) collective-permute-start(bf16[32,128]{1,0:T(8,128)(2,1)S(1)} %get-tuple-element.51.refs_2_), channel_id=1, source_target_pairs={{0,3},{1,2},{2,1},{3,0},{4,7},{5,6},{6,5},{7,4},{8,11},{9,10},{10,... | collective-permute-start | bytes 24584 | tf_op jit(solution)/shard_map/ppermute | solution.py:20
  73.1 8.9 %collective-permute-start.19 = (bf16[512,256]{1,0:T(8,128)(2,1)S(1)}, bf16[512,256]{1,0:T(8,128)(2,1)S(1)}, u32[]{:S(2)}, u32[]{:S(2)}) collective-permute-start(bf16[512,256]{1,0:T(8,128)(2,1)S(1)} %get-tuple-element.58), channel_id=1, source_target_pairs={{0,2},{1,3},{2,0},{3,1},{4,6},{5,7},{6,4},{7,5},{8,10},{9,11},{10,... | collective-permute-start | bytes 786440 | tf_op jit(solution)/shard_map/ppermute | solution.py:20
  73.6 8.8 %collective-permute-start.21 = (bf16[512,256]{1,0:T(8,128)(2,1)S(1)}, bf16[512,256]{1,0:T(8,128)(2,1)S(1)}, u32[]{:S(2)}, u32[]{:S(2)}) collective-permute-start(bf16[512,256]{1,0:T(8,128)(2,1)S(1)} %get-tuple-element.61), channel_id=1, source_target_pairs={{0,1},{1,0},{2,3},{3,2},{4,5},{5,4},{6,7},{7,6},{8,9},{9,8},{10,11... | collective-permute-start | bytes 786440 | tf_op jit(solution)/shard_map/ppermute | solution.py:20
  75.1 9.7 %collective-permute-start.22 = (bf16[512,256]{1,0:T(8,128)(2,1)S(1)}, bf16[512,256]{1,0:T(8,128)(2,1)S(1)}, u32[]{:S(2)}, u32[]{:S(2)}) collective-permute-start(bf16[512,256]{1,0:T(8,128)(2,1)S(1)} %get-tuple-element.63), channel_id=1, source_target_pairs={{0,2},{1,3},{2,0},{3,1},{4,6},{5,7},{6,4},{7,5},{8,10},{9,11},{10,... | collective-permute-start | bytes 786440 | tf_op jit(solution)/shard_map/ppermute | solution.py:20
  76.5 8.7 %collective-permute-start.23 = (bf16[512,256]{1,0:T(8,128)(2,1)S(1)}, bf16[512,256]{1,0:T(8,128)(2,1)S(1)}, u32[]{:S(2)}, u32[]{:S(2)}) collective-permute-start(bf16[512,256]{1,0:T(8,128)(2,1)S(1)} %get-tuple-element.64), channel_id=1, source_target_pairs={{0,1},{1,0},{2,3},{3,2},{4,5},{5,4},{6,7},{7,6},{8,9},{9,8},{10,11... | collective-permute-start | bytes 786440 | tf_op jit(solution)/shard_map/ppermute | solution.py:20

commit v7 on v6

--- a/solution.py
+++ b/solution.py
@@ -396,8 +396,8 @@
         ref[...] = whole_ref[:height, part * width : (part + 1) * width]
 
 
-def forward_body(own_ref, x_ref, y_ref, *refs):
-    pieces, (out_0_ref, out_1_ref, factor_ref, loads_ref) = refs[:-4], refs[-4:]
+def forward_body(own_ref, x_ref, y_ref, far_ref, *refs):
+    pieces, (out_0_ref, out_1_ref, turned_ref, factor_ref, loads_ref) = refs[:-5], refs[-5:]
     rows = own_ref.shape[0]
     width = out_0_ref.shape[1]
     for index, ref in enumerate((own_ref, x_ref, y_ref)):
@@ -408,16 +408,17 @@
         start += ref.shape[0]
     out_0_ref[...] = dot_tn(factor_ref[...], loads_ref[:, :width])
     out_1_ref[...] = dot_tn(factor_ref[...], loads_ref[:, width:])
-
-
-def far_body(far_ref, low_ref, high_ref, near_ref, dinv_ref, *refs, first):
+    turned_ref[...] = far_ref[...].T
+
+
+def far_body(far_ref, turned_ref, low_ref, high_ref, near_ref, dinv_ref, *refs, first):
     kept = refs[:-5]
     z_ref, relay_low_ref, relay_high_ref, loads_ref, part_ref = refs[-5:]
     split, half = low_ref.shape[0], relay_low_ref.shape[0]
     rest = loads_ref.shape[0] - split
     loads_ref[:split, :] = low_ref[...]
     loads_ref[split:, :] = high_ref[:rest, :]
-    part_ref[...] = near_ref[...] + dot_tn(far_ref[...], loads_ref[...])
+    part_ref[...] = near_ref[...] + dot_nn(turned_ref[...], loads_ref[...])
     pivots = dinv_ref[...].astype(F32)
     width = part_ref.shape[1]
     for tile in range(pivots.shape[0]):
@@ -469,20 +470,24 @@
         ref[half:, :] += y_high_ref[:, cols].astype(F32)
 
 
-def last_body(base_ref, low_ref, high_ref, out_ref):
-    block = out_ref.shape[0]
-    step = pl.program_id(0)
-    per_half = low_ref.shape[0] // block
-    rows = pl.ds(pl.multiple_of(step * block, block), block)
-    part = pl.ds(pl.multiple_of(step % per_half * block, block), block)
-
-    @pl.when(step < per_half)
-    def _():
-        out_ref[...] = base_ref[rows, :] + low_ref[part, :].astype(F32)
-
-    @pl.when(step >= per_half)
-    def _():
-        out_ref[...] = base_ref[rows, :] + high_ref[part, :].astype(F32)
+def last_body(base_ref, low_ref, high_ref, out_ref, sum_ref, sems, *, start, chunks):
+    rows, width = base_ref.shape
+    half, height = low_ref.shape[0], rows // chunks
+    copies = []
+    for chunk in range(chunks):
+        top = chunk * height
+        place = slice(top, top + height)
+        piece_ref, base = (low_ref, top) if top < half else (high_ref, top - half)
+        sum_ref[place, :] = base_ref[place, :] + piece_ref[base : base + height, :].astype(F32)
+        copy = pltpu.make_async_copy(
+            sum_ref.at[pl.ds(top, height), :],
+            out_ref.at[pl.ds(top, height), pl.ds(start, width)],
+            sems.at[chunk],
+        )
+        copy.start()
+        copies.append(copy)
+    for copy in copies:
+        copy.wait()
 
 
 def local_pairs(leaf_rhs, leaf_inv, ordering, leaf_dinv, leaf_link, sep_rhs, sep_factor, sep_dinv):
@@ -532,11 +537,11 @@
     low_cut = call(cut_body, (x_all,), [vmem()], [bf16(split, width // 2)] * 2, after=(blocks[0],))
     d_low = [exchange(low_cut[part], "grp", 2) for part in parts]
 
-    part_y = call(
+    *part_y, turned = call(
         forward_body,
-        (*blocks[:3], low, high, x_all, y_low, y_high),
-        [vmem()] * 8,
-        [f32(rows, width // 2)] * 2,
+        (*blocks, low, high, x_all, y_low, y_high),
+        [vmem()] * 9,
+        [f32(rows, width // 2)] * 2 + [bf16(rows, rows)],
         scratch_shapes=[pltpu.VMEM((3 * rows, rows), BF16), pltpu.VMEM((3 * rows, width), BF16)],
     )
     leaf_z, relay_low, relay_high = [], [], []
@@ -544,8 +549,16 @@
         shared = (kept,) if part == 0 else ()
         z_part, far_low, far_high = call(
             functools.partial(far_body, first=first),
-            (blocks[3], d_low[part], d_high[part], part_y[part], leaf_dinv.reshape(-1, LANES), *shared),
-            [vmem()] * (5 + len(shared)),
+            (
+                blocks[3],
+                turned,
+                d_low[part],
+                d_high[part],
+                part_y[part],
+                leaf_dinv.reshape(-1, LANES),
+                *shared,
+            ),
+            [vmem()] * (6 + len(shared)),
             (
                 bf16(rows, width // 2),
                 bf16(half, width // 2),
@@ -610,21 +623,22 @@
         [f32(rows, breadth) for breadth in breadths],
         scratch_shapes=[pltpu.VMEM((first, width), BF16)],
     )
-    block = rows // 4
-    leaf_x = ()
-    for part, start in zip(parts, (0, breadths[0] // breadths[1])):
+    chunks = 4
+    leaf_x, start = (), 0
+    for part, breadth in zip(parts, breadths):
         leaf_x = (
             call(
-                last_body,
+                functools.partial(last_body, start=start, chunks=chunks),
                 (base[part], sum_y_low[part], sum_x_high[part]),
                 [vmem()] * 3,
                 f32(rows, width),
                 after=leaf_x,
-                grid=(rows // block,),
-                out_specs=pl.BlockSpec((block, breadths[part]), lambda step, start=start: (step, start)),
+                out_specs=pl.BlockSpec(memory_space=pltpu.HBM),
+                scratch_shapes=[pltpu.VMEM((rows, breadth), F32), pltpu.SemaphoreType.DMA((chunks,))],
                 input_output_aliases={0: 0} if leaf_x else {},
             ),
         )
+        start += breadth
     return leaf_x[0], jnp.swapaxes(sep_turned, 1, 2)
 
 

time: 87 us -> 87.5 us (level)
  starting transfers between devices: 30.6 us -> 31.5 us
    ppermute x24, starting transfers between devices: 30.6 us -> 31.5 us  [exchange(): lax.ppermute(block, axis, [(low, low ^ mask) for low in range(count)])]
  transfers between devices with their start and end apart: 24 -> 24, of which waited for: 13 -> 12; matrix products, arithmetic and copies ran while one was open for 1% -> 1% of each run, Pallas kernels for 38% -> 38%
where the time goes in v7:
time: 87.5 us; the launch traced here: 87.3 us
  Pallas kernels  34.2 us (39%)
  starting transfers between devices  31.5 us (36%)
  waiting for transfers between devices  19.9 us (23%)
    pallas_call x16, Pallas kernels, call(): pl.pallas_call(skipping, out_shape=out_shape, in_specs=[pl.BlockSpec(memo...  34.2 us
    ppermute x24, starting transfers between devices, exchange(): lax.ppermute(block, axis, [(low, low ^ mask) for low in range(count)])  31.5 us
    ppermute x24, waiting for transfers between devices, exchange(): lax.ppermute(block, axis, [(low, low ^ mask) for low in range(count)])  19.9 us
  transfers between devices with their start and end apart: 24, of which 12 were waited for; matrix products, arithmetic and copies ran while one was open for 1% of the time, Pallas kernels for 38%

profile of v7, /device:TPU:0, one launch (start us, length us, event | category | flops | bytes accessed | tf_op | source)
XLA Modules:
  0.0 87.3 jit_solution(11164596860356418439)
XLA Ops:
  0.6 3.0 %collective-permute-start = (bf16[1024,512]{1,0:T(8,128)(2,1)}, bf16[1024,512]{1,0:T(8,128)(2,1)S(1)}, u32[]{:S(2)}, u32[]{:S(2)}) collective-permute-start(bf16[1024,512]{1,0:T(8,128)(2,1)} %refs_0_.1), channel_id=1, source_target_pairs={{0,1},{1,0},{2,3},{3,2},{4,5},{5,4},{6,7},{7,6},{8,9},{9,8},{10,11... | collective-permute-start | bytes 3145736 | tf_op jit(solution)/shard_map/ppermute | solution.py:20
  3.7 1.2 %shard_map.96 = (bf16[448,512]{1,0:T(8,128)(2,1)S(1)}, bf16[576,512]{1,0:T(8,128)(2,1)S(1)}) custom-call(bf16[1024,512]{1,0:T(8,128)(2,1)} %refs_0_.1), custom_call_target="tpu_custom_call" | custom-call | tf_op jit(solution)/shard_map/pallas_call | solution.py:52
  4.9 1.6 %collective-permute-start.2 = (bf16[576,512]{1,0:T(8,128)(2,1)S(1)}, bf16[576,512]{1,0:T(8,128)(2,1)S(1)}, u32[]{:S(2)}, u32[]{:S(2)}) collective-permute-start(bf16[576,512]{1,0:T(8,128)(2,1)S(1)} %get-tuple-element.40.refs_5_.refs_3_), channel_id=1, source_target_pairs={{0,2},{1,3},{2,0},{3,1},{4,6},{5,7},{6,4},{7,5},{8,10},{9,11},{10,... | collective-permute-start | bytes 1769480 | tf_op jit(solution)/shard_map/ppermute | solution.py:20
  6.5 0.5 collective-permute-start.1
  7.0 0.7 fusion.2.refs_0_
  7.7 16.0 %shard_map.95 = (bf16[1024,1024]{1,0:T(8,128)(2,1)S(1)}, bf16[1024,1024]{1,0:T(8,128)(2,1)S(1)}, bf16[1024,1024]{1,0:T(8,128)(2,1)S(1)}, bf16[1024,1024]{1,0:T(8,128)(2,1)S(1)}) custom-call(s32[4096]{0:T(1024)S(1)} %fusion.2.refs_0_, bf16[1024,4096]{1,0:T(8,128)(2,1)} %refs_1_.1), custom_call_target="tpu_custom_call" | custom-call | tf_op jit(solution)/shard_map/pallas_call | solution.py:52
  23.8 0.3 shard_map.99
  24.1 0.2 collective-permute-start.4
  24.3 3.6 %collective-permute-done.refs_6_.refs_1_ = bf16[1024,512]{1,0:T(8,128)(2,1)S(1)} collective-permute-done((bf16[1024,512]{1,0:T(8,128)(2,1)}, bf16[1024,512]{1,0:T(8,128)(2,1)S(1)}, u32[]{:S(2)}, u32[]{:S(2)}) %collective-permute-start) | collective-permute-done | bytes 1048608 | tf_op jit(solution)/shard_map/ppermute | solution.py:20
  27.9 2.1 %collective-permute-start.3 = (bf16[448,256]{1,0:T(8,128)(2,1)S(1)}, bf16[448,256]{1,0:T(8,128)(2,1)S(1)}, u32[]{:S(2)}, u32[]{:S(2)}) collective-permute-start(bf16[448,256]{1,0:T(8,128)(2,1)S(1)} %get-tuple-element.42), channel_id=1, source_target_pairs={{0,2},{1,3},{2,0},{3,1},{4,6},{5,7},{6,4},{7,5},{8,10},{9,11},{10,... | collective-permute-start | bytes 688136 | tf_op jit(solution)/shard_map/ppermute | solution.py:20
  30.0 1.5 %collective-permute-start.6 = (bf16[576,256]{1,0:T(8,128)(2,1)S(1)}, bf16[576,256]{1,0:T(8,128)(2,1)S(1)}, u32[]{:S(2)}, u32[]{:S(2)}) collective-permute-start(bf16[576,256]{1,0:T(8,128)(2,1)S(1)} %get-tuple-element.48), channel_id=1, source_target_pairs={{0,1},{1,0},{2,3},{3,2},{4,5},{5,4},{6,7},{7,6},{8,9},{9,8},{10,11... | collective-permute-start | bytes 884744 | tf_op jit(solution)/shard_map/ppermute | solution.py:20
  31.5 0.5 collective-permute-start.5
  32.0 3.9 %shard_map.97 = (f32[1024,256]{1,0:T(8,128)S(1)}, f32[1024,256]{1,0:T(8,128)S(1)}, bf16[1024,1024]{1,0:T(8,128)(2,1)S(1)}) custom-call(bf16[1024,1024]{1,0:T(8,128)(2,1)S(1)} %get-tuple-element.35.refs_0_, bf16[1024,1024]{1,0:T(8,128)(2,1)S(1)} %get-tuple-element.36.refs_1_, bf16[1024,1024]{1,0:T(8,128)(2,1)S(1)} %get-tuple-element.37.refs_2_, ...), custom_call_target="tpu_custom_call" | custom-call | tf_op jit(solution)/shard_map/pallas_call | solution.py:52
  36.0 0.5 collective-permute-done.3.refs_2_
  36.5 2.2 %shard_map.100 = (bf16[1024,256]{1,0:T(8,128)(2,1)S(1)}, bf16[512,256]{1,0:T(8,128)(2,1)S(1)}, bf16[544,256]{1,0:T(8,128)(2,1)S(1)}) custom-call(bf16[1024,1024]{1,0:T(8,128)(2,1)S(1)} %get-tuple-element.38.refs_3_.refs_0_, bf16[1024,1024]{1,0:T(8,128)(2,1)S(1)} %get-tuple-element.41.refs_1_, bf16[448,256]{1,0:T(8,128)(2,1)S(1)} %collective-permute-done.3.refs_2_, ...), custom_call_target="tpu_custom_call" | custom-call | tf_op jit(solution)/shard_map/pallas_call | solution.py:52
  38.7 2.0 %collective-permute-start.7 = (bf16[544,256]{1,0:T(8,128)(2,1)S(1)}, bf16[544,256]{1,0:T(8,128)(2,1)S(1)}, u32[]{:S(2)}, u32[]{:S(2)}) collective-permute-start(bf16[544,256]{1,0:T(8,128)(2,1)S(1)} %get-tuple-element.52), channel_id=1, source_target_pairs={{0,2},{1,3},{2,0},{3,1},{4,6},{5,7},{6,4},{7,5},{8,10},{9,11},{10,... | collective-permute-start | bytes 835592 | tf_op jit(solution)/shard_map/ppermute | solution.py:20
  40.8 2.2 %shard_map.101 = (bf16[1024,256]{1,0:T(8,128)(2,1)S(1)}, bf16[512,256]{1,0:T(8,128)(2,1)S(1)}, bf16[512,256]{1,0:T(8,128)(2,1)S(1)}) custom-call(bf16[1024,1024]{1,0:T(8,128)(2,1)S(1)} %get-tuple-element.38.refs_3_.refs_0_, bf16[1024,1024]{1,0:T(8,128)(2,1)S(1)} %get-tuple-element.41.refs_1_, bf16[448,256]{1,0:T(8,128)(2,1)S(1)} %collective-permute-done.5.refs_2_, ...), custom_call_target="tpu_custom_call" | custom-call | tf_op jit(solution)/shard_map/pallas_call | solution.py:52
  43.0 3.4 %shard_map.102 = (bf16[512,512]{1,0:T(8,128)(2,1)S(1)}, bf16[512,512]{1,0:T(8,128)(2,1)S(1)}, f32[512,512]{1,0:T(8,128)S(1)}, f32[512,512]{1,0:T(8,128)S(1)}, f32[1024,512]{1,0:T(8,128)S(1)}) custom-call(bf16[1024,1024]{1,0:T(8,128)(2,1)S(1)} %get-tuple-element.35.refs_0_, bf16[1024,1024]{1,0:T(8,128)(2,1)S(1)} %get-tuple-element.36.refs_1_, ...), custom_call_target="tpu_custom_call" | custom-call | tf_op jit(solution)/shard_map/pallas_call | solution.py:52
  46.5 1.2 %collective-permute-start.15 = (bf16[512,512]{1,0:T(8,128)(2,1)S(1)}, bf16[512,512]{1,0:T(8,128)(2,1)S(1)}, u32[]{:S(2)}, u32[]{:S(2)}) collective-permute-start(bf16[512,512]{1,0:T(8,128)(2,1)S(1)} %get-tuple-element.54), channel_id=1, source_target_pairs={{0,1},{1,0},{2,3},{3,2},{4,5},{5,4},{6,7},{7,6},{8,9},{9,8},{10,11... | collective-permute-start | bytes 1572872 | tf_op jit(solution)/shard_map/ppermute | solution.py:20
  47.7 0.1 shard_map.103.refs_0_
  47.9 1.2 %collective-permute-done.8.refs_1_ = bf16[144,128]{1,0:T(8,128)(2,1)S(1)} collective-permute-done((bf16[144,128]{1,0:T(8,128)(2,1)S(1)}, bf16[144,128]{1,0:T(8,128)(2,1)S(1)}, u32[]{:S(2)}, u32[]{:S(2)}) %collective-permute-start.8) | collective-permute-done | bytes 36896 | tf_op jit(solution)/shard_map/ppermute | solution.py:20
  49.1 1.6 %collective-permute-start.9 = (bf16[224,128]{1,0:T(8,128)(2,1)S(1)}, bf16[224,128]{1,0:T(8,128)(2,1)S(1)}, u32[]{:S(2)}, u32[]{:S(2)}) collective-permute-start(bf16[224,128]{1,0:T(8,128)(2,1)S(1)} %shard_map.104.refs_0_), channel_id=1, source_target_pairs={{0,8},{4,12},{8,0},{12,4},{16,24},{20,28},{24,16},{28,20},{1,9},{5... | collective-permute-start | bytes 172040 | tf_op jit(solution)/shard_map/ppermute | solution.py:20
  50.8 2.6 %collective-permute-start.10 = (bf16[224,128]{1,0:T(8,128)(2,1)S(1)}, bf16[224,128]{1,0:T(8,128)(2,1)S(1)}, u32[]{:S(2)}, u32[]{:S(2)}) collective-permute-start(bf16[224,128]{1,0:T(8,128)(2,1)S(1)} %shard_map.104.refs_0_), channel_id=1, source_target_pairs={{0,16},{4,20},{8,24},{12,28},{16,0},{20,4},{24,8},{28,12},{1,17},{... | collective-permute-start | bytes 172040 | tf_op jit(solution)/shard_map/ppermute | solution.py:20
  53.4 0.2 collective-permute-start.11
  53.6 0.9 collective-permute-start.17
  54.4 1.2 %collective-permute-start.18 = (bf16[512,256]{1,0:T(8,128)(2,1)S(1)}, bf16[512,256]{1,0:T(8,128)(2,1)S(1)}, u32[]{:S(2)}, u32[]{:S(2)}) collective-permute-start(bf16[512,256]{1,0:T(8,128)(2,1)S(1)} %get-tuple-element.59), channel_id=1, source_target_pairs={{0,1},{1,0},{2,3},{3,2},{4,5},{5,4},{6,7},{7,6},{8,9},{9,8},{10,11... | collective-permute-start | bytes 786440 | tf_op jit(solution)/shard_map/ppermute | solution.py:20
  55.6 1.6 %collective-permute-done.10.refs_2_ = bf16[224,128]{1,0:T(8,128)(2,1)S(1)} collective-permute-done((bf16[224,128]{1,0:T(8,128)(2,1)S(1)}, bf16[224,128]{1,0:T(8,128)(2,1)S(1)}, u32[]{:S(2)}, u32[]{:S(2)}) %collective-permute-start.10) | collective-permute-done | bytes 57376 | tf_op jit(solution)/shard_map/ppermute | solution.py:20
  57.2 1.5 %collective-permute-start.20 = (bf16[512,256]{1,0:T(8,128)(2,1)S(1)}, bf16[512,256]{1,0:T(8,128)(2,1)S(1)}, u32[]{:S(2)}, u32[]{:S(2)}) collective-permute-start(bf16[512,256]{1,0:T(8,128)(2,1)S(1)} %get-tuple-element.62), channel_id=1, source_target_pairs={{0,2},{1,3},{2,0},{3,1},{4,6},{5,7},{6,4},{7,5},{8,10},{9,11},{10,... | collective-permute-start | bytes 786440 | tf_op jit(solution)/shard_map/ppermute | solution.py:20
  58.7 0.6 collective-permute-done.11.refs_3_
  59.3 1.5 %collective-permute-start.16 = (bf16[512,512]{1,0:T(8,128)(2,1)S(1)}, bf16[512,512]{1,0:T(8,128)(2,1)S(1)}, u32[]{:S(2)}, u32[]{:S(2)}) collective-permute-start(bf16[512,512]{1,0:T(8,128)(2,1)S(1)} %get-tuple-element.55), channel_id=1, source_target_pairs={{0,2},{1,3},{2,0},{3,1},{4,6},{5,7},{6,4},{7,5},{8,10},{9,11},{10,... | collective-permute-start | bytes 1572872 | tf_op jit(solution)/shard_map/ppermute | solution.py:20
  60.9 1.9 %shard_map.105 = (bf16[32,128]{1,0:T(8,128)(2,1)S(1)}, f32[3,16,128]{2,1,0:T(8,128)}) custom-call(bf16[224,128]{1,0:T(8,128)(2,1)S(1)} %shard_map.104.refs_0_, bf16[224,128]{1,0:T(8,128)(2,1)S(1)} %collective-permute-done.9.refs_1_, bf16[224,128]{1,0:T(8,128)(2,1)S(1)} %collective-permute-done.10.refs_2_, bf16[224,128]{1,0:T(8,128)(2,1)S(1)} %collective-permute-done.11.refs_3_), custom_call_target="tpu_custom_call" | custom-call | tf_op jit(solution)/shard_map/pallas_call | solution.py:52
  62.8 4.2 %collective-permute-done.17.refs_1_ = bf16[512,256]{1,0:T(8,128)(2,1)S(1)} collective-permute-done((bf16[512,256]{1,0:T(8,128)(2,1)S(1)}, bf16[512,256]{1,0:T(8,128)(2,1)S(1)}, u32[]{:S(2)}, u32[]{:S(2)}) %collective-permute-start.17) | collective-permute-done | bytes 262176 | tf_op jit(solution)/shard_map/ppermute | solution.py:20
  67.0 1.2 %collective-permute-start.12 = (bf16[32,128]{1,0:T(8,128)(2,1)S(1)}, bf16[32,128]{1,0:T(8,128)(2,1)S(1)}, u32[]{:S(2)}, u32[]{:S(2)}) collective-permute-start(bf16[32,128]{1,0:T(8,128)(2,1)S(1)} %get-tuple-element.53.refs_2_), channel_id=1, source_target_pairs={{0,1},{1,0},{2,3},{3,2},{4,5},{5,4},{6,7},{7,6},{8,9},{9,8},{10,11... | collective-permute-start | bytes 24584 | tf_op jit(solution)/shard_map/ppermute | solution.py:20
  68.1 2.3 %collective-permute-done.18.refs_2_ = bf16[512,256]{1,0:T(8,128)(2,1)S(1)} collective-permute-done((bf16[512,256]{1,0:T(8,128)(2,1)S(1)}, bf16[512,256]{1,0:T(8,128)(2,1)S(1)}, u32[]{:S(2)}, u32[]{:S(2)}) %collective-permute-start.18) | collective-permute-done | bytes 262176 | tf_op jit(solution)/shard_map/ppermute | solution.py:20
  70.4 1.5 %collective-permute-start.13 = (bf16[32,128]{1,0:T(8,128)(2,1)S(1)}, bf16[32,128]{1,0:T(8,128)(2,1)S(1)}, u32[]{:S(2)}, u32[]{:S(2)}) collective-permute-start(bf16[32,128]{1,0:T(8,128)(2,1)S(1)} %get-tuple-element.53.refs_2_), channel_id=1, source_target_pairs={{0,2},{1,3},{2,0},{3,1},{4,6},{5,7},{6,4},{7,5},{8,10},{9,11},{10,... | collective-permute-start | bytes 24584 | tf_op jit(solution)/shard_map/ppermute | solution.py:20
  71.9 1.4 %collective-permute-start.14 = (bf16[32,128]{1,0:T(8,128)(2,1)S(1)}, bf16[32,128]{1,0:T(8,128)(2,1)S(1)}, u32[]{:S(2)}, u32[]{:S(2)}) collective-permute-start(bf16[32,128]{1,0:T(8,128)(2,1)S(1)} %get-tuple-element.53.refs_2_), channel_id=1, source_target_pairs={{0,3},{1,2},{2,1},{3,0},{4,7},{5,6},{6,5},{7,4},{8,11},{9,10},{10,... | collective-permute-start | bytes 24584 | tf_op jit(solution)/shard_map/ppermute | solution.py:20
  73.6 1.6 %collective-permute-start.19 = (bf16[512,256]{1,0:T(8,128)(2,1)S(1)}, bf16[512,256]{1,0:T(8,128)(2,1)S(1)}, u32[]{:S(2)}, u32[]{:S(2)}) collective-permute-start(bf16[512,256]{1,0:T(8,128)(2,1)S(1)} %get-tuple-element.60), channel_id=1, source_target_pairs={{0,2},{1,3},{2,0},{3,1},{4,6},{5,7},{6,4},{7,5},{8,10},{9,11},{10,... | collective-permute-start | bytes 786440 | tf_op jit(solution)/shard_map/ppermute | solution.py:20
  75.1 0.7 collective-permute-done.13.refs_4_
  75.9 1.3 %collective-permute-start.21 = (bf16[512,256]{1,0:T(8,128)(2,1)S(1)}, bf16[512,256]{1,0:T(8,128)(2,1)S(1)}, u32[]{:S(2)}, u32[]{:S(2)}) collective-permute-start(bf16[512,256]{1,0:T(8,128)(2,1)S(1)} %get-tuple-element.63), channel_id=1, source_target_pairs={{0,1},{1,0},{2,3},{3,2},{4,5},{5,4},{6,7},{7,6},{8,9},{9,8},{10,11... | collective-permute-start | bytes 786440 | tf_op jit(solution)/shard_map/ppermute | solution.py:20
  77.2 1.8 %collective-permute-start.22 = (bf16[512,256]{1,0:T(8,128)(2,1)S(1)}, bf16[512,256]{1,0:T(8,128)(2,1)S(1)}, u32[]{:S(2)}, u32[]{:S(2)}) collective-permute-start(bf16[512,256]{1,0:T(8,128)(2,1)S(1)} %get-tuple-element.65), channel_id=1, source_target_pairs={{0,2},{1,3},{2,0},{3,1},{4,6},{5,7},{6,4},{7,5},{8,10},{9,11},{10,... | collective-permute-start | bytes 786440 | tf_op jit(solution)/shard_map/ppermute | solution.py:20
  79.1 0.5 collective-permute-start.23
  79.5 0.5 shard_map.106
  80.0 2.8 %collective-permute-done.19.refs_1_ = bf16[512,256]{1,0:T(8,128)(2,1)S(1)} collective-permute-done((bf16[512,256]{1,0:T(8,128)(2,1)S(1)}, bf16[512,256]{1,0:T(8,128)(2,1)S(1)}, u32[]{:S(2)}, u32[]{:S(2)}) %collective-permute-start.19) | collective-permute-done | bytes 262176 | tf_op jit(solution)/shard_map/ppermute | solution.py:20
  82.8 0.6 collective-permute-done.21.refs_2_
  83.4 1.0 %shard_map.109.refs_0_ = f32[1024,512]{1,0:T(8,128)} custom-call(f32[1024,256]{1,0:T(8,128)S(1)} %get-tuple-element.56.refs_0_, bf16[512,256]{1,0:T(8,128)(2,1)S(1)} %collective-permute-done.19.refs_1_, bf16[512,256]{1,0:T(8,128)(2,1)S(1)} %collective-permute-done.21.refs_2_), custom_call_target="tpu_custom_call" | custom-call | tf_op jit(solution)/shard_map/pallas_call | solution.py:52
  84.5 1.6 %collective-permute-done.22.refs_2_ = bf16[512,256]{1,0:T(8,128)(2,1)S(1)} collective-permute-done((bf16[512,256]{1,0:T(8,128)(2,1)S(1)}, bf16[512,256]{1,0:T(8,128)(2,1)S(1)}, u32[]{:S(2)}, u32[]{:S(2)}) %collective-permute-start.22) | collective-permute-done | bytes 262176 | tf_op jit(solution)/shard_map/ppermute | solution.py:20
  86.1 0.1 collective-permute-done.23.refs_3_
  86.3 1.0 %shard_map.110 = f32[1024,512]{1,0:T(8,128)} custom-call(f32[1024,512]{1,0:T(8,128)} %shard_map.109.refs_0_, f32[1024,256]{1,0:T(8,128)S(1)} %get-tuple-element.64.refs_1_, bf16[512,256]{1,0:T(8,128)(2,1)S(1)} %collective-permute-done.22.refs_2_, bf16[512,256]{1,0:T(8,128)(2,1)S(1)} %collective-permute-done.23.refs_3_), custom_call_target="tpu_custom_call", output_to_operand_aliasing={{}: (0, {})} | custom-call | tf_op jit(solution)/shard_map/pallas_call | solution.py:52
  (27 shorter events, 0.3 us)
Async XLA Ops:
  0.6 27.3 %collective-permute-start = (bf16[1024,512]{1,0:T(8,128)(2,1)}, bf16[1024,512]{1,0:T(8,128)(2,1)S(1)}, u32[]{:S(2)}, u32[]{:S(2)}) collective-permute-start(bf16[1024,512]{1,0:T(8,128)(2,1)} %refs_0_.1), channel_id=1, source_target_pairs={{0,1},{1,0},{2,3},{3,2},{4,5},{5,4},{6,7},{7,6},{8,9},{9,8},{10,11... | collective-permute-start | bytes 3145736 | tf_op jit(solution)/shard_map/ppermute | solution.py:20
  4.9 18.9 %collective-permute-start.2 = (bf16[576,512]{1,0:T(8,128)(2,1)S(1)}, bf16[576,512]{1,0:T(8,128)(2,1)S(1)}, u32[]{:S(2)}, u32[]{:S(2)}) collective-permute-start(bf16[576,512]{1,0:T(8,128)(2,1)S(1)} %get-tuple-element.40.refs_5_.refs_3_), channel_id=1, source_target_pairs={{0,2},{1,3},{2,0},{3,1},{4,6},{5,7},{6,4},{7,5},{8,10},{9,11},{10,... | collective-permute-start | bytes 1769480 | tf_op jit(solution)/shard_map/ppermute | solution.py:20
  6.5 25.6 %collective-permute-start.1 = (bf16[448,512]{1,0:T(8,128)(2,1)S(1)}, bf16[448,512]{1,0:T(8,128)(2,1)S(1)}, u32[]{:S(2)}, u32[]{:S(2)}) collective-permute-start(bf16[448,512]{1,0:T(8,128)(2,1)S(1)} %get-tuple-element.39.refs_4_.refs_2_), channel_id=1, source_target_pairs={{0,2},{1,3},{2,0},{3,1},{4,6},{5,7},{6,4},{7,5},{8,10},{9,11},{10,... | collective-permute-start | bytes 1376264 | tf_op jit(solution)/shard_map/ppermute | solution.py:20
  7.7 16.0 %copy-start = (bf16[1024,32]{0,1:T(8,128)(2,1)S(1)}, bf16[1024,32]{0,1:T(8,128)(2,1)}, u32[]{:S(2)}) copy-start(bf16[1024,32]{0,1:T(8,128)(2,1)} %param.12) | copy-start | bytes 196612
  7.7 16.0 %copy-start.3 = (bf16[4,416]{1,0:T(4,128)(2,1)S(1)}, bf16[4,416]{1,0:T(4,128)(2,1)}, u32[]{:S(2)}) copy-start(bf16[4,416]{1,0:T(4,128)(2,1)} %refs_5_.2) | copy-start | bytes 9988
  24.1 11.8 %collective-permute-start.4 = (bf16[624,256]{1,0:T(8,128)(2,1)S(1)}, bf16[624,256]{1,0:T(8,128)(2,1)S(1)}, u32[]{:S(2)}, u32[]{:S(2)}) collective-permute-start(bf16[624,256]{1,0:T(8,128)(2,1)S(1)} %get-tuple-element.43), channel_id=1, source_target_pairs={{0,1},{1,0},{2,3},{3,2},{4,5},{5,4},{6,7},{7,6},{8,9},{9,8},{10,11... | collective-permute-start | bytes 958472 | tf_op jit(solution)/shard_map/ppermute | solution.py:20
  27.9 8.6 %collective-permute-start.3 = (bf16[448,256]{1,0:T(8,128)(2,1)S(1)}, bf16[448,256]{1,0:T(8,128)(2,1)S(1)}, u32[]{:S(2)}, u32[]{:S(2)}) collective-permute-start(bf16[448,256]{1,0:T(8,128)(2,1)S(1)} %get-tuple-element.42), channel_id=1, source_target_pairs={{0,2},{1,3},{2,0},{3,1},{4,6},{5,7},{6,4},{7,5},{8,10},{9,11},{10,... | collective-permute-start | bytes 688136 | tf_op jit(solution)/shard_map/ppermute | solution.py:20
  30.0 10.7 %collective-permute-start.6 = (bf16[576,256]{1,0:T(8,128)(2,1)S(1)}, bf16[576,256]{1,0:T(8,128)(2,1)S(1)}, u32[]{:S(2)}, u32[]{:S(2)}) collective-permute-start(bf16[576,256]{1,0:T(8,128)(2,1)S(1)} %get-tuple-element.48), channel_id=1, source_target_pairs={{0,1},{1,0},{2,3},{3,2},{4,5},{5,4},{6,7},{7,6},{8,9},{9,8},{10,11... | collective-permute-start | bytes 884744 | tf_op jit(solution)/shard_map/ppermute | solution.py:20
  31.5 9.2 %collective-permute-start.5 = (bf16[448,256]{1,0:T(8,128)(2,1)S(1)}, bf16[448,256]{1,0:T(8,128)(2,1)S(1)}, u32[]{:S(2)}, u32[]{:S(2)}) collective-permute-start(bf16[448,256]{1,0:T(8,128)(2,1)S(1)} %get-tuple-element.47), channel_id=1, source_target_pairs={{0,2},{1,3},{2,0},{3,1},{4,6},{5,7},{6,4},{7,5},{8,10},{9,11},{10,... | collective-permute-start | bytes 688136 | tf_op jit(solution)/shard_map/ppermute | solution.py:20
  32.0 4.5 %copy-start.2 = (bf16[1024]{0:T(1024)(128)(2,1)S(1)}, bf16[1024]{0:T(1024)(128)(2,1)}, u32[]{:S(2)}) copy-start(bf16[1024]{0:T(1024)(128)(2,1)} %param.11) | copy-start | bytes 6148
  38.7 9.0 %collective-permute-start.7 = (bf16[544,256]{1,0:T(8,128)(2,1)S(1)}, bf16[544,256]{1,0:T(8,128)(2,1)S(1)}, u32[]{:S(2)}, u32[]{:S(2)}) collective-permute-start(bf16[544,256]{1,0:T(8,128)(2,1)S(1)} %get-tuple-element.52), channel_id=1, source_target_pairs={{0,2},{1,3},{2,0},{3,1},{4,6},{5,7},{6,4},{7,5},{8,10},{9,11},{10,... | collective-permute-start | bytes 835592 | tf_op jit(solution)/shard_map/ppermute | solution.py:20
  43.0 4.7 %copy-start.1 = (bf16[3,128,16]{1,2,0:T(8,128)(2,1)S(1)}, bf16[3,128,16]{1,2,0:T(8,128)(2,1)}, u32[]{:S(2)}) copy-start(bf16[3,128,16]{1,2,0:T(8,128)(2,1)} %param.13) | copy-start | bytes 36868
  43.0 4.7 %copy-start.4 = (bf16[3,16]{1,0:T(4,128)(2,1)S(1)}, bf16[3,16]{1,0:T(4,128)(2,1)}, u32[]{:S(2)}) copy-start(bf16[3,16]{1,0:T(4,128)(2,1)} %refs_5_.3) | copy-start | bytes 292
  46.5 32.6 %collective-permute-start.15 = (bf16[512,512]{1,0:T(8,128)(2,1)S(1)}, bf16[512,512]{1,0:T(8,128)(2,1)S(1)}, u32[]{:S(2)}, u32[]{:S(2)}) collective-permute-start(bf16[512,512]{1,0:T(8,128)(2,1)S(1)} %get-tuple-element.54), channel_id=1, source_target_pairs={{0,1},{1,0},{2,3},{3,2},{4,5},{5,4},{6,7},{7,6},{8,9},{9,8},{10,11... | collective-permute-start | bytes 1572872 | tf_op jit(solution)/shard_map/ppermute | solution.py:20
  47.9 1.2 %collective-permute-start.8 = (bf16[144,128]{1,0:T(8,128)(2,1)S(1)}, bf16[144,128]{1,0:T(8,128)(2,1)S(1)}, u32[]{:S(2)}, u32[]{:S(2)}) collective-permute-start(bf16[144,128]{1,0:T(8,128)(2,1)S(1)} %shard_map.103.refs_0_), channel_id=1, source_target_pairs={{0,4},{4,0},{8,12},{12,8},{16,20},{20,16},{24,28},{28,24},{1,5},{5... | collective-permute-start | bytes 110600 | tf_op jit(solution)/shard_map/ppermute | solution.py:20
  49.1 5.3 %collective-permute-start.9 = (bf16[224,128]{1,0:T(8,128)(2,1)S(1)}, bf16[224,128]{1,0:T(8,128)(2,1)S(1)}, u32[]{:S(2)}, u32[]{:S(2)}) collective-permute-start(bf16[224,128]{1,0:T(8,128)(2,1)S(1)} %shard_map.104.refs_0_), channel_id=1, source_target_pairs={{0,8},{4,12},{8,0},{12,4},{16,24},{20,28},{24,16},{28,20},{1,9},{5... | collective-permute-start | bytes 172040 | tf_op jit(solution)/shard_map/ppermute | solution.py:20
  50.8 6.4 %collective-permute-start.10 = (bf16[224,128]{1,0:T(8,128)(2,1)S(1)}, bf16[224,128]{1,0:T(8,128)(2,1)S(1)}, u32[]{:S(2)}, u32[]{:S(2)}) collective-permute-start(bf16[224,128]{1,0:T(8,128)(2,1)S(1)} %shard_map.104.refs_0_), channel_id=1, source_target_pairs={{0,16},{4,20},{8,24},{12,28},{16,0},{20,4},{24,8},{28,12},{1,17},{... | collective-permute-start | bytes 172040 | tf_op jit(solution)/shard_map/ppermute | solution.py:20
  53.4 6.0 %collective-permute-start.11 = (bf16[224,128]{1,0:T(8,128)(2,1)S(1)}, bf16[224,128]{1,0:T(8,128)(2,1)S(1)}, u32[]{:S(2)}, u32[]{:S(2)}) collective-permute-start(bf16[224,128]{1,0:T(8,128)(2,1)S(1)} %shard_map.104.refs_0_), channel_id=1, source_target_pairs={{0,24},{4,28},{8,16},{12,20},{16,8},{20,12},{24,0},{28,4},{1,25},{... | collective-permute-start | bytes 172040 | tf_op jit(solution)/shard_map/ppermute | solution.py:20
  53.6 13.4 %collective-permute-start.17 = (bf16[512,256]{1,0:T(8,128)(2,1)S(1)}, bf16[512,256]{1,0:T(8,128)(2,1)S(1)}, u32[]{:S(2)}, u32[]{:S(2)}) collective-permute-start(bf16[512,256]{1,0:T(8,128)(2,1)S(1)} %get-tuple-element.58), channel_id=1, source_target_pairs={{0,1},{1,0},{2,3},{3,2},{4,5},{5,4},{6,7},{7,6},{8,9},{9,8},{10,11... | collective-permute-start | bytes 786440 | tf_op jit(solution)/shard_map/ppermute | solution.py:20
  54.4 16.0 %collective-permute-start.18 = (bf16[512,256]{1,0:T(8,128)(2,1)S(1)}, bf16[512,256]{1,0:T(8,128)(2,1)S(1)}, u32[]{:S(2)}, u32[]{:S(2)}) collective-permute-start(bf16[512,256]{1,0:T(8,128)(2,1)S(1)} %get-tuple-element.59), channel_id=1, source_target_pairs={{0,1},{1,0},{2,3},{3,2},{4,5},{5,4},{6,7},{7,6},{8,9},{9,8},{10,11... | collective-permute-start | bytes 786440 | tf_op jit(solution)/shard_map/ppermute | solution.py:20
  57.2 14.7 %collective-permute-start.20 = (bf16[512,256]{1,0:T(8,128)(2,1)S(1)}, bf16[512,256]{1,0:T(8,128)(2,1)S(1)}, u32[]{:S(2)}, u32[]{:S(2)}) collective-permute-start(bf16[512,256]{1,0:T(8,128)(2,1)S(1)} %get-tuple-element.62), channel_id=1, source_target_pairs={{0,2},{1,3},{2,0},{3,1},{4,6},{5,7},{6,4},{7,5},{8,10},{9,11},{10,... | collective-permute-start | bytes 786440 | tf_op jit(solution)/shard_map/ppermute | solution.py:20
  59.3 20.2 %collective-permute-start.16 = (bf16[512,512]{1,0:T(8,128)(2,1)S(1)}, bf16[512,512]{1,0:T(8,128)(2,1)S(1)}, u32[]{:S(2)}, u32[]{:S(2)}) collective-permute-start(bf16[512,512]{1,0:T(8,128)(2,1)S(1)} %get-tuple-element.55), channel_id=1, source_target_pairs={{0,2},{1,3},{2,0},{3,1},{4,6},{5,7},{6,4},{7,5},{8,10},{9,11},{10,... | collective-permute-start | bytes 1572872 | tf_op jit(solution)/shard_map/ppermute | solution.py:20
  67.0 6.6 %collective-permute-start.12 = (bf16[32,128]{1,0:T(8,128)(2,1)S(1)}, bf16[32,128]{1,0:T(8,128)(2,1)S(1)}, u32[]{:S(2)}, u32[]{:S(2)}) collective-permute-start(bf16[32,128]{1,0:T(8,128)(2,1)S(1)} %get-tuple-element.53.refs_2_), channel_id=1, source_target_pairs={{0,1},{1,0},{2,3},{3,2},{4,5},{5,4},{6,7},{7,6},{8,9},{9,8},{10,11... | collective-permute-start | bytes 24584 | tf_op jit(solution)/shard_map/ppermute | solution.py:20
  70.4 5.5 %collective-permute-start.13 = (bf16[32,128]{1,0:T(8,128)(2,1)S(1)}, bf16[32,128]{1,0:T(8,128)(2,1)S(1)}, u32[]{:S(2)}, u32[]{:S(2)}) collective-permute-start(bf16[32,128]{1,0:T(8,128)(2,1)S(1)} %get-tuple-element.53.refs_2_), channel_id=1, source_target_pairs={{0,2},{1,3},{2,0},{3,1},{4,6},{5,7},{6,4},{7,5},{8,10},{9,11},{10,... | collective-permute-start | bytes 24584 | tf_op jit(solution)/shard_map/ppermute | solution.py:20
  71.9 5.3 %collective-permute-start.14 = (bf16[32,128]{1,0:T(8,128)(2,1)S(1)}, bf16[32,128]{1,0:T(8,128)(2,1)S(1)}, u32[]{:S(2)}, u32[]{:S(2)}) collective-permute-start(bf16[32,128]{1,0:T(8,128)(2,1)S(1)} %get-tuple-element.53.refs_2_), channel_id=1, source_target_pairs={{0,3},{1,2},{2,1},{3,0},{4,7},{5,6},{6,5},{7,4},{8,11},{9,10},{10,... | collective-permute-start | bytes 24584 | tf_op jit(solution)/shard_map/ppermute | solution.py:20
  73.6 9.2 %collective-permute-start.19 = (bf16[512,256]{1,0:T(8,128)(2,1)S(1)}, bf16[512,256]{1,0:T(8,128)(2,1)S(1)}, u32[]{:S(2)}, u32[]{:S(2)}) collective-permute-start(bf16[512,256]{1,0:T(8,128)(2,1)S(1)} %get-tuple-element.60), channel_id=1, source_target_pairs={{0,2},{1,3},{2,0},{3,1},{4,6},{5,7},{6,4},{7,5},{8,10},{9,11},{10,... | collective-permute-start | bytes 786440 | tf_op jit(solution)/shard_map/ppermute | solution.py:20
  75.9 7.6 %collective-permute-start.21 = (bf16[512,256]{1,0:T(8,128)(2,1)S(1)}, bf16[512,256]{1,0:T(8,128)(2,1)S(1)}, u32[]{:S(2)}, u32[]{:S(2)}) collective-permute-start(bf16[512,256]{1,0:T(8,128)(2,1)S(1)} %get-tuple-element.63), channel_id=1, source_target_pairs={{0,1},{1,0},{2,3},{3,2},{4,5},{5,4},{6,7},{7,6},{8,9},{9,8},{10,11... | collective-permute-start | bytes 786440 | tf_op jit(solution)/shard_map/ppermute | solution.py:20
  77.2 8.9 %collective-permute-start.22 = (bf16[512,256]{1,0:T(8,128)(2,1)S(1)}, bf16[512,256]{1,0:T(8,128)(2,1)S(1)}, u32[]{:S(2)}, u32[]{:S(2)}) collective-permute-start(bf16[512,256]{1,0:T(8,128)(2,1)S(1)} %get-tuple-element.65), channel_id=1, source_target_pairs={{0,2},{1,3},{2,0},{3,1},{4,6},{5,7},{6,4},{7,5},{8,10},{9,11},{10,... | collective-permute-start | bytes 786440 | tf_op jit(solution)/shard_map/ppermute | solution.py:20
  79.1 7.2 %collective-permute-start.23 = (bf16[512,256]{1,0:T(8,128)(2,1)S(1)}, bf16[512,256]{1,0:T(8,128)(2,1)S(1)}, u32[]{:S(2)}, u32[]{:S(2)}) collective-permute-start(bf16[512,256]{1,0:T(8,128)(2,1)S(1)} %get-tuple-element.66), channel_id=1, source_target_pairs={{0,1},{1,0},{2,3},{3,2},{4,5},{5,4},{6,7},{7,6},{8,9},{9,8},{10,11... | collective-permute-start | bytes 786440 | tf_op jit(solution)/shard_map/ppermute | solution.py:20

commit v8 on v7

--- a/solution.py
+++ b/solution.py
@@ -378,16 +378,10 @@
     )
 
 
-def split_body(rhs_ref, low_ref, high_ref, sems):
-    split = low_ref.shape[0]
-    copies = [
-        pltpu.make_async_copy(rhs_ref.at[pl.ds(index * split, ref.shape[0]), :], ref, sems.at[index])
-        for index, ref in enumerate((low_ref, high_ref))
-    ]
-    for copy in copies:
-        copy.start()
-    for copy in copies:
-        copy.wait()
+def split_body(rhs_ref, out_ref, sem, *, top):
+    copy = pltpu.make_async_copy(rhs_ref.at[pl.ds(top, out_ref.shape[0]), :], out_ref, sem)
+    copy.start()
+    copy.wait()
 
 
 def cut_body(whole_ref, *outs):
@@ -396,8 +390,13 @@
         ref[...] = whole_ref[:height, part * width : (part + 1) * width]
 
 
-def forward_body(own_ref, x_ref, y_ref, far_ref, *refs):
-    pieces, (out_0_ref, out_1_ref, turned_ref, factor_ref, loads_ref) = refs[:-5], refs[-5:]
+def row_blocks(rows):
+    height = math.gcd(rows, 2 * LANES)
+    return [slice(top, top + height) for top in range(0, rows, height)]
+
+
+def forward_body(own_ref, x_ref, y_ref, far_ref, dinv_ref, *refs):
+    pieces, (out_0_ref, out_1_ref, turned_ref, scale_ref, factor_ref, loads_ref) = refs[:-6], refs[-6:]
     rows = own_ref.shape[0]
     width = out_0_ref.shape[1]
     for index, ref in enumerate((own_ref, x_ref, y_ref)):
@@ -406,28 +405,34 @@
     for ref in pieces:
         loads_ref[start : start + ref.shape[0], :] = ref[...]
         start += ref.shape[0]
-    out_0_ref[...] = dot_tn(factor_ref[...], loads_ref[:, :width])
-    out_1_ref[...] = dot_tn(factor_ref[...], loads_ref[:, width:])
+    for block in row_blocks(rows):
+        product = dot_tn(factor_ref[:, block], loads_ref[...])
+        out_0_ref[block, :] = product[:, :width]
+        out_1_ref[block, :] = product[:, width:]
     turned_ref[...] = far_ref[...].T
-
-
-def far_body(far_ref, turned_ref, low_ref, high_ref, near_ref, dinv_ref, *refs, first):
-    kept = refs[:-5]
-    z_ref, relay_low_ref, relay_high_ref, loads_ref, part_ref = refs[-5:]
+    pivots = dinv_ref[...].astype(F32)
+    for tile in range(pivots.shape[0]):
+        block = slice(tile * LANES, (tile + 1) * LANES)
+        scale_ref[block, :] = jnp.broadcast_to(pivots[tile : tile + 1, :], (LANES, LANES)).T
+
+
+def far_body(far_ref, turned_ref, low_ref, high_ref, near_ref, scale_ref, *refs, first):
+    kept = refs[:-4]
+    z_ref, relay_low_ref, relay_high_ref, loads_ref = refs[-4:]
     split, half = low_ref.shape[0], relay_low_ref.shape[0]
-    rest = loads_ref.shape[0] - split
+    rows, width = z_ref.shape
+    rest = rows - split
     loads_ref[:split, :] = low_ref[...]
     loads_ref[split:, :] = high_ref[:rest, :]
-    part_ref[...] = near_ref[...] + dot_nn(turned_ref[...], loads_ref[...])
-    pivots = dinv_ref[...].astype(F32)
-    width = part_ref.shape[1]
-    for tile in range(pivots.shape[0]):
-        rows = slice(tile * LANES, (tile + 1) * LANES)
-        scale = jnp.broadcast_to(pivots[tile : tile + 1, :], (LANES, LANES)).T
-        scale = jnp.concatenate([scale] * (width // LANES), axis=1)
-        z_ref[rows, :] = (scale * part_ref[rows, :]).astype(BF16)
-    relay_low_ref[...] = dot_nn(far_ref[:half, :], z_ref[...]).astype(BF16)
-    relay_high_ref[:half, :] = dot_nn(far_ref[half:, :], z_ref[...]).astype(BF16)
+    for block in row_blocks(rows):
+        leaf_y = near_ref[block, :] + dot_nn(turned_ref[block, :], loads_ref[...])
+        scale = jnp.concatenate([scale_ref[block, :]] * (width // LANES), axis=1)
+        z_ref[block, :] = (scale * leaf_y).astype(BF16)
+    for block in row_blocks(half):
+        relay_low_ref[block, :] = dot_nn(far_ref[block, :], z_ref[...]).astype(BF16)
+    for block in row_blocks(half):
+        below = slice(half + block.start, half + block.stop)
+        relay_high_ref[block, :] = dot_nn(far_ref[below, :], z_ref[...]).astype(BF16)
     for kept_ref in kept:
         crossing = kept_ref[:first, LANES:] + high_ref[rest : rest + first, LANES:].astype(F32)
         relay_high_ref[half:, :LANES] = crossing.astype(BF16)
@@ -439,11 +444,16 @@
     half, split = x_low_ref.shape[0], z_0_ref.shape[1]
     z_ref[:, :split] = z_0_ref[...]
     z_ref[:, split:] = z_1_ref[...]
-    x_low_ref[...] = dot_nn(x_ref[:half, :], z_ref[...]).astype(BF16)
-    y_high_ref[...] = dot_nn(y_ref[half:, :], z_ref[...]).astype(BF16)
-    x_high_ref[...] = dot_nn(x_ref[half:, :], z_ref[...])
-    y_low_ref[...] = dot_nn(y_ref[:half, :], z_ref[...])
-    out_ref[...] = dot_nn(own_ref[...], z_ref[...])
+    for factor_ref, top, ref in (
+        (x_ref, 0, x_low_ref),
+        (y_ref, half, y_high_ref),
+        (x_ref, half, x_high_ref),
+        (y_ref, 0, y_low_ref),
+        (own_ref, 0, out_ref),
+    ):
+        for block in row_blocks(ref.shape[0]):
+            part = slice(top + block.start, top + block.stop)
+            ref[block, :] = dot_nn(factor_ref[part, :], z_ref[...]).astype(ref.dtype)
 
 
 def add_body(near_ref, relay_0_ref, relay_1_ref, out_0_ref, out_1_ref):
@@ -509,12 +519,16 @@
         return jax.ShapeDtypeStruct((height, breadth), F32)
 
     x_all = exchange(leaf_rhs, "grp", 1)
-    low, high = call(
-        split_body,
-        (pltpu.with_memory_space_constraint(leaf_rhs, pltpu.HBM),),
-        [pl.BlockSpec(memory_space=pltpu.HBM)],
-        (bf16(split, width), bf16(rows - split, width)),
-        scratch_shapes=[pltpu.SemaphoreType.DMA((2,))],
+    loads = pltpu.with_memory_space_constraint(leaf_rhs, pltpu.HBM)
+    high, low = (
+        call(
+            functools.partial(split_body, top=top),
+            (loads,),
+            [pl.BlockSpec(memory_space=pltpu.HBM)],
+            bf16(height, width),
+            scratch_shapes=[pltpu.SemaphoreType.DMA],
+        )
+        for top, height in ((split, rows - split), (0, split))
     )
     y_high = exchange(high, "grp", 2)
     y_low = exchange(low, "grp", 2)
@@ -537,11 +551,11 @@
     low_cut = call(cut_body, (x_all,), [vmem()], [bf16(split, width // 2)] * 2, after=(blocks[0],))
     d_low = [exchange(low_cut[part], "grp", 2) for part in parts]
 
-    *part_y, turned = call(
+    *part_y, turned, scale = call(
         forward_body,
-        (*blocks, low, high, x_all, y_low, y_high),
-        [vmem()] * 9,
-        [f32(rows, width // 2)] * 2 + [bf16(rows, rows)],
+        (*blocks, leaf_dinv.reshape(-1, LANES), low, high, x_all, y_low, y_high),
+        [vmem()] * 10,
+        [f32(rows, width // 2)] * 2 + [bf16(rows, rows), f32(rows, LANES)],
         scratch_shapes=[pltpu.VMEM((3 * rows, rows), BF16), pltpu.VMEM((3 * rows, width), BF16)],
     )
     leaf_z, relay_low, relay_high = [], [], []
@@ -555,7 +569,7 @@
                 d_low[part],
                 d_high[part],
                 part_y[part],
-                leaf_dinv.reshape(-1, LANES),
+                scale,
                 *shared,
             ),
             [vmem()] * (6 + len(shared)),
@@ -564,7 +578,7 @@
                 bf16(half, width // 2),
                 bf16(half + first * len(shared), width // 2),
             ),
-            scratch_shapes=[pltpu.VMEM((rows, width // 2), BF16), pltpu.VMEM((rows, width // 2), F32)],
+            scratch_shapes=[pltpu.VMEM((rows, width // 2), BF16)],
         )
         leaf_z.append(z_part)
         relay_low.append(exchange(far_low, "grp", 1))

time: 87.5 us -> 87.8 us (level)
  waiting for transfers between devices: 19.9 us -> 21.8 us
  Pallas kernels: 34.2 us -> 32.9 us
    ppermute x24, waiting for transfers between devices: 19.9 us -> 21.8 us  [exchange(): lax.ppermute(block, axis, [(low, low ^ mask) for low in range(count)])]
    pallas_call x16 -> x17, Pallas kernels: 34.2 us -> 32.9 us  [call(): pl.pallas_call(skipping, out_shape=out_shape, in_specs=[pl.BlockSpec(memo...]
  transfers between devices with their start and end apart: 24 -> 24, of which waited for: 12 -> 14; matrix products, arithmetic and copies ran while one was open for 1% -> 0% of each run, Pallas kernels for 38% -> 36%
where the time goes in v8:
time: 87.8 us; the launch traced here: 87.5 us
  Pallas kernels  32.9 us (37%)
  starting transfers between devices  32 us (36%)
  waiting for transfers between devices  21.8 us (25%)
    pallas_call x17, Pallas kernels, call(): pl.pallas_call(skipping, out_shape=out_shape, in_specs=[pl.BlockSpec(memo...  32.9 us
    ppermute x24, starting transfers between devices, exchange(): lax.ppermute(block, axis, [(low, low ^ mask) for low in range(count)])  32 us
    ppermute x24, waiting for transfers between devices, exchange(): lax.ppermute(block, axis, [(low, low ^ mask) for low in range(count)])  21.8 us
  transfers between devices with their start and end apart: 24, of which 14 were waited for; matrix products, arithmetic and copies ran while one was open for 0% of the time, Pallas kernels for 36%

profile of v8, /device:TPU:0, one launch (start us, length us, event | category | flops | bytes accessed | tf_op | source)
XLA Modules:
  0.0 87.5 jit_solution(12699450910316444367)
XLA Ops:
  0.6 3.0 %collective-permute-start = (bf16[1024,512]{1,0:T(8,128)(2,1)}, bf16[1024,512]{1,0:T(8,128)(2,1)S(1)}, u32[]{:S(2)}, u32[]{:S(2)}) collective-permute-start(bf16[1024,512]{1,0:T(8,128)(2,1)} %refs_0_.3), channel_id=1, source_target_pairs={{0,1},{1,0},{2,3},{3,2},{4,5},{5,4},{6,7},{7,6},{8,9},{9,8},{10,11... | collective-permute-start | bytes 3145736 | tf_op jit(solution)/shard_map/ppermute | solution.py:20
  3.7 1.1 %shard_map.97.refs_6_.refs_3_ = bf16[576,512]{1,0:T(8,128)(2,1)S(1)} custom-call(bf16[1024,512]{1,0:T(8,128)(2,1)} %refs_0_.3), custom_call_target="tpu_custom_call" | custom-call | tf_op jit(solution)/shard_map/pallas_call | solution.py:52
  4.8 1.6 %collective-permute-start.2 = (bf16[576,512]{1,0:T(8,128)(2,1)S(1)}, bf16[576,512]{1,0:T(8,128)(2,1)S(1)}, u32[]{:S(2)}, u32[]{:S(2)}) collective-permute-start(bf16[576,512]{1,0:T(8,128)(2,1)S(1)} %shard_map.97.refs_6_.refs_3_), channel_id=1, source_target_pairs={{0,2},{1,3},{2,0},{3,1},{4,6},{5,7},{6,4},{7,5},{8,10},{9,11},{10,... | collective-permute-start | bytes 1769480 | tf_op jit(solution)/shard_map/ppermute | solution.py:20
  6.4 1.0 %shard_map.96.refs_5_.refs_2_ = bf16[448,512]{1,0:T(8,128)(2,1)S(1)} custom-call(bf16[1024,512]{1,0:T(8,128)(2,1)} %refs_0_.3), custom_call_target="tpu_custom_call" | custom-call | tf_op jit(solution)/shard_map/pallas_call | solution.py:52
  7.4 0.6 collective-permute-start.1
  8.0 16.0 %shard_map.95 = (bf16[1024,1024]{1,0:T(8,128)(2,1)S(1)}, bf16[1024,1024]{1,0:T(8,128)(2,1)S(1)}, bf16[1024,1024]{1,0:T(8,128)(2,1)S(1)}, bf16[1024,1024]{1,0:T(8,128)(2,1)S(1)}) custom-call(s32[4096]{0:T(1024)S(1)} %fusion.2.refs_0_, bf16[1024,4096]{1,0:T(8,128)(2,1)} %refs_1_.1), custom_call_target="tpu_custom_call" | custom-call | tf_op jit(solution)/shard_map/pallas_call | solution.py:52
  24.1 0.3 shard_map.100
  24.5 3.3 %collective-permute-done.refs_7_.refs_1_ = bf16[1024,512]{1,0:T(8,128)(2,1)S(1)} collective-permute-done((bf16[1024,512]{1,0:T(8,128)(2,1)}, bf16[1024,512]{1,0:T(8,128)(2,1)S(1)}, u32[]{:S(2)}, u32[]{:S(2)}) %collective-permute-start) | collective-permute-done | bytes 1048608 | tf_op jit(solution)/shard_map/ppermute | solution.py:20
  27.9 2.1 %collective-permute-start.3 = (bf16[448,256]{1,0:T(8,128)(2,1)S(1)}, bf16[448,256]{1,0:T(8,128)(2,1)S(1)}, u32[]{:S(2)}, u32[]{:S(2)}) collective-permute-start(bf16[448,256]{1,0:T(8,128)(2,1)S(1)} %get-tuple-element.39), channel_id=1, source_target_pairs={{0,2},{1,3},{2,0},{3,1},{4,6},{5,7},{6,4},{7,5},{8,10},{9,11},{10,... | collective-permute-start | bytes 688136 | tf_op jit(solution)/shard_map/ppermute | solution.py:20
  30.0 1.5 %collective-permute-start.6 = (bf16[576,256]{1,0:T(8,128)(2,1)S(1)}, bf16[576,256]{1,0:T(8,128)(2,1)S(1)}, u32[]{:S(2)}, u32[]{:S(2)}) collective-permute-start(bf16[576,256]{1,0:T(8,128)(2,1)S(1)} %get-tuple-element.46), channel_id=1, source_target_pairs={{0,1},{1,0},{2,3},{3,2},{4,5},{5,4},{6,7},{7,6},{8,9},{9,8},{10,11... | collective-permute-start | bytes 884744 | tf_op jit(solution)/shard_map/ppermute | solution.py:20
  31.5 0.5 collective-permute-start.5
  32.0 3.5 %shard_map.98 = (f32[1024,256]{1,0:T(8,128)S(1)}, f32[1024,256]{1,0:T(8,128)S(1)}, bf16[1024,1024]{1,0:T(8,128)(2,1)S(1)}, f32[1024,128]{1,0:T(8,128)S(1)}) custom-call(bf16[1024,1024]{1,0:T(8,128)(2,1)S(1)} %get-tuple-element.34.refs_0_, bf16[1024,1024]{1,0:T(8,128)(2,1)S(1)} %get-tuple-element.35.refs_1_, ...), custom_call_target="tpu_custom_call" | custom-call | tf_op jit(solution)/shard_map/pallas_call | solution.py:52
  35.6 0.9 %collective-permute-done.3.refs_2_ = bf16[448,256]{1,0:T(8,128)(2,1)S(1)} collective-permute-done((bf16[448,256]{1,0:T(8,128)(2,1)S(1)}, bf16[448,256]{1,0:T(8,128)(2,1)S(1)}, u32[]{:S(2)}, u32[]{:S(2)}) %collective-permute-start.3) | collective-permute-done | bytes 229408 | tf_op jit(solution)/shard_map/ppermute | solution.py:20
  36.5 1.3 %shard_map.101 = (bf16[1024,256]{1,0:T(8,128)(2,1)S(1)}, bf16[512,256]{1,0:T(8,128)(2,1)S(1)}, bf16[544,256]{1,0:T(8,128)(2,1)S(1)}) custom-call(bf16[1024,1024]{1,0:T(8,128)(2,1)S(1)} %get-tuple-element.37.refs_3_.refs_0_, bf16[1024,1024]{1,0:T(8,128)(2,1)S(1)} %get-tuple-element.38.refs_1_, bf16[448,256]{1,0:T(8,128)(2,1)S(1)} %collective-permute-done.3.refs_2_, ...), custom_call_target="tpu_custom_call" | custom-call | tf_op jit(solution)/shard_map/pallas_call | solution.py:52
  37.8 1.9 %collective-permute-start.7 = (bf16[544,256]{1,0:T(8,128)(2,1)S(1)}, bf16[544,256]{1,0:T(8,128)(2,1)S(1)}, u32[]{:S(2)}, u32[]{:S(2)}) collective-permute-start(bf16[544,256]{1,0:T(8,128)(2,1)S(1)} %get-tuple-element.50), channel_id=1, source_target_pairs={{0,2},{1,3},{2,0},{3,1},{4,6},{5,7},{6,4},{7,5},{8,10},{9,11},{10,... | collective-permute-start | bytes 835592 | tf_op jit(solution)/shard_map/ppermute | solution.py:20
  39.7 0.5 collective-permute-done.6.refs_3_
  40.2 1.2 %collective-permute-done.5.refs_2_ = bf16[448,256]{1,0:T(8,128)(2,1)S(1)} collective-permute-done((bf16[448,256]{1,0:T(8,128)(2,1)S(1)}, bf16[448,256]{1,0:T(8,128)(2,1)S(1)}, u32[]{:S(2)}, u32[]{:S(2)}) %collective-permute-start.5) | collective-permute-done | bytes 229408 | tf_op jit(solution)/shard_map/ppermute | solution.py:20
  41.4 1.3 %shard_map.102 = (bf16[1024,256]{1,0:T(8,128)(2,1)S(1)}, bf16[512,256]{1,0:T(8,128)(2,1)S(1)}, bf16[512,256]{1,0:T(8,128)(2,1)S(1)}) custom-call(bf16[1024,1024]{1,0:T(8,128)(2,1)S(1)} %get-tuple-element.37.refs_3_.refs_0_, bf16[1024,1024]{1,0:T(8,128)(2,1)S(1)} %get-tuple-element.38.refs_1_, bf16[448,256]{1,0:T(8,128)(2,1)S(1)} %collective-permute-done.5.refs_2_, ...), custom_call_target="tpu_custom_call" | custom-call | tf_op jit(solution)/shard_map/pallas_call | solution.py:52
  42.7 3.4 %shard_map.103 = (bf16[512,512]{1,0:T(8,128)(2,1)S(1)}, bf16[512,512]{1,0:T(8,128)(2,1)S(1)}, f32[512,512]{1,0:T(8,128)S(1)}, f32[512,512]{1,0:T(8,128)S(1)}, f32[1024,512]{1,0:T(8,128)S(1)}) custom-call(bf16[1024,1024]{1,0:T(8,128)(2,1)S(1)} %get-tuple-element.34.refs_0_, bf16[1024,1024]{1,0:T(8,128)(2,1)S(1)} %get-tuple-element.35.refs_1_, ...), custom_call_target="tpu_custom_call" | custom-call | tf_op jit(solution)/shard_map/pallas_call | solution.py:52
  46.2 0.7 collective-permute-start.15
  46.9 0.1 shard_map.104.refs_0_
  47.0 1.2 %collective-permute-done.8.refs_1_ = bf16[144,128]{1,0:T(8,128)(2,1)S(1)} collective-permute-done((bf16[144,128]{1,0:T(8,128)(2,1)S(1)}, bf16[144,128]{1,0:T(8,128)(2,1)S(1)}, u32[]{:S(2)}, u32[]{:S(2)}) %collective-permute-start.8) | collective-permute-done | bytes 36896 | tf_op jit(solution)/shard_map/ppermute | solution.py:20
  48.3 1.6 %collective-permute-start.9 = (bf16[224,128]{1,0:T(8,128)(2,1)S(1)}, bf16[224,128]{1,0:T(8,128)(2,1)S(1)}, u32[]{:S(2)}, u32[]{:S(2)}) collective-permute-start(bf16[224,128]{1,0:T(8,128)(2,1)S(1)} %shard_map.105.refs_0_), channel_id=1, source_target_pairs={{0,8},{4,12},{8,0},{12,4},{16,24},{20,28},{24,16},{28,20},{1,9},{5... | collective-permute-start | bytes 172040 | tf_op jit(solution)/shard_map/ppermute | solution.py:20
  49.9 2.6 %collective-permute-start.10 = (bf16[224,128]{1,0:T(8,128)(2,1)S(1)}, bf16[224,128]{1,0:T(8,128)(2,1)S(1)}, u32[]{:S(2)}, u32[]{:S(2)}) collective-permute-start(bf16[224,128]{1,0:T(8,128)(2,1)S(1)} %shard_map.105.refs_0_), channel_id=1, source_target_pairs={{0,16},{4,20},{8,24},{12,28},{16,0},{20,4},{24,8},{28,12},{1,17},{... | collective-permute-start | bytes 172040 | tf_op jit(solution)/shard_map/ppermute | solution.py:20
  52.5 0.2 collective-permute-start.11
  52.7 1.4 %collective-permute-start.17 = (bf16[512,256]{1,0:T(8,128)(2,1)S(1)}, bf16[512,256]{1,0:T(8,128)(2,1)S(1)}, u32[]{:S(2)}, u32[]{:S(2)}) collective-permute-start(bf16[512,256]{1,0:T(8,128)(2,1)S(1)} %get-tuple-element.56), channel_id=1, source_target_pairs={{0,1},{1,0},{2,3},{3,2},{4,5},{5,4},{6,7},{7,6},{8,9},{9,8},{10,11... | collective-permute-start | bytes 786440 | tf_op jit(solution)/shard_map/ppermute | solution.py:20
  54.1 0.6 collective-permute-start.18
  54.7 1.6 %collective-permute-done.10.refs_2_ = bf16[224,128]{1,0:T(8,128)(2,1)S(1)} collective-permute-done((bf16[224,128]{1,0:T(8,128)(2,1)S(1)}, bf16[224,128]{1,0:T(8,128)(2,1)S(1)}, u32[]{:S(2)}, u32[]{:S(2)}) %collective-permute-start.10) | collective-permute-done | bytes 57376 | tf_op jit(solution)/shard_map/ppermute | solution.py:20
  56.3 1.5 %collective-permute-start.20 = (bf16[512,256]{1,0:T(8,128)(2,1)S(1)}, bf16[512,256]{1,0:T(8,128)(2,1)S(1)}, u32[]{:S(2)}, u32[]{:S(2)}) collective-permute-start(bf16[512,256]{1,0:T(8,128)(2,1)S(1)} %get-tuple-element.60), channel_id=1, source_target_pairs={{0,2},{1,3},{2,0},{3,1},{4,6},{5,7},{6,4},{7,5},{8,10},{9,11},{10,... | collective-permute-start | bytes 786440 | tf_op jit(solution)/shard_map/ppermute | solution.py:20
  57.8 0.6 collective-permute-done.11.refs_3_
  58.5 1.5 %collective-permute-start.16 = (bf16[512,512]{1,0:T(8,128)(2,1)S(1)}, bf16[512,512]{1,0:T(8,128)(2,1)S(1)}, u32[]{:S(2)}, u32[]{:S(2)}) collective-permute-start(bf16[512,512]{1,0:T(8,128)(2,1)S(1)} %get-tuple-element.53), channel_id=1, source_target_pairs={{0,2},{1,3},{2,0},{3,1},{4,6},{5,7},{6,4},{7,5},{8,10},{9,11},{10,... | collective-permute-start | bytes 1572872 | tf_op jit(solution)/shard_map/ppermute | solution.py:20
  60.0 1.9 %shard_map.106 = (bf16[32,128]{1,0:T(8,128)(2,1)S(1)}, f32[3,16,128]{2,1,0:T(8,128)}) custom-call(bf16[224,128]{1,0:T(8,128)(2,1)S(1)} %shard_map.105.refs_0_, bf16[224,128]{1,0:T(8,128)(2,1)S(1)} %collective-permute-done.9.refs_1_, bf16[224,128]{1,0:T(8,128)(2,1)S(1)} %collective-permute-done.10.refs_2_, bf16[224,128]{1,0:T(8,128)(2,1)S(1)} %collective-permute-done.11.refs_3_), custom_call_target="tpu_custom_call" | custom-call | tf_op jit(solution)/shard_map/pallas_call | solution.py:52
  61.9 4.6 %collective-permute-done.17.refs_1_ = bf16[512,256]{1,0:T(8,128)(2,1)S(1)} collective-permute-done((bf16[512,256]{1,0:T(8,128)(2,1)S(1)}, bf16[512,256]{1,0:T(8,128)(2,1)S(1)}, u32[]{:S(2)}, u32[]{:S(2)}) %collective-permute-start.17) | collective-permute-done | bytes 262176 | tf_op jit(solution)/shard_map/ppermute | solution.py:20
  66.5 0.8 collective-permute-start.12
  67.3 2.0 %collective-permute-done.18.refs_2_ = bf16[512,256]{1,0:T(8,128)(2,1)S(1)} collective-permute-done((bf16[512,256]{1,0:T(8,128)(2,1)S(1)}, bf16[512,256]{1,0:T(8,128)(2,1)S(1)}, u32[]{:S(2)}, u32[]{:S(2)}) %collective-permute-start.18) | collective-permute-done | bytes 262176 | tf_op jit(solution)/shard_map/ppermute | solution.py:20
  69.3 1.6 %collective-permute-start.13 = (bf16[32,128]{1,0:T(8,128)(2,1)S(1)}, bf16[32,128]{1,0:T(8,128)(2,1)S(1)}, u32[]{:S(2)}, u32[]{:S(2)}) collective-permute-start(bf16[32,128]{1,0:T(8,128)(2,1)S(1)} %get-tuple-element.51.refs_2_), channel_id=1, source_target_pairs={{0,2},{1,3},{2,0},{3,1},{4,6},{5,7},{6,4},{7,5},{8,10},{9,11},{10,... | collective-permute-start | bytes 24584 | tf_op jit(solution)/shard_map/ppermute | solution.py:20
  71.0 1.4 %collective-permute-start.14 = (bf16[32,128]{1,0:T(8,128)(2,1)S(1)}, bf16[32,128]{1,0:T(8,128)(2,1)S(1)}, u32[]{:S(2)}, u32[]{:S(2)}) collective-permute-start(bf16[32,128]{1,0:T(8,128)(2,1)S(1)} %get-tuple-element.51.refs_2_), channel_id=1, source_target_pairs={{0,3},{1,2},{2,1},{3,0},{4,7},{5,6},{6,5},{7,4},{8,11},{9,10},{10,... | collective-permute-start | bytes 24584 | tf_op jit(solution)/shard_map/ppermute | solution.py:20
  72.6 1.6 %collective-permute-start.19 = (bf16[512,256]{1,0:T(8,128)(2,1)S(1)}, bf16[512,256]{1,0:T(8,128)(2,1)S(1)}, u32[]{:S(2)}, u32[]{:S(2)}) collective-permute-start(bf16[512,256]{1,0:T(8,128)(2,1)S(1)} %get-tuple-element.58), channel_id=1, source_target_pairs={{0,2},{1,3},{2,0},{3,1},{4,6},{5,7},{6,4},{7,5},{8,10},{9,11},{10,... | collective-permute-start | bytes 786440 | tf_op jit(solution)/shard_map/ppermute | solution.py:20
  74.2 0.9 %collective-permute-done.13.refs_4_ = bf16[32,128]{1,0:T(8,128)(2,1)S(1)} collective-permute-done((bf16[32,128]{1,0:T(8,128)(2,1)S(1)}, bf16[32,128]{1,0:T(8,128)(2,1)S(1)}, u32[]{:S(2)}, u32[]{:S(2)}) %collective-permute-start.13) | collective-permute-done | bytes 8224 | tf_op jit(solution)/shard_map/ppermute | solution.py:20
  75.2 2.8 %collective-permute-start.21 = (bf16[512,256]{1,0:T(8,128)(2,1)S(1)}, bf16[512,256]{1,0:T(8,128)(2,1)S(1)}, u32[]{:S(2)}, u32[]{:S(2)}) collective-permute-start(bf16[512,256]{1,0:T(8,128)(2,1)S(1)} %get-tuple-element.61), channel_id=1, source_target_pairs={{0,1},{1,0},{2,3},{3,2},{4,5},{5,4},{6,7},{7,6},{8,9},{9,8},{10,11... | collective-permute-start | bytes 786440 | tf_op jit(solution)/shard_map/ppermute | solution.py:20
  77.9 2.2 %collective-permute-start.22 = (bf16[512,256]{1,0:T(8,128)(2,1)S(1)}, bf16[512,256]{1,0:T(8,128)(2,1)S(1)}, u32[]{:S(2)}, u32[]{:S(2)}) collective-permute-start(bf16[512,256]{1,0:T(8,128)(2,1)S(1)} %get-tuple-element.63), channel_id=1, source_target_pairs={{0,2},{1,3},{2,0},{3,1},{4,6},{5,7},{6,4},{7,5},{8,10},{9,11},{10,... | collective-permute-start | bytes 786440 | tf_op jit(solution)/shard_map/ppermute | solution.py:20
  80.2 0.5 shard_map.107
  80.6 1.2 %collective-permute-done.19.refs_1_ = bf16[512,256]{1,0:T(8,128)(2,1)S(1)} collective-permute-done((bf16[512,256]{1,0:T(8,128)(2,1)S(1)}, bf16[512,256]{1,0:T(8,128)(2,1)S(1)}, u32[]{:S(2)}, u32[]{:S(2)}) %collective-permute-start.19) | collective-permute-done | bytes 262176 | tf_op jit(solution)/shard_map/ppermute | solution.py:20
  81.9 0.6 collective-permute-done.21.refs_2_
  82.5 1.0 %shard_map.110.refs_0_ = f32[1024,512]{1,0:T(8,128)} custom-call(f32[1024,256]{1,0:T(8,128)S(1)} %get-tuple-element.54.refs_0_, bf16[512,256]{1,0:T(8,128)(2,1)S(1)} %collective-permute-done.19.refs_1_, bf16[512,256]{1,0:T(8,128)(2,1)S(1)} %collective-permute-done.21.refs_2_), custom_call_target="tpu_custom_call" | custom-call | tf_op jit(solution)/shard_map/pallas_call | solution.py:52
  83.5 1.8 %collective-permute-done.22.refs_2_ = bf16[512,256]{1,0:T(8,128)(2,1)S(1)} collective-permute-done((bf16[512,256]{1,0:T(8,128)(2,1)S(1)}, bf16[512,256]{1,0:T(8,128)(2,1)S(1)}, u32[]{:S(2)}, u32[]{:S(2)}) %collective-permute-start.22) | collective-permute-done | bytes 262176 | tf_op jit(solution)/shard_map/ppermute | solution.py:20
  85.3 1.3 %collective-permute-done.23.refs_3_ = bf16[512,256]{1,0:T(8,128)(2,1)S(1)} collective-permute-done((bf16[512,256]{1,0:T(8,128)(2,1)S(1)}, bf16[512,256]{1,0:T(8,128)(2,1)S(1)}, u32[]{:S(2)}, u32[]{:S(2)}) %collective-permute-start.23) | collective-permute-done | bytes 262176 | tf_op jit(solution)/shard_map/ppermute | solution.py:20
  86.5 1.0 %shard_map.111 = f32[1024,512]{1,0:T(8,128)} custom-call(f32[1024,512]{1,0:T(8,128)} %shard_map.110.refs_0_, f32[1024,256]{1,0:T(8,128)S(1)} %get-tuple-element.62.refs_1_, bf16[512,256]{1,0:T(8,128)(2,1)S(1)} %collective-permute-done.22.refs_2_, bf16[512,256]{1,0:T(8,128)(2,1)S(1)} %collective-permute-done.23.refs_3_), custom_call_target="tpu_custom_call", output_to_operand_aliasing={{}: (0, {})} | custom-call | tf_op jit(solution)/shard_map/pallas_call | solution.py:52
  (30 shorter events, 0.5 us)
Async XLA Ops:
  0.6 7.3 %copy-start.5 = (s32[1,4096]{1,0:T(1,128)S(1)}, s32[1,4096]{1,0:T(1,128)}, u32[]{:S(2)}) copy-start(s32[1,4096]{1,0:T(1,128)} %param.10) | copy-start | bytes 49156
  0.6 27.3 %collective-permute-start = (bf16[1024,512]{1,0:T(8,128)(2,1)}, bf16[1024,512]{1,0:T(8,128)(2,1)S(1)}, u32[]{:S(2)}, u32[]{:S(2)}) collective-permute-start(bf16[1024,512]{1,0:T(8,128)(2,1)} %refs_0_.3), channel_id=1, source_target_pairs={{0,1},{1,0},{2,3},{3,2},{4,5},{5,4},{6,7},{7,6},{8,9},{9,8},{10,11... | collective-permute-start | bytes 3145736 | tf_op jit(solution)/shard_map/ppermute | solution.py:20
  4.8 19.3 %collective-permute-start.2 = (bf16[576,512]{1,0:T(8,128)(2,1)S(1)}, bf16[576,512]{1,0:T(8,128)(2,1)S(1)}, u32[]{:S(2)}, u32[]{:S(2)}) collective-permute-start(bf16[576,512]{1,0:T(8,128)(2,1)S(1)} %shard_map.97.refs_6_.refs_3_), channel_id=1, source_target_pairs={{0,2},{1,3},{2,0},{3,1},{4,6},{5,7},{6,4},{7,5},{8,10},{9,11},{10,... | collective-permute-start | bytes 1769480 | tf_op jit(solution)/shard_map/ppermute | solution.py:20
  7.4 24.6 %collective-permute-start.1 = (bf16[448,512]{1,0:T(8,128)(2,1)S(1)}, bf16[448,512]{1,0:T(8,128)(2,1)S(1)}, u32[]{:S(2)}, u32[]{:S(2)}) collective-permute-start(bf16[448,512]{1,0:T(8,128)(2,1)S(1)} %shard_map.96.refs_5_.refs_2_), channel_id=1, source_target_pairs={{0,2},{1,3},{2,0},{3,1},{4,6},{5,7},{6,4},{7,5},{8,10},{9,11},{10,... | collective-permute-start | bytes 1376264 | tf_op jit(solution)/shard_map/ppermute | solution.py:20
  8.0 16.0 %copy-start = (bf16[1024,32]{0,1:T(8,128)(2,1)S(1)}, bf16[1024,32]{0,1:T(8,128)(2,1)}, u32[]{:S(2)}) copy-start(bf16[1024,32]{0,1:T(8,128)(2,1)} %param.12) | copy-start | bytes 196612
  8.0 16.0 %copy-start.2 = (bf16[4,416]{1,0:T(4,128)(2,1)S(1)}, bf16[4,416]{1,0:T(4,128)(2,1)}, u32[]{:S(2)}) copy-start(bf16[4,416]{1,0:T(4,128)(2,1)} %refs_5_.2) | copy-start | bytes 9988
  24.4 7.6 %copy-start.3 = (bf16[1024]{0:T(1024)(128)(2,1)S(1)}, bf16[1024]{0:T(1024)(128)(2,1)}, u32[]{:S(2)}) copy-start(bf16[1024]{0:T(1024)(128)(2,1)} %param.11) | copy-start | bytes 6148
  24.4 11.1 %collective-permute-start.4 = (bf16[624,256]{1,0:T(8,128)(2,1)S(1)}, bf16[624,256]{1,0:T(8,128)(2,1)S(1)}, u32[]{:S(2)}, u32[]{:S(2)}) collective-permute-start(bf16[624,256]{1,0:T(8,128)(2,1)S(1)} %get-tuple-element.40), channel_id=1, source_target_pairs={{0,1},{1,0},{2,3},{3,2},{4,5},{5,4},{6,7},{7,6},{8,9},{9,8},{10,11... | collective-permute-start | bytes 958472 | tf_op jit(solution)/shard_map/ppermute | solution.py:20
  27.9 8.6 %collective-permute-start.3 = (bf16[448,256]{1,0:T(8,128)(2,1)S(1)}, bf16[448,256]{1,0:T(8,128)(2,1)S(1)}, u32[]{:S(2)}, u32[]{:S(2)}) collective-permute-start(bf16[448,256]{1,0:T(8,128)(2,1)S(1)} %get-tuple-element.39), channel_id=1, source_target_pairs={{0,2},{1,3},{2,0},{3,1},{4,6},{5,7},{6,4},{7,5},{8,10},{9,11},{10,... | collective-permute-start | bytes 688136 | tf_op jit(solution)/shard_map/ppermute | solution.py:20
  30.0 10.2 %collective-permute-start.6 = (bf16[576,256]{1,0:T(8,128)(2,1)S(1)}, bf16[576,256]{1,0:T(8,128)(2,1)S(1)}, u32[]{:S(2)}, u32[]{:S(2)}) collective-permute-start(bf16[576,256]{1,0:T(8,128)(2,1)S(1)} %get-tuple-element.46), channel_id=1, source_target_pairs={{0,1},{1,0},{2,3},{3,2},{4,5},{5,4},{6,7},{7,6},{8,9},{9,8},{10,11... | collective-permute-start | bytes 884744 | tf_op jit(solution)/shard_map/ppermute | solution.py:20
  31.5 9.9 %collective-permute-start.5 = (bf16[448,256]{1,0:T(8,128)(2,1)S(1)}, bf16[448,256]{1,0:T(8,128)(2,1)S(1)}, u32[]{:S(2)}, u32[]{:S(2)}) collective-permute-start(bf16[448,256]{1,0:T(8,128)(2,1)S(1)} %get-tuple-element.45), channel_id=1, source_target_pairs={{0,2},{1,3},{2,0},{3,1},{4,6},{5,7},{6,4},{7,5},{8,10},{9,11},{10,... | collective-permute-start | bytes 688136 | tf_op jit(solution)/shard_map/ppermute | solution.py:20
  37.8 9.1 %collective-permute-start.7 = (bf16[544,256]{1,0:T(8,128)(2,1)S(1)}, bf16[544,256]{1,0:T(8,128)(2,1)S(1)}, u32[]{:S(2)}, u32[]{:S(2)}) collective-permute-start(bf16[544,256]{1,0:T(8,128)(2,1)S(1)} %get-tuple-element.50), channel_id=1, source_target_pairs={{0,2},{1,3},{2,0},{3,1},{4,6},{5,7},{6,4},{7,5},{8,10},{9,11},{10,... | collective-permute-start | bytes 835592 | tf_op jit(solution)/shard_map/ppermute | solution.py:20
  42.7 4.2 %copy-start.1 = (bf16[3,128,16]{1,2,0:T(8,128)(2,1)S(1)}, bf16[3,128,16]{1,2,0:T(8,128)(2,1)}, u32[]{:S(2)}) copy-start(bf16[3,128,16]{1,2,0:T(8,128)(2,1)} %param.13) | copy-start | bytes 36868
  42.7 4.1 %copy-start.4 = (bf16[3,16]{1,0:T(4,128)(2,1)S(1)}, bf16[3,16]{1,0:T(4,128)(2,1)}, u32[]{:S(2)}) copy-start(bf16[3,16]{1,0:T(4,128)(2,1)} %refs_5_.3) | copy-start | bytes 292
  46.2 34.0 %collective-permute-start.15 = (bf16[512,512]{1,0:T(8,128)(2,1)S(1)}, bf16[512,512]{1,0:T(8,128)(2,1)S(1)}, u32[]{:S(2)}, u32[]{:S(2)}) collective-permute-start(bf16[512,512]{1,0:T(8,128)(2,1)S(1)} %get-tuple-element.52), channel_id=1, source_target_pairs={{0,1},{1,0},{2,3},{3,2},{4,5},{5,4},{6,7},{7,6},{8,9},{9,8},{10,11... | collective-permute-start | bytes 1572872 | tf_op jit(solution)/shard_map/ppermute | solution.py:20
  47.0 1.2 %collective-permute-start.8 = (bf16[144,128]{1,0:T(8,128)(2,1)S(1)}, bf16[144,128]{1,0:T(8,128)(2,1)S(1)}, u32[]{:S(2)}, u32[]{:S(2)}) collective-permute-start(bf16[144,128]{1,0:T(8,128)(2,1)S(1)} %shard_map.104.refs_0_), channel_id=1, source_target_pairs={{0,4},{4,0},{8,12},{12,8},{16,20},{20,16},{24,28},{28,24},{1,5},{5... | collective-permute-start | bytes 110600 | tf_op jit(solution)/shard_map/ppermute | solution.py:20
  48.3 5.9 %collective-permute-start.9 = (bf16[224,128]{1,0:T(8,128)(2,1)S(1)}, bf16[224,128]{1,0:T(8,128)(2,1)S(1)}, u32[]{:S(2)}, u32[]{:S(2)}) collective-permute-start(bf16[224,128]{1,0:T(8,128)(2,1)S(1)} %shard_map.105.refs_0_), channel_id=1, source_target_pairs={{0,8},{4,12},{8,0},{12,4},{16,24},{20,28},{24,16},{28,20},{1,9},{5... | collective-permute-start | bytes 172040 | tf_op jit(solution)/shard_map/ppermute | solution.py:20
  49.9 6.4 %collective-permute-start.10 = (bf16[224,128]{1,0:T(8,128)(2,1)S(1)}, bf16[224,128]{1,0:T(8,128)(2,1)S(1)}, u32[]{:S(2)}, u32[]{:S(2)}) collective-permute-start(bf16[224,128]{1,0:T(8,128)(2,1)S(1)} %shard_map.105.refs_0_), channel_id=1, source_target_pairs={{0,16},{4,20},{8,24},{12,28},{16,0},{20,4},{24,8},{28,12},{1,17},{... | collective-permute-start | bytes 172040 | tf_op jit(solution)/shard_map/ppermute | solution.py:20
  52.5 6.0 %collective-permute-start.11 = (bf16[224,128]{1,0:T(8,128)(2,1)S(1)}, bf16[224,128]{1,0:T(8,128)(2,1)S(1)}, u32[]{:S(2)}, u32[]{:S(2)}) collective-permute-start(bf16[224,128]{1,0:T(8,128)(2,1)S(1)} %shard_map.105.refs_0_), channel_id=1, source_target_pairs={{0,24},{4,28},{8,16},{12,20},{16,8},{20,12},{24,0},{28,4},{1,25},{... | collective-permute-start | bytes 172040 | tf_op jit(solution)/shard_map/ppermute | solution.py:20
  52.7 13.8 %collective-permute-start.17 = (bf16[512,256]{1,0:T(8,128)(2,1)S(1)}, bf16[512,256]{1,0:T(8,128)(2,1)S(1)}, u32[]{:S(2)}, u32[]{:S(2)}) collective-permute-start(bf16[512,256]{1,0:T(8,128)(2,1)S(1)} %get-tuple-element.56), channel_id=1, source_target_pairs={{0,1},{1,0},{2,3},{3,2},{4,5},{5,4},{6,7},{7,6},{8,9},{9,8},{10,11... | collective-permute-start | bytes 786440 | tf_op jit(solution)/shard_map/ppermute | solution.py:20
  54.1 15.2 %collective-permute-start.18 = (bf16[512,256]{1,0:T(8,128)(2,1)S(1)}, bf16[512,256]{1,0:T(8,128)(2,1)S(1)}, u32[]{:S(2)}, u32[]{:S(2)}) collective-permute-start(bf16[512,256]{1,0:T(8,128)(2,1)S(1)} %get-tuple-element.57), channel_id=1, source_target_pairs={{0,1},{1,0},{2,3},{3,2},{4,5},{5,4},{6,7},{7,6},{8,9},{9,8},{10,11... | collective-permute-start | bytes 786440 | tf_op jit(solution)/shard_map/ppermute | solution.py:20
  56.3 14.7 %collective-permute-start.20 = (bf16[512,256]{1,0:T(8,128)(2,1)S(1)}, bf16[512,256]{1,0:T(8,128)(2,1)S(1)}, u32[]{:S(2)}, u32[]{:S(2)}) collective-permute-start(bf16[512,256]{1,0:T(8,128)(2,1)S(1)} %get-tuple-element.60), channel_id=1, source_target_pairs={{0,2},{1,3},{2,0},{3,1},{4,6},{5,7},{6,4},{7,5},{8,10},{9,11},{10,... | collective-permute-start | bytes 786440 | tf_op jit(solution)/shard_map/ppermute | solution.py:20
  58.5 21.7 %collective-permute-start.16 = (bf16[512,512]{1,0:T(8,128)(2,1)S(1)}, bf16[512,512]{1,0:T(8,128)(2,1)S(1)}, u32[]{:S(2)}, u32[]{:S(2)}) collective-permute-start(bf16[512,512]{1,0:T(8,128)(2,1)S(1)} %get-tuple-element.53), channel_id=1, source_target_pairs={{0,2},{1,3},{2,0},{3,1},{4,6},{5,7},{6,4},{7,5},{8,10},{9,11},{10,... | collective-permute-start | bytes 1572872 | tf_op jit(solution)/shard_map/ppermute | solution.py:20
  66.5 6.1 %collective-permute-start.12 = (bf16[32,128]{1,0:T(8,128)(2,1)S(1)}, bf16[32,128]{1,0:T(8,128)(2,1)S(1)}, u32[]{:S(2)}, u32[]{:S(2)}) collective-permute-start(bf16[32,128]{1,0:T(8,128)(2,1)S(1)} %get-tuple-element.51.refs_2_), channel_id=1, source_target_pairs={{0,1},{1,0},{2,3},{3,2},{4,5},{5,4},{6,7},{7,6},{8,9},{9,8},{10,11... | collective-permute-start | bytes 24584 | tf_op jit(solution)/shard_map/ppermute | solution.py:20
  69.3 5.8 %collective-permute-start.13 = (bf16[32,128]{1,0:T(8,128)(2,1)S(1)}, bf16[32,128]{1,0:T(8,128)(2,1)S(1)}, u32[]{:S(2)}, u32[]{:S(2)}) collective-permute-start(bf16[32,128]{1,0:T(8,128)(2,1)S(1)} %get-tuple-element.51.refs_2_), channel_id=1, source_target_pairs={{0,2},{1,3},{2,0},{3,1},{4,6},{5,7},{6,4},{7,5},{8,10},{9,11},{10,... | collective-permute-start | bytes 24584 | tf_op jit(solution)/shard_map/ppermute | solution.py:20
  71.0 7.0 %collective-permute-start.14 = (bf16[32,128]{1,0:T(8,128)(2,1)S(1)}, bf16[32,128]{1,0:T(8,128)(2,1)S(1)}, u32[]{:S(2)}, u32[]{:S(2)}) collective-permute-start(bf16[32,128]{1,0:T(8,128)(2,1)S(1)} %get-tuple-element.51.refs_2_), channel_id=1, source_target_pairs={{0,3},{1,2},{2,1},{3,0},{4,7},{5,6},{6,5},{7,4},{8,11},{9,10},{10,... | collective-permute-start | bytes 24584 | tf_op jit(solution)/shard_map/ppermute | solution.py:20
  72.6 9.2 %collective-permute-start.19 = (bf16[512,256]{1,0:T(8,128)(2,1)S(1)}, bf16[512,256]{1,0:T(8,128)(2,1)S(1)}, u32[]{:S(2)}, u32[]{:S(2)}) collective-permute-start(bf16[512,256]{1,0:T(8,128)(2,1)S(1)} %get-tuple-element.58), channel_id=1, source_target_pairs={{0,2},{1,3},{2,0},{3,1},{4,6},{5,7},{6,4},{7,5},{8,10},{9,11},{10,... | collective-permute-start | bytes 786440 | tf_op jit(solution)/shard_map/ppermute | solution.py:20
  75.2 7.3 %collective-permute-start.21 = (bf16[512,256]{1,0:T(8,128)(2,1)S(1)}, bf16[512,256]{1,0:T(8,128)(2,1)S(1)}, u32[]{:S(2)}, u32[]{:S(2)}) collective-permute-start(bf16[512,256]{1,0:T(8,128)(2,1)S(1)} %get-tuple-element.61), channel_id=1, source_target_pairs={{0,1},{1,0},{2,3},{3,2},{4,5},{5,4},{6,7},{7,6},{8,9},{9,8},{10,11... | collective-permute-start | bytes 786440 | tf_op jit(solution)/shard_map/ppermute | solution.py:20
  77.9 7.3 %collective-permute-start.22 = (bf16[512,256]{1,0:T(8,128)(2,1)S(1)}, bf16[512,256]{1,0:T(8,128)(2,1)S(1)}, u32[]{:S(2)}, u32[]{:S(2)}) collective-permute-start(bf16[512,256]{1,0:T(8,128)(2,1)S(1)} %get-tuple-element.63), channel_id=1, source_target_pairs={{0,2},{1,3},{2,0},{3,1},{4,6},{5,7},{6,4},{7,5},{8,10},{9,11},{10,... | collective-permute-start | bytes 786440 | tf_op jit(solution)/shard_map/ppermute | solution.py:20
  80.1 6.4 %collective-permute-start.23 = (bf16[512,256]{1,0:T(8,128)(2,1)S(1)}, bf16[512,256]{1,0:T(8,128)(2,1)S(1)}, u32[]{:S(2)}, u32[]{:S(2)}) collective-permute-start(bf16[512,256]{1,0:T(8,128)(2,1)S(1)} %get-tuple-element.64), channel_id=1, source_target_pairs={{0,1},{1,0},{2,3},{3,2},{4,5},{5,4},{6,7},{7,6},{8,9},{9,8},{10,11... | collective-permute-start | bytes 786440 | tf_op jit(solution)/shard_map/ppermute | solution.py:20

commit v9 on v8

--- a/solution.py
+++ b/solution.py
@@ -12,6 +12,7 @@
 F32 = jnp.float32
 BF16 = jnp.bfloat16
 LANES = 128
+GRP, LEAF = "grp", "leaf"
 UNROLL = 32
 
 
@@ -69,11 +70,11 @@
 
 
 def partner(values, level_bit):
-    return from_partner(values.astype(jnp.bfloat16), "leaf", level_bit).astype(values.dtype)
+    return from_partner(values.astype(jnp.bfloat16), LEAF, level_bit).astype(values.dtype)
 
 
 def leaf_bit(level_bit):
-    return jnp.right_shift(lax.axis_index("leaf"), level_bit) % 2
+    return jnp.right_shift(lax.axis_index(LEAF), level_bit) % 2
 
 
 def spread(values, first_bit, last_bit):
@@ -98,7 +99,7 @@
 
 
 def group_rows(values):
-    return lax.all_gather(values, "grp", axis=0, tiled=True)
+    return lax.all_gather(values, GRP, axis=0, tiled=True)
 
 
 def level_width(sep_block, tree_level):
@@ -114,12 +115,12 @@
     picked = jnp.take(leaf_inv, inverse, axis=1)
     leaf_y = jnp.dot(
         picked,
-        lax.all_gather(leaf_rhs, "grp", axis=0, tiled=True),
+        lax.all_gather(leaf_rhs, GRP, axis=0, tiled=True),
         preferred_element_type=jnp.float32,
     )
     partial_sum = jnp.einsum("rk,rc->kc", leaf_rhs, leaf_link, preferred_element_type=jnp.float32)
     crossing = lax.psum_scatter(
-        partial_sum.astype(jnp.bfloat16), "grp", scatter_dimension=0, tiled=True
+        partial_sum.astype(jnp.bfloat16), GRP, scatter_dimension=0, tiled=True
     ).astype(jnp.float32)
     leaf_z = (leaf_dinv.astype(jnp.float32)[:, None] * leaf_y).astype(jnp.bfloat16)
     crossing = halve_sum(crossing, [0])
@@ -186,7 +187,7 @@
         jnp.einsum("rm,rk->mk", picked, leaf_z, preferred_element_type=jnp.float32).astype(
             jnp.bfloat16
         ),
-        "grp",
+        GRP,
         scatter_dimension=0,
         tiled=True,
     ).astype(jnp.float32)
@@ -196,7 +197,7 @@
     return (leaf_x, jnp.stack(solution, axis=0))
 
 
-def send_body(whole_ref, low_ref, high_ref, link_ref, fac_ref, out_0_ref, out_1_ref, kept_ref, crossing_ref):
+def run_send(whole_ref, low_ref, high_ref, link_ref, fac_ref, out_0_ref, out_1_ref, kept_ref, crossing_ref):
     height, width = out_1_ref.shape
     out_0_ref[:height, :] = whole_ref[:, :width]
     out_1_ref[...] = whole_ref[:, width:]
@@ -210,7 +211,7 @@
     factor = jnp.concatenate([factor, jnp.zeros((rows, tiles * LANES - cols), F32)], axis=1)
     folded = [factor[:, tile * LANES : (tile + 1) * LANES] for tile in range(tiles)]
     folded = jnp.concatenate(folded, axis=0)
-    me = lax.axis_index("grp")
+    me = lax.axis_index(GRP)
     kept_ref[first:, :] = jnp.concatenate([folded, folded], axis=1)
     out_0_ref[height + first :, :] = jnp.concatenate([folded, folded], axis=1).astype(BF16)
     for index, (mine, sent) in enumerate(((0, 1), (2, 3))):
@@ -221,11 +222,11 @@
         out_0_ref[height : height + first, place] = crossing_ref[:, lanes].astype(BF16)
 
 
-def leaf_body(kept_ref, x_ref, y_ref, sep_ref, dinv_ref, out_ref, *, rows, cols):
+def run_leaf(kept_ref, x_ref, y_ref, sep_ref, dinv_ref, out_ref, *, rows, cols):
     levels, sep_block, _ = sep_ref.shape
     first = kept_ref.shape[0] - sep_block
     tiles = sep_block // rows
-    me = lax.axis_index("grp")
+    me = lax.axis_index(GRP)
     x_part = x_ref[x_ref.shape[0] - first - sep_block :, :].astype(F32)
     y_part = y_ref[y_ref.shape[0] - first :, :].astype(F32)
     total = kept_ref[:first, :LANES] + x_part[:first, :LANES] + y_part[:, :LANES]
@@ -257,8 +258,8 @@
         ].astype(BF16)
 
 
-def pair_body(own_ref, other_ref, out_ref, *, first, sep_block):
-    is_odd = lax.axis_index("leaf") % 2 == 1
+def run_pair(own_ref, other_ref, out_ref, *, first, sep_block):
+    is_odd = lax.axis_index(LEAF) % 2 == 1
     own = own_ref[...].astype(F32)
     other = other_ref[...].astype(F32)
     even = jnp.where(is_odd, other, own)
@@ -272,10 +273,10 @@
         out_ref[index * first : (index + 1) * first, :] = both.astype(BF16)
 
 
-def tree_body(*refs, count, first, levels, sep_block, cols):
+def run_tree(*refs, count, first, levels, sep_block, cols):
     pairs = refs[:count]
     first_ref, sol_ref, stage_ref, factor_ref, val_ref = refs[count:]
-    leaf = lax.axis_index("leaf")
+    leaf = lax.axis_index(LEAF)
     pair = leaf // 2
     nsep, width = factor_ref.shape
     for index, ref in enumerate(pairs):
@@ -322,7 +323,7 @@
     first_ref[...] = val_ref[pl.ds(pl.multiple_of(pair * first, first), first), :].astype(BF16)
 
 
-def arrange_body(dest_ref, factor_ref, *refs):
+def run_arrange(dest_ref, factor_ref, *refs):
     outs, (turned_ref, sorted_ref) = refs[:-2], refs[-2:]
     step = pl.program_id(0)
     rows, width = factor_ref.shape
@@ -365,7 +366,7 @@
     width = math.gcd(cols, 4 * LANES)
     part = cols // count
     return call(
-        arrange_body,
+        run_arrange,
         (dest, pltpu.with_memory_space_constraint(factor, pltpu.HBM)),
         [smem(), pl.BlockSpec((rows, width), lambda step: (0, step))],
         [jax.ShapeDtypeStruct((part, rows), BF16)] * count,
@@ -378,13 +379,13 @@
     )
 
 
-def split_body(rhs_ref, out_ref, sem, *, top):
+def run_split(rhs_ref, out_ref, sem, *, top):
     copy = pltpu.make_async_copy(rhs_ref.at[pl.ds(top, out_ref.shape[0]), :], out_ref, sem)
     copy.start()
     copy.wait()
 
 
-def cut_body(whole_ref, *outs):
+def run_cut(whole_ref, *outs):
     for part, ref in enumerate(outs):
         height, width = ref.shape
         ref[...] = whole_ref[:height, part * width : (part + 1) * width]
@@ -395,7 +396,7 @@
     return [slice(top, top + height) for top in range(0, rows, height)]
 
 
-def forward_body(own_ref, x_ref, y_ref, far_ref, dinv_ref, *refs):
+def run_forward(own_ref, x_ref, y_ref, far_ref, dinv_ref, *refs):
     pieces, (out_0_ref, out_1_ref, turned_ref, scale_ref, factor_ref, loads_ref) = refs[:-6], refs[-6:]
     rows = own_ref.shape[0]
     width = out_0_ref.shape[1]
@@ -416,7 +417,7 @@
         scale_ref[block, :] = jnp.broadcast_to(pivots[tile : tile + 1, :], (LANES, LANES)).T
 
 
-def far_body(far_ref, turned_ref, low_ref, high_ref, near_ref, scale_ref, *refs, first):
+def run_far(far_ref, turned_ref, low_ref, high_ref, near_ref, scale_ref, *refs, first):
     kept = refs[:-4]
     z_ref, relay_low_ref, relay_high_ref, loads_ref = refs[-4:]
     split, half = low_ref.shape[0], relay_low_ref.shape[0]
@@ -440,7 +441,7 @@
         relay_high_ref[half:, LANES:] = jnp.concatenate(folds, axis=0).astype(BF16)
 
 
-def near_body(own_ref, x_ref, y_ref, z_0_ref, z_1_ref, x_low_ref, y_high_ref, x_high_ref, y_low_ref, out_ref, z_ref):
+def run_near(own_ref, x_ref, y_ref, z_0_ref, z_1_ref, x_low_ref, y_high_ref, x_high_ref, y_low_ref, out_ref, z_ref):
     half, split = x_low_ref.shape[0], z_0_ref.shape[1]
     z_ref[:, :split] = z_0_ref[...]
     z_ref[:, split:] = z_1_ref[...]
@@ -456,7 +457,7 @@
             ref[block, :] = dot_nn(factor_ref[part, :], z_ref[...]).astype(ref.dtype)
 
 
-def add_body(near_ref, relay_0_ref, relay_1_ref, out_0_ref, out_1_ref):
+def run_add(near_ref, relay_0_ref, relay_1_ref, out_0_ref, out_1_ref):
     half = near_ref.shape[0]
     relay = jnp.concatenate([relay_0_ref[:half, :], relay_1_ref[:half, :]], axis=1).astype(F32)
     total = (near_ref[...] + relay).astype(BF16)
@@ -465,9 +466,9 @@
     out_1_ref[...] = total[:, split:]
 
 
-def base_body(own_ref, link_ref, mine_ref, x_ref, y_ref, d_ref, x_low_ref, y_high_ref, out_0_ref, out_1_ref, first_ref):
+def run_base(own_ref, link_ref, mine_ref, x_ref, y_ref, d_ref, x_low_ref, y_high_ref, out_0_ref, out_1_ref, first_ref):
     half = x_low_ref.shape[0]
-    me = lax.axis_index("grp")
+    me = lax.axis_index(GRP)
     for mask, ref in enumerate((mine_ref, x_ref, y_ref, d_ref)):
         lanes = pl.ds(pl.multiple_of((me ^ mask) * LANES, LANES), LANES)
         first_ref[:, lanes] = ref[...]
@@ -480,7 +481,7 @@
         ref[half:, :] += y_high_ref[:, cols].astype(F32)
 
 
-def last_body(base_ref, low_ref, high_ref, out_ref, sum_ref, sems, *, start, chunks):
+def run_last(base_ref, low_ref, high_ref, out_ref, sum_ref, sems, *, start, chunks):
     rows, width = base_ref.shape
     half, height = low_ref.shape[0], rows // chunks
     copies = []
@@ -503,13 +504,13 @@
 def local_pairs(leaf_rhs, leaf_inv, ordering, leaf_dinv, leaf_link, sep_rhs, sep_factor, sep_dinv):
     rows, width = leaf_rhs.shape
     half, split = rows // 2, rows // 16 * 7
-    group = lax.axis_size("grp")
+    group = lax.axis_size(GRP)
     levels, slice_width, sep_block = sep_rhs.shape
     first = leaf_link.shape[1]
     fac_rows, cols = sep_factor.shape
     tiles = sep_block // fac_rows
     parts = range(2)
-    me = lax.axis_index("grp").astype(jnp.int32)
+    me = lax.axis_index(GRP).astype(jnp.int32)
     link_turned = leaf_link.T
 
     def bf16(height, breadth):
@@ -518,11 +519,11 @@
     def f32(height, breadth):
         return jax.ShapeDtypeStruct((height, breadth), F32)
 
-    x_all = exchange(leaf_rhs, "grp", 1)
+    x_all = exchange(leaf_rhs, GRP, 1)
     loads = pltpu.with_memory_space_constraint(leaf_rhs, pltpu.HBM)
     high, low = (
         call(
-            functools.partial(split_body, top=top),
+            functools.partial(run_split, top=top),
             (loads,),
             [pl.BlockSpec(memory_space=pltpu.HBM)],
             bf16(height, width),
@@ -530,13 +531,13 @@
         )
         for top, height in ((split, rows - split), (0, split))
     )
-    y_high = exchange(high, "grp", 2)
-    y_low = exchange(low, "grp", 2)
+    y_high = exchange(high, GRP, 2)
+    y_low = exchange(low, GRP, 2)
     dest = (ordering[0] // rows ^ me) * rows + ordering[0] % rows
     blocks = arrange(leaf_inv, dest, group)
 
     *high_cut, kept = call(
-        send_body,
+        run_send,
         (y_high, low, high, link_turned, sep_factor),
         [vmem()] * 5,
         [
@@ -547,12 +548,12 @@
         after=(blocks[0],),
         scratch_shapes=[pltpu.VMEM((first, width), F32)],
     )
-    d_high = [exchange(high_cut[part], "grp", 1) for part in parts]
-    low_cut = call(cut_body, (x_all,), [vmem()], [bf16(split, width // 2)] * 2, after=(blocks[0],))
-    d_low = [exchange(low_cut[part], "grp", 2) for part in parts]
+    d_high = [exchange(high_cut[part], GRP, 1) for part in parts]
+    low_cut = call(run_cut, (x_all,), [vmem()], [bf16(split, width // 2)] * 2, after=(blocks[0],))
+    d_low = [exchange(low_cut[part], GRP, 2) for part in parts]
 
     *part_y, turned, scale = call(
-        forward_body,
+        run_forward,
         (*blocks, leaf_dinv.reshape(-1, LANES), low, high, x_all, y_low, y_high),
         [vmem()] * 10,
         [f32(rows, width // 2)] * 2 + [bf16(rows, rows), f32(rows, LANES)],
@@ -562,7 +563,7 @@
     for part in parts:
         shared = (kept,) if part == 0 else ()
         z_part, far_low, far_high = call(
-            functools.partial(far_body, first=first),
+            functools.partial(run_far, first=first),
             (
                 blocks[3],
                 turned,
@@ -581,38 +582,38 @@
             scratch_shapes=[pltpu.VMEM((rows, width // 2), BF16)],
         )
         leaf_z.append(z_part)
-        relay_low.append(exchange(far_low, "grp", 1))
-        relay_high.append(exchange(far_high, "grp", 2))
+        relay_low.append(exchange(far_low, GRP, 1))
+        relay_high.append(exchange(far_high, GRP, 2))
 
     near_x_low, near_y_high, near_x_high, near_y_low, own = call(
-        near_body,
+        run_near,
         (*blocks[:3], *leaf_z),
         [vmem()] * 5,
         [bf16(half, width)] * 2 + [f32(half, width)] * 2 + [f32(rows, width)],
         scratch_shapes=[pltpu.VMEM((rows, width), BF16)],
     )
     leaf_block = call(
-        functools.partial(leaf_body, rows=fac_rows, cols=cols),
+        functools.partial(run_leaf, rows=fac_rows, cols=cols),
         (kept, d_high[0], relay_high[0], jnp.swapaxes(sep_rhs, 1, 2), sep_dinv),
         [vmem()] * 5,
         bf16(first + (levels + tiles) * sep_block, LANES),
         after=(own,),
     )
-    partner = exchange(leaf_block, "leaf", 1)
-    sum_x_low = exchange(near_x_low, "grp", 1)
-    sum_y_high = exchange(near_y_high, "grp", 2)
+    partner = exchange(leaf_block, LEAF, 1)
+    sum_x_low = exchange(near_x_low, GRP, 1)
+    sum_y_high = exchange(near_y_high, GRP, 2)
     pair_block = call(
-        functools.partial(pair_body, first=first, sep_block=sep_block),
+        functools.partial(run_pair, first=first, sep_block=sep_block),
         (leaf_block, partner),
         [vmem(), vmem()],
         bf16((levels + tiles) * first, LANES),
     )
-    count = lax.axis_size("leaf") // 2
-    pairs = [pair_block] + [exchange(pair_block, "leaf", 2 * mask) for mask in range(1, count)]
+    count = lax.axis_size(LEAF) // 2
+    pairs = [pair_block] + [exchange(pair_block, LEAF, 2 * mask) for mask in range(1, count)]
     nsep = count * first
     first_here, sep_turned = call(
         functools.partial(
-            tree_body, count=count, first=first, levels=levels, sep_block=sep_block, cols=cols
+            run_tree, count=count, first=first, levels=levels, sep_block=sep_block, cols=cols
         ),
         pairs,
         [vmem()] * count,
@@ -623,15 +624,15 @@
             pltpu.VMEM((nsep, LANES), F32),
         ],
     )
-    first_all = [first_here] + [exchange(first_here, "grp", mask) for mask in range(1, group)]
-    breadths = (width // 2, width // 2)
+    first_all = [first_here] + [exchange(first_here, GRP, mask) for mask in range(1, group)]
+    breadths = (width // 4 * 3, width // 4)
     into = [bf16(half, breadth) for breadth in breadths]
-    x_sums = call(add_body, (near_x_high, *relay_high), [vmem()] * 3, into)
-    y_sums = call(add_body, (near_y_low, *relay_low), [vmem()] * 3, into)
-    sum_x_high = [exchange(x_sums[part], "grp", 1) for part in parts]
-    sum_y_low = [exchange(y_sums[part], "grp", 2) for part in parts]
+    x_sums = call(run_add, (near_x_high, *relay_high), [vmem()] * 3, into)
+    y_sums = call(run_add, (near_y_low, *relay_low), [vmem()] * 3, into)
+    sum_x_high = [exchange(x_sums[part], GRP, 1) for part in parts]
+    sum_y_low = [exchange(y_sums[part], GRP, 2) for part in parts]
     base = call(
-        base_body,
+        run_base,
         (own, link_turned, *first_all, sum_x_low, sum_y_high),
         [vmem()] * (4 + group),
         [f32(rows, breadth) for breadth in breadths],
@@ -642,7 +643,7 @@
     for part, breadth in zip(parts, breadths):
         leaf_x = (
             call(
-                functools.partial(last_body, start=start, chunks=chunks),
+                functools.partial(run_last, start=start, chunks=chunks),
                 (base[part], sum_y_low[part], sum_x_high[part]),
                 [vmem()] * 3,
                 f32(rows, width),
@@ -659,8 +660,8 @@
 def fits(leaf_rhs, leaf_inv, sep_rhs, sep_factor, leaf_link):
     levels, slice_width, sep_block = sep_rhs.shape
     width = leaf_rhs.shape[1]
-    count = lax.axis_size("grp")
-    leaves = lax.axis_size("leaf")
+    count = lax.axis_size(GRP)
+    leaves = lax.axis_size(LEAF)
     return (
         count == 2**2
         and leaf_inv.shape[1] == count * leaf_rhs.shape[0]
@@ -686,19 +687,19 @@
 
 def solution(mesh):
     placed = (
-        P(("leaf", "grp"), None),
-        P(("leaf", "grp"), None),
-        P("leaf", None),
-        P(("leaf", "grp")),
-        P(("leaf", "grp"), None),
-        P(None, "grp", "leaf"),
-        P(("leaf", "grp"), None),
-        P(None, "leaf"),
+        P((LEAF, GRP), None),
+        P((LEAF, GRP), None),
+        P(LEAF, None),
+        P((LEAF, GRP)),
+        P((LEAF, GRP), None),
+        P(None, GRP, LEAF),
+        P((LEAF, GRP), None),
+        P(None, LEAF),
     )
     return jax.shard_map(
         local,
         mesh=mesh,
         in_specs=placed,
-        out_specs=(P(("leaf", "grp"), None), P(None, "grp", "leaf")),
+        out_specs=(P((LEAF, GRP), None), P(None, GRP, LEAF)),
         check_vma=False,
     )

time: 87.8 us -> 93.5 us (1.065)
  waiting for transfers between devices: 21.8 us -> 28.3 us
    ppermute x24, waiting for transfers between devices: 21.8 us -> 28.3 us  [exchange(): lax.ppermute(block, axis, [(low, low ^ mask) for low in range(count)])]
  transfers between devices with their start and end apart: 24 -> 24, of which waited for: 14 -> 13; matrix products, arithmetic and copies ran while one was open for 0% -> 0% of each run, Pallas kernels for 36% -> 34%
where the time goes in v9:
time: 93.5 us; the launch traced here: 93.3 us
  Pallas kernels  32.9 us (35%)
  starting transfers between devices  31.2 us (33%)
  waiting for transfers between devices  28.3 us (30%)
    pallas_call x17, Pallas kernels, call(): pl.pallas_call(skipping, out_shape=out_shape, in_specs=[pl.BlockSpec(memo...  32.9 us
    ppermute x24, starting transfers between devices, exchange(): lax.ppermute(block, axis, [(low, low ^ mask) for low in range(count)])  31.2 us
    ppermute x24, waiting for transfers between devices, exchange(): lax.ppermute(block, axis, [(low, low ^ mask) for low in range(count)])  28.3 us
  transfers between devices with their start and end apart: 24, of which 13 were waited for; matrix products, arithmetic and copies ran while one was open for 0% of the time, Pallas kernels for 34%

profile of v9, /device:TPU:0, one launch (start us, length us, event | category | flops | bytes accessed | tf_op | source)
XLA Modules:
  0.0 93.3 jit_solution(2947801187834526218)
XLA Ops:
  0.6 3.0 %collective-permute-start = (bf16[1024,512]{1,0:T(8,128)(2,1)}, bf16[1024,512]{1,0:T(8,128)(2,1)S(1)}, u32[]{:S(2)}, u32[]{:S(2)}) collective-permute-start(bf16[1024,512]{1,0:T(8,128)(2,1)} %refs_0_.3), channel_id=1, source_target_pairs={{0,1},{1,0},{2,3},{3,2},{4,5},{5,4},{6,7},{7,6},{8,9},{9,8},{10,11... | collective-permute-start | bytes 3145736 | tf_op jit(solution)/shard_map/ppermute | solution.py:21
  3.7 1.1 %shard_map.97.refs_6_.refs_3_ = bf16[576,512]{1,0:T(8,128)(2,1)S(1)} custom-call(bf16[1024,512]{1,0:T(8,128)(2,1)} %refs_0_.3), custom_call_target="tpu_custom_call" | custom-call | tf_op jit(solution)/shard_map/pallas_call | solution.py:53
  4.8 1.6 %collective-permute-start.2 = (bf16[576,512]{1,0:T(8,128)(2,1)S(1)}, bf16[576,512]{1,0:T(8,128)(2,1)S(1)}, u32[]{:S(2)}, u32[]{:S(2)}) collective-permute-start(bf16[576,512]{1,0:T(8,128)(2,1)S(1)} %shard_map.97.refs_6_.refs_3_), channel_id=1, source_target_pairs={{0,2},{1,3},{2,0},{3,1},{4,6},{5,7},{6,4},{7,5},{8,10},{9,11},{10,... | collective-permute-start | bytes 1769480 | tf_op jit(solution)/shard_map/ppermute | solution.py:21
  6.4 1.0 %shard_map.96.refs_5_.refs_2_ = bf16[448,512]{1,0:T(8,128)(2,1)S(1)} custom-call(bf16[1024,512]{1,0:T(8,128)(2,1)} %refs_0_.3), custom_call_target="tpu_custom_call" | custom-call | tf_op jit(solution)/shard_map/pallas_call | solution.py:53
  7.4 0.6 collective-permute-start.1
  8.0 16.0 %shard_map.95 = (bf16[1024,1024]{1,0:T(8,128)(2,1)S(1)}, bf16[1024,1024]{1,0:T(8,128)(2,1)S(1)}, bf16[1024,1024]{1,0:T(8,128)(2,1)S(1)}, bf16[1024,1024]{1,0:T(8,128)(2,1)S(1)}) custom-call(s32[4096]{0:T(1024)S(1)} %fusion.2.refs_0_, bf16[1024,4096]{1,0:T(8,128)(2,1)} %refs_1_.1), custom_call_target="tpu_custom_call" | custom-call | tf_op jit(solution)/shard_map/pallas_call | solution.py:53
  24.1 0.3 shard_map.100
  24.5 3.3 %collective-permute-done.refs_7_.refs_1_ = bf16[1024,512]{1,0:T(8,128)(2,1)S(1)} collective-permute-done((bf16[1024,512]{1,0:T(8,128)(2,1)}, bf16[1024,512]{1,0:T(8,128)(2,1)S(1)}, u32[]{:S(2)}, u32[]{:S(2)}) %collective-permute-start) | collective-permute-done | bytes 1048608 | tf_op jit(solution)/shard_map/ppermute | solution.py:21
  27.9 2.1 %collective-permute-start.3 = (bf16[448,256]{1,0:T(8,128)(2,1)S(1)}, bf16[448,256]{1,0:T(8,128)(2,1)S(1)}, u32[]{:S(2)}, u32[]{:S(2)}) collective-permute-start(bf16[448,256]{1,0:T(8,128)(2,1)S(1)} %get-tuple-element.39), channel_id=1, source_target_pairs={{0,2},{1,3},{2,0},{3,1},{4,6},{5,7},{6,4},{7,5},{8,10},{9,11},{10,... | collective-permute-start | bytes 688136 | tf_op jit(solution)/shard_map/ppermute | solution.py:21
  30.0 1.5 %collective-permute-start.6 = (bf16[576,256]{1,0:T(8,128)(2,1)S(1)}, bf16[576,256]{1,0:T(8,128)(2,1)S(1)}, u32[]{:S(2)}, u32[]{:S(2)}) collective-permute-start(bf16[576,256]{1,0:T(8,128)(2,1)S(1)} %get-tuple-element.46), channel_id=1, source_target_pairs={{0,1},{1,0},{2,3},{3,2},{4,5},{5,4},{6,7},{7,6},{8,9},{9,8},{10,11... | collective-permute-start | bytes 884744 | tf_op jit(solution)/shard_map/ppermute | solution.py:21
  31.5 0.5 collective-permute-start.5
  32.0 3.5 %shard_map.98 = (f32[1024,256]{1,0:T(8,128)S(1)}, f32[1024,256]{1,0:T(8,128)S(1)}, bf16[1024,1024]{1,0:T(8,128)(2,1)S(1)}, f32[1024,128]{1,0:T(8,128)S(1)}) custom-call(bf16[1024,1024]{1,0:T(8,128)(2,1)S(1)} %get-tuple-element.34.refs_0_, bf16[1024,1024]{1,0:T(8,128)(2,1)S(1)} %get-tuple-element.35.refs_1_, ...), custom_call_target="tpu_custom_call" | custom-call | tf_op jit(solution)/shard_map/pallas_call | solution.py:53
  35.6 0.9 collective-permute-done.3.refs_2_
  36.5 1.3 %shard_map.101 = (bf16[1024,256]{1,0:T(8,128)(2,1)S(1)}, bf16[512,256]{1,0:T(8,128)(2,1)S(1)}, bf16[544,256]{1,0:T(8,128)(2,1)S(1)}) custom-call(bf16[1024,1024]{1,0:T(8,128)(2,1)S(1)} %get-tuple-element.37.refs_3_.refs_0_, bf16[1024,1024]{1,0:T(8,128)(2,1)S(1)} %get-tuple-element.38.refs_1_, bf16[448,256]{1,0:T(8,128)(2,1)S(1)} %collective-permute-done.3.refs_2_, ...), custom_call_target="tpu_custom_call" | custom-call | tf_op jit(solution)/shard_map/pallas_call | solution.py:53
  37.8 1.4 %collective-permute-start.17 = (bf16[512,256]{1,0:T(8,128)(2,1)S(1)}, bf16[512,256]{1,0:T(8,128)(2,1)S(1)}, u32[]{:S(2)}, u32[]{:S(2)}) collective-permute-start(bf16[512,256]{1,0:T(8,128)(2,1)S(1)} %get-tuple-element.56), channel_id=1, source_target_pairs={{0,1},{1,0},{2,3},{3,2},{4,5},{5,4},{6,7},{7,6},{8,9},{9,8},{10,11... | collective-permute-start | bytes 786440 | tf_op jit(solution)/shard_map/ppermute | solution.py:21
  39.2 1.5 %collective-permute-start.7 = (bf16[544,256]{1,0:T(8,128)(2,1)S(1)}, bf16[544,256]{1,0:T(8,128)(2,1)S(1)}, u32[]{:S(2)}, u32[]{:S(2)}) collective-permute-start(bf16[544,256]{1,0:T(8,128)(2,1)S(1)} %get-tuple-element.50), channel_id=1, source_target_pairs={{0,2},{1,3},{2,0},{3,1},{4,6},{5,7},{6,4},{7,5},{8,10},{9,11},{10,... | collective-permute-start | bytes 835592 | tf_op jit(solution)/shard_map/ppermute | solution.py:21
  40.7 0.5 collective-permute-done.6.refs_3_
  41.2 1.3 %shard_map.102 = (bf16[1024,256]{1,0:T(8,128)(2,1)S(1)}, bf16[512,256]{1,0:T(8,128)(2,1)S(1)}, bf16[512,256]{1,0:T(8,128)(2,1)S(1)}) custom-call(bf16[1024,1024]{1,0:T(8,128)(2,1)S(1)} %get-tuple-element.37.refs_3_.refs_0_, bf16[1024,1024]{1,0:T(8,128)(2,1)S(1)} %get-tuple-element.38.refs_1_, bf16[448,256]{1,0:T(8,128)(2,1)S(1)} %collective-permute-done.5.refs_2_, ...), custom_call_target="tpu_custom_call" | custom-call | tf_op jit(solution)/shard_map/pallas_call | solution.py:53
  42.5 1.9 %collective-permute-start.18 = (bf16[512,256]{1,0:T(8,128)(2,1)S(1)}, bf16[512,256]{1,0:T(8,128)(2,1)S(1)}, u32[]{:S(2)}, u32[]{:S(2)}) collective-permute-start(bf16[512,256]{1,0:T(8,128)(2,1)S(1)} %get-tuple-element.57), channel_id=1, source_target_pairs={{0,1},{1,0},{2,3},{3,2},{4,5},{5,4},{6,7},{7,6},{8,9},{9,8},{10,11... | collective-permute-start | bytes 786440 | tf_op jit(solution)/shard_map/ppermute | solution.py:21
  44.4 1.5 %collective-permute-start.20 = (bf16[512,256]{1,0:T(8,128)(2,1)S(1)}, bf16[512,256]{1,0:T(8,128)(2,1)S(1)}, u32[]{:S(2)}, u32[]{:S(2)}) collective-permute-start(bf16[512,256]{1,0:T(8,128)(2,1)S(1)} %get-tuple-element.60), channel_id=1, source_target_pairs={{0,2},{1,3},{2,0},{3,1},{4,6},{5,7},{6,4},{7,5},{8,10},{9,11},{10,... | collective-permute-start | bytes 786440 | tf_op jit(solution)/shard_map/ppermute | solution.py:21
  46.0 3.4 %shard_map.103 = (bf16[512,512]{1,0:T(8,128)(2,1)S(1)}, bf16[512,512]{1,0:T(8,128)(2,1)S(1)}, f32[512,512]{1,0:T(8,128)S(1)}, f32[512,512]{1,0:T(8,128)S(1)}, f32[1024,512]{1,0:T(8,128)S(1)}) custom-call(bf16[1024,1024]{1,0:T(8,128)(2,1)S(1)} %get-tuple-element.34.refs_0_, bf16[1024,1024]{1,0:T(8,128)(2,1)S(1)} %get-tuple-element.35.refs_1_, ...), custom_call_target="tpu_custom_call" | custom-call | tf_op jit(solution)/shard_map/pallas_call | solution.py:53
  49.4 0.6 collective-permute-start.15
  50.0 0.1 collective-permute-start.16
  50.2 2.4 %collective-permute-done.18.refs_2_ = bf16[512,256]{1,0:T(8,128)(2,1)S(1)} collective-permute-done((bf16[512,256]{1,0:T(8,128)(2,1)S(1)}, bf16[512,256]{1,0:T(8,128)(2,1)S(1)}, u32[]{:S(2)}, u32[]{:S(2)}) %collective-permute-start.18) | collective-permute-done | bytes 262176 | tf_op jit(solution)/shard_map/ppermute | solution.py:21
  52.7 1.9 %collective-permute-start.19 = (bf16[512,384]{1,0:T(8,128)(2,1)S(1)}, bf16[512,384]{1,0:T(8,128)(2,1)S(1)}, u32[]{:S(2)}, u32[]{:S(2)}) collective-permute-start(bf16[512,384]{1,0:T(8,128)(2,1)S(1)} %get-tuple-element.58), channel_id=1, source_target_pairs={{0,2},{1,3},{2,0},{3,1},{4,6},{5,7},{6,4},{7,5},{8,10},{9,11},{10,... | collective-permute-start | bytes 1179656 | tf_op jit(solution)/shard_map/ppermute | solution.py:21
  54.8 1.4 %collective-permute-start.21 = (bf16[512,384]{1,0:T(8,128)(2,1)S(1)}, bf16[512,384]{1,0:T(8,128)(2,1)S(1)}, u32[]{:S(2)}, u32[]{:S(2)}) collective-permute-start(bf16[512,384]{1,0:T(8,128)(2,1)S(1)} %get-tuple-element.61), channel_id=1, source_target_pairs={{0,1},{1,0},{2,3},{3,2},{4,5},{5,4},{6,7},{7,6},{8,9},{9,8},{10,11... | collective-permute-start | bytes 1179656 | tf_op jit(solution)/shard_map/ppermute | solution.py:21
  56.2 0.1 shard_map.104.refs_0_
  56.4 1.2 %collective-permute-done.8.refs_1_ = bf16[144,128]{1,0:T(8,128)(2,1)S(1)} collective-permute-done((bf16[144,128]{1,0:T(8,128)(2,1)S(1)}, bf16[144,128]{1,0:T(8,128)(2,1)S(1)}, u32[]{:S(2)}, u32[]{:S(2)}) %collective-permute-start.8) | collective-permute-done | bytes 36896 | tf_op jit(solution)/shard_map/ppermute | solution.py:21
  57.6 1.6 %collective-permute-start.9 = (bf16[224,128]{1,0:T(8,128)(2,1)S(1)}, bf16[224,128]{1,0:T(8,128)(2,1)S(1)}, u32[]{:S(2)}, u32[]{:S(2)}) collective-permute-start(bf16[224,128]{1,0:T(8,128)(2,1)S(1)} %shard_map.105.refs_0_), channel_id=1, source_target_pairs={{0,8},{4,12},{8,0},{12,4},{16,24},{20,28},{24,16},{28,20},{1,9},{5... | collective-permute-start | bytes 172040 | tf_op jit(solution)/shard_map/ppermute | solution.py:21
  59.2 2.6 %collective-permute-done.9.refs_1_ = bf16[224,128]{1,0:T(8,128)(2,1)S(1)} collective-permute-done((bf16[224,128]{1,0:T(8,128)(2,1)S(1)}, bf16[224,128]{1,0:T(8,128)(2,1)S(1)}, u32[]{:S(2)}, u32[]{:S(2)}) %collective-permute-start.9) | collective-permute-done | bytes 57376 | tf_op jit(solution)/shard_map/ppermute | solution.py:21
  61.8 2.6 %collective-permute-start.10 = (bf16[224,128]{1,0:T(8,128)(2,1)S(1)}, bf16[224,128]{1,0:T(8,128)(2,1)S(1)}, u32[]{:S(2)}, u32[]{:S(2)}) collective-permute-start(bf16[224,128]{1,0:T(8,128)(2,1)S(1)} %shard_map.105.refs_0_), channel_id=1, source_target_pairs={{0,16},{4,20},{8,24},{12,28},{16,0},{20,4},{24,8},{28,12},{1,17},{... | collective-permute-start | bytes 172040 | tf_op jit(solution)/shard_map/ppermute | solution.py:21
  64.4 2.5 %collective-permute-done.10.refs_2_ = bf16[224,128]{1,0:T(8,128)(2,1)S(1)} collective-permute-done((bf16[224,128]{1,0:T(8,128)(2,1)S(1)}, bf16[224,128]{1,0:T(8,128)(2,1)S(1)}, u32[]{:S(2)}, u32[]{:S(2)}) %collective-permute-start.10) | collective-permute-done | bytes 57376 | tf_op jit(solution)/shard_map/ppermute | solution.py:21
  66.9 4.1 %collective-permute-start.11 = (bf16[224,128]{1,0:T(8,128)(2,1)S(1)}, bf16[224,128]{1,0:T(8,128)(2,1)S(1)}, u32[]{:S(2)}, u32[]{:S(2)}) collective-permute-start(bf16[224,128]{1,0:T(8,128)(2,1)S(1)} %shard_map.105.refs_0_), channel_id=1, source_target_pairs={{0,24},{4,28},{8,16},{12,20},{16,8},{20,12},{24,0},{28,4},{1,25},{... | collective-permute-start | bytes 172040 | tf_op jit(solution)/shard_map/ppermute | solution.py:21
  71.0 2.2 %collective-permute-done.11.refs_3_ = bf16[224,128]{1,0:T(8,128)(2,1)S(1)} collective-permute-done((bf16[224,128]{1,0:T(8,128)(2,1)S(1)}, bf16[224,128]{1,0:T(8,128)(2,1)S(1)}, u32[]{:S(2)}, u32[]{:S(2)}) %collective-permute-start.11) | collective-permute-done | bytes 57376 | tf_op jit(solution)/shard_map/ppermute | solution.py:21
  73.2 1.9 %shard_map.106 = (bf16[32,128]{1,0:T(8,128)(2,1)S(1)}, f32[3,16,128]{2,1,0:T(8,128)}) custom-call(bf16[224,128]{1,0:T(8,128)(2,1)S(1)} %shard_map.105.refs_0_, bf16[224,128]{1,0:T(8,128)(2,1)S(1)} %collective-permute-done.9.refs_1_, bf16[224,128]{1,0:T(8,128)(2,1)S(1)} %collective-permute-done.10.refs_2_, bf16[224,128]{1,0:T(8,128)(2,1)S(1)} %collective-permute-done.11.refs_3_), custom_call_target="tpu_custom_call" | custom-call | tf_op jit(solution)/shard_map/pallas_call | solution.py:53
  75.1 0.7 collective-permute-start.12
  75.8 3.0 %collective-permute-done.12.refs_3_ = bf16[32,128]{1,0:T(8,128)(2,1)S(1)} collective-permute-done((bf16[32,128]{1,0:T(8,128)(2,1)S(1)}, bf16[32,128]{1,0:T(8,128)(2,1)S(1)}, u32[]{:S(2)}, u32[]{:S(2)}) %collective-permute-start.12) | collective-permute-done | bytes 8224 | tf_op jit(solution)/shard_map/ppermute | solution.py:21
  78.8 0.5 collective-permute-start.13
  79.3 3.2 %collective-permute-done.13.refs_4_ = bf16[32,128]{1,0:T(8,128)(2,1)S(1)} collective-permute-done((bf16[32,128]{1,0:T(8,128)(2,1)S(1)}, bf16[32,128]{1,0:T(8,128)(2,1)S(1)}, u32[]{:S(2)}, u32[]{:S(2)}) %collective-permute-start.13) | collective-permute-done | bytes 8224 | tf_op jit(solution)/shard_map/ppermute | solution.py:21
  82.4 0.6 collective-permute-start.14
  83.1 3.9 %collective-permute-done.14.refs_5_ = bf16[32,128]{1,0:T(8,128)(2,1)S(1)} collective-permute-done((bf16[32,128]{1,0:T(8,128)(2,1)S(1)}, bf16[32,128]{1,0:T(8,128)(2,1)S(1)}, u32[]{:S(2)}, u32[]{:S(2)}) %collective-permute-start.14) | collective-permute-done | bytes 8224 | tf_op jit(solution)/shard_map/ppermute | solution.py:21
  87.0 0.5 collective-permute-start.22
  87.5 0.7 collective-permute-start.23
  88.2 0.5 shard_map.107
  88.7 1.2 %shard_map.110.refs_0_ = f32[1024,512]{1,0:T(8,128)} custom-call(f32[1024,384]{1,0:T(8,128)S(1)} %get-tuple-element.54.refs_0_, bf16[512,384]{1,0:T(8,128)(2,1)S(1)} %collective-permute-done.19.refs_1_, bf16[512,384]{1,0:T(8,128)(2,1)S(1)} %collective-permute-done.21.refs_2_), custom_call_target="tpu_custom_call" | custom-call | tf_op jit(solution)/shard_map/pallas_call | solution.py:53
  89.9 2.0 %collective-permute-done.22.refs_2_ = bf16[512,128]{1,0:T(8,128)(2,1)S(1)} collective-permute-done((bf16[512,128]{1,0:T(8,128)(2,1)S(1)}, bf16[512,128]{1,0:T(8,128)(2,1)S(1)}, u32[]{:S(2)}, u32[]{:S(2)}) %collective-permute-start.22) | collective-permute-done | bytes 131104 | tf_op jit(solution)/shard_map/ppermute | solution.py:21
  91.9 0.5 collective-permute-done.23.refs_3_
  92.4 0.8 shard_map.111
  (30 shorter events, 0.5 us)
Async XLA Ops:
  0.6 7.3 %copy-start.5 = (s32[1,4096]{1,0:T(1,128)S(1)}, s32[1,4096]{1,0:T(1,128)}, u32[]{:S(2)}) copy-start(s32[1,4096]{1,0:T(1,128)} %param.10) | copy-start | bytes 49156
  0.6 27.3 %collective-permute-start = (bf16[1024,512]{1,0:T(8,128)(2,1)}, bf16[1024,512]{1,0:T(8,128)(2,1)S(1)}, u32[]{:S(2)}, u32[]{:S(2)}) collective-permute-start(bf16[1024,512]{1,0:T(8,128)(2,1)} %refs_0_.3), channel_id=1, source_target_pairs={{0,1},{1,0},{2,3},{3,2},{4,5},{5,4},{6,7},{7,6},{8,9},{9,8},{10,11... | collective-permute-start | bytes 3145736 | tf_op jit(solution)/shard_map/ppermute | solution.py:21
  4.8 19.3 %collective-permute-start.2 = (bf16[576,512]{1,0:T(8,128)(2,1)S(1)}, bf16[576,512]{1,0:T(8,128)(2,1)S(1)}, u32[]{:S(2)}, u32[]{:S(2)}) collective-permute-start(bf16[576,512]{1,0:T(8,128)(2,1)S(1)} %shard_map.97.refs_6_.refs_3_), channel_id=1, source_target_pairs={{0,2},{1,3},{2,0},{3,1},{4,6},{5,7},{6,4},{7,5},{8,10},{9,11},{10,... | collective-permute-start | bytes 1769480 | tf_op jit(solution)/shard_map/ppermute | solution.py:21
  7.4 24.6 %collective-permute-start.1 = (bf16[448,512]{1,0:T(8,128)(2,1)S(1)}, bf16[448,512]{1,0:T(8,128)(2,1)S(1)}, u32[]{:S(2)}, u32[]{:S(2)}) collective-permute-start(bf16[448,512]{1,0:T(8,128)(2,1)S(1)} %shard_map.96.refs_5_.refs_2_), channel_id=1, source_target_pairs={{0,2},{1,3},{2,0},{3,1},{4,6},{5,7},{6,4},{7,5},{8,10},{9,11},{10,... | collective-permute-start | bytes 1376264 | tf_op jit(solution)/shard_map/ppermute | solution.py:21
  8.0 16.0 %copy-start = (bf16[1024,32]{0,1:T(8,128)(2,1)S(1)}, bf16[1024,32]{0,1:T(8,128)(2,1)}, u32[]{:S(2)}) copy-start(bf16[1024,32]{0,1:T(8,128)(2,1)} %param.12) | copy-start | bytes 196612
  8.0 16.0 %copy-start.2 = (bf16[4,416]{1,0:T(4,128)(2,1)S(1)}, bf16[4,416]{1,0:T(4,128)(2,1)}, u32[]{:S(2)}) copy-start(bf16[4,416]{1,0:T(4,128)(2,1)} %refs_5_.2) | copy-start | bytes 9988
  24.4 7.6 %copy-start.3 = (bf16[1024]{0:T(1024)(128)(2,1)S(1)}, bf16[1024]{0:T(1024)(128)(2,1)}, u32[]{:S(2)}) copy-start(bf16[1024]{0:T(1024)(128)(2,1)} %param.11) | copy-start | bytes 6148
  24.4 11.1 %collective-permute-start.4 = (bf16[624,256]{1,0:T(8,128)(2,1)S(1)}, bf16[624,256]{1,0:T(8,128)(2,1)S(1)}, u32[]{:S(2)}, u32[]{:S(2)}) collective-permute-start(bf16[624,256]{1,0:T(8,128)(2,1)S(1)} %get-tuple-element.40), channel_id=1, source_target_pairs={{0,1},{1,0},{2,3},{3,2},{4,5},{5,4},{6,7},{7,6},{8,9},{9,8},{10,11... | collective-permute-start | bytes 958472 | tf_op jit(solution)/shard_map/ppermute | solution.py:21
  27.9 8.6 %collective-permute-start.3 = (bf16[448,256]{1,0:T(8,128)(2,1)S(1)}, bf16[448,256]{1,0:T(8,128)(2,1)S(1)}, u32[]{:S(2)}, u32[]{:S(2)}) collective-permute-start(bf16[448,256]{1,0:T(8,128)(2,1)S(1)} %get-tuple-element.39), channel_id=1, source_target_pairs={{0,2},{1,3},{2,0},{3,1},{4,6},{5,7},{6,4},{7,5},{8,10},{9,11},{10,... | collective-permute-start | bytes 688136 | tf_op jit(solution)/shard_map/ppermute | solution.py:21
  30.0 11.2 %collective-permute-start.6 = (bf16[576,256]{1,0:T(8,128)(2,1)S(1)}, bf16[576,256]{1,0:T(8,128)(2,1)S(1)}, u32[]{:S(2)}, u32[]{:S(2)}) collective-permute-start(bf16[576,256]{1,0:T(8,128)(2,1)S(1)} %get-tuple-element.46), channel_id=1, source_target_pairs={{0,1},{1,0},{2,3},{3,2},{4,5},{5,4},{6,7},{7,6},{8,9},{9,8},{10,11... | collective-permute-start | bytes 884744 | tf_op jit(solution)/shard_map/ppermute | solution.py:21
  31.5 9.7 %collective-permute-start.5 = (bf16[448,256]{1,0:T(8,128)(2,1)S(1)}, bf16[448,256]{1,0:T(8,128)(2,1)S(1)}, u32[]{:S(2)}, u32[]{:S(2)}) collective-permute-start(bf16[448,256]{1,0:T(8,128)(2,1)S(1)} %get-tuple-element.45), channel_id=1, source_target_pairs={{0,2},{1,3},{2,0},{3,1},{4,6},{5,7},{6,4},{7,5},{8,10},{9,11},{10,... | collective-permute-start | bytes 688136 | tf_op jit(solution)/shard_map/ppermute | solution.py:21
  37.8 12.3 %collective-permute-start.17 = (bf16[512,256]{1,0:T(8,128)(2,1)S(1)}, bf16[512,256]{1,0:T(8,128)(2,1)S(1)}, u32[]{:S(2)}, u32[]{:S(2)}) collective-permute-start(bf16[512,256]{1,0:T(8,128)(2,1)S(1)} %get-tuple-element.56), channel_id=1, source_target_pairs={{0,1},{1,0},{2,3},{3,2},{4,5},{5,4},{6,7},{7,6},{8,9},{9,8},{10,11... | collective-permute-start | bytes 786440 | tf_op jit(solution)/shard_map/ppermute | solution.py:21
  39.2 15.5 %collective-permute-start.7 = (bf16[544,256]{1,0:T(8,128)(2,1)S(1)}, bf16[544,256]{1,0:T(8,128)(2,1)S(1)}, u32[]{:S(2)}, u32[]{:S(2)}) collective-permute-start(bf16[544,256]{1,0:T(8,128)(2,1)S(1)} %get-tuple-element.50), channel_id=1, source_target_pairs={{0,2},{1,3},{2,0},{3,1},{4,6},{5,7},{6,4},{7,5},{8,10},{9,11},{10,... | collective-permute-start | bytes 835592 | tf_op jit(solution)/shard_map/ppermute | solution.py:21
  42.5 10.1 %collective-permute-start.18 = (bf16[512,256]{1,0:T(8,128)(2,1)S(1)}, bf16[512,256]{1,0:T(8,128)(2,1)S(1)}, u32[]{:S(2)}, u32[]{:S(2)}) collective-permute-start(bf16[512,256]{1,0:T(8,128)(2,1)S(1)} %get-tuple-element.57), channel_id=1, source_target_pairs={{0,1},{1,0},{2,3},{3,2},{4,5},{5,4},{6,7},{7,6},{8,9},{9,8},{10,11... | collective-permute-start | bytes 786440 | tf_op jit(solution)/shard_map/ppermute | solution.py:21
  44.4 10.2 %collective-permute-start.20 = (bf16[512,256]{1,0:T(8,128)(2,1)S(1)}, bf16[512,256]{1,0:T(8,128)(2,1)S(1)}, u32[]{:S(2)}, u32[]{:S(2)}) collective-permute-start(bf16[512,256]{1,0:T(8,128)(2,1)S(1)} %get-tuple-element.60), channel_id=1, source_target_pairs={{0,2},{1,3},{2,0},{3,1},{4,6},{5,7},{6,4},{7,5},{8,10},{9,11},{10,... | collective-permute-start | bytes 786440 | tf_op jit(solution)/shard_map/ppermute | solution.py:21
  49.4 6.8 %copy-start.1 = (bf16[3,128,16]{1,2,0:T(8,128)(2,1)S(1)}, bf16[3,128,16]{1,2,0:T(8,128)(2,1)}, u32[]{:S(2)}) copy-start(bf16[3,128,16]{1,2,0:T(8,128)(2,1)} %param.13) | copy-start | bytes 36868
  49.4 6.8 %copy-start.4 = (bf16[3,16]{1,0:T(4,128)(2,1)S(1)}, bf16[3,16]{1,0:T(4,128)(2,1)}, u32[]{:S(2)}) copy-start(bf16[3,16]{1,0:T(4,128)(2,1)} %refs_5_.3) | copy-start | bytes 292
  49.4 38.0 %collective-permute-start.15 = (bf16[512,512]{1,0:T(8,128)(2,1)S(1)}, bf16[512,512]{1,0:T(8,128)(2,1)S(1)}, u32[]{:S(2)}, u32[]{:S(2)}) collective-permute-start(bf16[512,512]{1,0:T(8,128)(2,1)S(1)} %get-tuple-element.52), channel_id=1, source_target_pairs={{0,1},{1,0},{2,3},{3,2},{4,5},{5,4},{6,7},{7,6},{8,9},{9,8},{10,11... | collective-permute-start | bytes 1572872 | tf_op jit(solution)/shard_map/ppermute | solution.py:21
  50.0 38.1 %collective-permute-start.16 = (bf16[512,512]{1,0:T(8,128)(2,1)S(1)}, bf16[512,512]{1,0:T(8,128)(2,1)S(1)}, u32[]{:S(2)}, u32[]{:S(2)}) collective-permute-start(bf16[512,512]{1,0:T(8,128)(2,1)S(1)} %get-tuple-element.53), channel_id=1, source_target_pairs={{0,2},{1,3},{2,0},{3,1},{4,6},{5,7},{6,4},{7,5},{8,10},{9,11},{10,... | collective-permute-start | bytes 1572872 | tf_op jit(solution)/shard_map/ppermute | solution.py:21
  52.7 35.9 %collective-permute-start.19 = (bf16[512,384]{1,0:T(8,128)(2,1)S(1)}, bf16[512,384]{1,0:T(8,128)(2,1)S(1)}, u32[]{:S(2)}, u32[]{:S(2)}) collective-permute-start(bf16[512,384]{1,0:T(8,128)(2,1)S(1)} %get-tuple-element.58), channel_id=1, source_target_pairs={{0,2},{1,3},{2,0},{3,1},{4,6},{5,7},{6,4},{7,5},{8,10},{9,11},{10,... | collective-permute-start | bytes 1179656 | tf_op jit(solution)/shard_map/ppermute | solution.py:21
  54.8 33.9 %collective-permute-start.21 = (bf16[512,384]{1,0:T(8,128)(2,1)S(1)}, bf16[512,384]{1,0:T(8,128)(2,1)S(1)}, u32[]{:S(2)}, u32[]{:S(2)}) collective-permute-start(bf16[512,384]{1,0:T(8,128)(2,1)S(1)} %get-tuple-element.61), channel_id=1, source_target_pairs={{0,1},{1,0},{2,3},{3,2},{4,5},{5,4},{6,7},{7,6},{8,9},{9,8},{10,11... | collective-permute-start | bytes 1179656 | tf_op jit(solution)/shard_map/ppermute | solution.py:21
  56.3 1.2 %collective-permute-start.8 = (bf16[144,128]{1,0:T(8,128)(2,1)S(1)}, bf16[144,128]{1,0:T(8,128)(2,1)S(1)}, u32[]{:S(2)}, u32[]{:S(2)}) collective-permute-start(bf16[144,128]{1,0:T(8,128)(2,1)S(1)} %shard_map.104.refs_0_), channel_id=1, source_target_pairs={{0,4},{4,0},{8,12},{12,8},{16,20},{20,16},{24,28},{28,24},{1,5},{5... | collective-permute-start | bytes 110600 | tf_op jit(solution)/shard_map/ppermute | solution.py:21
  57.6 4.2 %collective-permute-start.9 = (bf16[224,128]{1,0:T(8,128)(2,1)S(1)}, bf16[224,128]{1,0:T(8,128)(2,1)S(1)}, u32[]{:S(2)}, u32[]{:S(2)}) collective-permute-start(bf16[224,128]{1,0:T(8,128)(2,1)S(1)} %shard_map.105.refs_0_), channel_id=1, source_target_pairs={{0,8},{4,12},{8,0},{12,4},{16,24},{20,28},{24,16},{28,20},{1,9},{5... | collective-permute-start | bytes 172040 | tf_op jit(solution)/shard_map/ppermute | solution.py:21
  61.8 5.1 %collective-permute-start.10 = (bf16[224,128]{1,0:T(8,128)(2,1)S(1)}, bf16[224,128]{1,0:T(8,128)(2,1)S(1)}, u32[]{:S(2)}, u32[]{:S(2)}) collective-permute-start(bf16[224,128]{1,0:T(8,128)(2,1)S(1)} %shard_map.105.refs_0_), channel_id=1, source_target_pairs={{0,16},{4,20},{8,24},{12,28},{16,0},{20,4},{24,8},{28,12},{1,17},{... | collective-permute-start | bytes 172040 | tf_op jit(solution)/shard_map/ppermute | solution.py:21
  66.9 6.3 %collective-permute-start.11 = (bf16[224,128]{1,0:T(8,128)(2,1)S(1)}, bf16[224,128]{1,0:T(8,128)(2,1)S(1)}, u32[]{:S(2)}, u32[]{:S(2)}) collective-permute-start(bf16[224,128]{1,0:T(8,128)(2,1)S(1)} %shard_map.105.refs_0_), channel_id=1, source_target_pairs={{0,24},{4,28},{8,16},{12,20},{16,8},{20,12},{24,0},{28,4},{1,25},{... | collective-permute-start | bytes 172040 | tf_op jit(solution)/shard_map/ppermute | solution.py:21
  75.1 3.7 %collective-permute-start.12 = (bf16[32,128]{1,0:T(8,128)(2,1)S(1)}, bf16[32,128]{1,0:T(8,128)(2,1)S(1)}, u32[]{:S(2)}, u32[]{:S(2)}) collective-permute-start(bf16[32,128]{1,0:T(8,128)(2,1)S(1)} %get-tuple-element.51.refs_2_), channel_id=1, source_target_pairs={{0,1},{1,0},{2,3},{3,2},{4,5},{5,4},{6,7},{7,6},{8,9},{9,8},{10,11... | collective-permute-start | bytes 24584 | tf_op jit(solution)/shard_map/ppermute | solution.py:21
  78.8 3.7 %collective-permute-start.13 = (bf16[32,128]{1,0:T(8,128)(2,1)S(1)}, bf16[32,128]{1,0:T(8,128)(2,1)S(1)}, u32[]{:S(2)}, u32[]{:S(2)}) collective-permute-start(bf16[32,128]{1,0:T(8,128)(2,1)S(1)} %get-tuple-element.51.refs_2_), channel_id=1, source_target_pairs={{0,2},{1,3},{2,0},{3,1},{4,6},{5,7},{6,4},{7,5},{8,10},{9,11},{10,... | collective-permute-start | bytes 24584 | tf_op jit(solution)/shard_map/ppermute | solution.py:21
  82.4 4.5 %collective-permute-start.14 = (bf16[32,128]{1,0:T(8,128)(2,1)S(1)}, bf16[32,128]{1,0:T(8,128)(2,1)S(1)}, u32[]{:S(2)}, u32[]{:S(2)}) collective-permute-start(bf16[32,128]{1,0:T(8,128)(2,1)S(1)} %get-tuple-element.51.refs_2_), channel_id=1, source_target_pairs={{0,3},{1,2},{2,1},{3,0},{4,7},{5,6},{6,5},{7,4},{8,11},{9,10},{10,... | collective-permute-start | bytes 24584 | tf_op jit(solution)/shard_map/ppermute | solution.py:21
  87.0 5.0 %collective-permute-start.22 = (bf16[512,128]{1,0:T(8,128)(2,1)S(1)}, bf16[512,128]{1,0:T(8,128)(2,1)S(1)}, u32[]{:S(2)}, u32[]{:S(2)}) collective-permute-start(bf16[512,128]{1,0:T(8,128)(2,1)S(1)} %get-tuple-element.63), channel_id=1, source_target_pairs={{0,2},{1,3},{2,0},{3,1},{4,6},{5,7},{6,4},{7,5},{8,10},{9,11},{10,... | collective-permute-start | bytes 393224 | tf_op jit(solution)/shard_map/ppermute | solution.py:21
  87.5 5.0 %collective-permute-start.23 = (bf16[512,128]{1,0:T(8,128)(2,1)S(1)}, bf16[512,128]{1,0:T(8,128)(2,1)S(1)}, u32[]{:S(2)}, u32[]{:S(2)}) collective-permute-start(bf16[512,128]{1,0:T(8,128)(2,1)S(1)} %get-tuple-element.64), channel_id=1, source_target_pairs={{0,1},{1,0},{2,3},{3,2},{4,5},{5,4},{6,7},{7,6},{8,9},{9,8},{10,11... | collective-permute-start | bytes 393224 | tf_op jit(solution)/shard_map/ppermute | solution.py:21

commit v10 on v9

--- a/solution.py
+++ b/solution.py
@@ -16,9 +16,24 @@
 UNROLL = 32
 
 
+def group_mask(index, leaf):
+    return index + (0, 1, -1, 0)[index] * (leaf % 2)
+
+
 def exchange(block, axis, mask):
     count = lax.axis_size(axis)
-    return lax.ppermute(block, axis, [(low, low ^ mask) for low in range(count)])
+    if axis == LEAF:
+        return lax.ppermute(block, axis, [(low, low ^ mask) for low in range(count)])
+    pairs = []
+    for leaf in range(lax.axis_size(LEAF)):
+        for low in range(count):
+            base = leaf * count
+            pairs.append((base + low, base + (low ^ group_mask(mask, leaf))))
+    return lax.ppermute(block, (LEAF, axis), pairs)
+
+
+def owner(index):
+    return lax.axis_index(GRP) ^ group_mask(index, lax.axis_index(LEAF))
 
 
 def level_offset(sep_block, tree_level):
@@ -211,14 +226,13 @@
     factor = jnp.concatenate([factor, jnp.zeros((rows, tiles * LANES - cols), F32)], axis=1)
     folded = [factor[:, tile * LANES : (tile + 1) * LANES] for tile in range(tiles)]
     folded = jnp.concatenate(folded, axis=0)
-    me = lax.axis_index(GRP)
     kept_ref[first:, :] = jnp.concatenate([folded, folded], axis=1)
     out_0_ref[height + first :, :] = jnp.concatenate([folded, folded], axis=1).astype(BF16)
     for index, (mine, sent) in enumerate(((0, 1), (2, 3))):
         place = slice(index * LANES, (index + 1) * LANES)
-        lanes = pl.ds(pl.multiple_of((me ^ mine) * LANES, LANES), LANES)
+        lanes = pl.ds(pl.multiple_of(owner(mine) * LANES, LANES), LANES)
         kept_ref[:first, place] = crossing_ref[:, lanes]
-        lanes = pl.ds(pl.multiple_of((me ^ sent) * LANES, LANES), LANES)
+        lanes = pl.ds(pl.multiple_of(owner(sent) * LANES, LANES), LANES)
         out_0_ref[height : height + first, place] = crossing_ref[:, lanes].astype(BF16)
 
 
@@ -226,7 +240,6 @@
     levels, sep_block, _ = sep_ref.shape
     first = kept_ref.shape[0] - sep_block
     tiles = sep_block // rows
-    me = lax.axis_index(GRP)
     x_part = x_ref[x_ref.shape[0] - first - sep_block :, :].astype(F32)
     y_part = y_ref[y_ref.shape[0] - first :, :].astype(F32)
     total = kept_ref[:first, :LANES] + x_part[:first, :LANES] + y_part[:, :LANES]
@@ -246,7 +259,7 @@
         block = [folded[tile * rows : (tile + 1) * rows, :] for tile in range(tiles)]
         block = jnp.concatenate(block, axis=1)
         tiled = jnp.concatenate([block] * (sep_block // rows), axis=0)
-        factor = factor + jnp.where(row_owner == (me ^ index), tiled, 0.0)
+        factor = factor + jnp.where(row_owner == owner(index), tiled, 0.0)
     pivots = dinv_ref[...].astype(F32).T
     for level in range(levels):
         column = jnp.broadcast_to(pivots[:, level : level + 1], factor.shape)
@@ -468,9 +481,8 @@
 
 def run_base(own_ref, link_ref, mine_ref, x_ref, y_ref, d_ref, x_low_ref, y_high_ref, out_0_ref, out_1_ref, first_ref):
     half = x_low_ref.shape[0]
-    me = lax.axis_index(GRP)
     for mask, ref in enumerate((mine_ref, x_ref, y_ref, d_ref)):
-        lanes = pl.ds(pl.multiple_of((me ^ mask) * LANES, LANES), LANES)
+        lanes = pl.ds(pl.multiple_of(owner(mask) * LANES, LANES), LANES)
         first_ref[:, lanes] = ref[...]
     start = 0
     for ref in (out_0_ref, out_1_ref):
@@ -503,7 +515,7 @@
 
 def local_pairs(leaf_rhs, leaf_inv, ordering, leaf_dinv, leaf_link, sep_rhs, sep_factor, sep_dinv):
     rows, width = leaf_rhs.shape
-    half, split = rows // 2, rows // 16 * 7
+    half, split = rows // 2, rows // 2
     group = lax.axis_size(GRP)
     levels, slice_width, sep_block = sep_rhs.shape
     first = leaf_link.shape[1]
@@ -533,7 +545,9 @@
     )
     y_high = exchange(high, GRP, 2)
     y_low = exchange(low, GRP, 2)
-    dest = (ordering[0] // rows ^ me) * rows + ordering[0] % rows
+    distance = ordering[0] // rows ^ me
+    swapped = (lax.axis_index(LEAF) % 2 == 1) & (distance % 3 != 0)
+    dest = jnp.where(swapped, 3 - distance, distance) * rows + ordering[0] % rows
     blocks = arrange(leaf_inv, dest, group)
 
     *high_cut, kept = call(

time: 93.5 us -> 92.8 us (level)
  waiting for transfers between devices: 28.3 us -> 26.2 us
  starting transfers between devices: 31.2 us -> 32.6 us
    ppermute x0 -> x20, starting transfers between devices: none -> 24.2 us  [exchange(): return lax.ppermute(block, (LEAF, axis), pairs)]
    ppermute x24 -> x4, starting transfers between devices: 31.2 us -> 8.35 us  [exchange(): lax.ppermute(block, axis, [(low, low ^ mask) for low in range(count)])]
    ppermute x24 -> x4, waiting for transfers between devices: 28.3 us -> 8.44 us  [exchange(): lax.ppermute(block, axis, [(low, low ^ mask) for low in range(count)])]
    ppermute x0 -> x20, waiting for transfers between devices: none -> 17.7 us  [exchange(): return lax.ppermute(block, (LEAF, axis), pairs)]
  transfers between devices with their start and end apart: 24 -> 24, of which waited for: 13 -> 12; matrix products, arithmetic and copies ran while one was open for 0% -> 0% of each run, Pallas kernels for 34% -> 35%
where the time goes in v10:
time: 92.8 us; the launch traced here: 92.5 us
  Pallas kernels  32.9 us (35%)
  starting transfers between devices  32.6 us (35%)
  waiting for transfers between devices  26.2 us (28%)
    pallas_call x17, Pallas kernels, call(): pl.pallas_call(skipping, out_shape=out_shape, in_specs=[pl.BlockSpec(memo...  32.9 us
    ppermute x20, starting transfers between devices, exchange(): return lax.ppermute(block, (LEAF, axis), pairs)  24.2 us
    ppermute x20, waiting for transfers between devices, exchange(): return lax.ppermute(block, (LEAF, axis), pairs)  17.7 us
    ppermute x4, waiting for transfers between devices, exchange(): lax.ppermute(block, axis, [(low, low ^ mask) for low in range(count)])  8.44 us
    ppermute x4, starting transfers between devices, exchange(): lax.ppermute(block, axis, [(low, low ^ mask) for low in range(count)])  8.35 us
  transfers between devices with their start and end apart: 24, of which 12 were waited for; matrix products, arithmetic and copies ran while one was open for 0% of the time, Pallas kernels for 35%

profile of v10, /device:TPU:0, one launch (start us, length us, event | category | flops | bytes accessed | tf_op | source)
XLA Modules:
  0.0 92.5 jit_solution(17295662041451973089)
XLA Ops:
  0.6 3.0 %collective-permute-start = (bf16[1024,512]{1,0:T(8,128)(2,1)}, bf16[1024,512]{1,0:T(8,128)(2,1)S(1)}, u32[]{:S(2)}, u32[]{:S(2)}) collective-permute-start(bf16[1024,512]{1,0:T(8,128)(2,1)} %refs_0_.3), channel_id=1, source_target_pairs={{0,1},{1,0},{2,3},{3,2},{4,6},{5,7},{6,4},{7,5},{8,9},{9,8},{10,11... | collective-permute-start | bytes 3145736 | tf_op jit(solution)/shard_map/ppermute | solution.py:32
  3.7 1.1 %shard_map.97.refs_6_.refs_3_ = bf16[512,512]{1,0:T(8,128)(2,1)S(1)} custom-call(bf16[1024,512]{1,0:T(8,128)(2,1)} %refs_0_.3), custom_call_target="tpu_custom_call" | custom-call | tf_op jit(solution)/shard_map/pallas_call | solution.py:68
  4.8 1.6 %collective-permute-start.2 = (bf16[512,512]{1,0:T(8,128)(2,1)S(1)}, bf16[512,512]{1,0:T(8,128)(2,1)S(1)}, u32[]{:S(2)}, u32[]{:S(2)}) collective-permute-start(bf16[512,512]{1,0:T(8,128)(2,1)S(1)} %shard_map.97.refs_6_.refs_3_), channel_id=1, source_target_pairs={{0,2},{1,3},{2,0},{3,1},{4,5},{5,4},{6,7},{7,6},{8,10},{9,11},{10,... | collective-permute-start | bytes 1572872 | tf_op jit(solution)/shard_map/ppermute | solution.py:32
  6.3 1.0 %shard_map.96.refs_5_.refs_2_ = bf16[512,512]{1,0:T(8,128)(2,1)S(1)} custom-call(bf16[1024,512]{1,0:T(8,128)(2,1)} %refs_0_.3), custom_call_target="tpu_custom_call" | custom-call | tf_op jit(solution)/shard_map/pallas_call | solution.py:68
  7.4 0.6 collective-permute-start.1
  8.0 16.0 %shard_map.95 = (bf16[1024,1024]{1,0:T(8,128)(2,1)S(1)}, bf16[1024,1024]{1,0:T(8,128)(2,1)S(1)}, bf16[1024,1024]{1,0:T(8,128)(2,1)S(1)}, bf16[1024,1024]{1,0:T(8,128)(2,1)S(1)}) custom-call(s32[4096]{0:T(1024)S(1)} %fusion.3.refs_0_, bf16[1024,4096]{1,0:T(8,128)(2,1)} %refs_1_.1), custom_call_target="tpu_custom_call" | custom-call | tf_op jit(solution)/shard_map/pallas_call | solution.py:68
  24.1 0.3 shard_map.100
  24.4 0.1 collective-permute-start.4
  24.5 2.0 %collective-permute-done.refs_7_.refs_1_ = bf16[1024,512]{1,0:T(8,128)(2,1)S(1)} collective-permute-done((bf16[1024,512]{1,0:T(8,128)(2,1)}, bf16[1024,512]{1,0:T(8,128)(2,1)S(1)}, u32[]{:S(2)}, u32[]{:S(2)}) %collective-permute-start) | collective-permute-done | bytes 1048608 | tf_op jit(solution)/shard_map/ppermute | solution.py:32
  26.5 3.5 %collective-permute-start.3 = (bf16[512,256]{1,0:T(8,128)(2,1)S(1)}, bf16[512,256]{1,0:T(8,128)(2,1)S(1)}, u32[]{:S(2)}, u32[]{:S(2)}) collective-permute-start(bf16[512,256]{1,0:T(8,128)(2,1)S(1)} %get-tuple-element.39), channel_id=1, source_target_pairs={{0,2},{1,3},{2,0},{3,1},{4,5},{5,4},{6,7},{7,6},{8,10},{9,11},{10,... | collective-permute-start | bytes 786440 | tf_op jit(solution)/shard_map/ppermute | solution.py:32
  30.0 1.5 %collective-permute-start.6 = (bf16[512,256]{1,0:T(8,128)(2,1)S(1)}, bf16[512,256]{1,0:T(8,128)(2,1)S(1)}, u32[]{:S(2)}, u32[]{:S(2)}) collective-permute-start(bf16[512,256]{1,0:T(8,128)(2,1)S(1)} %get-tuple-element.46), channel_id=1, source_target_pairs={{0,1},{1,0},{2,3},{3,2},{4,6},{5,7},{6,4},{7,5},{8,9},{9,8},{10,11... | collective-permute-start | bytes 786440 | tf_op jit(solution)/shard_map/ppermute | solution.py:32
  31.6 3.5 %shard_map.98 = (f32[1024,256]{1,0:T(8,128)S(1)}, f32[1024,256]{1,0:T(8,128)S(1)}, bf16[1024,1024]{1,0:T(8,128)(2,1)S(1)}, f32[1024,128]{1,0:T(8,128)S(1)}) custom-call(bf16[1024,1024]{1,0:T(8,128)(2,1)S(1)} %get-tuple-element.34.refs_0_, bf16[1024,1024]{1,0:T(8,128)(2,1)S(1)} %get-tuple-element.35.refs_1_, ...), custom_call_target="tpu_custom_call" | custom-call | tf_op jit(solution)/shard_map/pallas_call | solution.py:68
  35.1 0.6 collective-permute-done.3.refs_2_
  35.8 1.3 %shard_map.101 = (bf16[1024,256]{1,0:T(8,128)(2,1)S(1)}, bf16[512,256]{1,0:T(8,128)(2,1)S(1)}, bf16[544,256]{1,0:T(8,128)(2,1)S(1)}) custom-call(bf16[1024,1024]{1,0:T(8,128)(2,1)S(1)} %get-tuple-element.37.refs_3_.refs_0_, bf16[1024,1024]{1,0:T(8,128)(2,1)S(1)} %get-tuple-element.38.refs_1_, bf16[512,256]{1,0:T(8,128)(2,1)S(1)} %collective-permute-done.3.refs_2_, ...), custom_call_target="tpu_custom_call" | custom-call | tf_op jit(solution)/shard_map/pallas_call | solution.py:68
  37.0 1.8 %collective-permute-start.17 = (bf16[512,256]{1,0:T(8,128)(2,1)S(1)}, bf16[512,256]{1,0:T(8,128)(2,1)S(1)}, u32[]{:S(2)}, u32[]{:S(2)}) collective-permute-start(bf16[512,256]{1,0:T(8,128)(2,1)S(1)} %get-tuple-element.56), channel_id=1, source_target_pairs={{0,1},{1,0},{2,3},{3,2},{4,6},{5,7},{6,4},{7,5},{8,9},{9,8},{10,11... | collective-permute-start | bytes 786440 | tf_op jit(solution)/shard_map/ppermute | solution.py:32
  38.8 1.5 %collective-permute-start.7 = (bf16[544,256]{1,0:T(8,128)(2,1)S(1)}, bf16[544,256]{1,0:T(8,128)(2,1)S(1)}, u32[]{:S(2)}, u32[]{:S(2)}) collective-permute-start(bf16[544,256]{1,0:T(8,128)(2,1)S(1)} %get-tuple-element.50), channel_id=1, source_target_pairs={{0,2},{1,3},{2,0},{3,1},{4,5},{5,4},{6,7},{7,6},{8,10},{9,11},{10,... | collective-permute-start | bytes 835592 | tf_op jit(solution)/shard_map/ppermute | solution.py:32
  40.3 1.3 %shard_map.102 = (bf16[1024,256]{1,0:T(8,128)(2,1)S(1)}, bf16[512,256]{1,0:T(8,128)(2,1)S(1)}, bf16[512,256]{1,0:T(8,128)(2,1)S(1)}) custom-call(bf16[1024,1024]{1,0:T(8,128)(2,1)S(1)} %get-tuple-element.37.refs_3_.refs_0_, bf16[1024,1024]{1,0:T(8,128)(2,1)S(1)} %get-tuple-element.38.refs_1_, bf16[512,256]{1,0:T(8,128)(2,1)S(1)} %collective-permute-done.5.refs_2_, ...), custom_call_target="tpu_custom_call" | custom-call | tf_op jit(solution)/shard_map/pallas_call | solution.py:68
  41.6 0.6 collective-permute-start.18
  42.2 2.3 %collective-permute-start.20 = (bf16[512,256]{1,0:T(8,128)(2,1)S(1)}, bf16[512,256]{1,0:T(8,128)(2,1)S(1)}, u32[]{:S(2)}, u32[]{:S(2)}) collective-permute-start(bf16[512,256]{1,0:T(8,128)(2,1)S(1)} %get-tuple-element.60), channel_id=1, source_target_pairs={{0,2},{1,3},{2,0},{3,1},{4,5},{5,4},{6,7},{7,6},{8,10},{9,11},{10,... | collective-permute-start | bytes 786440 | tf_op jit(solution)/shard_map/ppermute | solution.py:32
  44.5 3.5 %shard_map.103 = (bf16[512,512]{1,0:T(8,128)(2,1)S(1)}, bf16[512,512]{1,0:T(8,128)(2,1)S(1)}, f32[512,512]{1,0:T(8,128)S(1)}, f32[512,512]{1,0:T(8,128)S(1)}, f32[1024,512]{1,0:T(8,128)S(1)}) custom-call(bf16[1024,1024]{1,0:T(8,128)(2,1)S(1)} %get-tuple-element.34.refs_0_, bf16[1024,1024]{1,0:T(8,128)(2,1)S(1)} %get-tuple-element.35.refs_1_, ...), custom_call_target="tpu_custom_call" | custom-call | tf_op jit(solution)/shard_map/pallas_call | solution.py:68
  48.0 0.6 collective-permute-start.15
  48.7 0.7 collective-permute-start.16
  49.3 1.9 %collective-permute-done.18.refs_2_ = bf16[512,256]{1,0:T(8,128)(2,1)S(1)} collective-permute-done((bf16[512,256]{1,0:T(8,128)(2,1)S(1)}, bf16[512,256]{1,0:T(8,128)(2,1)S(1)}, u32[]{:S(2)}, u32[]{:S(2)}) %collective-permute-start.18) | collective-permute-done | bytes 262176 | tf_op jit(solution)/shard_map/ppermute | solution.py:32
  51.4 2.5 %collective-permute-start.19 = (bf16[512,384]{1,0:T(8,128)(2,1)S(1)}, bf16[512,384]{1,0:T(8,128)(2,1)S(1)}, u32[]{:S(2)}, u32[]{:S(2)}) collective-permute-start(bf16[512,384]{1,0:T(8,128)(2,1)S(1)} %get-tuple-element.58), channel_id=1, source_target_pairs={{0,2},{1,3},{2,0},{3,1},{4,5},{5,4},{6,7},{7,6},{8,10},{9,11},{10,... | collective-permute-start | bytes 1179656 | tf_op jit(solution)/shard_map/ppermute | solution.py:32
  53.8 0.1 shard_map.109
  54.0 1.6 %collective-permute-start.21 = (bf16[512,384]{1,0:T(8,128)(2,1)S(1)}, bf16[512,384]{1,0:T(8,128)(2,1)S(1)}, u32[]{:S(2)}, u32[]{:S(2)}) collective-permute-start(bf16[512,384]{1,0:T(8,128)(2,1)S(1)} %get-tuple-element.61), channel_id=1, source_target_pairs={{0,1},{1,0},{2,3},{3,2},{4,6},{5,7},{6,4},{7,5},{8,9},{9,8},{10,11... | collective-permute-start | bytes 1179656 | tf_op jit(solution)/shard_map/ppermute | solution.py:32
  55.5 0.1 shard_map.104.refs_0_
  55.7 1.2 %collective-permute-done.8.refs_1_ = bf16[144,128]{1,0:T(8,128)(2,1)S(1)} collective-permute-done((bf16[144,128]{1,0:T(8,128)(2,1)S(1)}, bf16[144,128]{1,0:T(8,128)(2,1)S(1)}, u32[]{:S(2)}, u32[]{:S(2)}) %collective-permute-start.8) | collective-permute-done | bytes 36896 | tf_op jit(solution)/shard_map/ppermute | solution.py:26
  56.9 1.6 %collective-permute-start.9 = (bf16[224,128]{1,0:T(8,128)(2,1)S(1)}, bf16[224,128]{1,0:T(8,128)(2,1)S(1)}, u32[]{:S(2)}, u32[]{:S(2)}) collective-permute-start(bf16[224,128]{1,0:T(8,128)(2,1)S(1)} %shard_map.105.refs_0_), channel_id=1, source_target_pairs={{0,8},{4,12},{8,0},{12,4},{16,24},{20,28},{24,16},{28,20},{1,9},{5... | collective-permute-start | bytes 172040 | tf_op jit(solution)/shard_map/ppermute | solution.py:26
  58.5 2.6 %collective-permute-done.9.refs_1_ = bf16[224,128]{1,0:T(8,128)(2,1)S(1)} collective-permute-done((bf16[224,128]{1,0:T(8,128)(2,1)S(1)}, bf16[224,128]{1,0:T(8,128)(2,1)S(1)}, u32[]{:S(2)}, u32[]{:S(2)}) %collective-permute-start.9) | collective-permute-done | bytes 57376 | tf_op jit(solution)/shard_map/ppermute | solution.py:26
  61.1 2.6 %collective-permute-start.10 = (bf16[224,128]{1,0:T(8,128)(2,1)S(1)}, bf16[224,128]{1,0:T(8,128)(2,1)S(1)}, u32[]{:S(2)}, u32[]{:S(2)}) collective-permute-start(bf16[224,128]{1,0:T(8,128)(2,1)S(1)} %shard_map.105.refs_0_), channel_id=1, source_target_pairs={{0,16},{4,20},{8,24},{12,28},{16,0},{20,4},{24,8},{28,12},{1,17},{... | collective-permute-start | bytes 172040 | tf_op jit(solution)/shard_map/ppermute | solution.py:26
  63.7 2.5 %collective-permute-done.10.refs_2_ = bf16[224,128]{1,0:T(8,128)(2,1)S(1)} collective-permute-done((bf16[224,128]{1,0:T(8,128)(2,1)S(1)}, bf16[224,128]{1,0:T(8,128)(2,1)S(1)}, u32[]{:S(2)}, u32[]{:S(2)}) %collective-permute-start.10) | collective-permute-done | bytes 57376 | tf_op jit(solution)/shard_map/ppermute | solution.py:26
  66.2 4.1 %collective-permute-start.11 = (bf16[224,128]{1,0:T(8,128)(2,1)S(1)}, bf16[224,128]{1,0:T(8,128)(2,1)S(1)}, u32[]{:S(2)}, u32[]{:S(2)}) collective-permute-start(bf16[224,128]{1,0:T(8,128)(2,1)S(1)} %shard_map.105.refs_0_), channel_id=1, source_target_pairs={{0,24},{4,28},{8,16},{12,20},{16,8},{20,12},{24,0},{28,4},{1,25},{... | collective-permute-start | bytes 172040 | tf_op jit(solution)/shard_map/ppermute | solution.py:26
  70.3 2.2 %collective-permute-done.11.refs_3_ = bf16[224,128]{1,0:T(8,128)(2,1)S(1)} collective-permute-done((bf16[224,128]{1,0:T(8,128)(2,1)S(1)}, bf16[224,128]{1,0:T(8,128)(2,1)S(1)}, u32[]{:S(2)}, u32[]{:S(2)}) %collective-permute-start.11) | collective-permute-done | bytes 57376 | tf_op jit(solution)/shard_map/ppermute | solution.py:26
  72.5 1.9 %shard_map.106 = (bf16[32,128]{1,0:T(8,128)(2,1)S(1)}, f32[3,16,128]{2,1,0:T(8,128)}) custom-call(bf16[224,128]{1,0:T(8,128)(2,1)S(1)} %shard_map.105.refs_0_, bf16[224,128]{1,0:T(8,128)(2,1)S(1)} %collective-permute-done.9.refs_1_, bf16[224,128]{1,0:T(8,128)(2,1)S(1)} %collective-permute-done.10.refs_2_, bf16[224,128]{1,0:T(8,128)(2,1)S(1)} %collective-permute-done.11.refs_3_), custom_call_target="tpu_custom_call" | custom-call | tf_op jit(solution)/shard_map/pallas_call | solution.py:68
  74.4 0.5 collective-permute-start.12
  75.0 3.1 %collective-permute-done.12.refs_3_ = bf16[32,128]{1,0:T(8,128)(2,1)S(1)} collective-permute-done((bf16[32,128]{1,0:T(8,128)(2,1)S(1)}, bf16[32,128]{1,0:T(8,128)(2,1)S(1)}, u32[]{:S(2)}, u32[]{:S(2)}) %collective-permute-start.12) | collective-permute-done | bytes 8224 | tf_op jit(solution)/shard_map/ppermute | solution.py:32
  78.1 0.4 collective-permute-start.13
  78.5 3.2 %collective-permute-done.13.refs_4_ = bf16[32,128]{1,0:T(8,128)(2,1)S(1)} collective-permute-done((bf16[32,128]{1,0:T(8,128)(2,1)S(1)}, bf16[32,128]{1,0:T(8,128)(2,1)S(1)}, u32[]{:S(2)}, u32[]{:S(2)}) %collective-permute-start.13) | collective-permute-done | bytes 8224 | tf_op jit(solution)/shard_map/ppermute | solution.py:32
  81.7 0.4 collective-permute-start.14
  82.1 4.1 %collective-permute-done.14.refs_5_ = bf16[32,128]{1,0:T(8,128)(2,1)S(1)} collective-permute-done((bf16[32,128]{1,0:T(8,128)(2,1)S(1)}, bf16[32,128]{1,0:T(8,128)(2,1)S(1)}, u32[]{:S(2)}, u32[]{:S(2)}) %collective-permute-start.14) | collective-permute-done | bytes 8224 | tf_op jit(solution)/shard_map/ppermute | solution.py:32
  86.3 0.4 collective-permute-start.22
  86.7 0.5 collective-permute-start.23
  87.3 0.5 shard_map.107
  87.8 1.2 %shard_map.110.refs_0_ = f32[1024,512]{1,0:T(8,128)} custom-call(f32[1024,384]{1,0:T(8,128)S(1)} %get-tuple-element.54.refs_0_, bf16[512,384]{1,0:T(8,128)(2,1)S(1)} %collective-permute-done.19.refs_1_, bf16[512,384]{1,0:T(8,128)(2,1)S(1)} %collective-permute-done.21.refs_2_), custom_call_target="tpu_custom_call" | custom-call | tf_op jit(solution)/shard_map/pallas_call | solution.py:68
  89.0 2.3 %collective-permute-done.22.refs_2_ = bf16[512,128]{1,0:T(8,128)(2,1)S(1)} collective-permute-done((bf16[512,128]{1,0:T(8,128)(2,1)S(1)}, bf16[512,128]{1,0:T(8,128)(2,1)S(1)}, u32[]{:S(2)}, u32[]{:S(2)}) %collective-permute-start.22) | collective-permute-done | bytes 131104 | tf_op jit(solution)/shard_map/ppermute | solution.py:32
  91.2 0.4 collective-permute-done.23.refs_3_
  91.7 0.8 shard_map.111
  (30 shorter events, 0.4 us)
Async XLA Ops:
  0.6 7.3 %copy-start.5 = (s32[1,4096]{1,0:T(1,128)S(1)}, s32[1,4096]{1,0:T(1,128)}, u32[]{:S(2)}) copy-start(s32[1,4096]{1,0:T(1,128)} %param.10) | copy-start | bytes 49156
  0.6 25.8 %collective-permute-start = (bf16[1024,512]{1,0:T(8,128)(2,1)}, bf16[1024,512]{1,0:T(8,128)(2,1)S(1)}, u32[]{:S(2)}, u32[]{:S(2)}) collective-permute-start(bf16[1024,512]{1,0:T(8,128)(2,1)} %refs_0_.3), channel_id=1, source_target_pairs={{0,1},{1,0},{2,3},{3,2},{4,6},{5,7},{6,4},{7,5},{8,9},{9,8},{10,11... | collective-permute-start | bytes 3145736 | tf_op jit(solution)/shard_map/ppermute | solution.py:32
  4.8 19.3 %collective-permute-start.2 = (bf16[512,512]{1,0:T(8,128)(2,1)S(1)}, bf16[512,512]{1,0:T(8,128)(2,1)S(1)}, u32[]{:S(2)}, u32[]{:S(2)}) collective-permute-start(bf16[512,512]{1,0:T(8,128)(2,1)S(1)} %shard_map.97.refs_6_.refs_3_), channel_id=1, source_target_pairs={{0,2},{1,3},{2,0},{3,1},{4,5},{5,4},{6,7},{7,6},{8,10},{9,11},{10,... | collective-permute-start | bytes 1572872 | tf_op jit(solution)/shard_map/ppermute | solution.py:32
  7.4 24.2 %collective-permute-start.1 = (bf16[512,512]{1,0:T(8,128)(2,1)S(1)}, bf16[512,512]{1,0:T(8,128)(2,1)S(1)}, u32[]{:S(2)}, u32[]{:S(2)}) collective-permute-start(bf16[512,512]{1,0:T(8,128)(2,1)S(1)} %shard_map.96.refs_5_.refs_2_), channel_id=1, source_target_pairs={{0,2},{1,3},{2,0},{3,1},{4,5},{5,4},{6,7},{7,6},{8,10},{9,11},{10,... | collective-permute-start | bytes 1572872 | tf_op jit(solution)/shard_map/ppermute | solution.py:32
  8.0 16.0 %copy-start = (bf16[1024,32]{0,1:T(8,128)(2,1)S(1)}, bf16[1024,32]{0,1:T(8,128)(2,1)}, u32[]{:S(2)}) copy-start(bf16[1024,32]{0,1:T(8,128)(2,1)} %param.12) | copy-start | bytes 196612
  8.0 16.0 %copy-start.2 = (bf16[4,416]{1,0:T(4,128)(2,1)S(1)}, bf16[4,416]{1,0:T(4,128)(2,1)}, u32[]{:S(2)}) copy-start(bf16[4,416]{1,0:T(4,128)(2,1)} %refs_5_.2) | copy-start | bytes 9988
  24.4 7.2 %copy-start.3 = (bf16[1024]{0:T(1024)(128)(2,1)S(1)}, bf16[1024]{0:T(1024)(128)(2,1)}, u32[]{:S(2)}) copy-start(bf16[1024]{0:T(1024)(128)(2,1)} %param.11) | copy-start | bytes 6148
  24.4 10.7 %collective-permute-start.4 = (bf16[560,256]{1,0:T(8,128)(2,1)S(1)}, bf16[560,256]{1,0:T(8,128)(2,1)S(1)}, u32[]{:S(2)}, u32[]{:S(2)}) collective-permute-start(bf16[560,256]{1,0:T(8,128)(2,1)S(1)} %get-tuple-element.40), channel_id=1, source_target_pairs={{0,1},{1,0},{2,3},{3,2},{4,6},{5,7},{6,4},{7,5},{8,9},{9,8},{10,11... | collective-permute-start | bytes 860168 | tf_op jit(solution)/shard_map/ppermute | solution.py:32
  26.5 9.2 %collective-permute-start.3 = (bf16[512,256]{1,0:T(8,128)(2,1)S(1)}, bf16[512,256]{1,0:T(8,128)(2,1)S(1)}, u32[]{:S(2)}, u32[]{:S(2)}) collective-permute-start(bf16[512,256]{1,0:T(8,128)(2,1)S(1)} %get-tuple-element.39), channel_id=1, source_target_pairs={{0,2},{1,3},{2,0},{3,1},{4,5},{5,4},{6,7},{7,6},{8,10},{9,11},{10,... | collective-permute-start | bytes 786440 | tf_op jit(solution)/shard_map/ppermute | solution.py:32
  30.0 10.3 %collective-permute-start.6 = (bf16[512,256]{1,0:T(8,128)(2,1)S(1)}, bf16[512,256]{1,0:T(8,128)(2,1)S(1)}, u32[]{:S(2)}, u32[]{:S(2)}) collective-permute-start(bf16[512,256]{1,0:T(8,128)(2,1)S(1)} %get-tuple-element.46), channel_id=1, source_target_pairs={{0,1},{1,0},{2,3},{3,2},{4,6},{5,7},{6,4},{7,5},{8,9},{9,8},{10,11... | collective-permute-start | bytes 786440 | tf_op jit(solution)/shard_map/ppermute | solution.py:32
  31.5 8.8 %collective-permute-start.5 = (bf16[512,256]{1,0:T(8,128)(2,1)S(1)}, bf16[512,256]{1,0:T(8,128)(2,1)S(1)}, u32[]{:S(2)}, u32[]{:S(2)}) collective-permute-start(bf16[512,256]{1,0:T(8,128)(2,1)S(1)} %get-tuple-element.45), channel_id=1, source_target_pairs={{0,2},{1,3},{2,0},{3,1},{4,5},{5,4},{6,7},{7,6},{8,10},{9,11},{10,... | collective-permute-start | bytes 786440 | tf_op jit(solution)/shard_map/ppermute | solution.py:32
  37.0 11.6 %collective-permute-start.17 = (bf16[512,256]{1,0:T(8,128)(2,1)S(1)}, bf16[512,256]{1,0:T(8,128)(2,1)S(1)}, u32[]{:S(2)}, u32[]{:S(2)}) collective-permute-start(bf16[512,256]{1,0:T(8,128)(2,1)S(1)} %get-tuple-element.56), channel_id=1, source_target_pairs={{0,1},{1,0},{2,3},{3,2},{4,6},{5,7},{6,4},{7,5},{8,9},{9,8},{10,11... | collective-permute-start | bytes 786440 | tf_op jit(solution)/shard_map/ppermute | solution.py:32
  38.8 15.0 %collective-permute-start.7 = (bf16[544,256]{1,0:T(8,128)(2,1)S(1)}, bf16[544,256]{1,0:T(8,128)(2,1)S(1)}, u32[]{:S(2)}, u32[]{:S(2)}) collective-permute-start(bf16[544,256]{1,0:T(8,128)(2,1)S(1)} %get-tuple-element.50), channel_id=1, source_target_pairs={{0,2},{1,3},{2,0},{3,1},{4,5},{5,4},{6,7},{7,6},{8,10},{9,11},{10,... | collective-permute-start | bytes 835592 | tf_op jit(solution)/shard_map/ppermute | solution.py:32
  41.6 9.6 %collective-permute-start.18 = (bf16[512,256]{1,0:T(8,128)(2,1)S(1)}, bf16[512,256]{1,0:T(8,128)(2,1)S(1)}, u32[]{:S(2)}, u32[]{:S(2)}) collective-permute-start(bf16[512,256]{1,0:T(8,128)(2,1)S(1)} %get-tuple-element.57), channel_id=1, source_target_pairs={{0,1},{1,0},{2,3},{3,2},{4,6},{5,7},{6,4},{7,5},{8,9},{9,8},{10,11... | collective-permute-start | bytes 786440 | tf_op jit(solution)/shard_map/ppermute | solution.py:32
  42.2 11.6 %collective-permute-start.20 = (bf16[512,256]{1,0:T(8,128)(2,1)S(1)}, bf16[512,256]{1,0:T(8,128)(2,1)S(1)}, u32[]{:S(2)}, u32[]{:S(2)}) collective-permute-start(bf16[512,256]{1,0:T(8,128)(2,1)S(1)} %get-tuple-element.60), channel_id=1, source_target_pairs={{0,2},{1,3},{2,0},{3,1},{4,5},{5,4},{6,7},{7,6},{8,10},{9,11},{10,... | collective-permute-start | bytes 786440 | tf_op jit(solution)/shard_map/ppermute | solution.py:32
  48.0 7.5 %copy-start.1 = (bf16[3,128,16]{1,2,0:T(8,128)(2,1)S(1)}, bf16[3,128,16]{1,2,0:T(8,128)(2,1)}, u32[]{:S(2)}) copy-start(bf16[3,128,16]{1,2,0:T(8,128)(2,1)} %param.13) | copy-start | bytes 36868
  48.0 7.5 %copy-start.4 = (bf16[3,16]{1,0:T(4,128)(2,1)S(1)}, bf16[3,16]{1,0:T(4,128)(2,1)}, u32[]{:S(2)}) copy-start(bf16[3,16]{1,0:T(4,128)(2,1)} %refs_5_.3) | copy-start | bytes 292
  48.0 38.7 %collective-permute-start.15 = (bf16[512,512]{1,0:T(8,128)(2,1)S(1)}, bf16[512,512]{1,0:T(8,128)(2,1)S(1)}, u32[]{:S(2)}, u32[]{:S(2)}) collective-permute-start(bf16[512,512]{1,0:T(8,128)(2,1)S(1)} %get-tuple-element.52), channel_id=1, source_target_pairs={{0,1},{1,0},{2,3},{3,2},{4,6},{5,7},{6,4},{7,5},{8,9},{9,8},{10,11... | collective-permute-start | bytes 1572872 | tf_op jit(solution)/shard_map/ppermute | solution.py:32
  48.7 38.6 %collective-permute-start.16 = (bf16[512,512]{1,0:T(8,128)(2,1)S(1)}, bf16[512,512]{1,0:T(8,128)(2,1)S(1)}, u32[]{:S(2)}, u32[]{:S(2)}) collective-permute-start(bf16[512,512]{1,0:T(8,128)(2,1)S(1)} %get-tuple-element.53), channel_id=1, source_target_pairs={{0,2},{1,3},{2,0},{3,1},{4,5},{5,4},{6,7},{7,6},{8,10},{9,11},{10,... | collective-permute-start | bytes 1572872 | tf_op jit(solution)/shard_map/ppermute | solution.py:32
  51.4 36.4 %collective-permute-start.19 = (bf16[512,384]{1,0:T(8,128)(2,1)S(1)}, bf16[512,384]{1,0:T(8,128)(2,1)S(1)}, u32[]{:S(2)}, u32[]{:S(2)}) collective-permute-start(bf16[512,384]{1,0:T(8,128)(2,1)S(1)} %get-tuple-element.58), channel_id=1, source_target_pairs={{0,2},{1,3},{2,0},{3,1},{4,5},{5,4},{6,7},{7,6},{8,10},{9,11},{10,... | collective-permute-start | bytes 1179656 | tf_op jit(solution)/shard_map/ppermute | solution.py:32
  54.0 33.8 %collective-permute-start.21 = (bf16[512,384]{1,0:T(8,128)(2,1)S(1)}, bf16[512,384]{1,0:T(8,128)(2,1)S(1)}, u32[]{:S(2)}, u32[]{:S(2)}) collective-permute-start(bf16[512,384]{1,0:T(8,128)(2,1)S(1)} %get-tuple-element.61), channel_id=1, source_target_pairs={{0,1},{1,0},{2,3},{3,2},{4,6},{5,7},{6,4},{7,5},{8,9},{9,8},{10,11... | collective-permute-start | bytes 1179656 | tf_op jit(solution)/shard_map/ppermute | solution.py:32
  55.7 1.2 %collective-permute-start.8 = (bf16[144,128]{1,0:T(8,128)(2,1)S(1)}, bf16[144,128]{1,0:T(8,128)(2,1)S(1)}, u32[]{:S(2)}, u32[]{:S(2)}) collective-permute-start(bf16[144,128]{1,0:T(8,128)(2,1)S(1)} %shard_map.104.refs_0_), channel_id=1, source_target_pairs={{0,4},{4,0},{8,12},{12,8},{16,20},{20,16},{24,28},{28,24},{1,5},{5... | collective-permute-start | bytes 110600 | tf_op jit(solution)/shard_map/ppermute | solution.py:26
  56.9 4.2 %collective-permute-start.9 = (bf16[224,128]{1,0:T(8,128)(2,1)S(1)}, bf16[224,128]{1,0:T(8,128)(2,1)S(1)}, u32[]{:S(2)}, u32[]{:S(2)}) collective-permute-start(bf16[224,128]{1,0:T(8,128)(2,1)S(1)} %shard_map.105.refs_0_), channel_id=1, source_target_pairs={{0,8},{4,12},{8,0},{12,4},{16,24},{20,28},{24,16},{28,20},{1,9},{5... | collective-permute-start | bytes 172040 | tf_op jit(solution)/shard_map/ppermute | solution.py:26
  61.1 5.1 %collective-permute-start.10 = (bf16[224,128]{1,0:T(8,128)(2,1)S(1)}, bf16[224,128]{1,0:T(8,128)(2,1)S(1)}, u32[]{:S(2)}, u32[]{:S(2)}) collective-permute-start(bf16[224,128]{1,0:T(8,128)(2,1)S(1)} %shard_map.105.refs_0_), channel_id=1, source_target_pairs={{0,16},{4,20},{8,24},{12,28},{16,0},{20,4},{24,8},{28,12},{1,17},{... | collective-permute-start | bytes 172040 | tf_op jit(solution)/shard_map/ppermute | solution.py:26
  66.2 6.3 %collective-permute-start.11 = (bf16[224,128]{1,0:T(8,128)(2,1)S(1)}, bf16[224,128]{1,0:T(8,128)(2,1)S(1)}, u32[]{:S(2)}, u32[]{:S(2)}) collective-permute-start(bf16[224,128]{1,0:T(8,128)(2,1)S(1)} %shard_map.105.refs_0_), channel_id=1, source_target_pairs={{0,24},{4,28},{8,16},{12,20},{16,8},{20,12},{24,0},{28,4},{1,25},{... | collective-permute-start | bytes 172040 | tf_op jit(solution)/shard_map/ppermute | solution.py:26
  74.4 3.7 %collective-permute-start.12 = (bf16[32,128]{1,0:T(8,128)(2,1)S(1)}, bf16[32,128]{1,0:T(8,128)(2,1)S(1)}, u32[]{:S(2)}, u32[]{:S(2)}) collective-permute-start(bf16[32,128]{1,0:T(8,128)(2,1)S(1)} %get-tuple-element.51.refs_2_), channel_id=1, source_target_pairs={{0,1},{1,0},{2,3},{3,2},{4,6},{5,7},{6,4},{7,5},{8,9},{9,8},{10,11... | collective-permute-start | bytes 24584 | tf_op jit(solution)/shard_map/ppermute | solution.py:32
  78.1 3.7 %collective-permute-start.13 = (bf16[32,128]{1,0:T(8,128)(2,1)S(1)}, bf16[32,128]{1,0:T(8,128)(2,1)S(1)}, u32[]{:S(2)}, u32[]{:S(2)}) collective-permute-start(bf16[32,128]{1,0:T(8,128)(2,1)S(1)} %get-tuple-element.51.refs_2_), channel_id=1, source_target_pairs={{0,2},{1,3},{2,0},{3,1},{4,5},{5,4},{6,7},{7,6},{8,10},{9,11},{10,... | collective-permute-start | bytes 24584 | tf_op jit(solution)/shard_map/ppermute | solution.py:32
  81.7 4.5 %collective-permute-start.14 = (bf16[32,128]{1,0:T(8,128)(2,1)S(1)}, bf16[32,128]{1,0:T(8,128)(2,1)S(1)}, u32[]{:S(2)}, u32[]{:S(2)}) collective-permute-start(bf16[32,128]{1,0:T(8,128)(2,1)S(1)} %get-tuple-element.51.refs_2_), channel_id=1, source_target_pairs={{0,3},{1,2},{2,1},{3,0},{4,7},{5,6},{6,5},{7,4},{8,11},{9,10},{10,... | collective-permute-start | bytes 24584 | tf_op jit(solution)/shard_map/ppermute | solution.py:32
  86.3 5.0 %collective-permute-start.22 = (bf16[512,128]{1,0:T(8,128)(2,1)S(1)}, bf16[512,128]{1,0:T(8,128)(2,1)S(1)}, u32[]{:S(2)}, u32[]{:S(2)}) collective-permute-start(bf16[512,128]{1,0:T(8,128)(2,1)S(1)} %get-tuple-element.63), channel_id=1, source_target_pairs={{0,2},{1,3},{2,0},{3,1},{4,5},{5,4},{6,7},{7,6},{8,10},{9,11},{10,... | collective-permute-start | bytes 393224 | tf_op jit(solution)/shard_map/ppermute | solution.py:32
  86.7 5.0 %collective-permute-start.23 = (bf16[512,128]{1,0:T(8,128)(2,1)S(1)}, bf16[512,128]{1,0:T(8,128)(2,1)S(1)}, u32[]{:S(2)}, u32[]{:S(2)}) collective-permute-start(bf16[512,128]{1,0:T(8,128)(2,1)S(1)} %get-tuple-element.64), channel_id=1, source_target_pairs={{0,1},{1,0},{2,3},{3,2},{4,6},{5,7},{6,4},{7,5},{8,9},{9,8},{10,11... | collective-permute-start | bytes 393224 | tf_op jit(solution)/shard_map/ppermute | solution.py:32
